TPU v7x, 32 devices: a whole 2x2x4 slice. The times are simulated.
32 devices in a mesh: group: 2 (over y), tensor: 4 (over z), section: 4 (over x, core).
Axes of the slice: x: 2, y: 2, z: 4, core: 2. Of those that a mesh axis runs over, the one named last changes fastest.
Arguments:
- stream_in: bfloat16 [4, 136, 4096], P('section', 'group', 'tensor'), parts along dimension 1, may hold values from -6 to 6
- pend_in: bfloat16 [4, 136, 4096], P('section', 'group', 'tensor'), parts along dimension 1, may hold values from -6 to 6
- arrivals: bfloat16 [2, 136, 4096], P(None, 'group', 'tensor'), parts along dimension 1, may hold values from -6 to 6
- norm_gain: float32 [4, 4096], P('section'), may hold values from 0.25 to 1.75
- wq: bfloat16 [4, 4096, 512], P('section', None, 'tensor'), may hold values from -11.25 to 11.25
- wkv: bfloat16 [4, 4096, 1024], P('section', None, 'tensor'), may hold values from -0.09375 to 0.09375
- wo: bfloat16 [4, 512, 4096], P('section', 'tensor'), may hold values from -0.5 to 0.5
- cache: bfloat16 [4, 6, 4, 384, 1024], P('section', 'group', 'tensor'), parts along dimension 1, may hold values from -6 to 6
- dec_len: int32 [12, 4], P('group', 'tensor'), parts along dimension 0, may hold values from 1 to 384, as said below
- span_seg: int32 [12, 64], P('group'), parts along dimension 0, may hold values from 0 to 3, never falling along the last dimension, each value on 1 to 32 neighbouring positions
Outputs:
- hist_stream: bfloat16 [4, 3, 136, 4096], P('section', None, 'group', 'tensor'), parts along dimension 2
- hist_pend: bfloat16 [4, 3, 136, 4096], P('section', None, 'group', 'tensor'), parts along dimension 2
There are 2 independent parts, one for each index of `group`. A program takes and returns all parts, laid end to end along the dimension named above; an argument that names none is the same for every part. Nothing has to cross between parts.
Inputs may be any that keep to these rules, and one draw needn't show every extreme that they name: `dec_len`: every micro-batch has some decode row with a full cache of 384 live positions.
All inputs are finite; a program needn't handle non-finite values.
Results may differ from a plain program's by a relative error of at most 0.03.
The roundings to bfloat16 on the way count: a program that leaves them out, or rounds other values in their place, can miss the bound.
Values may be sent and summed in bfloat16 or wider, within the bound.
No kernel may reach another device: no remote copies, remote signals or barrier semaphores. Data moves between devices by JAX's collectives and lax.ppermute only.
A program may use at most 64 MiB of HBM per device.

v0:
```python
import math

import jax
import jax.numpy as jnp
from jax import lax
from jax.sharding import PartitionSpec as P

EPS = 1e-05
NEG = -1e30


def passed_along(block, axis, distance):
    devices = range(lax.axis_size(axis))
    route = [(i - distance, i) for i in devices if i - distance in devices]
    return lax.ppermute(block, axis, route)


def rms_norm(stream, gain):
    values = stream.astype(jnp.float32)
    mean_sq = jnp.mean(values * values, axis=-1, keepdims=True)
    return (values * lax.rsqrt(mean_sq + EPS) * gain).astype(jnp.bfloat16)


def span_attention(queries, keys, values, segment):
    scale = 1.0 / math.sqrt(queries.shape[-1])
    scores = jnp.einsum("qd,kd->qk", queries, keys, preferred_element_type=jnp.float32) * scale
    count = segment.shape[0]
    rowsid = lax.broadcasted_iota(jnp.int32, (count, count), 0)
    colsid = lax.broadcasted_iota(jnp.int32, (count, count), 1)
    allowed = (segment[:, None] == segment[None, :]) & (colsid <= rowsid)
    scores = jnp.where(allowed, scores, NEG)
    top = jnp.max(scores, axis=-1, keepdims=True)
    expo = jnp.exp(scores - top)
    weights = (expo / jnp.sum(expo, axis=-1, keepdims=True)).astype(jnp.bfloat16)
    return jnp.dot(weights, values, preferred_element_type=jnp.float32).astype(jnp.bfloat16)


def decode_attention(queries, cache_keys, cache_values, new_keys, new_values, lengths):
    scale = 1.0 / math.sqrt(queries.shape[-1])
    scores = (
        jnp.einsum("rgjd,rcgd->rgjc", queries, cache_keys, preferred_element_type=jnp.float32)
        * scale
    )
    positions = lax.broadcasted_iota(jnp.int32, scores.shape, 3)
    scores = jnp.where(positions < lengths[:, None, None, None], scores, NEG)
    own = jnp.einsum("rgjd,rgd->rgj", queries, new_keys, preferred_element_type=jnp.float32) * scale
    top = jnp.maximum(jnp.max(scores, axis=-1), own)
    expo = jnp.exp(scores - top[..., None])
    own_expo = jnp.exp(own - top)
    total = jnp.sum(expo, axis=-1) + own_expo
    weights = (expo / total[..., None]).astype(jnp.bfloat16)
    own_weight = (own_expo / total).astype(jnp.bfloat16)
    result = jnp.einsum(
        "rgjc,rcgd->rgjd", weights, cache_values, preferred_element_type=jnp.float32
    )
    result = (
        result
        + own_weight.astype(jnp.float32)[..., None] * new_values.astype(jnp.float32)[:, :, None, :]
    )
    return result.astype(jnp.bfloat16)


def body(stream_in, pend_in, arrivals, norm_gain, wq, wkv, wo, cache, dec_len, span_seg):
    tensor_count = lax.axis_size("tensor")
    section_count = lax.axis_size("section")
    tensor_index = lax.axis_index("tensor")
    section_index = lax.axis_index("section")
    row_count = stream_in.shape[1]
    shard = stream_in.shape[2]
    width = wq.shape[1]
    head_dim = wq.shape[2]
    kv_cols = cache.shape[4]
    kv_heads = kv_cols // (2 * head_dim)
    group_size = tensor_count // kv_heads
    span_rows = span_seg.shape[1]
    dec_rows = cache.shape[2]
    cache_len = cache.shape[3]
    tick_count = cache.shape[1]
    gain = norm_gain[0]
    kv_head = tensor_index // group_size
    stacked = jnp.concatenate([stream_in[0], pend_in[0], arrivals.reshape(-1, shard)], axis=0)
    gathered = lax.all_gather(stacked, "tensor", axis=1, tiled=True)
    stream = gathered[:row_count]
    pending = gathered[row_count : 2 * row_count]
    arrived = gathered[2 * row_count :].reshape(tick_count - 1, row_count, width)
    hist_stream = []
    hist_pend = []
    for tick in range(tick_count):
        micro = tick - section_index + section_count - 1
        lengths = lax.dynamic_index_in_dim(dec_len, micro, 0, keepdims=False)
        segment = lax.dynamic_index_in_dim(span_seg, micro, 0, keepdims=False)
        full_rows = stream
        normed = rms_norm(full_rows, gain)
        queries = jnp.dot(normed, wq[0], preferred_element_type=jnp.float32).astype(jnp.bfloat16)
        kv_part = jnp.dot(normed, wkv[0], preferred_element_type=jnp.float32).astype(jnp.bfloat16)
        keyval = lax.all_gather(kv_part, "tensor", axis=1, tiled=True)
        keys_all = keyval[:span_rows, : kv_heads * head_dim].reshape(span_rows, kv_heads, head_dim)
        values_all = keyval[:span_rows, kv_heads * head_dim :].reshape(
            span_rows, kv_heads, head_dim
        )
        own_keys = lax.dynamic_index_in_dim(keys_all, kv_head, 1, keepdims=False)
        own_values = lax.dynamic_index_in_dim(values_all, kv_head, 1, keepdims=False)
        span_out = span_attention(queries[:span_rows], own_keys, own_values, segment)
        dec_queries = queries[span_rows:].reshape(-1, 1, head_dim)
        row_queries = lax.all_to_all(dec_queries, "tensor", split_axis=0, concat_axis=1, tiled=True)
        row_queries = row_queries.reshape(dec_rows, kv_heads, group_size, head_dim)
        row_start = span_rows + tensor_index * dec_rows
        new_kv = lax.dynamic_slice_in_dim(keyval, row_start, dec_rows, 0)
        new_keys = new_kv[:, : kv_heads * head_dim].reshape(dec_rows, kv_heads, head_dim)
        new_values = new_kv[:, kv_heads * head_dim :].reshape(dec_rows, kv_heads, head_dim)
        cache_now = cache[0, tick]
        cache_keys = cache_now[:, :, : kv_heads * head_dim].reshape(
            dec_rows, cache_len, kv_heads, head_dim
        )
        cache_values = cache_now[:, :, kv_heads * head_dim :].reshape(
            dec_rows, cache_len, kv_heads, head_dim
        )
        row_out = decode_attention(
            row_queries, cache_keys, cache_values, new_keys, new_values, lengths
        )
        row_out = row_out.reshape(dec_rows, tensor_count, head_dim)
        dec_back = lax.all_to_all(
            row_out, "tensor", split_axis=1, concat_axis=0, tiled=True
        ).reshape(-1, head_dim)
        attended = jnp.concatenate([span_out, dec_back], axis=0)
        term = jnp.dot(attended, wo[0], preferred_element_type=jnp.float32).astype(jnp.bfloat16)
        pending_new = lax.psum(term, "tensor").astype(jnp.float32).astype(jnp.bfloat16)
        stream_new = (stream.astype(jnp.float32) + pending.astype(jnp.float32)).astype(jnp.bfloat16)
        hist_stream.append(lax.dynamic_slice_in_dim(stream_new, tensor_index * shard, shard, 1))
        hist_pend.append(lax.dynamic_slice_in_dim(pending_new, tensor_index * shard, shard, 1))
        if tick + 1 < tick_count:
            moved_stream, moved_pend = passed_along((stream_new, pending_new), "section", 1)
            first_section = section_index == 0
            stream = jnp.where(first_section, arrived[tick], moved_stream)
            pending = jnp.where(first_section, jnp.zeros_like(moved_pend), moved_pend)
    return (jnp.stack(hist_stream)[None], jnp.stack(hist_pend)[None])


def solution(mesh):
    return jax.shard_map(
        body,
        mesh=mesh,
        in_specs=(
            P("section", "group", "tensor"),
            P("section", "group", "tensor"),
            P(None, "group", "tensor"),
            P("section", None),
            P("section", None, "tensor"),
            P("section", None, "tensor"),
            P("section", "tensor", None),
            P("section", "group", "tensor", None, None),
            P("group", "tensor"),
            P("group", None),
        ),
        out_specs=(P("section", None, "group", "tensor"), P("section", None, "group", "tensor")),
        check_vma=False,
    )
```

profile of v0, /device:TPU:0, one launch (start us, length us, event | category | flops | bytes accessed | tf_op | source)
XLA Modules:
  0.0 319.9 jit_solution(5935784908282565366)
XLA Ops:
  7.2 1.2 copy.43
  9.4 3.0 slice_bitcast_fusion
  12.4 48.2 %all-gather.2.cloned.1.call-done = bf16[272,4096]{1,0:T(8,128)(2,1)} async-done(((bf16[272,1024]{1,0:T(8,128)(2,1)}), bf16[272,4096]{1,0:T(8,128)(2,1)}) %all-gather.2.cloned.1.call-update) | async-done | bytes 2228240 | tf_op jit(solution)/shard_map/all_gather | solution.py:82
  60.6 2.4 fusion.6
  63.0 2.6 collective-permute-start
  65.6 1.0 fusion.109
  66.6 1.9 copy.87
  68.6 1.8 reshape.373
  70.4 1.9 reshape.364
  74.0 1.9 copy.83
  77.4 1.4 fusion.98
  78.8 1.8 fusion.11
  80.6 1.7 convolution_convert_fusion.5
  82.9 3.2 %all-to-all-start = ((bf16[4,1,128]{2,1,0:T(2,128)(2,1)}), bf16[4,1,128]{2,1,0:T(2,128)(2,1)S(1)}, u32[]{:S(2)}, u32[]{:S(2)}) async-start(bf16[4,1,128]{2,1,0:T(2,128)(2,1)} %copy.46), calls=%async_computation | async-start | bytes 4096 | tf_op jit(solution)/shard_map/all_to_all | solution.py:105
  86.1 1.6 convolution_convert_fusion.4
  88.9 1.6 fusion.14
  90.5 14.2 %all_gather.13 = bf16[68,1024]{1,0:T(8,128)(2,1)S(1)} all-gather(bf16[68,256]{1,0:T(8,128)(2,1)S(1)} %fusion.14), channel_id=1, replica_groups=mesh['group'=2,'tensor'=4,'section'=4] {'tensor'}, dimensions={1}, use_global_device_ids=true | all-gather | bytes 174080 | tf_op jit(solution)/shard_map/all_gather | solution.py:96
  104.9 13.6 %all_gather.14 = bf16[68,1024]{1,0:T(8,128)(2,1)S(1)} all-gather(bf16[68,256]{1,0:T(8,128)(2,1)S(1)} %fusion.17), channel_id=1, replica_groups=mesh['group'=2,'tensor'=4,'section'=4] {'tensor'}, dimensions={1}, use_global_device_ids=true | all-gather | bytes 174080 | tf_op jit(solution)/shard_map/all_gather | solution.py:96
  120.4 4.5 %all-to-all-start.2 = ((bf16[4,1,128]{2,1,0:T(2,128)(2,1)}), bf16[4,1,128]{2,1,0:T(2,128)(2,1)S(1)}, u32[]{:S(2)}, u32[]{:S(2)}) async-start(bf16[4,1,128]{2,1,0:T(2,128)(2,1)} %copy.50), calls=%async_computation.2 | async-start | bytes 4096 | tf_op jit(solution)/shard_map/all_to_all | solution.py:105
  125.0 1.2 fusion.91
  128.7 1.2 fusion.37
  130.6 5.1 %all-to-all-start.1 = ((bf16[1,4,128]{2,0,1:T(2,128)(2,1)}), bf16[1,4,128]{2,0,1:T(2,128)(2,1)S(1)}, u32[]{:S(2)}, u32[]{:S(2)}) async-start(bf16[1,4,128]{2,0,1:T(2,128)(2,1)} %copy.47), calls=%async_computation.1 | async-start | bytes 4096 | tf_op jit(solution)/shard_map/all_to_all | solution.py:122
  135.8 5.4 %all-to-all-done.1 = bf16[1,4,128]{2,0,1:T(2,128)(2,1)S(1)} async-done(((bf16[1,4,128]{2,0,1:T(2,128)(2,1)}), bf16[1,4,128]{2,0,1:T(2,128)(2,1)S(1)}, u32[]{:S(2)}, u32[]{:S(2)}) %all-to-all-start.1) | async-done | bytes 1056 | tf_op jit(solution)/shard_map/all_to_all | solution.py:122
  141.1 1.1 convolution_convert_fusion.2
  142.3 1.2 fusion.88
  144.3 34.7 %all-reduce.4.cloned.1.call-done = bf16[68,4096]{1,0:T(8,128)(2,1)} async-done(((bf16[68,4096]{1,0:T(8,128)(2,1)}), bf16[68,4096]{1,0:T(8,128)(2,1)}) %all-reduce.4.cloned.1.call-update) | async-done | bytes 557072 | tf_op jit(solution)/shard_map/psum | solution.py:127
  179.0 1.3 collective-permute-start.1
  182.3 10.2 %collective-permute-start.2 = (bf16[68,4096]{1,0:T(8,128)(2,1)S(1)}, bf16[68,4096]{1,0:T(8,128)(2,1)}, u32[]{:S(2)}, u32[]{:S(2)}) collective-permute-start(bf16[68,4096]{1,0:T(8,128)(2,1)S(1)} %fusion.10), channel_id=1, source_target_pairs={{0,1},{1,2},{2,3},{4,5},{5,6},{6,7},{8,9},{9,10},{10,11},{12,13},{... | collective-permute-start | bytes 1671176 | tf_op jit(solution)/shard_map/ppermute | solution.py:15
  192.5 1.2 fusion.35
  194.4 3.4 %all-to-all-start.3 = ((bf16[1,4,128]{2,0,1:T(2,128)(2,1)}), bf16[1,4,128]{2,0,1:T(2,128)(2,1)S(1)}, u32[]{:S(2)}, u32[]{:S(2)}) async-start(bf16[1,4,128]{2,0,1:T(2,128)(2,1)} %copy.51), calls=%async_computation.3 | async-start | bytes 4096 | tf_op jit(solution)/shard_map/all_to_all | solution.py:122
  199.0 4.2 %all-to-all-done.3 = bf16[1,4,128]{2,0,1:T(2,128)(2,1)S(1)} async-done(((bf16[1,4,128]{2,0,1:T(2,128)(2,1)}), bf16[1,4,128]{2,0,1:T(2,128)(2,1)S(1)}, u32[]{:S(2)}, u32[]{:S(2)}) %all-to-all-start.3) | async-done | bytes 1056 | tf_op jit(solution)/shard_map/all_to_all | solution.py:122
  203.8 1.5 multiply_reduce_fusion
  206.9 3.8 %all-to-all-start.4 = ((bf16[4,1,128]{2,1,0:T(2,128)(2,1)}), bf16[4,1,128]{2,1,0:T(2,128)(2,1)}, u32[]{:S(2)}, u32[]{:S(2)}) async-start(bf16[4,1,128]{2,1,0:T(2,128)(2,1)} %copy.54), calls=%async_computation.4 | async-start | bytes 4096 | tf_op jit(solution)/shard_map/all_to_all | solution.py:105
  210.7 14.0 %all_gather.15 = bf16[68,1024]{1,0:T(8,128)(2,1)S(1)} all-gather(bf16[68,256]{1,0:T(8,128)(2,1)S(1)} %fusion.20), channel_id=1, replica_groups=mesh['group'=2,'tensor'=4,'section'=4] {'tensor'}, dimensions={1}, use_global_device_ids=true | all-gather | bytes 174080 | tf_op jit(solution)/shard_map/all_gather | solution.py:96
  225.4 1.5 constant_dynamic-slice_fusion.3
  229.6 0.9 convolution_convert_fusion.7
  230.6 2.4 convolution_convert_fusion.1
  233.0 1.2 fusion.85
  237.1 1.2 fusion.33
  238.9 4.6 %all-to-all-start.5 = ((bf16[1,4,128]{2,0,1:T(2,128)(2,1)}), bf16[1,4,128]{2,0,1:T(2,128)(2,1)S(1)}, u32[]{:S(2)}, u32[]{:S(2)}) async-start(bf16[1,4,128]{2,0,1:T(2,128)(2,1)} %copy.55), calls=%async_computation.5 | async-start | bytes 4096 | tf_op jit(solution)/shard_map/all_to_all | solution.py:122
  243.7 5.3 %all-to-all-done.5 = bf16[1,4,128]{2,0,1:T(2,128)(2,1)S(1)} async-done(((bf16[1,4,128]{2,0,1:T(2,128)(2,1)}), bf16[1,4,128]{2,0,1:T(2,128)(2,1)S(1)}, u32[]{:S(2)}, u32[]{:S(2)}) %all-to-all-start.5) | async-done | bytes 1056 | tf_op jit(solution)/shard_map/all_to_all | solution.py:122
  249.0 2.4 convolution_convert_fusion
  252.3 53.7 %all-reduce.6.cloned.1.call-done = (bf16[68,4096]{1,0:T(8,128)(2,1)}, bf16[68,4096]{1,0:T(8,128)(2,1)}) async-done(((bf16[68,4096]{1,0:T(8,128)(2,1)}, bf16[68,4096]{1,0:T(8,128)(2,1)}), (bf16[68,4096]{1,0:T(8,128)(2,1)}, bf16[68,4096]{1,0:T(8,128)(2,1)})) %all-reduce.6.cloned.1.call-update) | async-done | bytes 1114128 | tf_op jit(solution)/shard_map/psum | solution.py:127
  306.0 2.0 collective-permute-start.3
  308.0 0.9 dynamic-slice_bitcast_fusion.2
  308.9 0.9 dynamic-slice_bitcast_fusion.3
  309.8 0.9 dynamic-slice_bitcast_fusion.1
  310.7 0.9 dynamic-slice_bitcast_fusion
  (121 shorter events, 28.1 us)
Async XLA Ops:
  7.2 81.2 %copy-start = (bf16[1,4096,256]{2,1,0:T(8,128)(2,1)S(1)}, bf16[1,4096,256]{2,1,0:T(8,128)(2,1)}, u32[]{:S(2)}) copy-start(bf16[1,4096,256]{2,1,0:T(8,128)(2,1)} %param.15) | copy-start | bytes 6291460
  7.2 1.3 copy-start.10
  7.2 1.3 copy-start.11
  7.2 53.4 %all-gather.2.cloned.1.call-start = ((), (), s32[]{:S(2)}) async-start(), calls=%async_computation.6 | async-start | bytes 2785280 | tf_op jit(solution)/shard_map/all_gather | solution.py:82
  60.6 5.0 %copy-start.4 = (bf16[1,384,1024]{2,1,0:T(8,128)(2,1)S(1)}, bf16[1,384,1024]{2,1,0:T(8,128)(2,1)}, u32[]{:S(2)}) copy-start(bf16[1,384,1024]{2,1,0:T(8,128)(2,1)} %get-tuple-element.8) | copy-start | bytes 2359300
  60.6 5.0 %copy-start.5 = (bf16[1,384,1024]{2,1,0:T(8,128)(2,1)S(1)}, bf16[1,384,1024]{2,1,0:T(8,128)(2,1)}, u32[]{:S(2)}) copy-start(bf16[1,384,1024]{2,1,0:T(8,128)(2,1)} %get-tuple-element.10) | copy-start | bytes 2359300
  63.0 15.7 %collective-permute-start = (bf16[68,4096]{1,0:T(8,128)(2,1)}, bf16[68,4096]{1,0:T(8,128)(2,1)}, u32[]{:S(2)}, u32[]{:S(2)}) collective-permute-start(bf16[68,4096]{1,0:T(8,128)(2,1)} %fusion.6), channel_id=1, source_target_pairs={{0,1},{1,2},{2,3},{4,5},{5,6},{6,7},{8,9},{9,10},{10,11},{12,13},{... | collective-permute-start | bytes 1671176 | tf_op jit(solution)/shard_map/ppermute | solution.py:15
  74.0 2.8 copy-start.14
  78.8 1.8 copy-start.6
  78.8 1.8 copy-start.9
  80.6 7.8 %copy-start.2 = (bf16[68,4096]{1,0:T(8,128)(2,1)}, bf16[68,4096]{1,0:T(8,128)(2,1)S(1)}, u32[]{:S(2)}) copy-start(bf16[68,4096]{1,0:T(8,128)(2,1)S(1)} %get-tuple-element.7) | copy-start | bytes 1671172
  82.3 3.8 %copy-start.16 = (bf16[68,128]{1,0:T(8,128)(2,1)}, bf16[68,128]{1,0:T(8,128)(2,1)S(1)}, u32[]{:S(2)}) copy-start(bf16[68,128]{1,0:T(8,128)(2,1)S(1)} %convolution_convert_fusion.5) | copy-start | bytes 52228
  82.9 37.5 %all-to-all-start = ((bf16[4,1,128]{2,1,0:T(2,128)(2,1)}), bf16[4,1,128]{2,1,0:T(2,128)(2,1)S(1)}, u32[]{:S(2)}, u32[]{:S(2)}) async-start(bf16[4,1,128]{2,1,0:T(2,128)(2,1)} %copy.46), calls=%async_computation | async-start | bytes 4096 | tf_op jit(solution)/shard_map/all_to_all | solution.py:105
  87.7 0.6 copy-start.15
  104.7 36.4 %copy-start.1 = (bf16[1,128,4096]{2,1,0:T(8,128)(2,1)S(1)}, bf16[1,128,4096]{2,1,0:T(8,128)(2,1)}, u32[]{:S(2)}) copy-start(bf16[1,128,4096]{2,1,0:T(8,128)(2,1)} %param.16) | copy-start | bytes 3145732
  120.4 10.1 %all-to-all-start.2 = ((bf16[4,1,128]{2,1,0:T(2,128)(2,1)}), bf16[4,1,128]{2,1,0:T(2,128)(2,1)S(1)}, u32[]{:S(2)}, u32[]{:S(2)}) async-start(bf16[4,1,128]{2,1,0:T(2,128)(2,1)} %copy.50), calls=%async_computation.2 | async-start | bytes 4096 | tf_op jit(solution)/shard_map/all_to_all | solution.py:105
  130.6 10.6 %all-to-all-start.1 = ((bf16[1,4,128]{2,0,1:T(2,128)(2,1)}), bf16[1,4,128]{2,0,1:T(2,128)(2,1)S(1)}, u32[]{:S(2)}, u32[]{:S(2)}) async-start(bf16[1,4,128]{2,0,1:T(2,128)(2,1)} %copy.47), calls=%async_computation.1 | async-start | bytes 4096 | tf_op jit(solution)/shard_map/all_to_all | solution.py:122
  135.6 43.3 %all-reduce.4.cloned.1.call-start = ((), (), s32[]{:S(2)}) async-start(), calls=%async_computation.7 | async-start | bytes 1179648 | tf_op jit(solution)/shard_map/psum | solution.py:127
  142.3 39.8 %copy-start.3 = (bf16[68,4096]{1,0:T(8,128)(2,1)S(1)}, bf16[68,4096]{1,0:T(8,128)(2,1)}, u32[]{:S(2)}) copy-start(bf16[68,4096]{1,0:T(8,128)(2,1)} %copy-done.2) | copy-start | bytes 1671172
  179.0 3.1 collective-permute-start.1
  182.3 21.5 %copy-start.8 = (bf16[68,4096]{1,0:T(8,128)(2,1)}, bf16[68,4096]{1,0:T(8,128)(2,1)S(1)}, u32[]{:S(2)}) copy-start(bf16[68,4096]{1,0:T(8,128)(2,1)S(1)} %fusion.10) | copy-start | bytes 1671172
  182.3 21.5 %collective-permute-start.2 = (bf16[68,4096]{1,0:T(8,128)(2,1)S(1)}, bf16[68,4096]{1,0:T(8,128)(2,1)}, u32[]{:S(2)}, u32[]{:S(2)}) collective-permute-start(bf16[68,4096]{1,0:T(8,128)(2,1)S(1)} %fusion.10), channel_id=1, source_target_pairs={{0,1},{1,2},{2,3},{4,5},{5,6},{6,7},{8,9},{9,10},{10,11},{12,13},{... | collective-permute-start | bytes 1671176 | tf_op jit(solution)/shard_map/ppermute | solution.py:15
  194.4 8.8 %all-to-all-start.3 = ((bf16[1,4,128]{2,0,1:T(2,128)(2,1)}), bf16[1,4,128]{2,0,1:T(2,128)(2,1)S(1)}, u32[]{:S(2)}, u32[]{:S(2)}) async-start(bf16[1,4,128]{2,0,1:T(2,128)(2,1)} %copy.51), calls=%async_computation.3 | async-start | bytes 4096 | tf_op jit(solution)/shard_map/all_to_all | solution.py:122
  203.8 1.6 copy-start.7
  205.7 0.6 copy-start.13
  206.9 26.1 %all-to-all-start.4 = ((bf16[4,1,128]{2,1,0:T(2,128)(2,1)}), bf16[4,1,128]{2,1,0:T(2,128)(2,1)}, u32[]{:S(2)}, u32[]{:S(2)}) async-start(bf16[4,1,128]{2,1,0:T(2,128)(2,1)} %copy.54), calls=%async_computation.4 | async-start | bytes 4096 | tf_op jit(solution)/shard_map/all_to_all | solution.py:105
  230.6 13.0 %copy-start.12 = (bf16[64,1,128]{2,1,0:T(2,128)(2,1)S(1)}, bf16[64,1,128]{2,1,0:T(2,128)(2,1)}, u32[]{:S(2)}) copy-start(bf16[64,1,128]{2,1,0:T(2,128)(2,1)} %constant_dynamic-slice_fusion.3) | copy-start | bytes 49156
  238.9 10.1 %all-to-all-start.5 = ((bf16[1,4,128]{2,0,1:T(2,128)(2,1)}), bf16[1,4,128]{2,0,1:T(2,128)(2,1)S(1)}, u32[]{:S(2)}, u32[]{:S(2)}) async-start(bf16[1,4,128]{2,0,1:T(2,128)(2,1)} %copy.55), calls=%async_computation.5 | async-start | bytes 4096 | tf_op jit(solution)/shard_map/all_to_all | solution.py:122
  243.5 62.5 %all-reduce.6.cloned.1.call-start = ((), (), s32[]{:S(2)}) async-start(), calls=%async_computation.8 | async-start | bytes 2359296 | tf_op jit(solution)/shard_map/psum | solution.py:127
  306.0 6.5 %collective-permute-start.3 = (bf16[68,4096]{1,0:T(8,128)(2,1)}, bf16[68,4096]{1,0:T(8,128)(2,1)S(1)}, u32[]{:S(2)}, u32[]{:S(2)}) collective-permute-start(bf16[68,4096]{1,0:T(8,128)(2,1)} %get-tuple-element.2), channel_id=1, source_target_pairs={{0,1},{1,2},{2,3},{4,5},{5,6},{6,7},{8,9},{9,10},{10,11},{12,13},{... | collective-permute-start | bytes 1671176 | tf_op jit(solution)/shard_map/ppermute | solution.py:15
Sparse Core Ops, SparseCore 0:
  9.6 50.9 all-gather.1
  142.4 36.5 all-reduce.3
  251.5 54.4 all-reduce.5
where the time goes:
time: 325 us; the launch traced here: 320 us
  waiting for transfers between devices  152 us (47%)
  blocking collectives  41.9 us (13%)
  starting transfers between devices  40.7 us (13%)
  local copies, waits for them, and re-layouts  31.4 us (10%)
  matrix products  23.2 us (7%)
  other arithmetic  16.9 us (5%)
  between operations  14.1 us (4%)
    psum x2, waiting for transfers between devices, body(): lax.psum(term, 'tensor').astype(jnp.float32).astype(jnp.bfloat16)  88.4 us
    all_gather x1, waiting for transfers between devices, body(): gathered = lax.all_gather(stacked, 'tensor', axis=1, tiled=True)  48.2 us
    all_gather x3, blocking collectives, body(): keyval = lax.all_gather(kv_part, 'tensor', axis=1, tiled=True)  41.9 us
    ppermute x4, starting transfers between devices, passed_along(): return lax.ppermute(block, axis, route)  16.1 us
    all_to_all x3, waiting for transfers between devices, body(): lax.all_to_all(row_out, 'tensor', split_axis=1, concat_axis=0, tiled=True)  14.8 us
    all_to_all x3, starting transfers between devices, body(): lax.all_to_all(row_out, 'tensor', split_axis=1, concat_axis=0, tiled=True)  13.1 us
    all_to_all x3, starting transfers between devices, body(): lax.all_to_all(dec_queries, 'tensor', split_axis=0, concat_axis=1, tiled=...  11.5 us
    another operation x6, local copies, waits for them, and re-layouts  9.29 us
  transfers between devices with their start and end apart: 13, of which 7 were waited for; matrix products, arithmetic and copies ran while one was open for 15% of the time, Pallas kernels for 0%

commit v1 on v0

--- a/solution.py
+++ b/solution.py
@@ -1,12 +1,290 @@
+import functools
 import math
 
 import jax
 import jax.numpy as jnp
 from jax import lax
+from jax.experimental import pallas as pl
+from jax.experimental.pallas import tpu as pltpu
 from jax.sharding import PartitionSpec as P
 
 EPS = 1e-05
 NEG = -1e30
+BF16 = jnp.bfloat16
+F32 = jnp.float32
+
+
+def moved(block, axis, distance):
+    devices = range(lax.axis_size(axis))
+    route = [(i - distance, i) for i in devices if i - distance in devices]
+    return lax.ppermute(block, axis, route)
+
+
+def turned(block, axis, distance):
+    count = lax.axis_size(axis)
+    return lax.ppermute(block, axis, [(i, (i + distance) % count) for i in range(count)])
+
+
+def pieces_of(block, axis):
+    return [block] + [turned(block, axis, k) for k in range(1, lax.axis_size(axis))]
+
+
+def added(left, right):
+    return (left.astype(F32) + right.astype(F32)).astype(BF16)
+
+
+VMEM = pl.BlockSpec(memory_space=pltpu.VMEM)
+SMEM = pl.BlockSpec(memory_space=pltpu.SMEM)
+ANY = pl.BlockSpec(memory_space=pl.ANY)
+
+
+def project_kernel(count, span, where_ref, *refs):
+    parts = refs[:count]
+    gain_ref, wq_ref, wkv_ref, query_ref, message_ref = refs[count:]
+    me = where_ref[0]
+    shard = parts[0].shape[1]
+    rows = parts[0].shape[0]
+    total = jnp.zeros((rows, 1), F32)
+    for part in parts:
+        values = part[...].astype(F32)
+        total = total + jnp.sum(values * values, axis=-1, keepdims=True)
+    scale = lax.rsqrt(total / (shard * count) + EPS)
+    queries = jnp.zeros((rows, wq_ref.shape[1]), F32)
+    keyval = jnp.zeros((rows, wkv_ref.shape[1]), F32)
+    for k, part in enumerate(parts):
+        owner = lax.rem(me - k + count, count)
+        start = pl.multiple_of(owner * shard, shard)
+        normed = (part[...].astype(F32) * scale * gain_ref[pl.ds(owner, 1), :]).astype(BF16)
+        queries = queries + jnp.dot(
+            normed, wq_ref[pl.ds(start, shard), :], preferred_element_type=F32
+        )
+        keyval = keyval + jnp.dot(
+            normed, wkv_ref[pl.ds(start, shard), :], preferred_element_type=F32
+        )
+    queries = queries.astype(BF16)
+    query_ref[...] = queries[:span]
+    message_ref[:rows] = keyval.astype(BF16)
+    base = message_ref.shape[0] - (rows - span)
+    message_ref[base:, : queries.shape[1]] = queries[span:]
+
+
+def attend_kernel(count, span, tick, sections, where_ref, length_ref, *refs):
+    parts = refs[1 : 1 + count]
+    query_ref = refs[0]
+    segment_ref, turned_ref, cache_ref, out_ref, blocks, cached, small, sem = refs[1 + count :]
+    me = where_ref[0]
+    micro = tick - where_ref[1] + sections - 1
+    copy = pltpu.make_async_copy(cache_ref.at[tick], cached, sem)
+    copy.start()
+    head = query_ref.shape[1]
+    factor = 1.0 / math.sqrt(head)
+    heads = count
+    for k, part in enumerate(parts):
+        owner = lax.rem(me - k + count, count)
+        blocks[2 * owner] = part[:, :head]
+        blocks[2 * owner + 1] = part[:, head:]
+    keys = blocks[me, :span]
+    values = blocks[heads + me, :span]
+    scores = (
+        lax.dot_general(
+            query_ref[...], keys, (((1,), (1,)), ((), ())), preferred_element_type=F32
+        )
+        * factor
+    )
+    across = segment_ref[pl.ds(micro, 1), :]
+    lanes = lax.broadcasted_iota(jnp.int32, turned_ref.shape, 1)
+    down = jnp.sum(jnp.where(lanes == micro, turned_ref[...], 0), axis=1, keepdims=True)
+    row_ids = lax.broadcasted_iota(jnp.int32, (span, span), 0)
+    col_ids = lax.broadcasted_iota(jnp.int32, (span, span), 1)
+    scores = jnp.where((down == across) & (col_ids <= row_ids), scores, NEG)
+    expo = jnp.exp(scores - jnp.max(scores, axis=-1, keepdims=True))
+    weights = (expo / jnp.sum(expo, axis=-1, keepdims=True)).astype(BF16)
+    out_ref[:span] = jnp.dot(weights, values, preferred_element_type=F32).astype(BF16)
+    small[...] = jnp.zeros_like(small)
+    last = parts[0].shape[0] - count
+    picked = lax.broadcasted_iota(jnp.int32, (count, head), 0) == me
+
+    def own_row(block):
+        return jnp.sum(jnp.where(picked, block.astype(F32), 0.0), axis=0, keepdims=True)
+
+    for h in range(heads):
+        small[0, h : h + 1, :] = own_row(blocks[2 * h, last:])
+        small[1, h : h + 1, :] = own_row(blocks[h, span : span + count])
+        small[2, h : h + 1, :] = own_row(blocks[heads + h, span : span + count])
+    queries = small[0]
+    line = lax.broadcasted_iota(jnp.int32, queries.shape, 0)
+    spread = jnp.concatenate(
+        [jnp.where(line == h, queries, 0.0) for h in range(heads)], axis=1
+    ).astype(BF16)
+    own = jnp.sum(queries * small[1], axis=-1, keepdims=True) * factor
+    copy.wait()
+    dec_scores = (
+        lax.dot_general(
+            spread,
+            cached[:, : heads * head],
+            (((1,), (1,)), ((), ())),
+            preferred_element_type=F32,
+        )
+        * factor
+    )
+    positions = lax.broadcasted_iota(jnp.int32, dec_scores.shape, 1)
+    dec_scores = jnp.where(positions < length_ref[micro, 0], dec_scores, NEG)
+    top = jnp.maximum(jnp.max(dec_scores, axis=-1, keepdims=True), own)
+    dec_expo = jnp.exp(dec_scores - top)
+    own_expo = jnp.exp(own - top)
+    total = jnp.sum(dec_expo, axis=-1, keepdims=True) + own_expo
+    dec_weights = (dec_expo / total).astype(BF16)
+    own_weight = (own_expo / total).astype(BF16).astype(F32)
+    result = jnp.dot(dec_weights, cached[:, heads * head :], preferred_element_type=F32)
+    extra = own_weight * small[2]
+    for h in range(heads):
+        row = result[h : h + 1, h * head : (h + 1) * head] + extra[h : h + 1]
+        small[3, h : h + 1, :] = row
+    out_ref[span:] = small[3, :heads].astype(BF16)
+
+
+def output_kernel(count, span, where_ref, *refs):
+    parts = refs[:count]
+    weights = refs[count : 2 * count]
+    out_ref, rows_ref, decode = refs[2 * count :]
+    me = where_ref[0]
+    for k, part in enumerate(parts):
+        decode[count * k : count * (k + 1)] = part[span:].astype(F32)
+    size = count * count
+    line = lax.broadcasted_iota(jnp.int32, (size, size), 0)
+    lane = lax.broadcasted_iota(jnp.int32, (size, size), 1)
+    want_head = lax.rem(me - line // count + count, count)
+    from_row = lax.rem(me - lane // count + count, count)
+    chosen = (lane % count == want_head) & (line % count == from_row)
+    picked = jnp.dot(
+        jnp.where(chosen, 1.0, 0.0).astype(BF16),
+        decode[...].astype(BF16),
+        preferred_element_type=F32,
+    )
+    total = None
+    for k, part in enumerate(parts):
+        rows_ref[k, :span] = part[:span]
+        rows_ref[k, span : span + count] = picked[count * k : count * (k + 1)].astype(BF16)
+        term = jnp.dot(rows_ref[k], weights[k][...], preferred_element_type=F32)
+        term = term.astype(BF16).astype(F32)
+        total = term if total is None else total + term
+    out_ref[...] = total[: span + count].astype(BF16)
+
+
+def fast_body(
+    stream_in, pend_in, arrivals, norm_gain, wq, wkv, wo, cache, dec_len, span_seg
+):
+    count = lax.axis_size("tensor")
+    sections = lax.axis_size("section")
+    tensor_index = lax.axis_index("tensor")
+    section_index = lax.axis_index("section")
+    rows, shard = stream_in.shape[1:]
+    head = wq.shape[2]
+    span = span_seg.shape[1]
+    length = cache.shape[3]
+    ticks = cache.shape[1]
+    where = jnp.stack([tensor_index, section_index]).astype(jnp.int32)
+    gain = norm_gain.reshape(count, shard)
+    cached = cache.reshape(ticks, length, cache.shape[4])
+    segments = span_seg
+    segments_turned = span_seg.T
+    message_rows = (rows + 7) // 8 * 8 + count
+    limit = pltpu.CompilerParams(vmem_limit_bytes=24 * 1024 * 1024)
+
+    def project(parts):
+        return pl.pallas_call(
+            functools.partial(project_kernel, count, span),
+            out_shape=(
+                jax.ShapeDtypeStruct((span, head), BF16),
+                jax.ShapeDtypeStruct((message_rows, 2 * head), BF16),
+            ),
+            in_specs=[SMEM] + [VMEM] * (count + 3),
+            out_specs=(VMEM, VMEM),
+            compiler_params=limit,
+            cost_estimate=pl.CostEstimate(
+                flops=2 * rows * shard * count * 3 * head,
+                bytes_accessed=2 * shard * count * (3 * head + rows),
+                transcendentals=rows,
+            ),
+            name="project",
+        )(where, *parts, gain, wq[0], wkv[0])
+
+    def attend(queries, parts, tick):
+        return pl.pallas_call(
+            functools.partial(attend_kernel, count, span, tick, sections),
+            out_shape=jax.ShapeDtypeStruct((span + count, head), BF16),
+            in_specs=[SMEM, SMEM] + [VMEM] * (count + 3) + [ANY],
+            out_specs=VMEM,
+            scratch_shapes=[
+                pltpu.VMEM((2 * count, message_rows, head), BF16),
+                pltpu.VMEM((length, cache.shape[4]), BF16),
+                pltpu.VMEM((4, 8, head), F32),
+                pltpu.SemaphoreType.DMA,
+            ],
+            compiler_params=limit,
+            cost_estimate=pl.CostEstimate(
+                flops=4 * 8 * length * 4 * head,
+                bytes_accessed=4 * length * 4 * head + count * message_rows * 4 * head,
+                transcendentals=span * span,
+            ),
+            name="attend",
+        )(where, dec_len, queries, *parts, segments, segments_turned, cached)
+
+    def output(parts, weights):
+        return pl.pallas_call(
+            functools.partial(output_kernel, count, span),
+            out_shape=jax.ShapeDtypeStruct((rows, shard), BF16),
+            in_specs=[SMEM] + [VMEM] * (2 * count),
+            out_specs=VMEM,
+            scratch_shapes=[
+                pltpu.VMEM((count, (rows + 7) // 8 * 8, head), BF16),
+                pltpu.VMEM((count * count, head), F32),
+            ],
+            compiler_params=limit,
+            cost_estimate=pl.CostEstimate(
+                flops=2 * rows * shard * count * head,
+                bytes_accessed=2 * shard * (count * head + rows),
+                transcendentals=0,
+            ),
+            name="output",
+        )(where, *parts, *weights)
+
+    stream_parts = pieces_of(stream_in[0], "tensor")
+    first_new = added(stream_in[0], pend_in[0])
+    one_on = moved(first_new, "section", 1)
+    two_on = moved(first_new, "section", 2)
+    out_weights = []
+    for k in range(count):
+        target = lax.rem(tensor_index + k, count)
+        block = lax.dynamic_slice_in_dim(wo[0], target * shard, shard, 1)
+        out_weights.append(block if k == 0 else turned(block, "tensor", k))
+    second = jnp.where(section_index == 0, arrivals[0], one_on)
+
+    queries, message = project(stream_parts)
+    attended = attend(queries, pieces_of(message, "tensor"), 0)
+    pend_first = output(pieces_of(attended, "tensor"), out_weights)
+    pend_two_on = moved(pend_first, "section", 2)
+    pend_one_on = moved(pend_first, "section", 1)
+
+    queries, message = project(pieces_of(second, "tensor"))
+    attended = attend(queries, pieces_of(message, "tensor"), 1)
+    pend_second = output(pieces_of(attended, "tensor"), out_weights)
+    second_new = added(second, pend_one_on)
+    pend_last_in = moved(pend_second, "section", 1)
+
+    third = jnp.where(
+        section_index == 0,
+        arrivals[1],
+        jnp.where(section_index == 1, arrivals[0], added(two_on, pend_two_on)),
+    )
+    queries, message = project(pieces_of(third, "tensor"))
+    attended = attend(queries, pieces_of(message, "tensor"), 2)
+    pend_third = output(pieces_of(attended, "tensor"), out_weights)
+    third_new = added(third, pend_last_in)
+    return (
+        jnp.stack([first_new, second_new, third_new])[None],
+        jnp.stack([pend_first, pend_second, pend_third])[None],
+    )
 
 
 def passed_along(block, axis, distance):
@@ -60,7 +338,7 @@
     return result.astype(jnp.bfloat16)
 
 
-def body(stream_in, pend_in, arrivals, norm_gain, wq, wkv, wo, cache, dec_len, span_seg):
+def plain_body(stream_in, pend_in, arrivals, norm_gain, wq, wkv, wo, cache, dec_len, span_seg):
     tensor_count = lax.axis_size("tensor")
     section_count = lax.axis_size("section")
     tensor_index = lax.axis_index("tensor")
@@ -136,6 +414,26 @@
     return (jnp.stack(hist_stream)[None], jnp.stack(hist_pend)[None])
 
 
+def body(stream_in, pend_in, arrivals, norm_gain, wq, wkv, wo, cache, dec_len, span_seg):
+    count = lax.axis_size("tensor")
+    head = wq.shape[2]
+    fits = (
+        head == 128
+        and count <= 8
+        and cache.shape[1] == 3
+        and cache.shape[2] == 1
+        and cache.shape[4] == 2 * head * count
+        and wkv.shape[2] == 2 * head
+        and stream_in.shape[2] % 128 == 0
+        and span_seg.shape[1] % 16 == 0
+        and stream_in.shape[1] == span_seg.shape[1] + count
+    )
+    chosen = fast_body if fits else plain_body
+    return chosen(
+        stream_in, pend_in, arrivals, norm_gain, wq, wkv, wo, cache, dec_len, span_seg
+    )
+
+
 def solution(mesh):
     return jax.shard_map(
         body,

time: 325 us -> 151 us (0.46); the launches traced: 320 us -> 150 us
  waiting for transfers between devices: 152 us -> 48.9 us
  blocking collectives: 41.9 us -> 0 us
  matrix products: 23.2 us -> 0 us
  starting transfers between devices: 40.7 us -> 61.7 us
  local copies, waits for them, and re-layouts: 31.4 us -> 14.8 us
  Pallas kernels: 0 us -> 16 us
  between operations: 14.1 us -> 0.94 us
  other arithmetic: 16.9 us -> 7.95 us
    psum x2 -> x0, waiting for transfers between devices: 88.4 us -> none  [body(): lax.psum(term, 'tensor').astype(jnp.float32).astype(jnp.bfloat16)]
    ppermute x4 -> x35, waiting for transfers between devices: 0.23 us -> 48.9 us  [the longest x30 48.2 us: turned(): lax.ppermute(block, axis, [(i, (i + distance) % count) for i in range(cou...]
    all_gather x1 -> x0, waiting for transfers between devices: 48.2 us -> none  [body(): gathered = lax.all_gather(stacked, 'tensor', axis=1, tiled=True)]
    ppermute x4 -> x35, starting transfers between devices: 16.1 us -> 61.7 us  [the longest x30 50.5 us: turned(): lax.ppermute(block, axis, [(i, (i + distance) % count) for i in range(cou...]
    all_gather x3 -> x0, blocking collectives: 41.9 us -> none  [body(): keyval = lax.all_gather(kv_part, 'tensor', axis=1, tiled=True)]
    all_to_all x6 -> x0, starting transfers between devices: 24.6 us -> none  [the longest x3 13.1 us: body(): lax.all_to_all(row_out, 'tensor', split_axis=1, concat_axis=0, tiled=True)]
    dot_general x21 -> x0, matrix products: 23.2 us -> none  [the longest x3 5.86 us: body(): jnp.dot(attended, wo[0], preferred_element_type=jnp.float32)]
    pallas_call x0 -> x9, Pallas kernels: none -> 16 us  [the longest x3 6.06 us: output(): pl.pallas_call(functools.partial(output_kernel, count, span), out_shape=j...]
  transfers between devices with their start and end apart: 13 -> 35, of which waited for: 7 -> 16; matrix products, arithmetic and copies ran while one was open for 15% -> 5% of each run, Pallas kernels for 0% -> 5%
where the time goes in v1:
time: 151 us; the launch traced here: 150 us
  starting transfers between devices  61.7 us (41%)
  waiting for transfers between devices  48.9 us (32%)
  Pallas kernels  16 us (11%)
  local copies, waits for them, and re-layouts  14.8 us (10%)
  other arithmetic  7.95 us (5%)
    ppermute x30, starting transfers between devices, turned(): lax.ppermute(block, axis, [(i, (i + distance) % count) for i in range(cou...  50.5 us
    ppermute x30, waiting for transfers between devices, turned(): lax.ppermute(block, axis, [(i, (i + distance) % count) for i in range(cou...  48.2 us
    unnamed x69, local copies, waits for them, and re-layouts  11.6 us
    ppermute x5, starting transfers between devices, moved(): return lax.ppermute(block, axis, route)  11.2 us
    pallas_call x3, Pallas kernels, output(): pl.pallas_call(functools.partial(output_kernel, count, span), out_shape=j...  6.06 us
    pallas_call x3, Pallas kernels, attend(): pl.pallas_call(functools.partial(attend_kernel, count, span, tick, sectio...  5.78 us
    pallas_call x3, Pallas kernels, project(): pl.pallas_call(functools.partial(project_kernel, count, span), out_shape=...  4.15 us
  transfers between devices with their start and end apart: 35, of which 16 were waited for; matrix products, arithmetic and copies ran while one was open for 5% of the time, Pallas kernels for 5%

profile of v1, /device:TPU:0, one launch (start us, length us, event | category | flops | bytes accessed | tf_op | source)
XLA Modules:
  0.0 150.3 jit_solution(1054041056454482634)
XLA Ops:
  0.6 3.1 %collective-permute-start.1 = (bf16[68,1024]{1,0:T(8,128)(2,1)}, bf16[68,1024]{1,0:T(8,128)(2,1)S(1)}, u32[]{:S(2)}, u32[]{:S(2)}) collective-permute-start(bf16[68,1024]{1,0:T(8,128)(2,1)} %bitcast.55), channel_id=1, source_target_pairs={{0,4},{4,8},{8,12},{12,0},{1,5},{5,9},{9,13},{13,1},{2,6},{6,10},{... | collective-permute-start | bytes 417800 | tf_op jit(solution)/shard_map/ppermute | solution.py:25
  3.7 2.6 %collective-permute-start.2 = (bf16[68,1024]{1,0:T(8,128)(2,1)}, bf16[68,1024]{1,0:T(8,128)(2,1)S(1)}, u32[]{:S(2)}, u32[]{:S(2)}) collective-permute-start(bf16[68,1024]{1,0:T(8,128)(2,1)} %bitcast.56), channel_id=1, source_target_pairs={{0,8},{4,12},{8,0},{12,4},{1,9},{5,13},{9,1},{13,5},{2,10},{6,14},... | collective-permute-start | bytes 417800 | tf_op jit(solution)/shard_map/ppermute | solution.py:25
  6.3 1.3 collective-permute-start.3
  8.2 1.4 reduce.3
  10.7 5.5 %collective-permute-done.2.refs_2_ = bf16[68,1024]{1,0:T(8,128)(2,1)S(1)} collective-permute-done((bf16[68,1024]{1,0:T(8,128)(2,1)}, bf16[68,1024]{1,0:T(8,128)(2,1)S(1)}, u32[]{:S(2)}, u32[]{:S(2)}) %collective-permute-start.2) | collective-permute-done | bytes 139296 | tf_op jit(solution)/shard_map/ppermute | solution.py:25
  16.2 1.6 %copy-done.1 = bf16[1,4096,256]{2,1,0:T(8,128)(2,1)S(1)} copy-done((bf16[1,4096,256]{2,1,0:T(8,128)(2,1)S(1)}, bf16[1,4096,256]{2,1,0:T(8,128)(2,1)}, u32[]{:S(2)}) %copy-start.1) | copy-done | bytes 2097176
  19.9 1.4 project.3
  21.3 3.7 %collective-permute-start.4 = (bf16[76,256]{1,0:T(8,128)(2,1)S(1)}, bf16[76,256]{1,0:T(8,128)(2,1)S(1)}, u32[]{:S(2)}, u32[]{:S(2)}) collective-permute-start(bf16[76,256]{1,0:T(8,128)(2,1)S(1)} %get-tuple-element.9.refs_1_), channel_id=1, source_target_pairs={{0,4},{4,8},{8,12},{12,0},{1,5},{5,9},{9,13},{13,1},{2,6},{6,10},{... | collective-permute-start | bytes 116744 | tf_op jit(solution)/shard_map/ppermute | solution.py:25
  25.0 1.6 %collective-permute-start.5 = (bf16[76,256]{1,0:T(8,128)(2,1)S(1)}, bf16[76,256]{1,0:T(8,128)(2,1)S(1)}, u32[]{:S(2)}, u32[]{:S(2)}) collective-permute-start(bf16[76,256]{1,0:T(8,128)(2,1)S(1)} %get-tuple-element.9.refs_1_), channel_id=1, source_target_pairs={{0,8},{4,12},{8,0},{12,4},{1,9},{5,13},{9,1},{13,5},{2,10},{6,14},... | collective-permute-start | bytes 116744 | tf_op jit(solution)/shard_map/ppermute | solution.py:25
  29.6 1.3 collective-permute-start.11
  30.9 1.3 collective-permute-start.12
  33.1 2.3 %attend.3.refs_0_ = bf16[68,128]{1,0:T(8,128)(2,1)} custom-call(s32[2]{0:T(128)S(1)} %pad_add_fusion.where_ref, s32[6,1]{1,0:T(8,128)S(1)} %copy.14.length_ref, bf16[64,128]{1,0:T(8,128)(2,1)S(1)} %get-tuple-element.8.refs_0_, bf16[76,256]{1,0:T(8,128)(2,1)S(1)} %get-tuple-element.9.refs_1_, bf16[76,256]{1,0:T(8,128)(2,1)S(1)} %collective-permute-done.4.refs_2_, ...), custom_call_target="tpu_custom_call" | custom-call | flops 6291456 | bytes 942080 | tf_op jit(solution)/shard_map/attend/pallas_call | solution.py:213
  36.7 1.6 %collective-permute-start.8 = (bf16[68,128]{1,0:T(8,128)(2,1)}, bf16[68,128]{1,0:T(8,128)(2,1)}, u32[]{:S(2)}, u32[]{:S(2)}) collective-permute-start(bf16[68,128]{1,0:T(8,128)(2,1)} %attend.3.refs_0_), channel_id=1, source_target_pairs={{0,8},{4,12},{8,0},{12,4},{1,9},{5,13},{9,1},{13,5},{2,10},{6,14},... | collective-permute-start | bytes 52232 | tf_op jit(solution)/shard_map/ppermute | solution.py:25
  38.3 11.8 %collective-permute-done.7.refs_1_ = bf16[68,128]{1,0:T(8,128)(2,1)S(1)} collective-permute-done((bf16[68,128]{1,0:T(8,128)(2,1)}, bf16[68,128]{1,0:T(8,128)(2,1)S(1)}, u32[]{:S(2)}, u32[]{:S(2)}) %collective-permute-start.7) | collective-permute-done | bytes 17440 | tf_op jit(solution)/shard_map/ppermute | solution.py:25
  50.7 1.6 %fusion.2 = bf16[68,1024]{1,0:T(8,128)(2,1)} fusion(bf16[1,68,1024]{2,1,0:T(8,128)(2,1)} %param.11, bf16[1,68,1024]{2,1,0:T(8,128)(2,1)S(1)} %copy-done.10), kind=kLoop, calls=%fused_computation.6 | loop fusion | flops 278528 | bytes 417792 | tf_op jit(solution)/shard_map/convert_element_type | solution.py:33
  52.3 3.1 %collective-permute-done.8.refs_2_ = bf16[68,128]{1,0:T(8,128)(2,1)} collective-permute-done((bf16[68,128]{1,0:T(8,128)(2,1)}, bf16[68,128]{1,0:T(8,128)(2,1)}, u32[]{:S(2)}, u32[]{:S(2)}) %collective-permute-start.8) | collective-permute-done | bytes 17440 | tf_op jit(solution)/shard_map/ppermute | solution.py:25
  55.4 1.3 collective-permute-start
  59.1 2.3 %output.3 = bf16[68,1024]{1,0:T(8,128)(2,1)} custom-call(s32[2]{0:T(128)S(1)} %copy-done.24, bf16[68,128]{1,0:T(8,128)(2,1)} %attend.3.refs_0_, bf16[68,128]{1,0:T(8,128)(2,1)S(1)} %copy-done.27, bf16[68,128]{1,0:T(8,128)(2,1)} %collective-permute-done.8.refs_2_, bf16[68,128]{1,0:T(8,128)(2,1)} %collective-permute-done.9.refs_3_, ...), custom_call_target="tpu_custom_call" | custom-call | flops 71303168 | bytes 1187840 | tf_op jit(solution)/shard_map/output/pallas_call | solution.py:234
  61.4 4.1 %collective-permute-start.13 = (bf16[68,1024]{1,0:T(8,128)(2,1)}, bf16[68,1024]{1,0:T(8,128)(2,1)S(1)}, u32[]{:S(2)}, u32[]{:S(2)}) collective-permute-start(bf16[68,1024]{1,0:T(8,128)(2,1)} %output.3), channel_id=1, source_target_pairs={{0,1},{1,2},{2,3},{4,5},{5,6},{6,7},{8,9},{9,10},{10,11},{12,13},{... | collective-permute-start | bytes 417800 | tf_op jit(solution)/shard_map/ppermute | solution.py:20
  65.5 2.3 %fusion.8 = (bf16[1,68,1024]{2,0,1:T(2,128)(2,1)}, bf16[1,68,1024]{2,0,1:T(2,128)(2,1)S(1)}) fusion(bf16[2,68,1024]{2,0,1:T(2,128)(2,1)} %param.12), kind=kLoop, calls=%fused_computation.22 | loop fusion | bytes 557056 | tf_op jit(solution)/shard_map/slice | solution.py:277
  69.4 4.0 %collective-permute-start.17 = (bf16[68,1024]{1,0:T(8,128)(2,1)S(1)}, bf16[68,1024]{1,0:T(8,128)(2,1)S(1)}, u32[]{:S(2)}, u32[]{:S(2)}) collective-permute-start(bf16[68,1024]{1,0:T(8,128)(2,1)S(1)} %get-tuple-element.15.refs_0_), channel_id=1, source_target_pairs={{0,8},{4,12},{8,0},{12,4},{1,9},{5,13},{9,1},{13,5},{2,10},{6,14},... | collective-permute-start | bytes 417800 | tf_op jit(solution)/shard_map/ppermute | solution.py:25
  74.3 3.3 %collective-permute-done.16.refs_1_ = bf16[68,1024]{1,0:T(8,128)(2,1)S(1)} collective-permute-done((bf16[68,1024]{1,0:T(8,128)(2,1)S(1)}, bf16[68,1024]{1,0:T(8,128)(2,1)S(1)}, u32[]{:S(2)}, u32[]{:S(2)}) %collective-permute-start.16) | collective-permute-done | bytes 139296 | tf_op jit(solution)/shard_map/ppermute | solution.py:25
  77.5 5.7 %collective-permute-done.17.refs_2_ = bf16[68,1024]{1,0:T(8,128)(2,1)S(1)} collective-permute-done((bf16[68,1024]{1,0:T(8,128)(2,1)S(1)}, bf16[68,1024]{1,0:T(8,128)(2,1)S(1)}, u32[]{:S(2)}, u32[]{:S(2)}) %collective-permute-start.17) | collective-permute-done | bytes 139296 | tf_op jit(solution)/shard_map/ppermute | solution.py:25
  83.3 1.4 project.4
  84.7 3.7 %collective-permute-start.19 = (bf16[76,256]{1,0:T(8,128)(2,1)S(1)}, bf16[76,256]{1,0:T(8,128)(2,1)S(1)}, u32[]{:S(2)}, u32[]{:S(2)}) collective-permute-start(bf16[76,256]{1,0:T(8,128)(2,1)S(1)} %get-tuple-element.11.refs_1_), channel_id=1, source_target_pairs={{0,4},{4,8},{8,12},{12,0},{1,5},{5,9},{9,13},{13,1},{2,6},{6,10},{... | collective-permute-start | bytes 116744 | tf_op jit(solution)/shard_map/ppermute | solution.py:25
  88.4 1.6 %collective-permute-start.20 = (bf16[76,256]{1,0:T(8,128)(2,1)S(1)}, bf16[76,256]{1,0:T(8,128)(2,1)S(1)}, u32[]{:S(2)}, u32[]{:S(2)}) collective-permute-start(bf16[76,256]{1,0:T(8,128)(2,1)S(1)} %get-tuple-element.11.refs_1_), channel_id=1, source_target_pairs={{0,8},{4,12},{8,0},{12,4},{1,9},{5,13},{9,1},{13,5},{2,10},{6,14},... | collective-permute-start | bytes 116744 | tf_op jit(solution)/shard_map/ppermute | solution.py:25
  91.4 2.2 %collective-permute-done.20.refs_3_ = bf16[76,256]{1,0:T(8,128)(2,1)S(1)} collective-permute-done((bf16[76,256]{1,0:T(8,128)(2,1)S(1)}, bf16[76,256]{1,0:T(8,128)(2,1)S(1)}, u32[]{:S(2)}, u32[]{:S(2)}) %collective-permute-start.20) | collective-permute-done | bytes 38944 | tf_op jit(solution)/shard_map/ppermute | solution.py:25
  94.1 1.7 %attend.4.refs_0_ = bf16[68,128]{1,0:T(8,128)(2,1)S(1)} custom-call(s32[2]{0:T(128)S(1)} %copy-done.24, s32[6,1]{1,0:T(8,128)S(1)} %copy-done.21, bf16[64,128]{1,0:T(8,128)(2,1)S(1)} %get-tuple-element.10.refs_0_, bf16[76,256]{1,0:T(8,128)(2,1)S(1)} %get-tuple-element.11.refs_1_, bf16[76,256]{1,0:T(8,128)(2,1)S(1)} %collective-permute-done.19.refs_2_, ...), custom_call_target="tpu_custom_call" | custom-call | flops 6291456 | bytes 942080 | tf_op jit(solution)/shard_map/attend/pallas_call | solution.py:213
  96.4 2.6 %collective-permute-start.23 = (bf16[68,128]{1,0:T(8,128)(2,1)S(1)}, bf16[68,128]{1,0:T(8,128)(2,1)S(1)}, u32[]{:S(2)}, u32[]{:S(2)}) collective-permute-start(bf16[68,128]{1,0:T(8,128)(2,1)S(1)} %attend.4.refs_0_), channel_id=1, source_target_pairs={{0,8},{4,12},{8,0},{12,4},{1,9},{5,13},{9,1},{13,5},{2,10},{6,14},... | collective-permute-start | bytes 52232 | tf_op jit(solution)/shard_map/ppermute | solution.py:25
  100.0 1.9 %collective-permute-start.14 = (bf16[68,1024]{1,0:T(8,128)(2,1)}, bf16[68,1024]{1,0:T(8,128)(2,1)}, u32[]{:S(2)}, u32[]{:S(2)}) collective-permute-start(bf16[68,1024]{1,0:T(8,128)(2,1)} %fusion.2), channel_id=1, source_target_pairs={{0,2},{1,3},{4,6},{5,7},{8,10},{9,11},{12,14},{13,15},{16,18},{17,... | collective-permute-start | bytes 417800 | tf_op jit(solution)/shard_map/ppermute | solution.py:20
  102.0 1.9 %collective-permute-start.15 = (bf16[68,1024]{1,0:T(8,128)(2,1)}, bf16[68,1024]{1,0:T(8,128)(2,1)}, u32[]{:S(2)}, u32[]{:S(2)}) collective-permute-start(bf16[68,1024]{1,0:T(8,128)(2,1)} %output.3), channel_id=1, source_target_pairs={{0,2},{1,3},{4,6},{5,7},{8,10},{9,11},{12,14},{13,15},{16,18},{17,... | collective-permute-start | bytes 417800 | tf_op jit(solution)/shard_map/ppermute | solution.py:20
  104.0 2.2 %output.4 = bf16[68,1024]{1,0:T(8,128)(2,1)} custom-call(s32[2]{0:T(128)S(1)} %copy-done.24, bf16[68,128]{1,0:T(8,128)(2,1)S(1)} %attend.4.refs_0_, bf16[68,128]{1,0:T(8,128)(2,1)S(1)} %collective-permute-done.22.refs_1_, bf16[68,128]{1,0:T(8,128)(2,1)S(1)} %collective-permute-done.23.refs_2_, bf16[68,128]{1,0:T(8,128)(2,1)S(1)} %collective-permute-done.24.refs_3_, ...), custom_call_target="tpu_custom_call" | custom-call | flops 71303168 | bytes 1187840 | tf_op jit(solution)/shard_map/output/pallas_call | solution.py:234
  106.2 1.9 %collective-permute-start.25 = (bf16[68,1024]{1,0:T(8,128)(2,1)}, bf16[68,1024]{1,0:T(8,128)(2,1)}, u32[]{:S(2)}, u32[]{:S(2)}) collective-permute-start(bf16[68,1024]{1,0:T(8,128)(2,1)} %output.4), channel_id=1, source_target_pairs={{0,1},{1,2},{2,3},{4,5},{5,6},{6,7},{8,9},{9,10},{10,11},{12,13},{... | collective-permute-start | bytes 417800 | tf_op jit(solution)/shard_map/ppermute | solution.py:20
  108.8 1.4 fusion.6
  111.3 1.2 collective-permute-start.27
  112.5 2.4 %collective-permute-start.28 = (bf16[68,1024]{1,0:T(8,128)(2,1)S(1)}, bf16[68,1024]{1,0:T(8,128)(2,1)S(1)}, u32[]{:S(2)}, u32[]{:S(2)}) collective-permute-start(bf16[68,1024]{1,0:T(8,128)(2,1)S(1)} %get-tuple-element.17.refs_0_), channel_id=1, source_target_pairs={{0,12},{4,0},{8,4},{12,8},{1,13},{5,1},{9,5},{13,9},{2,14},{6,2},{... | collective-permute-start | bytes 417800 | tf_op jit(solution)/shard_map/ppermute | solution.py:25
  114.9 4.0 %collective-permute-done.26.refs_1_ = bf16[68,1024]{1,0:T(8,128)(2,1)S(1)} collective-permute-done((bf16[68,1024]{1,0:T(8,128)(2,1)S(1)}, bf16[68,1024]{1,0:T(8,128)(2,1)S(1)}, u32[]{:S(2)}, u32[]{:S(2)}) %collective-permute-start.26) | collective-permute-done | bytes 139296 | tf_op jit(solution)/shard_map/ppermute | solution.py:25
  118.9 5.8 %collective-permute-done.27.refs_2_ = bf16[68,1024]{1,0:T(8,128)(2,1)S(1)} collective-permute-done((bf16[68,1024]{1,0:T(8,128)(2,1)S(1)}, bf16[68,1024]{1,0:T(8,128)(2,1)S(1)}, u32[]{:S(2)}, u32[]{:S(2)}) %collective-permute-start.27) | collective-permute-done | bytes 139296 | tf_op jit(solution)/shard_map/ppermute | solution.py:25
  124.7 1.6 %copy-done.3 = bf16[1,4096,256]{2,1,0:T(8,128)(2,1)S(1)} copy-done((bf16[1,4096,256]{2,1,0:T(8,128)(2,1)S(1)}, bf16[1,4096,256]{2,1,0:T(8,128)(2,1)}, u32[]{:S(2)}) %copy-start.3) | copy-done | bytes 2097176
  127.7 1.4 project.5
  129.1 3.5 %collective-permute-start.29 = (bf16[76,256]{1,0:T(8,128)(2,1)S(1)}, bf16[76,256]{1,0:T(8,128)(2,1)S(1)}, u32[]{:S(2)}, u32[]{:S(2)}) collective-permute-start(bf16[76,256]{1,0:T(8,128)(2,1)S(1)} %get-tuple-element.13.refs_1_), channel_id=1, source_target_pairs={{0,4},{4,8},{8,12},{12,0},{1,5},{5,9},{9,13},{13,1},{2,6},{6,10},{... | collective-permute-start | bytes 116744 | tf_op jit(solution)/shard_map/ppermute | solution.py:25
  133.5 1.5 %collective-permute-start.31 = (bf16[76,256]{1,0:T(8,128)(2,1)S(1)}, bf16[76,256]{1,0:T(8,128)(2,1)S(1)}, u32[]{:S(2)}, u32[]{:S(2)}) collective-permute-start(bf16[76,256]{1,0:T(8,128)(2,1)S(1)} %get-tuple-element.13.refs_1_), channel_id=1, source_target_pairs={{0,12},{4,0},{8,4},{12,8},{1,13},{5,1},{9,5},{13,9},{2,14},{6,2},{... | collective-permute-start | bytes 116744 | tf_op jit(solution)/shard_map/ppermute | solution.py:25
  135.1 2.6 %collective-permute-done.30.refs_3_ = bf16[76,256]{1,0:T(8,128)(2,1)S(1)} collective-permute-done((bf16[76,256]{1,0:T(8,128)(2,1)S(1)}, bf16[76,256]{1,0:T(8,128)(2,1)S(1)}, u32[]{:S(2)}, u32[]{:S(2)}) %collective-permute-start.30) | collective-permute-done | bytes 38944 | tf_op jit(solution)/shard_map/ppermute | solution.py:25
  137.9 1.7 %attend.5.refs_0_ = bf16[68,128]{1,0:T(8,128)(2,1)S(1)} custom-call(s32[2]{0:T(128)S(1)} %copy-done.25, s32[6,1]{1,0:T(8,128)S(1)} %copy-done.22, bf16[64,128]{1,0:T(8,128)(2,1)S(1)} %get-tuple-element.12.refs_0_, bf16[76,256]{1,0:T(8,128)(2,1)S(1)} %get-tuple-element.13.refs_1_, bf16[76,256]{1,0:T(8,128)(2,1)S(1)} %collective-permute-done.29.refs_2_, ...), custom_call_target="tpu_custom_call" | custom-call | flops 6291456 | bytes 942080 | tf_op jit(solution)/shard_map/attend/pallas_call | solution.py:213
  140.4 2.8 %collective-permute-start.33 = (bf16[68,128]{1,0:T(8,128)(2,1)S(1)}, bf16[68,128]{1,0:T(8,128)(2,1)S(1)}, u32[]{:S(2)}, u32[]{:S(2)}) collective-permute-start(bf16[68,128]{1,0:T(8,128)(2,1)S(1)} %attend.5.refs_0_), channel_id=1, source_target_pairs={{0,8},{4,12},{8,0},{12,4},{1,9},{5,13},{9,1},{13,5},{2,10},{6,14},... | collective-permute-start | bytes 52232 | tf_op jit(solution)/shard_map/ppermute | solution.py:25
  145.3 1.6 %collective-permute-done.34.refs_3_ = bf16[68,128]{1,0:T(8,128)(2,1)S(1)} collective-permute-done((bf16[68,128]{1,0:T(8,128)(2,1)S(1)}, bf16[68,128]{1,0:T(8,128)(2,1)S(1)}, u32[]{:S(2)}, u32[]{:S(2)}) %collective-permute-start.34) | collective-permute-done | bytes 17440 | tf_op jit(solution)/shard_map/ppermute | solution.py:25
  146.9 1.6 %output.5 = bf16[68,1024]{1,0:T(8,128)(2,1)S(1)} custom-call(s32[2]{0:T(128)S(1)} %copy-done.25, bf16[68,128]{1,0:T(8,128)(2,1)S(1)} %attend.5.refs_0_, bf16[68,128]{1,0:T(8,128)(2,1)S(1)} %collective-permute-done.32.refs_1_, bf16[68,128]{1,0:T(8,128)(2,1)S(1)} %collective-permute-done.33.refs_2_, bf16[68,128]{1,0:T(8,128)(2,1)S(1)} %collective-permute-done.34.refs_3_, ...), custom_call_target="tpu_custom_call" | custom-call | flops 71303168 | bytes 1187840 | tf_op jit(solution)/shard_map/output/pallas_call | solution.py:234
  148.5 1.8 %maximum_bitcast_fusion.1 = bf16[1,3,68,1024]{3,2,1,0:T(8,128)(2,1)} fusion(bf16[1,68,1024]{2,1,0:T(8,128)(2,1)S(1)} %bitcast.59, bf16[1,68,1024]{2,1,0:T(8,128)(2,1)} %bitcast.18, bf16[1,68,1024]{2,1,0:T(8,128)(2,1)} %bitcast.17), kind=kLoop, calls=%fused_computation.1 | loop fusion | flops 417792 | bytes 835584 | tf_op jit(solution)/shard_map/broadcast_in_dim | solution.py:286
  (111 shorter events, 25.0 us)
Async XLA Ops:
  0.6 10.1 %collective-permute-start.1 = (bf16[68,1024]{1,0:T(8,128)(2,1)}, bf16[68,1024]{1,0:T(8,128)(2,1)S(1)}, u32[]{:S(2)}, u32[]{:S(2)}) collective-permute-start(bf16[68,1024]{1,0:T(8,128)(2,1)} %bitcast.55), channel_id=1, source_target_pairs={{0,4},{4,8},{8,12},{12,0},{1,5},{5,9},{9,13},{13,1},{2,6},{6,10},{... | collective-permute-start | bytes 417800 | tf_op jit(solution)/shard_map/ppermute | solution.py:25
  3.7 12.5 %collective-permute-start.2 = (bf16[68,1024]{1,0:T(8,128)(2,1)}, bf16[68,1024]{1,0:T(8,128)(2,1)S(1)}, u32[]{:S(2)}, u32[]{:S(2)}) collective-permute-start(bf16[68,1024]{1,0:T(8,128)(2,1)} %bitcast.56), channel_id=1, source_target_pairs={{0,8},{4,12},{8,0},{12,4},{1,9},{5,13},{9,1},{13,5},{2,10},{6,14},... | collective-permute-start | bytes 417800 | tf_op jit(solution)/shard_map/ppermute | solution.py:25
  6.3 9.9 %collective-permute-start.3 = (bf16[68,1024]{1,0:T(8,128)(2,1)}, bf16[68,1024]{1,0:T(8,128)(2,1)S(1)}, u32[]{:S(2)}, u32[]{:S(2)}) collective-permute-start(bf16[68,1024]{1,0:T(8,128)(2,1)} %bitcast.57), channel_id=1, source_target_pairs={{0,12},{4,0},{8,4},{12,8},{1,13},{5,1},{9,5},{13,9},{2,14},{6,2},{... | collective-permute-start | bytes 417800 | tf_op jit(solution)/shard_map/ppermute | solution.py:25
  9.7 22.8 %copy-start.23 = (s32[2]{0:T(128)}, s32[2]{0:T(128)S(1)}, u32[]{:S(2)}) copy-start(s32[2]{0:T(128)S(1)} %pad_add_fusion.where_ref) | copy-start | bytes 28
  21.3 29.4 %copy-start.10 = (bf16[1,68,1024]{2,1,0:T(8,128)(2,1)S(1)}, bf16[1,68,1024]{2,1,0:T(8,128)(2,1)}, u32[]{:S(2)}) copy-start(bf16[1,68,1024]{2,1,0:T(8,128)(2,1)} %param.10) | copy-start | bytes 417796
  21.3 9.6 %collective-permute-start.4 = (bf16[76,256]{1,0:T(8,128)(2,1)S(1)}, bf16[76,256]{1,0:T(8,128)(2,1)S(1)}, u32[]{:S(2)}, u32[]{:S(2)}) collective-permute-start(bf16[76,256]{1,0:T(8,128)(2,1)S(1)} %get-tuple-element.9.refs_1_), channel_id=1, source_target_pairs={{0,4},{4,8},{8,12},{12,0},{1,5},{5,9},{9,13},{13,1},{2,6},{6,10},{... | collective-permute-start | bytes 116744 | tf_op jit(solution)/shard_map/ppermute | solution.py:25
  25.0 7.5 %collective-permute-start.5 = (bf16[76,256]{1,0:T(8,128)(2,1)S(1)}, bf16[76,256]{1,0:T(8,128)(2,1)S(1)}, u32[]{:S(2)}, u32[]{:S(2)}) collective-permute-start(bf16[76,256]{1,0:T(8,128)(2,1)S(1)} %get-tuple-element.9.refs_1_), channel_id=1, source_target_pairs={{0,8},{4,12},{8,0},{12,4},{1,9},{5,13},{9,1},{13,5},{2,10},{6,14},... | collective-permute-start | bytes 116744 | tf_op jit(solution)/shard_map/ppermute | solution.py:25
  26.6 5.8 %collective-permute-start.6 = (bf16[76,256]{1,0:T(8,128)(2,1)S(1)}, bf16[76,256]{1,0:T(8,128)(2,1)S(1)}, u32[]{:S(2)}, u32[]{:S(2)}) collective-permute-start(bf16[76,256]{1,0:T(8,128)(2,1)S(1)} %get-tuple-element.9.refs_1_), channel_id=1, source_target_pairs={{0,12},{4,0},{8,4},{12,8},{1,13},{5,1},{9,5},{13,9},{2,14},{6,2},{... | collective-permute-start | bytes 116744 | tf_op jit(solution)/shard_map/ppermute | solution.py:25
  28.4 28.3 %collective-permute-start.10 = (bf16[128,1024]{1,0:T(8,128)(2,1)}, bf16[128,1024]{1,0:T(8,128)(2,1)}, u32[]{:S(2)}, u32[]{:S(2)}) collective-permute-start(bf16[128,1024]{1,0:T(8,128)(2,1)} %get-tuple-element.19), channel_id=1, source_target_pairs={{0,4},{4,8},{8,12},{12,0},{1,5},{5,9},{9,13},{13,1},{2,6},{6,10},{... | collective-permute-start | bytes 786440 | tf_op jit(solution)/shard_map/ppermute | solution.py:25
  29.6 27.1 %collective-permute-start.11 = (bf16[128,1024]{1,0:T(8,128)(2,1)}, bf16[128,1024]{1,0:T(8,128)(2,1)}, u32[]{:S(2)}, u32[]{:S(2)}) collective-permute-start(bf16[128,1024]{1,0:T(8,128)(2,1)} %get-tuple-element.21), channel_id=1, source_target_pairs={{0,8},{4,12},{8,0},{12,4},{1,9},{5,13},{9,1},{13,5},{2,10},{6,14},... | collective-permute-start | bytes 786440 | tf_op jit(solution)/shard_map/ppermute | solution.py:25
  30.9 25.8 %collective-permute-start.12 = (bf16[128,1024]{1,0:T(8,128)(2,1)}, bf16[128,1024]{1,0:T(8,128)(2,1)}, u32[]{:S(2)}, u32[]{:S(2)}) collective-permute-start(bf16[128,1024]{1,0:T(8,128)(2,1)} %get-tuple-element.18), channel_id=1, source_target_pairs={{0,12},{4,0},{8,4},{12,8},{1,13},{5,1},{9,5},{13,9},{2,14},{6,2},{... | collective-permute-start | bytes 786440 | tf_op jit(solution)/shard_map/ppermute | solution.py:25
  36.0 47.3 %copy-start.5 = (bf16[1,4096,128]{2,1,0:T(8,128)(2,1)S(1)}, bf16[1,4096,128]{2,1,0:T(8,128)(2,1)}, u32[]{:S(2)}) copy-start(bf16[1,4096,128]{2,1,0:T(8,128)(2,1)} %param.14) | copy-start | bytes 3145732
  36.0 14.1 %collective-permute-start.7 = (bf16[68,128]{1,0:T(8,128)(2,1)}, bf16[68,128]{1,0:T(8,128)(2,1)S(1)}, u32[]{:S(2)}, u32[]{:S(2)}) collective-permute-start(bf16[68,128]{1,0:T(8,128)(2,1)} %attend.3.refs_0_), channel_id=1, source_target_pairs={{0,4},{4,8},{8,12},{12,0},{1,5},{5,9},{9,13},{13,1},{2,6},{6,10},{... | collective-permute-start | bytes 52232 | tf_op jit(solution)/shard_map/ppermute | solution.py:25
  36.7 18.7 %collective-permute-start.8 = (bf16[68,128]{1,0:T(8,128)(2,1)}, bf16[68,128]{1,0:T(8,128)(2,1)}, u32[]{:S(2)}, u32[]{:S(2)}) collective-permute-start(bf16[68,128]{1,0:T(8,128)(2,1)} %attend.3.refs_0_), channel_id=1, source_target_pairs={{0,8},{4,12},{8,0},{12,4},{1,9},{5,13},{9,1},{13,5},{2,10},{6,14},... | collective-permute-start | bytes 52232 | tf_op jit(solution)/shard_map/ppermute | solution.py:25
  50.7 6.0 %collective-permute-start.9 = (bf16[68,128]{1,0:T(8,128)(2,1)}, bf16[68,128]{1,0:T(8,128)(2,1)}, u32[]{:S(2)}, u32[]{:S(2)}) collective-permute-start(bf16[68,128]{1,0:T(8,128)(2,1)} %attend.3.refs_0_), channel_id=1, source_target_pairs={{0,12},{4,0},{8,4},{12,8},{1,13},{5,1},{9,5},{13,9},{2,14},{6,2},{... | collective-permute-start | bytes 52232 | tf_op jit(solution)/shard_map/ppermute | solution.py:25
  52.3 31.0 %copy-start.2 = (bf16[1,4096,256]{2,1,0:T(8,128)(2,1)S(1)}, bf16[1,4096,256]{2,1,0:T(8,128)(2,1)}, u32[]{:S(2)}) copy-start(bf16[1,4096,256]{2,1,0:T(8,128)(2,1)} %param.15) | copy-start | bytes 6291460
  55.4 12.4 %collective-permute-start = (bf16[68,1024]{1,0:T(8,128)(2,1)}, bf16[68,1024]{1,0:T(8,128)(2,1)S(1)}, u32[]{:S(2)}, u32[]{:S(2)}) collective-permute-start(bf16[68,1024]{1,0:T(8,128)(2,1)} %fusion.2), channel_id=1, source_target_pairs={{0,1},{1,2},{2,3},{4,5},{5,6},{6,7},{8,9},{9,10},{10,11},{12,13},{... | collective-permute-start | bytes 417800 | tf_op jit(solution)/shard_map/ppermute | solution.py:20
  59.1 24.2 %copy-start.15 = (f32[4,1024]{1,0:T(4,128)S(1)}, f32[4,1024]{1,0:T(4,128)}, u32[]{:S(2)}) copy-start(f32[4,1024]{1,0:T(4,128)} %copy-done.14) | copy-start | bytes 49156
  61.4 6.4 %collective-permute-start.13 = (bf16[68,1024]{1,0:T(8,128)(2,1)}, bf16[68,1024]{1,0:T(8,128)(2,1)S(1)}, u32[]{:S(2)}, u32[]{:S(2)}) collective-permute-start(bf16[68,1024]{1,0:T(8,128)(2,1)} %output.3), channel_id=1, source_target_pairs={{0,1},{1,2},{2,3},{4,5},{5,6},{6,7},{8,9},{9,10},{10,11},{12,13},{... | collective-permute-start | bytes 417800 | tf_op jit(solution)/shard_map/ppermute | solution.py:20
  67.8 26.3 %copy-start.12 = (s32[6,64]{0,1:T(8,128)S(1)}, s32[6,64]{0,1:T(8,128)}, u32[]{:S(2)}) copy-start(s32[6,64]{0,1:T(8,128)} %copy-done.11) | copy-start | bytes 4612
  67.8 26.3 %copy-start.18 = (s32[6,64]{1,0:T(8,128)S(1)}, s32[6,64]{1,0:T(8,128)}, u32[]{:S(2)}) copy-start(s32[6,64]{1,0:T(8,128)} %refs_5_.5) | copy-start | bytes 4612
  67.8 26.3 %copy-start.21 = (s32[6,1]{1,0:T(8,128)S(1)}, s32[6,1]{1,0:T(8,128)}, u32[]{:S(2)}) copy-start(s32[6,1]{1,0:T(8,128)} %copy-done.20) | copy-start | bytes 76
  68.6 35.4 %copy-start.7 = (bf16[128,1024]{1,0:T(8,128)(2,1)S(1)}, bf16[128,1024]{1,0:T(8,128)(2,1)}, u32[]{:S(2)}) copy-start(bf16[128,1024]{1,0:T(8,128)(2,1)} %get-tuple-element.20.refs_4_) | copy-start | bytes 786436
  68.6 9.0 %collective-permute-start.16 = (bf16[68,1024]{1,0:T(8,128)(2,1)S(1)}, bf16[68,1024]{1,0:T(8,128)(2,1)S(1)}, u32[]{:S(2)}, u32[]{:S(2)}) collective-permute-start(bf16[68,1024]{1,0:T(8,128)(2,1)S(1)} %get-tuple-element.15.refs_0_), channel_id=1, source_target_pairs={{0,4},{4,8},{8,12},{12,0},{1,5},{5,9},{9,13},{13,1},{2,6},{6,10},{... | collective-permute-start | bytes 417800 | tf_op jit(solution)/shard_map/ppermute | solution.py:25
  69.4 13.9 %collective-permute-start.17 = (bf16[68,1024]{1,0:T(8,128)(2,1)S(1)}, bf16[68,1024]{1,0:T(8,128)(2,1)S(1)}, u32[]{:S(2)}, u32[]{:S(2)}) collective-permute-start(bf16[68,1024]{1,0:T(8,128)(2,1)S(1)} %get-tuple-element.15.refs_0_), channel_id=1, source_target_pairs={{0,8},{4,12},{8,0},{12,4},{1,9},{5,13},{9,1},{13,5},{2,10},{6,14},... | collective-permute-start | bytes 417800 | tf_op jit(solution)/shard_map/ppermute | solution.py:25
  73.4 9.9 %collective-permute-start.18 = (bf16[68,1024]{1,0:T(8,128)(2,1)S(1)}, bf16[68,1024]{1,0:T(8,128)(2,1)S(1)}, u32[]{:S(2)}, u32[]{:S(2)}) collective-permute-start(bf16[68,1024]{1,0:T(8,128)(2,1)S(1)} %get-tuple-element.15.refs_0_), channel_id=1, source_target_pairs={{0,12},{4,0},{8,4},{12,8},{1,13},{5,1},{9,5},{13,9},{2,14},{6,2},{... | collective-permute-start | bytes 417800 | tf_op jit(solution)/shard_map/ppermute | solution.py:25
  84.7 6.7 %collective-permute-start.19 = (bf16[76,256]{1,0:T(8,128)(2,1)S(1)}, bf16[76,256]{1,0:T(8,128)(2,1)S(1)}, u32[]{:S(2)}, u32[]{:S(2)}) collective-permute-start(bf16[76,256]{1,0:T(8,128)(2,1)S(1)} %get-tuple-element.11.refs_1_), channel_id=1, source_target_pairs={{0,4},{4,8},{8,12},{12,0},{1,5},{5,9},{9,13},{13,1},{2,6},{6,10},{... | collective-permute-start | bytes 116744 | tf_op jit(solution)/shard_map/ppermute | solution.py:25
  88.4 5.2 %collective-permute-start.20 = (bf16[76,256]{1,0:T(8,128)(2,1)S(1)}, bf16[76,256]{1,0:T(8,128)(2,1)S(1)}, u32[]{:S(2)}, u32[]{:S(2)}) collective-permute-start(bf16[76,256]{1,0:T(8,128)(2,1)S(1)} %get-tuple-element.11.refs_1_), channel_id=1, source_target_pairs={{0,8},{4,12},{8,0},{12,4},{1,9},{5,13},{9,1},{13,5},{2,10},{6,14},... | collective-permute-start | bytes 116744 | tf_op jit(solution)/shard_map/ppermute | solution.py:25
  90.0 4.1 %collective-permute-start.21 = (bf16[76,256]{1,0:T(8,128)(2,1)S(1)}, bf16[76,256]{1,0:T(8,128)(2,1)S(1)}, u32[]{:S(2)}, u32[]{:S(2)}) collective-permute-start(bf16[76,256]{1,0:T(8,128)(2,1)S(1)} %get-tuple-element.11.refs_1_), channel_id=1, source_target_pairs={{0,12},{4,0},{8,4},{12,8},{1,13},{5,1},{9,5},{13,9},{2,14},{6,2},{... | collective-permute-start | bytes 116744 | tf_op jit(solution)/shard_map/ppermute | solution.py:25
  95.8 8.1 %collective-permute-start.22 = (bf16[68,128]{1,0:T(8,128)(2,1)S(1)}, bf16[68,128]{1,0:T(8,128)(2,1)S(1)}, u32[]{:S(2)}, u32[]{:S(2)}) collective-permute-start(bf16[68,128]{1,0:T(8,128)(2,1)S(1)} %attend.4.refs_0_), channel_id=1, source_target_pairs={{0,4},{4,8},{8,12},{12,0},{1,5},{5,9},{9,13},{13,1},{2,6},{6,10},{... | collective-permute-start | bytes 52232 | tf_op jit(solution)/shard_map/ppermute | solution.py:25
  96.4 7.5 %collective-permute-start.23 = (bf16[68,128]{1,0:T(8,128)(2,1)S(1)}, bf16[68,128]{1,0:T(8,128)(2,1)S(1)}, u32[]{:S(2)}, u32[]{:S(2)}) collective-permute-start(bf16[68,128]{1,0:T(8,128)(2,1)S(1)} %attend.4.refs_0_), channel_id=1, source_target_pairs={{0,8},{4,12},{8,0},{12,4},{1,9},{5,13},{9,1},{13,5},{2,10},{6,14},... | collective-permute-start | bytes 52232 | tf_op jit(solution)/shard_map/ppermute | solution.py:25
  99.0 4.9 %collective-permute-start.24 = (bf16[68,128]{1,0:T(8,128)(2,1)S(1)}, bf16[68,128]{1,0:T(8,128)(2,1)S(1)}, u32[]{:S(2)}, u32[]{:S(2)}) collective-permute-start(bf16[68,128]{1,0:T(8,128)(2,1)S(1)} %attend.4.refs_0_), channel_id=1, source_target_pairs={{0,12},{4,0},{8,4},{12,8},{1,13},{5,1},{9,5},{13,9},{2,14},{6,2},{... | collective-permute-start | bytes 52232 | tf_op jit(solution)/shard_map/ppermute | solution.py:25
  100.0 8.1 %collective-permute-start.14 = (bf16[68,1024]{1,0:T(8,128)(2,1)}, bf16[68,1024]{1,0:T(8,128)(2,1)}, u32[]{:S(2)}, u32[]{:S(2)}) collective-permute-start(bf16[68,1024]{1,0:T(8,128)(2,1)} %fusion.2), channel_id=1, source_target_pairs={{0,2},{1,3},{4,6},{5,7},{8,10},{9,11},{12,14},{13,15},{16,18},{17,... | collective-permute-start | bytes 417800 | tf_op jit(solution)/shard_map/ppermute | solution.py:20
  102.0 6.1 %collective-permute-start.15 = (bf16[68,1024]{1,0:T(8,128)(2,1)}, bf16[68,1024]{1,0:T(8,128)(2,1)}, u32[]{:S(2)}, u32[]{:S(2)}) collective-permute-start(bf16[68,1024]{1,0:T(8,128)(2,1)} %output.3), channel_id=1, source_target_pairs={{0,2},{1,3},{4,6},{5,7},{8,10},{9,11},{12,14},{13,15},{16,18},{17,... | collective-permute-start | bytes 417800 | tf_op jit(solution)/shard_map/ppermute | solution.py:20
  106.2 2.6 %collective-permute-start.25 = (bf16[68,1024]{1,0:T(8,128)(2,1)}, bf16[68,1024]{1,0:T(8,128)(2,1)}, u32[]{:S(2)}, u32[]{:S(2)}) collective-permute-start(bf16[68,1024]{1,0:T(8,128)(2,1)} %output.4), channel_id=1, source_target_pairs={{0,1},{1,2},{2,3},{4,5},{5,6},{6,7},{8,9},{9,10},{10,11},{12,13},{... | collective-permute-start | bytes 417800 | tf_op jit(solution)/shard_map/ppermute | solution.py:20
  108.8 26.2 %copy-start.30 = (bf16[1,68,1024]{2,1,0:T(8,128)(2,1)S(1)}, bf16[1,68,1024]{2,1,0:T(8,128)(2,1)}, u32[]{:S(2)}) copy-start(bf16[1,68,1024]{2,1,0:T(8,128)(2,1)} %param.11) | copy-start | bytes 417796
  108.8 29.1 %copy-start.13 = (s32[6,64]{0,1:T(8,128)S(1)}, s32[6,64]{0,1:T(8,128)}, u32[]{:S(2)}) copy-start(s32[6,64]{0,1:T(8,128)} %copy-done.11) | copy-start | bytes 4612
  108.8 29.1 %copy-start.19 = (s32[6,64]{1,0:T(8,128)S(1)}, s32[6,64]{1,0:T(8,128)}, u32[]{:S(2)}) copy-start(s32[6,64]{1,0:T(8,128)} %refs_5_.5) | copy-start | bytes 4612
  108.8 29.1 %copy-start.22 = (s32[6,1]{1,0:T(8,128)S(1)}, s32[6,1]{1,0:T(8,128)}, u32[]{:S(2)}) copy-start(s32[6,1]{1,0:T(8,128)} %copy-done.20) | copy-start | bytes 76
  110.2 8.7 %collective-permute-start.26 = (bf16[68,1024]{1,0:T(8,128)(2,1)S(1)}, bf16[68,1024]{1,0:T(8,128)(2,1)S(1)}, u32[]{:S(2)}, u32[]{:S(2)}) collective-permute-start(bf16[68,1024]{1,0:T(8,128)(2,1)S(1)} %get-tuple-element.17.refs_0_), channel_id=1, source_target_pairs={{0,4},{4,8},{8,12},{12,0},{1,5},{5,9},{9,13},{13,1},{2,6},{6,10},{... | collective-permute-start | bytes 417800 | tf_op jit(solution)/shard_map/ppermute | solution.py:25
  111.3 13.4 %collective-permute-start.27 = (bf16[68,1024]{1,0:T(8,128)(2,1)S(1)}, bf16[68,1024]{1,0:T(8,128)(2,1)S(1)}, u32[]{:S(2)}, u32[]{:S(2)}) collective-permute-start(bf16[68,1024]{1,0:T(8,128)(2,1)S(1)} %get-tuple-element.17.refs_0_), channel_id=1, source_target_pairs={{0,8},{4,12},{8,0},{12,4},{1,9},{5,13},{9,1},{13,5},{2,10},{6,14},... | collective-permute-start | bytes 417800 | tf_op jit(solution)/shard_map/ppermute | solution.py:25
  112.5 12.2 %collective-permute-start.28 = (bf16[68,1024]{1,0:T(8,128)(2,1)S(1)}, bf16[68,1024]{1,0:T(8,128)(2,1)S(1)}, u32[]{:S(2)}, u32[]{:S(2)}) collective-permute-start(bf16[68,1024]{1,0:T(8,128)(2,1)S(1)} %get-tuple-element.17.refs_0_), channel_id=1, source_target_pairs={{0,12},{4,0},{8,4},{12,8},{1,13},{5,1},{9,5},{13,9},{2,14},{6,2},{... | collective-permute-start | bytes 417800 | tf_op jit(solution)/shard_map/ppermute | solution.py:25
  129.1 6.0 %collective-permute-start.29 = (bf16[76,256]{1,0:T(8,128)(2,1)S(1)}, bf16[76,256]{1,0:T(8,128)(2,1)S(1)}, u32[]{:S(2)}, u32[]{:S(2)}) collective-permute-start(bf16[76,256]{1,0:T(8,128)(2,1)S(1)} %get-tuple-element.13.refs_1_), channel_id=1, source_target_pairs={{0,4},{4,8},{8,12},{12,0},{1,5},{5,9},{9,13},{13,1},{2,6},{6,10},{... | collective-permute-start | bytes 116744 | tf_op jit(solution)/shard_map/ppermute | solution.py:25
  132.6 5.1 %collective-permute-start.30 = (bf16[76,256]{1,0:T(8,128)(2,1)S(1)}, bf16[76,256]{1,0:T(8,128)(2,1)S(1)}, u32[]{:S(2)}, u32[]{:S(2)}) collective-permute-start(bf16[76,256]{1,0:T(8,128)(2,1)S(1)} %get-tuple-element.13.refs_1_), channel_id=1, source_target_pairs={{0,8},{4,12},{8,0},{12,4},{1,9},{5,13},{9,1},{13,5},{2,10},{6,14},... | collective-permute-start | bytes 116744 | tf_op jit(solution)/shard_map/ppermute | solution.py:25
  133.5 4.4 %collective-permute-start.31 = (bf16[76,256]{1,0:T(8,128)(2,1)S(1)}, bf16[76,256]{1,0:T(8,128)(2,1)S(1)}, u32[]{:S(2)}, u32[]{:S(2)}) collective-permute-start(bf16[76,256]{1,0:T(8,128)(2,1)S(1)} %get-tuple-element.13.refs_1_), channel_id=1, source_target_pairs={{0,12},{4,0},{8,4},{12,8},{1,13},{5,1},{9,5},{13,9},{2,14},{6,2},{... | collective-permute-start | bytes 116744 | tf_op jit(solution)/shard_map/ppermute | solution.py:25
  139.7 5.6 %collective-permute-start.32 = (bf16[68,128]{1,0:T(8,128)(2,1)S(1)}, bf16[68,128]{1,0:T(8,128)(2,1)S(1)}, u32[]{:S(2)}, u32[]{:S(2)}) collective-permute-start(bf16[68,128]{1,0:T(8,128)(2,1)S(1)} %attend.5.refs_0_), channel_id=1, source_target_pairs={{0,4},{4,8},{8,12},{12,0},{1,5},{5,9},{9,13},{13,1},{2,6},{6,10},{... | collective-permute-start | bytes 52232 | tf_op jit(solution)/shard_map/ppermute | solution.py:25
  140.4 4.9 %collective-permute-start.33 = (bf16[68,128]{1,0:T(8,128)(2,1)S(1)}, bf16[68,128]{1,0:T(8,128)(2,1)S(1)}, u32[]{:S(2)}, u32[]{:S(2)}) collective-permute-start(bf16[68,128]{1,0:T(8,128)(2,1)S(1)} %attend.5.refs_0_), channel_id=1, source_target_pairs={{0,8},{4,12},{8,0},{12,4},{1,9},{5,13},{9,1},{13,5},{2,10},{6,14},... | collective-permute-start | bytes 52232 | tf_op jit(solution)/shard_map/ppermute | solution.py:25
  143.2 3.8 %collective-permute-start.34 = (bf16[68,128]{1,0:T(8,128)(2,1)S(1)}, bf16[68,128]{1,0:T(8,128)(2,1)S(1)}, u32[]{:S(2)}, u32[]{:S(2)}) collective-permute-start(bf16[68,128]{1,0:T(8,128)(2,1)S(1)} %attend.5.refs_0_), channel_id=1, source_target_pairs={{0,12},{4,0},{8,4},{12,8},{1,13},{5,1},{9,5},{13,9},{2,14},{6,2},{... | collective-permute-start | bytes 52232 | tf_op jit(solution)/shard_map/ppermute | solution.py:25
  (20 other events, 123.6 us)

commit v2 on v1

--- a/solution.py
+++ b/solution.py
@@ -34,14 +34,60 @@
 
 
 VMEM = pl.BlockSpec(memory_space=pltpu.VMEM)
-SMEM = pl.BlockSpec(memory_space=pltpu.SMEM)
+HBM = pl.BlockSpec(memory_space=pltpu.HBM)
 ANY = pl.BlockSpec(memory_space=pl.ANY)
 
 
-def project_kernel(count, span, where_ref, *refs):
+def in_hbm(array):
+    return pltpu.with_memory_space_constraint(array, pltpu.HBM)
+
+
+def in_vmem(array):
+    return pltpu.with_memory_space_constraint(array, pltpu.VMEM)
+
+
+def owner_of(k, count):
+    return lax.rem(lax.axis_index("tensor") - k + count, count)
+
+
+def load_kernel(count, gain_ref, wq_ref, wkv_ref, gain_out, wq_out, wkv_out, sems):
+    rows = wq_ref.shape[0] // count
+    copies = [pltpu.make_async_copy(gain_ref, gain_out, sems.at[2, 0])]
+    for k in range(count):
+        part = pl.ds(k * rows, rows)
+        copies.append(pltpu.make_async_copy(wq_ref.at[part], wq_out.at[part], sems.at[0, k]))
+        copies.append(pltpu.make_async_copy(wkv_ref.at[part], wkv_out.at[part], sems.at[1, k]))
+    for copy in copies:
+        copy.start()
+    for copy in copies:
+        copy.wait()
+
+
+def place_kernel(count, mine_ref, other_ref, weights, sems):
+    half = mine_ref.shape[1]
+    begin = pl.multiple_of(lax.axis_index("group") * half, half)
+    rest = pl.multiple_of(half - lax.axis_index("group") * half, half)
+    copies = []
+    for h in range(count):
+        copies.append(
+            pltpu.make_async_copy(
+                mine_ref.at[h], weights.at[h, pl.ds(begin, half)], sems.at[0, h]
+            )
+        )
+        copies.append(
+            pltpu.make_async_copy(
+                other_ref.at[h], weights.at[h, pl.ds(rest, half)], sems.at[1, h]
+            )
+        )
+    for copy in copies:
+        copy.start()
+    for copy in copies:
+        copy.wait()
+
+
+def project_kernel(count, span, *refs):
     parts = refs[:count]
     gain_ref, wq_ref, wkv_ref, query_ref, message_ref = refs[count:]
-    me = where_ref[0]
     shard = parts[0].shape[1]
     rows = parts[0].shape[0]
     total = jnp.zeros((rows, 1), F32)
@@ -52,15 +98,10 @@
     queries = jnp.zeros((rows, wq_ref.shape[1]), F32)
     keyval = jnp.zeros((rows, wkv_ref.shape[1]), F32)
     for k, part in enumerate(parts):
-        owner = lax.rem(me - k + count, count)
-        start = pl.multiple_of(owner * shard, shard)
-        normed = (part[...].astype(F32) * scale * gain_ref[pl.ds(owner, 1), :]).astype(BF16)
-        queries = queries + jnp.dot(
-            normed, wq_ref[pl.ds(start, shard), :], preferred_element_type=F32
-        )
-        keyval = keyval + jnp.dot(
-            normed, wkv_ref[pl.ds(start, shard), :], preferred_element_type=F32
-        )
+        here = pl.ds(pl.multiple_of(owner_of(k, count) * shard, shard), shard)
+        normed = (part[...].astype(F32) * scale * gain_ref[:, here]).astype(BF16)
+        queries = queries + jnp.dot(normed, wq_ref[here, :], preferred_element_type=F32)
+        keyval = keyval + jnp.dot(normed, wkv_ref[here, :], preferred_element_type=F32)
     queries = queries.astype(BF16)
     query_ref[...] = queries[:span]
     message_ref[:rows] = keyval.astype(BF16)
@@ -68,21 +109,23 @@
     message_ref[base:, : queries.shape[1]] = queries[span:]
 
 
-def attend_kernel(count, span, tick, sections, where_ref, length_ref, *refs):
+def attend_kernel(count, span, tick, *refs):
+    query_ref = refs[0]
     parts = refs[1 : 1 + count]
-    query_ref = refs[0]
-    segment_ref, turned_ref, cache_ref, out_ref, blocks, cached, small, sem = refs[1 + count :]
-    me = where_ref[0]
-    micro = tick - where_ref[1] + sections - 1
+    table_ref, cache_ref, out_ref, blocks, cached, table, small, sem, table_sem = refs[1 + count :]
+    me = lax.axis_index("tensor")
+    micro = tick - lax.axis_index("section") + lax.axis_size("section") - 1
+    table_copy = pltpu.make_async_copy(table_ref.at[pl.ds(micro, 1)], table, table_sem)
+    table_copy.start()
     copy = pltpu.make_async_copy(cache_ref.at[tick], cached, sem)
     copy.start()
     head = query_ref.shape[1]
     factor = 1.0 / math.sqrt(head)
     heads = count
     for k, part in enumerate(parts):
-        owner = lax.rem(me - k + count, count)
+        owner = owner_of(k, count)
         blocks[2 * owner] = part[:, :head]
-        blocks[2 * owner + 1] = part[:, head:]
+        blocks[2 * owner + 1] = part[:, head : 2 * head]
     keys = blocks[me, :span]
     values = blocks[heads + me, :span]
     scores = (
@@ -91,11 +134,11 @@
         )
         * factor
     )
-    across = segment_ref[pl.ds(micro, 1), :]
-    lanes = lax.broadcasted_iota(jnp.int32, turned_ref.shape, 1)
-    down = jnp.sum(jnp.where(lanes == micro, turned_ref[...], 0), axis=1, keepdims=True)
+    table_copy.wait()
+    across = table[:, :span]
     row_ids = lax.broadcasted_iota(jnp.int32, (span, span), 0)
     col_ids = lax.broadcasted_iota(jnp.int32, (span, span), 1)
+    down = jnp.sum(jnp.where(row_ids == col_ids, across, 0), axis=1, keepdims=True)
     scores = jnp.where((down == across) & (col_ids <= row_ids), scores, NEG)
     expo = jnp.exp(scores - jnp.max(scores, axis=-1, keepdims=True))
     weights = (expo / jnp.sum(expo, axis=-1, keepdims=True)).astype(BF16)
@@ -128,7 +171,7 @@
         * factor
     )
     positions = lax.broadcasted_iota(jnp.int32, dec_scores.shape, 1)
-    dec_scores = jnp.where(positions < length_ref[micro, 0], dec_scores, NEG)
+    dec_scores = jnp.where(positions < table[:, span : span + 1], dec_scores, NEG)
     top = jnp.maximum(jnp.max(dec_scores, axis=-1, keepdims=True), own)
     dec_expo = jnp.exp(dec_scores - top)
     own_expo = jnp.exp(own - top)
@@ -143,53 +186,113 @@
     out_ref[span:] = small[3, :heads].astype(BF16)
 
 
-def output_kernel(count, span, where_ref, *refs):
-    parts = refs[:count]
-    weights = refs[count : 2 * count]
-    out_ref, rows_ref, decode = refs[2 * count :]
-    me = where_ref[0]
+def summed_terms(count, span, parts, weights, scratch):
+    rows_ref, decode, placed = scratch
     for k, part in enumerate(parts):
-        decode[count * k : count * (k + 1)] = part[span:].astype(F32)
-    size = count * count
-    line = lax.broadcasted_iota(jnp.int32, (size, size), 0)
-    lane = lax.broadcasted_iota(jnp.int32, (size, size), 1)
-    want_head = lax.rem(me - line // count + count, count)
-    from_row = lax.rem(me - lane // count + count, count)
-    chosen = (lane % count == want_head) & (line % count == from_row)
-    picked = jnp.dot(
-        jnp.where(chosen, 1.0, 0.0).astype(BF16),
-        decode[...].astype(BF16),
-        preferred_element_type=F32,
-    )
+        owner = owner_of(k, count)
+        rows_ref[owner, :span] = part[:span]
+        decode[owner, :count] = part[span:].astype(F32)
+    for h in range(count):
+        for r in range(count):
+            placed[h, r : r + 1, :] = decode[r, h : h + 1, :]
+        rows_ref[h, span : span + count] = placed[h, :count].astype(BF16)
     total = None
-    for k, part in enumerate(parts):
-        rows_ref[k, :span] = part[:span]
-        rows_ref[k, span : span + count] = picked[count * k : count * (k + 1)].astype(BF16)
-        term = jnp.dot(rows_ref[k], weights[k][...], preferred_element_type=F32)
+    for h in range(count):
+        term = jnp.dot(rows_ref[h], weights[h], preferred_element_type=F32)
         term = term.astype(BF16).astype(F32)
         total = term if total is None else total + term
-    out_ref[...] = total[: span + count].astype(BF16)
+    return total[: span + count].astype(BF16)
+
+
+def first_output_kernel(count, span, *refs):
+    parts = refs[:count]
+    weights, out_ref = refs[count : count + 2]
+    out_ref[...] = summed_terms(count, span, parts, weights, refs[count + 2 :])
+
+
+def second_output_kernel(count, span, *refs):
+    parts = refs[:count]
+    weights, first_new, pend_first, second, pend_in = refs[count : count + 5]
+    out_ref, hist_stream, hist_pend = refs[count + 5 : count + 8]
+    scratch = refs[count + 8 : -2]
+    fresh, sems = refs[-2:]
+    fresh[...] = (second[...].astype(F32) + pend_in[...].astype(F32)).astype(BF16)
+    copies = [
+        pltpu.make_async_copy(first_new, hist_stream.at[0], sems.at[0]),
+        pltpu.make_async_copy(fresh, hist_stream.at[1], sems.at[1]),
+        pltpu.make_async_copy(pend_first, hist_pend.at[0], sems.at[2]),
+    ]
+    for copy in copies:
+        copy.start()
+    out_ref[...] = summed_terms(count, span, parts, weights, scratch)
+    last = pltpu.make_async_copy(out_ref, hist_pend.at[1], sems.at[3])
+    last.start()
+    for copy in copies:
+        copy.wait()
+    last.wait()
+
+
+def third_output_kernel(count, span, *refs):
+    parts = refs[:count]
+    weights, third, pend_in = refs[count : count + 3]
+    hist_stream, hist_pend = refs[count + 5 : count + 7]
+    scratch = refs[count + 7 : -3]
+    fresh, result, sems = refs[-3:]
+    fresh[...] = (third[...].astype(F32) + pend_in[...].astype(F32)).astype(BF16)
+    copy = pltpu.make_async_copy(fresh, hist_stream.at[2], sems.at[0])
+    copy.start()
+    result[...] = summed_terms(count, span, parts, weights, scratch)
+    last = pltpu.make_async_copy(result, hist_pend.at[2], sems.at[1])
+    last.start()
+    copy.wait()
+    last.wait()
 
 
 def fast_body(
     stream_in, pend_in, arrivals, norm_gain, wq, wkv, wo, cache, dec_len, span_seg
 ):
     count = lax.axis_size("tensor")
-    sections = lax.axis_size("section")
-    tensor_index = lax.axis_index("tensor")
     section_index = lax.axis_index("section")
+    group_index = lax.axis_index("group")
     rows, shard = stream_in.shape[1:]
     head = wq.shape[2]
     span = span_seg.shape[1]
     length = cache.shape[3]
     ticks = cache.shape[1]
-    where = jnp.stack([tensor_index, section_index]).astype(jnp.int32)
-    gain = norm_gain.reshape(count, shard)
-    cached = cache.reshape(ticks, length, cache.shape[4])
-    segments = span_seg
-    segments_turned = span_seg.T
-    message_rows = (rows + 7) // 8 * 8 + count
-    limit = pltpu.CompilerParams(vmem_limit_bytes=24 * 1024 * 1024)
+    half = head // 2
+    cached = in_hbm(cache.reshape(ticks, length, cache.shape[4]))
+    table = in_hbm(
+        jnp.pad(
+            jnp.concatenate([span_seg, dec_len], axis=1),
+            ((0, 0), (0, 2 * head - span - 1)),
+        )
+    )
+    padded = (rows + 7) // 8 * 8
+    message_rows = padded + count
+    limit = pltpu.CompilerParams(vmem_limit_bytes=16 * 1024 * 1024)
+    block = jax.ShapeDtypeStruct((rows, shard), BF16)
+    history = jax.ShapeDtypeStruct((ticks, rows, shard), BF16)
+
+    def cost(flops, moved_bytes):
+        return pl.CostEstimate(
+            flops=int(0 * flops), bytes_accessed=int(0 * moved_bytes), transcendentals=0
+        )
+
+    gain, wq_here, wkv_here = pl.pallas_call(
+        functools.partial(load_kernel, count),
+        out_shape=(
+            jax.ShapeDtypeStruct(norm_gain.shape, F32),
+            jax.ShapeDtypeStruct(wq.shape[1:], BF16),
+            jax.ShapeDtypeStruct(wkv.shape[1:], BF16),
+        ),
+        in_specs=[HBM] * 3,
+        out_specs=(VMEM,) * 3,
+        scratch_shapes=[pltpu.SemaphoreType.DMA((3, count))],
+        compiler_params=limit,
+        cost_estimate=cost(0, 4 * wq.shape[1] * 3 * head),
+        name="load",
+    )(in_hbm(norm_gain), in_hbm(wq[0]), in_hbm(wkv[0]))
+    gain, wq_here, wkv_here = in_vmem(gain), in_vmem(wq_here), in_vmem(wkv_here)
 
     def project(parts):
         return pl.pallas_call(
@@ -198,93 +301,151 @@
                 jax.ShapeDtypeStruct((span, head), BF16),
                 jax.ShapeDtypeStruct((message_rows, 2 * head), BF16),
             ),
-            in_specs=[SMEM] + [VMEM] * (count + 3),
+            in_specs=[VMEM] * (count + 3),
             out_specs=(VMEM, VMEM),
             compiler_params=limit,
-            cost_estimate=pl.CostEstimate(
-                flops=2 * rows * shard * count * 3 * head,
-                bytes_accessed=2 * shard * count * (3 * head + rows),
-                transcendentals=rows,
+            cost_estimate=cost(
+                2 * rows * shard * count * 3 * head, 2 * shard * count * (3 * head + rows)
             ),
             name="project",
-        )(where, *parts, gain, wq[0], wkv[0])
+        )(*[in_vmem(part) for part in parts], gain, wq_here, wkv_here)
 
     def attend(queries, parts, tick):
         return pl.pallas_call(
-            functools.partial(attend_kernel, count, span, tick, sections),
+            functools.partial(attend_kernel, count, span, tick),
             out_shape=jax.ShapeDtypeStruct((span + count, head), BF16),
-            in_specs=[SMEM, SMEM] + [VMEM] * (count + 3) + [ANY],
+            in_specs=[VMEM] * (count + 1) + [HBM] * 2,
             out_specs=VMEM,
             scratch_shapes=[
                 pltpu.VMEM((2 * count, message_rows, head), BF16),
                 pltpu.VMEM((length, cache.shape[4]), BF16),
+                pltpu.VMEM((1, 2 * head), jnp.int32),
                 pltpu.VMEM((4, 8, head), F32),
+                pltpu.SemaphoreType.DMA,
                 pltpu.SemaphoreType.DMA,
             ],
             compiler_params=limit,
-            cost_estimate=pl.CostEstimate(
-                flops=4 * 8 * length * 4 * head,
-                bytes_accessed=4 * length * 4 * head + count * message_rows * 4 * head,
-                transcendentals=span * span,
+            cost_estimate=cost(
+                4 * 8 * length * 4 * head,
+                4 * length * 4 * head + count * message_rows * 4 * head,
             ),
             name="attend",
-        )(where, dec_len, queries, *parts, segments, segments_turned, cached)
-
-    def output(parts, weights):
-        return pl.pallas_call(
-            functools.partial(output_kernel, count, span),
-            out_shape=jax.ShapeDtypeStruct((rows, shard), BF16),
-            in_specs=[SMEM] + [VMEM] * (2 * count),
-            out_specs=VMEM,
-            scratch_shapes=[
-                pltpu.VMEM((count, (rows + 7) // 8 * 8, head), BF16),
-                pltpu.VMEM((count * count, head), F32),
-            ],
-            compiler_params=limit,
-            cost_estimate=pl.CostEstimate(
-                flops=2 * rows * shard * count * head,
-                bytes_accessed=2 * shard * (count * head + rows),
-                transcendentals=0,
-            ),
-            name="output",
-        )(where, *parts, *weights)
+        )(queries, *[in_vmem(part) for part in parts], table, cached)
+
+    output_scratch = [
+        pltpu.VMEM((count, padded, head), BF16),
+        pltpu.VMEM((count, 8, head), F32),
+        pltpu.VMEM((count, 8, head), F32),
+    ]
+    output_cost = cost(2 * rows * shard * count * head, 2 * shard * (count * head + rows))
+    barrier = lax.optimization_barrier
 
     stream_parts = pieces_of(stream_in[0], "tensor")
+    own_wo = wo[0]
+    own_half = lax.dynamic_slice_in_dim(own_wo, group_index * half, half, 0)
+    own_half = own_half.reshape(half, count, shard).transpose(1, 0, 2)
     first_new = added(stream_in[0], pend_in[0])
     one_on = moved(first_new, "section", 1)
+    own_half, stream_parts[1] = barrier((own_half, stream_parts[1]))
+    mine = lax.all_to_all(own_half, "tensor", split_axis=0, concat_axis=0, tiled=True)
+    other = turned(mine, "group", 1)
+    weights = in_vmem(
+        pl.pallas_call(
+            functools.partial(place_kernel, count),
+            out_shape=jax.ShapeDtypeStruct((count, head, shard), BF16),
+            in_specs=[ANY] * 2,
+            out_specs=VMEM,
+            scratch_shapes=[pltpu.SemaphoreType.DMA((2, count))],
+            compiler_params=limit,
+            cost_estimate=cost(0, 4 * count * head * shard),
+            name="place",
+        )(mine, other)
+    )
+    early, late = arrivals[0], arrivals[1]
+    second = jnp.where(section_index == 0, early, one_on)
+
+    queries, message = project(stream_parts)
+    message_parts = pieces_of(message, "tensor")
+    attended = attend(queries, message_parts, 0)
+    attended_parts = pieces_of(attended, "tensor")
+    second, attended = barrier((second, attended))
+    second_parts = pieces_of(second, "tensor")
     two_on = moved(first_new, "section", 2)
-    out_weights = []
-    for k in range(count):
-        target = lax.rem(tensor_index + k, count)
-        block = lax.dynamic_slice_in_dim(wo[0], target * shard, shard, 1)
-        out_weights.append(block if k == 0 else turned(block, "tensor", k))
-    second = jnp.where(section_index == 0, arrivals[0], one_on)
-
-    queries, message = project(stream_parts)
-    attended = attend(queries, pieces_of(message, "tensor"), 0)
-    pend_first = output(pieces_of(attended, "tensor"), out_weights)
+    base = barrier(
+        jnp.where(section_index == 0, late, jnp.where(section_index == 1, early, two_on))
+    )
+    pend_first = pl.pallas_call(
+        functools.partial(first_output_kernel, count, span),
+        out_shape=block,
+        in_specs=[VMEM] * (count + 1),
+        out_specs=VMEM,
+        scratch_shapes=output_scratch,
+        compiler_params=limit,
+        cost_estimate=output_cost,
+        name="output_first",
+    )(*[in_vmem(part) for part in attended_parts], weights)
     pend_two_on = moved(pend_first, "section", 2)
-    pend_one_on = moved(pend_first, "section", 1)
-
-    queries, message = project(pieces_of(second, "tensor"))
-    attended = attend(queries, pieces_of(message, "tensor"), 1)
-    pend_second = output(pieces_of(attended, "tensor"), out_weights)
-    second_new = added(second, pend_one_on)
+
+    queries, message = project(second_parts)
+    message_parts = pieces_of(message, "tensor")
+    base, message_parts[1] = barrier((base, message_parts[1]))
+    third = added(base, pend_two_on)
+    third_parts = pieces_of(third, "tensor")
+    pend_late = pend_first
+    pend_late, third_parts[1] = barrier((pend_late, third_parts[1]))
+    pend_one_on = moved(pend_late, "section", 1)
+    attended = attend(queries, message_parts, 1)
+    attended_parts = pieces_of(attended, "tensor")
+    third, attended = barrier((third, attended))
+    third_queries, third_message = project([third] + third_parts[1:])
+    third_message_parts = pieces_of(third_message, "tensor")
+    attended_parts[1], third_message_parts[1] = barrier((attended_parts[1], third_message_parts[1]))
+    pend_second, hist_stream, hist_pend = pl.pallas_call(
+        functools.partial(second_output_kernel, count, span),
+        out_shape=(block, history, history),
+        in_specs=[VMEM] * (count + 5),
+        out_specs=(VMEM, HBM, HBM),
+        scratch_shapes=output_scratch
+        + [pltpu.VMEM((rows, shard), BF16), pltpu.SemaphoreType.DMA((4,))],
+        compiler_params=limit,
+        cost_estimate=output_cost,
+        name="output_second",
+    )(
+        *[in_vmem(part) for part in attended_parts],
+        weights,
+        in_vmem(first_new),
+        in_vmem(pend_first),
+        in_vmem(second),
+        in_vmem(pend_one_on),
+    )
     pend_last_in = moved(pend_second, "section", 1)
-
-    third = jnp.where(
-        section_index == 0,
-        arrivals[1],
-        jnp.where(section_index == 1, arrivals[0], added(two_on, pend_two_on)),
-    )
-    queries, message = project(pieces_of(third, "tensor"))
-    attended = attend(queries, pieces_of(message, "tensor"), 2)
-    pend_third = output(pieces_of(attended, "tensor"), out_weights)
-    third_new = added(third, pend_last_in)
-    return (
-        jnp.stack([first_new, second_new, third_new])[None],
-        jnp.stack([pend_first, pend_second, pend_third])[None],
-    )
+    third_queries, pend_second = barrier((third_queries, pend_second))
+    attended = attend(third_queries, third_message_parts, 2)
+    attended_parts = pieces_of(attended, "tensor")
+    hist_stream, hist_pend = pl.pallas_call(
+        functools.partial(third_output_kernel, count, span),
+        out_shape=(history, history),
+        in_specs=[VMEM] * (count + 3) + [HBM] * 2,
+        out_specs=(HBM, HBM),
+        scratch_shapes=output_scratch
+        + [
+            pltpu.VMEM((rows, shard), BF16),
+            pltpu.VMEM((rows, shard), BF16),
+            pltpu.SemaphoreType.DMA((2,)),
+        ],
+        input_output_aliases={count + 3: 0, count + 4: 1},
+        compiler_params=limit,
+        cost_estimate=output_cost,
+        name="output_third",
+    )(
+        *[in_vmem(part) for part in attended_parts],
+        weights,
+        in_vmem(third),
+        in_vmem(pend_last_in),
+        hist_stream,
+        hist_pend,
+    )
+    return hist_stream[None], hist_pend[None]
 
 
 def passed_along(block, axis, distance):
@@ -419,6 +580,7 @@
     head = wq.shape[2]
     fits = (
         head == 128
+        and lax.axis_size("group") == 2
         and count <= 8
         and cache.shape[1] == 3
         and cache.shape[2] == 1

time: 151 us -> 124 us (0.82)
  local copies, waits for them, and re-layouts: 14.8 us -> 2.49 us
  starting transfers between devices: 61.7 us -> 50.9 us
  other arithmetic: 7.95 us -> 0.26 us
  waiting for transfers between devices: 48.9 us -> 55 us
  Pallas kernels: 16 us -> 13.9 us
    ppermute x30 -> x28, starting transfers between devices: 50.5 us -> 36 us  [turned(): lax.ppermute(block, axis, [(i, (i + distance) % count) for i in range(cou...]
    unnamed x69 -> x13, local copies, waits for them, and re-layouts: 11.6 us -> 0.12 us
    all_to_all x0 -> x1, waiting for transfers between devices: none -> 7.39 us  [fast_body(): lax.all_to_all(own_half, 'tensor', split_axis=0, concat_axis=0, tiled=True)]
    all_to_all x0 -> x1, starting transfers between devices: none -> 3.6 us  [fast_body(): lax.all_to_all(own_half, 'tensor', split_axis=0, concat_axis=0, tiled=True)]
    broadcast_in_dim x2 -> x0, other arithmetic: 2.61 us -> none  [the longest x1 1.8 us: fast_body(): jnp.stack([pend_first, pend_second, pend_third])[None]]
    another operation x3 -> x0, other arithmetic: 2.29 us -> none  [the longest x2 2.21 us: fast_body(): jnp.stack([first_new, second_new, third_new])[None]]
    slice x1, local copies, waits for them, and re-layouts: 2.27 us -> 0.39 us  [fast_body(): early, late = (arrivals[0], arrivals[1])]
    pallas_call x3, Pallas kernels: 4.15 us -> 2.59 us  [project(): pl.pallas_call(functools.partial(project_kernel, count, span), out_shape=...]
  transfers between devices with their start and end apart: 35 -> 34, of which waited for: 16 -> 19; matrix products, arithmetic and copies ran while one was open for 5% -> 2% of each run, Pallas kernels for 5% -> 9%
where the time goes in v2:
time: 124 us; the launch traced here: 123 us
  waiting for transfers between devices  55 us (44%)
  starting transfers between devices  50.9 us (41%)
  Pallas kernels  13.9 us (11%)
  local copies, waits for them, and re-layouts  2.49 us (2%)
    ppermute x28, waiting for transfers between devices, turned(): lax.ppermute(block, axis, [(i, (i + distance) % count) for i in range(cou...  47.6 us
    ppermute x28, starting transfers between devices, turned(): lax.ppermute(block, axis, [(i, (i + distance) % count) for i in range(cou...  36 us
    ppermute x5, starting transfers between devices, moved(): return lax.ppermute(block, axis, route)  11.3 us
    all_to_all x1, waiting for transfers between devices, fast_body(): lax.all_to_all(own_half, 'tensor', split_axis=0, concat_axis=0, tiled=True)  7.39 us
    pallas_call x3, Pallas kernels, attend(): pl.pallas_call(functools.partial(attend_kernel, count, span, tick), out_s...  5.36 us
    all_to_all x1, starting transfers between devices, fast_body(): lax.all_to_all(own_half, 'tensor', split_axis=0, concat_axis=0, tiled=True)  3.6 us
    pallas_call x3, Pallas kernels, project(): pl.pallas_call(functools.partial(project_kernel, count, span), out_shape=...  2.59 us
  transfers between devices with their start and end apart: 34, of which 19 were waited for; matrix products, arithmetic and copies ran while one was open for 2% of the time, Pallas kernels for 9%

profile of v2, /device:TPU:0, one launch (start us, length us, event | category | flops | bytes accessed | tf_op | source)
XLA Modules:
  0.0 123.5 jit_solution(5680200013821695936)
XLA Ops:
  0.6 3.1 %collective-permute-start.2 = (bf16[68,1024]{1,0:T(8,128)(2,1)}, bf16[68,1024]{1,0:T(8,128)(2,1)S(1)}, u32[]{:S(2)}, u32[]{:S(2)}) collective-permute-start(bf16[68,1024]{1,0:T(8,128)(2,1)} %bitcast.23), channel_id=1, source_target_pairs={{0,4},{4,8},{8,12},{12,0},{1,5},{5,9},{9,13},{13,1},{2,6},{6,10},{... | collective-permute-start | bytes 417800 | tf_op jit(solution)/shard_map/ppermute | solution.py:25
  4.2 1.0 copy.32
  5.1 4.7 %collective-permute-done.2.refs_1_ = bf16[68,1024]{1,0:T(8,128)(2,1)S(1)} collective-permute-done((bf16[68,1024]{1,0:T(8,128)(2,1)}, bf16[68,1024]{1,0:T(8,128)(2,1)S(1)}, u32[]{:S(2)}, u32[]{:S(2)}) %collective-permute-start.2) | collective-permute-done | bytes 139296 | tf_op jit(solution)/shard_map/ppermute | solution.py:25
  9.8 3.6 %all-to-all-start = ((bf16[4,64,1024]{2,1,0:T(8,128)(2,1)}), bf16[4,64,1024]{2,1,0:T(8,128)(2,1)S(1)}, u32[]{:S(2)}, u32[]{:S(2)}) async-start(bf16[4,64,1024]{2,1,0:T(8,128)(2,1)} %bitcast.22), calls=%async_computation | async-start | bytes 1048576 | tf_op jit(solution)/shard_map/all_to_all | solution.py:350
  13.5 1.3 %collective-permute-start.1 = (bf16[68,1024]{1,0:T(8,128)(2,1)S(1)}, bf16[68,1024]{1,0:T(8,128)(2,1)S(1)}, u32[]{:S(2)}, u32[]{:S(2)}) collective-permute-start(bf16[68,1024]{1,0:T(8,128)(2,1)S(1)} %fusion.refs_5_), channel_id=1, source_target_pairs={{0,1},{1,2},{2,3},{4,5},{5,6},{6,7},{8,9},{9,10},{10,11},{12,13},{... | collective-permute-start | bytes 417800 | tf_op jit(solution)/shard_map/ppermute | solution.py:20
  14.8 4.0 %collective-permute-start = (bf16[68,1024]{1,0:T(8,128)(2,1)S(1)}, bf16[68,1024]{1,0:T(8,128)(2,1)S(1)}, u32[]{:S(2)}, u32[]{:S(2)}) collective-permute-start(bf16[68,1024]{1,0:T(8,128)(2,1)S(1)} %fusion.refs_5_), channel_id=1, source_target_pairs={{0,2},{1,3},{4,6},{5,7},{8,10},{9,11},{12,14},{13,15},{16,18},{17,... | collective-permute-start | bytes 417800 | tf_op jit(solution)/shard_map/ppermute | solution.py:20
  18.8 3.8 %collective-permute-start.4 = (bf16[68,1024]{1,0:T(8,128)(2,1)S(1)}, bf16[68,1024]{1,0:T(8,128)(2,1)S(1)}, u32[]{:S(2)}, u32[]{:S(2)}) collective-permute-start(bf16[68,1024]{1,0:T(8,128)(2,1)S(1)} %bitcast.24), channel_id=1, source_target_pairs={{0,12},{4,0},{8,4},{12,8},{1,13},{5,1},{9,5},{13,9},{2,14},{6,2},{... | collective-permute-start | bytes 417800 | tf_op jit(solution)/shard_map/ppermute | solution.py:25
  22.7 7.4 %all-to-all-done.mine_ref = bf16[4,64,1024]{2,1,0:T(8,128)(2,1)S(1)} async-done(((bf16[4,64,1024]{2,1,0:T(8,128)(2,1)}), bf16[4,64,1024]{2,1,0:T(8,128)(2,1)S(1)}, u32[]{:S(2)}, u32[]{:S(2)}) %all-to-all-start) | async-done | bytes 524320 | tf_op jit(solution)/shard_map/all_to_all | solution.py:350
  30.1 1.4 %collective-permute-start.15 = (bf16[4,64,1024]{2,1,0:T(8,128)(2,1)S(1)}, bf16[4,64,1024]{2,1,0:T(8,128)(2,1)S(1)}, u32[]{:S(2)}, u32[]{:S(2)}) collective-permute-start(bf16[4,64,1024]{2,1,0:T(8,128)(2,1)S(1)} %all-to-all-done.mine_ref), channel_id=1, source_target_pairs={{0,16},{16,0},{1,17},{17,1},{2,18},{18,2},{3,19},{19,3},{4,20},{20... | collective-permute-start | bytes 1572872 | tf_op jit(solution)/shard_map/ppermute | solution.py:25
  32.2 1.9 %load.1 = (f32[1,4096]{1,0:T(1,128)S(1)}, bf16[4096,128]{1,0:T(8,128)(2,1)S(1)}, bf16[4096,256]{1,0:T(8,128)(2,1)S(1)}) custom-call(f32[1,4096]{1,0:T(1,128)} %gain_ref.1, bf16[4096,128]{1,0:T(8,128)(2,1)} %bitcast.31, bf16[4096,256]{1,0:T(8,128)(2,1)} %bitcast.30), custom_call_target="tpu_custom_call" | custom-call | tf_op jit(solution)/shard_map/load/pallas_call | solution.py:281
  34.6 2.5 %collective-permute-done.3.refs_2_ = bf16[68,1024]{1,0:T(8,128)(2,1)S(1)} collective-permute-done((bf16[68,1024]{1,0:T(8,128)(2,1)S(1)}, bf16[68,1024]{1,0:T(8,128)(2,1)S(1)}, u32[]{:S(2)}, u32[]{:S(2)}) %collective-permute-start.3) | collective-permute-done | bytes 139296 | tf_op jit(solution)/shard_map/ppermute | solution.py:25
  37.1 0.9 project.3
  37.9 4.1 %collective-permute-start.7 = (bf16[76,256]{1,0:T(8,128)(2,1)S(1)}, bf16[76,256]{1,0:T(8,128)(2,1)S(1)}, u32[]{:S(2)}, u32[]{:S(2)}) collective-permute-start(bf16[76,256]{1,0:T(8,128)(2,1)S(1)} %get-tuple-element.32.refs_1_), channel_id=1, source_target_pairs={{0,12},{4,0},{8,4},{12,8},{1,13},{5,1},{9,5},{13,9},{2,14},{6,2},{... | collective-permute-start | bytes 116744 | tf_op jit(solution)/shard_map/ppermute | solution.py:25
  42.8 0.9 collective-permute-done.7.refs_4_
  43.8 3.5 %collective-permute-done.6.refs_3_ = bf16[76,256]{1,0:T(8,128)(2,1)S(1)} collective-permute-done((bf16[76,256]{1,0:T(8,128)(2,1)S(1)}, bf16[76,256]{1,0:T(8,128)(2,1)S(1)}, u32[]{:S(2)}, u32[]{:S(2)}) %collective-permute-start.6) | collective-permute-done | bytes 38944 | tf_op jit(solution)/shard_map/ppermute | solution.py:25
  47.3 0.7 collective-permute-done.5.refs_2_
  48.0 1.8 %attend.3.refs_0_ = bf16[68,128]{1,0:T(8,128)(2,1)S(1)} custom-call(bf16[64,128]{1,0:T(8,128)(2,1)S(1)} %get-tuple-element.31.refs_0_, bf16[76,256]{1,0:T(8,128)(2,1)S(1)} %get-tuple-element.32.refs_1_, bf16[76,256]{1,0:T(8,128)(2,1)S(1)} %collective-permute-done.5.refs_2_, bf16[76,256]{1,0:T(8,128)(2,1)S(1)} %collective-permute-done.6.refs_3_, ...), custom_call_target="tpu_custom_call" | custom-call | tf_op jit(solution)/shard_map/attend/pallas_call | solution.py:314
  50.9 1.9 %collective-permute-start.8 = (bf16[68,1024]{1,0:T(8,128)(2,1)S(1)}, bf16[68,1024]{1,0:T(8,128)(2,1)S(1)}, u32[]{:S(2)}, u32[]{:S(2)}) collective-permute-start(bf16[68,1024]{1,0:T(8,128)(2,1)S(1)} %get-tuple-element.33.refs_0_.refs_7_), channel_id=1, source_target_pairs={{0,4},{4,8},{8,12},{12,0},{1,5},{5,9},{9,13},{13,1},{2,6},{6,10},{... | collective-permute-start | bytes 417800 | tf_op jit(solution)/shard_map/ppermute | solution.py:25
  52.9 1.9 %collective-permute-start.14 = (bf16[68,128]{1,0:T(8,128)(2,1)S(1)}, bf16[68,128]{1,0:T(8,128)(2,1)S(1)}, u32[]{:S(2)}, u32[]{:S(2)}) collective-permute-start(bf16[68,128]{1,0:T(8,128)(2,1)S(1)} %attend.3.refs_0_), channel_id=1, source_target_pairs={{0,12},{4,0},{8,4},{12,8},{1,13},{5,1},{9,5},{13,9},{2,14},{6,2},{... | collective-permute-start | bytes 52232 | tf_op jit(solution)/shard_map/ppermute | solution.py:25
  54.8 1.9 %collective-permute-done.14.refs_3_ = bf16[68,128]{1,0:T(8,128)(2,1)S(1)} collective-permute-done((bf16[68,128]{1,0:T(8,128)(2,1)S(1)}, bf16[68,128]{1,0:T(8,128)(2,1)S(1)}, u32[]{:S(2)}, u32[]{:S(2)}) %collective-permute-start.14) | collective-permute-done | bytes 17440 | tf_op jit(solution)/shard_map/ppermute | solution.py:25
  56.7 4.1 %collective-permute-start.13 = (bf16[68,128]{1,0:T(8,128)(2,1)S(1)}, bf16[68,128]{1,0:T(8,128)(2,1)S(1)}, u32[]{:S(2)}, u32[]{:S(2)}) collective-permute-start(bf16[68,128]{1,0:T(8,128)(2,1)S(1)} %attend.3.refs_0_), channel_id=1, source_target_pairs={{0,8},{4,12},{8,0},{12,4},{1,9},{5,13},{9,1},{13,5},{2,10},{6,14},... | collective-permute-start | bytes 52232 | tf_op jit(solution)/shard_map/ppermute | solution.py:25
  60.8 1.0 collective-permute-start.12
  61.8 1.4 %place.1.refs_4_ = bf16[4,128,1024]{2,1,0:T(8,128)(2,1)S(1)} custom-call(bf16[4,64,1024]{2,1,0:T(8,128)(2,1)S(1)} %all-to-all-done.mine_ref, bf16[4,64,1024]{2,1,0:T(8,128)(2,1)S(1)} %collective-permute-done.15.other_ref), custom_call_target="tpu_custom_call" | custom-call | tf_op jit(solution)/shard_map/place/pallas_call | solution.py:353
  63.2 3.1 %collective-permute-done.12.refs_1_ = bf16[68,128]{1,0:T(8,128)(2,1)S(1)} collective-permute-done((bf16[68,128]{1,0:T(8,128)(2,1)S(1)}, bf16[68,128]{1,0:T(8,128)(2,1)S(1)}, u32[]{:S(2)}, u32[]{:S(2)}) %collective-permute-start.12) | collective-permute-done | bytes 17440 | tf_op jit(solution)/shard_map/ppermute | solution.py:25
  66.7 3.4 %collective-permute-start.16 = (bf16[68,1024]{1,0:T(8,128)(2,1)S(1)}, bf16[68,1024]{1,0:T(8,128)(2,1)S(1)}, u32[]{:S(2)}, u32[]{:S(2)}) collective-permute-start(bf16[68,1024]{1,0:T(8,128)(2,1)S(1)} %output_first.1.refs_6_), channel_id=1, source_target_pairs={{0,2},{1,3},{4,6},{5,7},{8,10},{9,11},{12,14},{13,15},{16,18},{17,... | collective-permute-start | bytes 417800 | tf_op jit(solution)/shard_map/ppermute | solution.py:20
  70.1 0.9 project.4
  71.2 6.3 %collective-permute-done.11.refs_2_ = bf16[76,256]{1,0:T(8,128)(2,1)S(1)} collective-permute-done((bf16[76,256]{1,0:T(8,128)(2,1)S(1)}, bf16[76,256]{1,0:T(8,128)(2,1)S(1)}, u32[]{:S(2)}, u32[]{:S(2)}) %collective-permute-start.11) | collective-permute-done | bytes 38944 | tf_op jit(solution)/shard_map/ppermute | solution.py:25
  77.6 3.8 %collective-permute-start.21 = (bf16[68,1024]{1,0:T(8,128)(2,1)S(1)}, bf16[68,1024]{1,0:T(8,128)(2,1)S(1)}, u32[]{:S(2)}, u32[]{:S(2)}) collective-permute-start(bf16[68,1024]{1,0:T(8,128)(2,1)S(1)} %add_convert_fusion.refs_0_.refs_5_), channel_id=1, source_target_pairs={{0,12},{4,0},{8,4},{12,8},{1,13},{5,1},{9,5},{13,9},{2,14},{6,2},{... | collective-permute-start | bytes 417800 | tf_op jit(solution)/shard_map/ppermute | solution.py:25
  81.4 3.1 %collective-permute-done.19.refs_1_ = bf16[68,1024]{1,0:T(8,128)(2,1)S(1)} collective-permute-done((bf16[68,1024]{1,0:T(8,128)(2,1)S(1)}, bf16[68,1024]{1,0:T(8,128)(2,1)S(1)}, u32[]{:S(2)}, u32[]{:S(2)}) %collective-permute-start.19) | collective-permute-done | bytes 139296 | tf_op jit(solution)/shard_map/ppermute | solution.py:25
  84.5 1.3 %collective-permute-start.26 = (bf16[68,1024]{1,0:T(8,128)(2,1)S(1)}, bf16[68,1024]{1,0:T(8,128)(2,1)S(1)}, u32[]{:S(2)}, u32[]{:S(2)}) collective-permute-start(bf16[68,1024]{1,0:T(8,128)(2,1)S(1)} %output_first.1.refs_6_), channel_id=1, source_target_pairs={{0,1},{1,2},{2,3},{4,5},{5,6},{6,7},{8,9},{9,10},{10,11},{12,13},{... | collective-permute-start | bytes 417800 | tf_op jit(solution)/shard_map/ppermute | solution.py:20
  86.0 5.1 %collective-permute-done.18.refs_4_ = bf16[76,256]{1,0:T(8,128)(2,1)S(1)} collective-permute-done((bf16[76,256]{1,0:T(8,128)(2,1)S(1)}, bf16[76,256]{1,0:T(8,128)(2,1)S(1)}, u32[]{:S(2)}, u32[]{:S(2)}) %collective-permute-start.18) | collective-permute-done | bytes 38944 | tf_op jit(solution)/shard_map/ppermute | solution.py:25
  91.3 1.8 %attend.4.refs_0_ = bf16[68,128]{1,0:T(8,128)(2,1)S(1)} custom-call(bf16[64,128]{1,0:T(8,128)(2,1)S(1)} %get-tuple-element.37.refs_0_, bf16[76,256]{1,0:T(8,128)(2,1)S(1)} %get-tuple-element.34.refs_1_, bf16[76,256]{1,0:T(8,128)(2,1)S(1)} %collective-permute-done.11.refs_2_, bf16[76,256]{1,0:T(8,128)(2,1)S(1)} %collective-permute-done.17.refs_3_, ...), custom_call_target="tpu_custom_call" | custom-call | tf_op jit(solution)/shard_map/attend/pallas_call | solution.py:314
  93.1 0.9 project.5
  94.0 1.6 %collective-permute-start.23 = (bf16[76,256]{1,0:T(8,128)(2,1)S(1)}, bf16[76,256]{1,0:T(8,128)(2,1)S(1)}, u32[]{:S(2)}, u32[]{:S(2)}) collective-permute-start(bf16[76,256]{1,0:T(8,128)(2,1)S(1)} %get-tuple-element.42.refs_1_), channel_id=1, source_target_pairs={{0,4},{4,8},{8,12},{12,0},{1,5},{5,9},{9,13},{13,1},{2,6},{6,10},{... | collective-permute-start | bytes 116744 | tf_op jit(solution)/shard_map/ppermute | solution.py:25
  95.6 3.8 %collective-permute-start.25 = (bf16[68,128]{1,0:T(8,128)(2,1)S(1)}, bf16[68,128]{1,0:T(8,128)(2,1)S(1)}, u32[]{:S(2)}, u32[]{:S(2)}) collective-permute-start(bf16[68,128]{1,0:T(8,128)(2,1)S(1)} %attend.4.refs_0_), channel_id=1, source_target_pairs={{0,12},{4,0},{8,4},{12,8},{1,13},{5,1},{9,5},{13,9},{2,14},{6,2},{... | collective-permute-start | bytes 52232 | tf_op jit(solution)/shard_map/ppermute | solution.py:25
  99.4 1.8 %collective-permute-done.22.refs_1_ = bf16[68,128]{1,0:T(8,128)(2,1)S(1)} collective-permute-done((bf16[68,128]{1,0:T(8,128)(2,1)S(1)}, bf16[68,128]{1,0:T(8,128)(2,1)S(1)}, u32[]{:S(2)}, u32[]{:S(2)}) %collective-permute-start.22) | collective-permute-done | bytes 17440 | tf_op jit(solution)/shard_map/ppermute | solution.py:25
  101.2 2.8 %collective-permute-done.24.refs_2_ = bf16[68,128]{1,0:T(8,128)(2,1)S(1)} collective-permute-done((bf16[68,128]{1,0:T(8,128)(2,1)S(1)}, bf16[68,128]{1,0:T(8,128)(2,1)S(1)}, u32[]{:S(2)}, u32[]{:S(2)}) %collective-permute-start.24) | collective-permute-done | bytes 17440 | tf_op jit(solution)/shard_map/ppermute | solution.py:25
  104.0 1.2 output_second.1
  105.2 1.3 %collective-permute-start.32 = (bf16[68,1024]{1,0:T(8,128)(2,1)S(1)}, bf16[68,1024]{1,0:T(8,128)(2,1)S(1)}, u32[]{:S(2)}, u32[]{:S(2)}) collective-permute-start(bf16[68,1024]{1,0:T(8,128)(2,1)S(1)} %get-tuple-element.45), channel_id=1, source_target_pairs={{0,1},{1,2},{2,3},{4,5},{5,6},{6,7},{8,9},{9,10},{10,11},{12,13},{... | collective-permute-start | bytes 417800 | tf_op jit(solution)/shard_map/ppermute | solution.py:20
  106.5 1.0 collective-permute-start.28
  107.5 3.3 %collective-permute-done.28.refs_4_ = bf16[76,256]{1,0:T(8,128)(2,1)S(1)} collective-permute-done((bf16[76,256]{1,0:T(8,128)(2,1)S(1)}, bf16[76,256]{1,0:T(8,128)(2,1)S(1)}, u32[]{:S(2)}, u32[]{:S(2)}) %collective-permute-start.28) | collective-permute-done | bytes 38944 | tf_op jit(solution)/shard_map/ppermute | solution.py:25
  110.7 2.5 %collective-permute-done.27.refs_3_ = bf16[76,256]{1,0:T(8,128)(2,1)S(1)} collective-permute-done((bf16[76,256]{1,0:T(8,128)(2,1)S(1)}, bf16[76,256]{1,0:T(8,128)(2,1)S(1)}, u32[]{:S(2)}, u32[]{:S(2)}) %collective-permute-start.27) | collective-permute-done | bytes 38944 | tf_op jit(solution)/shard_map/ppermute | solution.py:25
  113.2 1.8 %attend.5.refs_0_ = bf16[68,128]{1,0:T(8,128)(2,1)S(1)} custom-call(bf16[64,128]{1,0:T(8,128)(2,1)S(1)} %get-tuple-element.46.refs_0_, bf16[76,256]{1,0:T(8,128)(2,1)S(1)} %get-tuple-element.42.refs_1_, bf16[76,256]{1,0:T(8,128)(2,1)S(1)} %collective-permute-done.23.refs_2_, bf16[76,256]{1,0:T(8,128)(2,1)S(1)} %collective-permute-done.27.refs_3_, ...), custom_call_target="tpu_custom_call" | custom-call | tf_op jit(solution)/shard_map/attend/pallas_call | solution.py:314
  115.0 1.7 %collective-permute-start.31 = (bf16[68,128]{1,0:T(8,128)(2,1)S(1)}, bf16[68,128]{1,0:T(8,128)(2,1)S(1)}, u32[]{:S(2)}, u32[]{:S(2)}) collective-permute-start(bf16[68,128]{1,0:T(8,128)(2,1)S(1)} %attend.5.refs_0_), channel_id=1, source_target_pairs={{0,12},{4,0},{8,4},{12,8},{1,13},{5,1},{9,5},{13,9},{2,14},{6,2},{... | collective-permute-start | bytes 52232 | tf_op jit(solution)/shard_map/ppermute | solution.py:25
  117.4 1.5 %collective-permute-done.31.refs_3_ = bf16[68,128]{1,0:T(8,128)(2,1)S(1)} collective-permute-done((bf16[68,128]{1,0:T(8,128)(2,1)S(1)}, bf16[68,128]{1,0:T(8,128)(2,1)S(1)}, u32[]{:S(2)}, u32[]{:S(2)}) %collective-permute-start.31) | collective-permute-done | bytes 17440 | tf_op jit(solution)/shard_map/ppermute | solution.py:25
  118.9 2.5 %collective-permute-done.30.refs_2_ = bf16[68,128]{1,0:T(8,128)(2,1)S(1)} collective-permute-done((bf16[68,128]{1,0:T(8,128)(2,1)S(1)}, bf16[68,128]{1,0:T(8,128)(2,1)S(1)}, u32[]{:S(2)}, u32[]{:S(2)}) %collective-permute-start.30) | collective-permute-done | bytes 17440 | tf_op jit(solution)/shard_map/ppermute | solution.py:25
  121.4 1.0 collective-permute-done.29.refs_1_
  122.4 1.1 output_third.1
  (53 shorter events, 5.3 us)
Async XLA Ops:
  0.6 3.1 %copy-start = (bf16[1,128,4096]{2,1,0:T(8,128)(2,1)S(1)}, bf16[1,128,4096]{2,1,0:T(8,128)(2,1)}, u32[]{:S(2)}) copy-start(bf16[1,128,4096]{2,1,0:T(8,128)(2,1)} %param.16) | copy-start | bytes 3145732
  0.6 9.2 %collective-permute-start.2 = (bf16[68,1024]{1,0:T(8,128)(2,1)}, bf16[68,1024]{1,0:T(8,128)(2,1)S(1)}, u32[]{:S(2)}, u32[]{:S(2)}) collective-permute-start(bf16[68,1024]{1,0:T(8,128)(2,1)} %bitcast.23), channel_id=1, source_target_pairs={{0,4},{4,8},{8,12},{12,0},{1,5},{5,9},{9,13},{13,1},{2,6},{6,10},{... | collective-permute-start | bytes 417800 | tf_op jit(solution)/shard_map/ppermute | solution.py:25
  3.7 9.7 %copy-start.1 = (bf16[1,68,1024]{2,1,0:T(8,128)(2,1)S(1)}, bf16[1,68,1024]{2,1,0:T(8,128)(2,1)}, u32[]{:S(2)}) copy-start(bf16[1,68,1024]{2,1,0:T(8,128)(2,1)} %param.10) | copy-start | bytes 417796
  3.7 9.7 %copy-start.3 = (bf16[1,68,1024]{2,1,0:T(8,128)(2,1)S(1)}, bf16[1,68,1024]{2,1,0:T(8,128)(2,1)}, u32[]{:S(2)}) copy-start(bf16[1,68,1024]{2,1,0:T(8,128)(2,1)} %param.11) | copy-start | bytes 417796
  3.7 18.9 %copy-start.5 = (s32[6,1]{0,1:T(1,128)S(1)}, s32[6,1]{0,1:T(1,128)}, u32[]{:S(2)}) copy-start(s32[6,1]{0,1:T(1,128)} %param.18) | copy-start | bytes 76
  3.7 27.8 %copy-start.4 = (s32[6,64]{1,0:T(8,128)S(1)}, s32[6,64]{1,0:T(8,128)}, u32[]{:S(2)}) copy-start(s32[6,64]{1,0:T(8,128)} %param.19) | copy-start | bytes 4612
  9.8 24.4 %copy-start.2 = (bf16[2,68,1024]{2,0,1:T(2,128)(2,1)S(1)}, bf16[2,68,1024]{2,0,1:T(2,128)(2,1)}, u32[]{:S(2)}) copy-start(bf16[2,68,1024]{2,0,1:T(2,128)(2,1)} %param.12) | copy-start | bytes 835588
  9.8 20.3 %all-to-all-start = ((bf16[4,64,1024]{2,1,0:T(8,128)(2,1)}), bf16[4,64,1024]{2,1,0:T(8,128)(2,1)S(1)}, u32[]{:S(2)}, u32[]{:S(2)}) async-start(bf16[4,64,1024]{2,1,0:T(8,128)(2,1)} %bitcast.22), calls=%async_computation | async-start | bytes 1048576 | tf_op jit(solution)/shard_map/all_to_all | solution.py:350
  13.5 28.6 %collective-permute-start.1 = (bf16[68,1024]{1,0:T(8,128)(2,1)S(1)}, bf16[68,1024]{1,0:T(8,128)(2,1)S(1)}, u32[]{:S(2)}, u32[]{:S(2)}) collective-permute-start(bf16[68,1024]{1,0:T(8,128)(2,1)S(1)} %fusion.refs_5_), channel_id=1, source_target_pairs={{0,1},{1,2},{2,3},{4,5},{5,6},{6,7},{8,9},{9,10},{10,11},{12,13},{... | collective-permute-start | bytes 417800 | tf_op jit(solution)/shard_map/ppermute | solution.py:20
  14.8 27.9 %collective-permute-start = (bf16[68,1024]{1,0:T(8,128)(2,1)S(1)}, bf16[68,1024]{1,0:T(8,128)(2,1)S(1)}, u32[]{:S(2)}, u32[]{:S(2)}) collective-permute-start(bf16[68,1024]{1,0:T(8,128)(2,1)S(1)} %fusion.refs_5_), channel_id=1, source_target_pairs={{0,2},{1,3},{4,6},{5,7},{8,10},{9,11},{12,14},{13,15},{16,18},{17,... | collective-permute-start | bytes 417800 | tf_op jit(solution)/shard_map/ppermute | solution.py:20
  18.8 15.7 %collective-permute-start.4 = (bf16[68,1024]{1,0:T(8,128)(2,1)S(1)}, bf16[68,1024]{1,0:T(8,128)(2,1)S(1)}, u32[]{:S(2)}, u32[]{:S(2)}) collective-permute-start(bf16[68,1024]{1,0:T(8,128)(2,1)S(1)} %bitcast.24), channel_id=1, source_target_pairs={{0,12},{4,0},{8,4},{12,8},{1,13},{5,1},{9,5},{13,9},{2,14},{6,2},{... | collective-permute-start | bytes 417800 | tf_op jit(solution)/shard_map/ppermute | solution.py:25
  22.6 14.4 %collective-permute-start.3 = (bf16[68,1024]{1,0:T(8,128)(2,1)S(1)}, bf16[68,1024]{1,0:T(8,128)(2,1)S(1)}, u32[]{:S(2)}, u32[]{:S(2)}) collective-permute-start(bf16[68,1024]{1,0:T(8,128)(2,1)S(1)} %bitcast.25), channel_id=1, source_target_pairs={{0,8},{4,12},{8,0},{12,4},{1,9},{5,13},{9,1},{13,5},{2,10},{6,14},... | collective-permute-start | bytes 417800 | tf_op jit(solution)/shard_map/ppermute | solution.py:25
  30.1 30.6 %collective-permute-start.15 = (bf16[4,64,1024]{2,1,0:T(8,128)(2,1)S(1)}, bf16[4,64,1024]{2,1,0:T(8,128)(2,1)S(1)}, u32[]{:S(2)}, u32[]{:S(2)}) collective-permute-start(bf16[4,64,1024]{2,1,0:T(8,128)(2,1)S(1)} %all-to-all-done.mine_ref), channel_id=1, source_target_pairs={{0,16},{16,0},{1,17},{17,1},{2,18},{18,2},{3,19},{19,3},{4,20},{20... | collective-permute-start | bytes 1572872 | tf_op jit(solution)/shard_map/ppermute | solution.py:25
  37.9 5.8 %collective-permute-start.7 = (bf16[76,256]{1,0:T(8,128)(2,1)S(1)}, bf16[76,256]{1,0:T(8,128)(2,1)S(1)}, u32[]{:S(2)}, u32[]{:S(2)}) collective-permute-start(bf16[76,256]{1,0:T(8,128)(2,1)S(1)} %get-tuple-element.32.refs_1_), channel_id=1, source_target_pairs={{0,12},{4,0},{8,4},{12,8},{1,13},{5,1},{9,5},{13,9},{2,14},{6,2},{... | collective-permute-start | bytes 116744 | tf_op jit(solution)/shard_map/ppermute | solution.py:25
  42.1 5.2 %collective-permute-start.6 = (bf16[76,256]{1,0:T(8,128)(2,1)S(1)}, bf16[76,256]{1,0:T(8,128)(2,1)S(1)}, u32[]{:S(2)}, u32[]{:S(2)}) collective-permute-start(bf16[76,256]{1,0:T(8,128)(2,1)S(1)} %get-tuple-element.32.refs_1_), channel_id=1, source_target_pairs={{0,8},{4,12},{8,0},{12,4},{1,9},{5,13},{9,1},{13,5},{2,10},{6,14},... | collective-permute-start | bytes 116744 | tf_op jit(solution)/shard_map/ppermute | solution.py:25
  42.1 5.9 %collective-permute-start.5 = (bf16[76,256]{1,0:T(8,128)(2,1)S(1)}, bf16[76,256]{1,0:T(8,128)(2,1)S(1)}, u32[]{:S(2)}, u32[]{:S(2)}) collective-permute-start(bf16[76,256]{1,0:T(8,128)(2,1)S(1)} %get-tuple-element.32.refs_1_), channel_id=1, source_target_pairs={{0,4},{4,8},{8,12},{12,0},{1,5},{5,9},{9,13},{13,1},{2,6},{6,10},{... | collective-permute-start | bytes 116744 | tf_op jit(solution)/shard_map/ppermute | solution.py:25
  49.8 20.3 %collective-permute-start.10 = (bf16[68,1024]{1,0:T(8,128)(2,1)S(1)}, bf16[68,1024]{1,0:T(8,128)(2,1)S(1)}, u32[]{:S(2)}, u32[]{:S(2)}) collective-permute-start(bf16[68,1024]{1,0:T(8,128)(2,1)S(1)} %get-tuple-element.33.refs_0_.refs_7_), channel_id=1, source_target_pairs={{0,12},{4,0},{8,4},{12,8},{1,13},{5,1},{9,5},{13,9},{2,14},{6,2},{... | collective-permute-start | bytes 417800 | tf_op jit(solution)/shard_map/ppermute | solution.py:25
  50.3 19.8 %collective-permute-start.9 = (bf16[68,1024]{1,0:T(8,128)(2,1)S(1)}, bf16[68,1024]{1,0:T(8,128)(2,1)S(1)}, u32[]{:S(2)}, u32[]{:S(2)}) collective-permute-start(bf16[68,1024]{1,0:T(8,128)(2,1)S(1)} %get-tuple-element.33.refs_0_.refs_7_), channel_id=1, source_target_pairs={{0,8},{4,12},{8,0},{12,4},{1,9},{5,13},{9,1},{13,5},{2,10},{6,14},... | collective-permute-start | bytes 417800 | tf_op jit(solution)/shard_map/ppermute | solution.py:25
  50.9 19.2 %collective-permute-start.8 = (bf16[68,1024]{1,0:T(8,128)(2,1)S(1)}, bf16[68,1024]{1,0:T(8,128)(2,1)S(1)}, u32[]{:S(2)}, u32[]{:S(2)}) collective-permute-start(bf16[68,1024]{1,0:T(8,128)(2,1)S(1)} %get-tuple-element.33.refs_0_.refs_7_), channel_id=1, source_target_pairs={{0,4},{4,8},{8,12},{12,0},{1,5},{5,9},{9,13},{13,1},{2,6},{6,10},{... | collective-permute-start | bytes 417800 | tf_op jit(solution)/shard_map/ppermute | solution.py:25
  52.9 3.8 %collective-permute-start.14 = (bf16[68,128]{1,0:T(8,128)(2,1)S(1)}, bf16[68,128]{1,0:T(8,128)(2,1)S(1)}, u32[]{:S(2)}, u32[]{:S(2)}) collective-permute-start(bf16[68,128]{1,0:T(8,128)(2,1)S(1)} %attend.3.refs_0_), channel_id=1, source_target_pairs={{0,12},{4,0},{8,4},{12,8},{1,13},{5,1},{9,5},{13,9},{2,14},{6,2},{... | collective-permute-start | bytes 52232 | tf_op jit(solution)/shard_map/ppermute | solution.py:25
  56.7 6.5 %collective-permute-start.13 = (bf16[68,128]{1,0:T(8,128)(2,1)S(1)}, bf16[68,128]{1,0:T(8,128)(2,1)S(1)}, u32[]{:S(2)}, u32[]{:S(2)}) collective-permute-start(bf16[68,128]{1,0:T(8,128)(2,1)S(1)} %attend.3.refs_0_), channel_id=1, source_target_pairs={{0,8},{4,12},{8,0},{12,4},{1,9},{5,13},{9,1},{13,5},{2,10},{6,14},... | collective-permute-start | bytes 52232 | tf_op jit(solution)/shard_map/ppermute | solution.py:25
  60.8 5.6 %collective-permute-start.12 = (bf16[68,128]{1,0:T(8,128)(2,1)S(1)}, bf16[68,128]{1,0:T(8,128)(2,1)S(1)}, u32[]{:S(2)}, u32[]{:S(2)}) collective-permute-start(bf16[68,128]{1,0:T(8,128)(2,1)S(1)} %attend.3.refs_0_), channel_id=1, source_target_pairs={{0,4},{4,8},{8,12},{12,0},{1,5},{5,9},{9,13},{13,1},{2,6},{6,10},{... | collective-permute-start | bytes 52232 | tf_op jit(solution)/shard_map/ppermute | solution.py:25
  66.7 10.8 %collective-permute-start.16 = (bf16[68,1024]{1,0:T(8,128)(2,1)S(1)}, bf16[68,1024]{1,0:T(8,128)(2,1)S(1)}, u32[]{:S(2)}, u32[]{:S(2)}) collective-permute-start(bf16[68,1024]{1,0:T(8,128)(2,1)S(1)} %output_first.1.refs_6_), channel_id=1, source_target_pairs={{0,2},{1,3},{4,6},{5,7},{8,10},{9,11},{12,14},{13,15},{16,18},{17,... | collective-permute-start | bytes 417800 | tf_op jit(solution)/shard_map/ppermute | solution.py:20
  71.0 6.5 %collective-permute-start.11 = (bf16[76,256]{1,0:T(8,128)(2,1)S(1)}, bf16[76,256]{1,0:T(8,128)(2,1)S(1)}, u32[]{:S(2)}, u32[]{:S(2)}) collective-permute-start(bf16[76,256]{1,0:T(8,128)(2,1)S(1)} %get-tuple-element.34.refs_1_), channel_id=1, source_target_pairs={{0,4},{4,8},{8,12},{12,0},{1,5},{5,9},{9,13},{13,1},{2,6},{6,10},{... | collective-permute-start | bytes 116744 | tf_op jit(solution)/shard_map/ppermute | solution.py:25
  77.5 7.0 %collective-permute-start.19 = (bf16[68,1024]{1,0:T(8,128)(2,1)S(1)}, bf16[68,1024]{1,0:T(8,128)(2,1)S(1)}, u32[]{:S(2)}, u32[]{:S(2)}) collective-permute-start(bf16[68,1024]{1,0:T(8,128)(2,1)S(1)} %add_convert_fusion.refs_0_.refs_5_), channel_id=1, source_target_pairs={{0,4},{4,8},{8,12},{12,0},{1,5},{5,9},{9,13},{13,1},{2,6},{6,10},{... | collective-permute-start | bytes 417800 | tf_op jit(solution)/shard_map/ppermute | solution.py:25
  77.6 15.5 %collective-permute-start.21 = (bf16[68,1024]{1,0:T(8,128)(2,1)S(1)}, bf16[68,1024]{1,0:T(8,128)(2,1)S(1)}, u32[]{:S(2)}, u32[]{:S(2)}) collective-permute-start(bf16[68,1024]{1,0:T(8,128)(2,1)S(1)} %add_convert_fusion.refs_0_.refs_5_), channel_id=1, source_target_pairs={{0,12},{4,0},{8,4},{12,8},{1,13},{5,1},{9,5},{13,9},{2,14},{6,2},{... | collective-permute-start | bytes 417800 | tf_op jit(solution)/shard_map/ppermute | solution.py:25
  81.4 11.7 %collective-permute-start.20 = (bf16[68,1024]{1,0:T(8,128)(2,1)S(1)}, bf16[68,1024]{1,0:T(8,128)(2,1)S(1)}, u32[]{:S(2)}, u32[]{:S(2)}) collective-permute-start(bf16[68,1024]{1,0:T(8,128)(2,1)S(1)} %add_convert_fusion.refs_0_.refs_5_), channel_id=1, source_target_pairs={{0,8},{4,12},{8,0},{12,4},{1,9},{5,13},{9,1},{13,5},{2,10},{6,14},... | collective-permute-start | bytes 417800 | tf_op jit(solution)/shard_map/ppermute | solution.py:25
  84.5 19.5 %collective-permute-start.26 = (bf16[68,1024]{1,0:T(8,128)(2,1)S(1)}, bf16[68,1024]{1,0:T(8,128)(2,1)S(1)}, u32[]{:S(2)}, u32[]{:S(2)}) collective-permute-start(bf16[68,1024]{1,0:T(8,128)(2,1)S(1)} %output_first.1.refs_6_), channel_id=1, source_target_pairs={{0,1},{1,2},{2,3},{4,5},{5,6},{6,7},{8,9},{9,10},{10,11},{12,13},{... | collective-permute-start | bytes 417800 | tf_op jit(solution)/shard_map/ppermute | solution.py:20
  85.8 5.2 %collective-permute-start.18 = (bf16[76,256]{1,0:T(8,128)(2,1)S(1)}, bf16[76,256]{1,0:T(8,128)(2,1)S(1)}, u32[]{:S(2)}, u32[]{:S(2)}) collective-permute-start(bf16[76,256]{1,0:T(8,128)(2,1)S(1)} %get-tuple-element.34.refs_1_), channel_id=1, source_target_pairs={{0,12},{4,0},{8,4},{12,8},{1,13},{5,1},{9,5},{13,9},{2,14},{6,2},{... | collective-permute-start | bytes 116744 | tf_op jit(solution)/shard_map/ppermute | solution.py:25
  85.9 5.4 %collective-permute-start.17 = (bf16[76,256]{1,0:T(8,128)(2,1)S(1)}, bf16[76,256]{1,0:T(8,128)(2,1)S(1)}, u32[]{:S(2)}, u32[]{:S(2)}) collective-permute-start(bf16[76,256]{1,0:T(8,128)(2,1)S(1)} %get-tuple-element.34.refs_1_), channel_id=1, source_target_pairs={{0,8},{4,12},{8,0},{12,4},{1,9},{5,13},{9,1},{13,5},{2,10},{6,14},... | collective-permute-start | bytes 116744 | tf_op jit(solution)/shard_map/ppermute | solution.py:25
  94.0 7.2 %collective-permute-start.23 = (bf16[76,256]{1,0:T(8,128)(2,1)S(1)}, bf16[76,256]{1,0:T(8,128)(2,1)S(1)}, u32[]{:S(2)}, u32[]{:S(2)}) collective-permute-start(bf16[76,256]{1,0:T(8,128)(2,1)S(1)} %get-tuple-element.42.refs_1_), channel_id=1, source_target_pairs={{0,4},{4,8},{8,12},{12,0},{1,5},{5,9},{9,13},{13,1},{2,6},{6,10},{... | collective-permute-start | bytes 116744 | tf_op jit(solution)/shard_map/ppermute | solution.py:25
  95.5 5.6 %collective-permute-start.22 = (bf16[68,128]{1,0:T(8,128)(2,1)S(1)}, bf16[68,128]{1,0:T(8,128)(2,1)S(1)}, u32[]{:S(2)}, u32[]{:S(2)}) collective-permute-start(bf16[68,128]{1,0:T(8,128)(2,1)S(1)} %attend.4.refs_0_), channel_id=1, source_target_pairs={{0,4},{4,8},{8,12},{12,0},{1,5},{5,9},{9,13},{13,1},{2,6},{6,10},{... | collective-permute-start | bytes 52232 | tf_op jit(solution)/shard_map/ppermute | solution.py:25
  95.6 5.6 %collective-permute-start.25 = (bf16[68,128]{1,0:T(8,128)(2,1)S(1)}, bf16[68,128]{1,0:T(8,128)(2,1)S(1)}, u32[]{:S(2)}, u32[]{:S(2)}) collective-permute-start(bf16[68,128]{1,0:T(8,128)(2,1)S(1)} %attend.4.refs_0_), channel_id=1, source_target_pairs={{0,12},{4,0},{8,4},{12,8},{1,13},{5,1},{9,5},{13,9},{2,14},{6,2},{... | collective-permute-start | bytes 52232 | tf_op jit(solution)/shard_map/ppermute | solution.py:25
  99.4 4.7 %collective-permute-start.24 = (bf16[68,128]{1,0:T(8,128)(2,1)S(1)}, bf16[68,128]{1,0:T(8,128)(2,1)S(1)}, u32[]{:S(2)}, u32[]{:S(2)}) collective-permute-start(bf16[68,128]{1,0:T(8,128)(2,1)S(1)} %attend.4.refs_0_), channel_id=1, source_target_pairs={{0,8},{4,12},{8,0},{12,4},{1,9},{5,13},{9,1},{13,5},{2,10},{6,14},... | collective-permute-start | bytes 52232 | tf_op jit(solution)/shard_map/ppermute | solution.py:25
  105.2 17.2 %collective-permute-start.32 = (bf16[68,1024]{1,0:T(8,128)(2,1)S(1)}, bf16[68,1024]{1,0:T(8,128)(2,1)S(1)}, u32[]{:S(2)}, u32[]{:S(2)}) collective-permute-start(bf16[68,1024]{1,0:T(8,128)(2,1)S(1)} %get-tuple-element.45), channel_id=1, source_target_pairs={{0,1},{1,2},{2,3},{4,5},{5,6},{6,7},{8,9},{9,10},{10,11},{12,13},{... | collective-permute-start | bytes 417800 | tf_op jit(solution)/shard_map/ppermute | solution.py:20
  106.5 4.2 %collective-permute-start.28 = (bf16[76,256]{1,0:T(8,128)(2,1)S(1)}, bf16[76,256]{1,0:T(8,128)(2,1)S(1)}, u32[]{:S(2)}, u32[]{:S(2)}) collective-permute-start(bf16[76,256]{1,0:T(8,128)(2,1)S(1)} %get-tuple-element.42.refs_1_), channel_id=1, source_target_pairs={{0,12},{4,0},{8,4},{12,8},{1,13},{5,1},{9,5},{13,9},{2,14},{6,2},{... | collective-permute-start | bytes 116744 | tf_op jit(solution)/shard_map/ppermute | solution.py:25
  107.5 5.8 %collective-permute-start.27 = (bf16[76,256]{1,0:T(8,128)(2,1)S(1)}, bf16[76,256]{1,0:T(8,128)(2,1)S(1)}, u32[]{:S(2)}, u32[]{:S(2)}) collective-permute-start(bf16[76,256]{1,0:T(8,128)(2,1)S(1)} %get-tuple-element.42.refs_1_), channel_id=1, source_target_pairs={{0,8},{4,12},{8,0},{12,4},{1,9},{5,13},{9,1},{13,5},{2,10},{6,14},... | collective-permute-start | bytes 116744 | tf_op jit(solution)/shard_map/ppermute | solution.py:25
  115.0 3.9 %collective-permute-start.31 = (bf16[68,128]{1,0:T(8,128)(2,1)S(1)}, bf16[68,128]{1,0:T(8,128)(2,1)S(1)}, u32[]{:S(2)}, u32[]{:S(2)}) collective-permute-start(bf16[68,128]{1,0:T(8,128)(2,1)S(1)} %attend.5.refs_0_), channel_id=1, source_target_pairs={{0,12},{4,0},{8,4},{12,8},{1,13},{5,1},{9,5},{13,9},{2,14},{6,2},{... | collective-permute-start | bytes 52232 | tf_op jit(solution)/shard_map/ppermute | solution.py:25
  116.7 4.7 %collective-permute-start.30 = (bf16[68,128]{1,0:T(8,128)(2,1)S(1)}, bf16[68,128]{1,0:T(8,128)(2,1)S(1)}, u32[]{:S(2)}, u32[]{:S(2)}) collective-permute-start(bf16[68,128]{1,0:T(8,128)(2,1)S(1)} %attend.5.refs_0_), channel_id=1, source_target_pairs={{0,8},{4,12},{8,0},{12,4},{1,9},{5,13},{9,1},{13,5},{2,10},{6,14},... | collective-permute-start | bytes 52232 | tf_op jit(solution)/shard_map/ppermute | solution.py:25
  116.8 5.6 %collective-permute-start.29 = (bf16[68,128]{1,0:T(8,128)(2,1)S(1)}, bf16[68,128]{1,0:T(8,128)(2,1)S(1)}, u32[]{:S(2)}, u32[]{:S(2)}) collective-permute-start(bf16[68,128]{1,0:T(8,128)(2,1)S(1)} %attend.5.refs_0_), channel_id=1, source_target_pairs={{0,4},{4,8},{8,12},{12,0},{1,5},{5,9},{9,13},{13,1},{2,6},{6,10},{... | collective-permute-start | bytes 52232 | tf_op jit(solution)/shard_map/ppermute | solution.py:25

commit v3 on v2

--- a/solution.py
+++ b/solution.py
@@ -29,11 +29,8 @@
     return [block] + [turned(block, axis, k) for k in range(1, lax.axis_size(axis))]
 
 
-def added(left, right):
-    return (left.astype(F32) + right.astype(F32)).astype(BF16)
-
-
 VMEM = pl.BlockSpec(memory_space=pltpu.VMEM)
+SMEM = pl.BlockSpec(memory_space=pltpu.SMEM)
 HBM = pl.BlockSpec(memory_space=pltpu.HBM)
 ANY = pl.BlockSpec(memory_space=pl.ANY)
 
@@ -63,20 +60,59 @@
         copy.wait()
 
 
-def place_kernel(count, mine_ref, other_ref, weights, sems):
-    half = mine_ref.shape[1]
-    begin = pl.multiple_of(lax.axis_index("group") * half, half)
-    rest = pl.multiple_of(half - lax.axis_index("group") * half, half)
+def begin_kernel(stream_ref, pend_ref, out_ref):
+    out_ref[...] = (stream_ref[...].astype(F32) + pend_ref[...].astype(F32)).astype(BF16)
+
+
+def choose_kernel(arrived_ref, moved_ref, out_ref):
+    out_ref[...] = jnp.where(
+        lax.axis_index("section") == 0, arrived_ref[...], moved_ref[...]
+    )
+
+
+def cut_kernel(count, wo_ref, *refs):
+    blocks, sems = refs[:-1], refs[-1]
+    half, shard = blocks[0].shape
+    rows = pl.ds(pl.multiple_of(lax.axis_index("group") * half, half), half)
     copies = []
-    for h in range(count):
+    for k in range(1, count):
+        target = lax.rem(lax.axis_index("tensor") + k, count)
+        columns = pl.ds(pl.multiple_of(target * shard, shard), shard)
+        copies.append(
+            pltpu.make_async_copy(wo_ref.at[rows, columns], blocks[k - 1], sems.at[k - 1])
+        )
+    for copy in copies:
+        copy.start()
+    for copy in copies:
+        copy.wait()
+
+
+def stack_kernel(*refs):
+    out_ref = refs[-1]
+    for k, block in enumerate(refs[:-1]):
+        out_ref[k] = block[...]
+
+
+def place_kernel(count, *refs):
+    wo_ref = refs[0]
+    got = refs[1:count]
+    other_ref, weights, sems = refs[count:]
+    me, half_index = lax.axis_index("tensor"), lax.axis_index("group")
+    half, shard = got[0].shape
+    begin = pl.multiple_of(half_index * half, half)
+    rest = pl.multiple_of(half - half_index * half, half)
+    columns = pl.ds(pl.multiple_of(me * shard, shard), shard)
+    copies = [pltpu.make_async_copy(wo_ref.at[:, columns], weights.at[me], sems.at[0, 0])]
+    for k in range(1, count):
+        owner = owner_of(k, count)
         copies.append(
             pltpu.make_async_copy(
-                mine_ref.at[h], weights.at[h, pl.ds(begin, half)], sems.at[0, h]
+                got[k - 1], weights.at[owner, pl.ds(begin, half)], sems.at[0, k]
             )
         )
         copies.append(
             pltpu.make_async_copy(
-                other_ref.at[h], weights.at[h, pl.ds(rest, half)], sems.at[1, h]
+                other_ref.at[k - 1], weights.at[owner, pl.ds(rest, half)], sems.at[1, k]
             )
         )
     for copy in copies:
@@ -85,113 +121,122 @@
         copy.wait()
 
 
-def project_kernel(count, span, *refs):
-    parts = refs[:count]
-    gain_ref, wq_ref, wkv_ref, query_ref, message_ref = refs[count:]
-    shard = parts[0].shape[1]
-    rows = parts[0].shape[0]
-    total = jnp.zeros((rows, 1), F32)
-    for part in parts:
-        values = part[...].astype(F32)
-        total = total + jnp.sum(values * values, axis=-1, keepdims=True)
-    scale = lax.rsqrt(total / (shard * count) + EPS)
-    queries = jnp.zeros((rows, wq_ref.shape[1]), F32)
-    keyval = jnp.zeros((rows, wkv_ref.shape[1]), F32)
-    for k, part in enumerate(parts):
-        here = pl.ds(pl.multiple_of(owner_of(k, count) * shard, shard), shard)
-        normed = (part[...].astype(F32) * scale * gain_ref[:, here]).astype(BF16)
-        queries = queries + jnp.dot(normed, wq_ref[here, :], preferred_element_type=F32)
-        keyval = keyval + jnp.dot(normed, wkv_ref[here, :], preferred_element_type=F32)
-    queries = queries.astype(BF16)
-    query_ref[...] = queries[:span]
-    message_ref[:rows] = keyval.astype(BF16)
-    base = message_ref.shape[0] - (rows - span)
-    message_ref[base:, : queries.shape[1]] = queries[span:]
-
-
-def attend_kernel(count, span, tick, *refs):
+def project_kernel(count, span, batch, *refs):
+    parts = refs[: batch * count]
+    gain_ref, wq_ref, wkv_ref, query_ref, message_ref = refs[batch * count :]
+    rows, shard = parts[0].shape
+    block = message_ref.shape[0] // batch
+    last = block - (rows - span)
+    for b in range(batch):
+        own = parts[b * count : (b + 1) * count]
+        total = jnp.zeros((rows, 1), F32)
+        for part in own:
+            values = part[...].astype(F32)
+            total = total + jnp.sum(values * values, axis=-1, keepdims=True)
+        scale = lax.rsqrt(total / (shard * count) + EPS)
+        queries = jnp.zeros((rows, wq_ref.shape[1]), F32)
+        keyval = jnp.zeros((rows, wkv_ref.shape[1]), F32)
+        for k, part in enumerate(own):
+            here = pl.ds(pl.multiple_of(owner_of(k, count) * shard, shard), shard)
+            normed = (part[...].astype(F32) * scale * gain_ref[:, here]).astype(BF16)
+            queries = queries + jnp.dot(normed, wq_ref[here, :], preferred_element_type=F32)
+            keyval = keyval + jnp.dot(normed, wkv_ref[here, :], preferred_element_type=F32)
+        queries = queries.astype(BF16)
+        query_ref[b] = queries[:span]
+        message_ref[b * block : b * block + rows] = keyval.astype(BF16)
+        message_ref[b * block + last : (b + 1) * block, : queries.shape[1]] = queries[span:]
+
+
+def attend_kernel(count, span, ticks, *refs):
     query_ref = refs[0]
     parts = refs[1 : 1 + count]
-    table_ref, cache_ref, out_ref, blocks, cached, table, small, sem, table_sem = refs[1 + count :]
+    segment_ref, length_ref, cache_ref, out_ref, blocks, cached, small, sems = refs[1 + count :]
     me = lax.axis_index("tensor")
-    micro = tick - lax.axis_index("section") + lax.axis_size("section") - 1
-    table_copy = pltpu.make_async_copy(table_ref.at[pl.ds(micro, 1)], table, table_sem)
-    table_copy.start()
-    copy = pltpu.make_async_copy(cache_ref.at[tick], cached, sem)
-    copy.start()
-    head = query_ref.shape[1]
+    head = query_ref.shape[2]
     factor = 1.0 / math.sqrt(head)
     heads = count
+    block = parts[0].shape[0] // len(ticks)
+    last = block - count
+    copies = []
+    for b, tick in enumerate(ticks):
+        copy = pltpu.make_async_copy(cache_ref.at[tick], cached.at[b], sems.at[b])
+        copy.start()
+        copies.append(copy)
     for k, part in enumerate(parts):
         owner = owner_of(k, count)
         blocks[2 * owner] = part[:, :head]
-        blocks[2 * owner + 1] = part[:, head : 2 * head]
-    keys = blocks[me, :span]
-    values = blocks[heads + me, :span]
-    scores = (
-        lax.dot_general(
-            query_ref[...], keys, (((1,), (1,)), ((), ())), preferred_element_type=F32
-        )
-        * factor
-    )
-    table_copy.wait()
-    across = table[:, :span]
+        blocks[2 * owner + 1] = part[:, head:]
+    small[...] = jnp.zeros_like(small)
     row_ids = lax.broadcasted_iota(jnp.int32, (span, span), 0)
     col_ids = lax.broadcasted_iota(jnp.int32, (span, span), 1)
-    down = jnp.sum(jnp.where(row_ids == col_ids, across, 0), axis=1, keepdims=True)
-    scores = jnp.where((down == across) & (col_ids <= row_ids), scores, NEG)
-    expo = jnp.exp(scores - jnp.max(scores, axis=-1, keepdims=True))
-    weights = (expo / jnp.sum(expo, axis=-1, keepdims=True)).astype(BF16)
-    out_ref[:span] = jnp.dot(weights, values, preferred_element_type=F32).astype(BF16)
-    small[...] = jnp.zeros_like(small)
-    last = parts[0].shape[0] - count
     picked = lax.broadcasted_iota(jnp.int32, (count, head), 0) == me
 
-    def own_row(block):
-        return jnp.sum(jnp.where(picked, block.astype(F32), 0.0), axis=0, keepdims=True)
-
-    for h in range(heads):
-        small[0, h : h + 1, :] = own_row(blocks[2 * h, last:])
-        small[1, h : h + 1, :] = own_row(blocks[h, span : span + count])
-        small[2, h : h + 1, :] = own_row(blocks[heads + h, span : span + count])
-    queries = small[0]
-    line = lax.broadcasted_iota(jnp.int32, queries.shape, 0)
-    spread = jnp.concatenate(
-        [jnp.where(line == h, queries, 0.0) for h in range(heads)], axis=1
-    ).astype(BF16)
-    own = jnp.sum(queries * small[1], axis=-1, keepdims=True) * factor
-    copy.wait()
-    dec_scores = (
-        lax.dot_general(
-            spread,
-            cached[:, : heads * head],
-            (((1,), (1,)), ((), ())),
-            preferred_element_type=F32,
-        )
-        * factor
-    )
-    positions = lax.broadcasted_iota(jnp.int32, dec_scores.shape, 1)
-    dec_scores = jnp.where(positions < table[:, span : span + 1], dec_scores, NEG)
-    top = jnp.maximum(jnp.max(dec_scores, axis=-1, keepdims=True), own)
-    dec_expo = jnp.exp(dec_scores - top)
-    own_expo = jnp.exp(own - top)
-    total = jnp.sum(dec_expo, axis=-1, keepdims=True) + own_expo
-    dec_weights = (dec_expo / total).astype(BF16)
-    own_weight = (own_expo / total).astype(BF16).astype(F32)
-    result = jnp.dot(dec_weights, cached[:, heads * head :], preferred_element_type=F32)
-    extra = own_weight * small[2]
-    for h in range(heads):
-        row = result[h : h + 1, h * head : (h + 1) * head] + extra[h : h + 1]
-        small[3, h : h + 1, :] = row
-    out_ref[span:] = small[3, :heads].astype(BF16)
-
-
-def summed_terms(count, span, parts, weights, scratch):
+    def own_row(rows):
+        return jnp.sum(jnp.where(picked, rows.astype(F32), 0.0), axis=0, keepdims=True)
+
+    for b, tick in enumerate(ticks):
+        micro = tick - lax.axis_index("section") + lax.axis_size("section") - 1
+        first = b * block
+        out = b * (span + count)
+        keys = blocks[me, first : first + span]
+        values = blocks[heads + me, first : first + span]
+        scores = (
+            lax.dot_general(
+                query_ref[b], keys, (((1,), (1,)), ((), ())), preferred_element_type=F32
+            )
+            * factor
+        )
+        across = segment_ref[pl.ds(micro, 1), :]
+        down = jnp.sum(jnp.where(row_ids == col_ids, across, 0), axis=1, keepdims=True)
+        scores = jnp.where((down == across) & (col_ids <= row_ids), scores, NEG)
+        expo = jnp.exp(scores - jnp.max(scores, axis=-1, keepdims=True))
+        weights = (expo / jnp.sum(expo, axis=-1, keepdims=True)).astype(BF16)
+        out_ref[out : out + span] = jnp.dot(
+            weights, values, preferred_element_type=F32
+        ).astype(BF16)
+        new = slice(first + span, first + span + count)
+        for h in range(heads):
+            small[b, 0, h : h + 1, :] = own_row(blocks[2 * h, first + last : first + block])
+            small[b, 1, h : h + 1, :] = own_row(blocks[h, new])
+            small[b, 2, h : h + 1, :] = own_row(blocks[heads + h, new])
+        queries = small[b, 0]
+        line = lax.broadcasted_iota(jnp.int32, queries.shape, 0)
+        spread = jnp.concatenate(
+            [jnp.where(line == h, queries, 0.0) for h in range(heads)], axis=1
+        ).astype(BF16)
+        own = jnp.sum(queries * small[b, 1], axis=-1, keepdims=True) * factor
+        copies[b].wait()
+        dec_scores = (
+            lax.dot_general(
+                spread,
+                cached[b, :, : heads * head],
+                (((1,), (1,)), ((), ())),
+                preferred_element_type=F32,
+            )
+            * factor
+        )
+        positions = lax.broadcasted_iota(jnp.int32, dec_scores.shape, 1)
+        dec_scores = jnp.where(positions < length_ref[0, micro], dec_scores, NEG)
+        top = jnp.maximum(jnp.max(dec_scores, axis=-1, keepdims=True), own)
+        dec_expo = jnp.exp(dec_scores - top)
+        own_expo = jnp.exp(own - top)
+        total = jnp.sum(dec_expo, axis=-1, keepdims=True) + own_expo
+        dec_weights = (dec_expo / total).astype(BF16)
+        own_weight = (own_expo / total).astype(BF16).astype(F32)
+        result = jnp.dot(dec_weights, cached[b, :, heads * head :], preferred_element_type=F32)
+        extra = own_weight * small[b, 2]
+        for h in range(heads):
+            row = result[h : h + 1, h * head : (h + 1) * head] + extra[h : h + 1]
+            small[b, 3, h : h + 1, :] = row
+        out_ref[out + span : out + span + count] = small[b, 3, :heads].astype(BF16)
+
+
+def summed_terms(count, span, first, parts, weights, scratch):
     rows_ref, decode, placed = scratch
     for k, part in enumerate(parts):
         owner = owner_of(k, count)
-        rows_ref[owner, :span] = part[:span]
-        decode[owner, :count] = part[span:].astype(F32)
+        rows_ref[owner, :span] = part[first : first + span]
+        decode[owner, :count] = part[first + span : first + span + count].astype(F32)
     for h in range(count):
         for r in range(count):
             placed[h, r : r + 1, :] = decode[r, h : h + 1, :]
@@ -206,25 +251,32 @@
 
 def first_output_kernel(count, span, *refs):
     parts = refs[:count]
-    weights, out_ref = refs[count : count + 2]
-    out_ref[...] = summed_terms(count, span, parts, weights, refs[count + 2 :])
+    weights, first_new, early, late, out_ref, one_ref, two_ref = refs[count : count + 7]
+    section = lax.axis_index("section")
+    sections = lax.axis_size("section")
+    out_ref[...] = summed_terms(count, span, 0, parts, weights, refs[count + 7 :])
+    fresh = (first_new[...].astype(F32) + out_ref[...].astype(F32)).astype(BF16)
+    is_last = section == sections - 1
+    one_ref[...] = jnp.where(is_last, early[...], fresh)
+    two_ref[...] = jnp.where(
+        section == sections - 2, late[...], jnp.where(is_last, early[...], fresh)
+    )
 
 
 def second_output_kernel(count, span, *refs):
     parts = refs[:count]
-    weights, first_new, pend_first, second, pend_in = refs[count : count + 5]
-    out_ref, hist_stream, hist_pend = refs[count + 5 : count + 8]
-    scratch = refs[count + 8 : -2]
-    fresh, sems = refs[-2:]
-    fresh[...] = (second[...].astype(F32) + pend_in[...].astype(F32)).astype(BF16)
+    weights, first_new, pend_first, second_new = refs[count : count + 4]
+    out_ref, hist_stream, hist_pend = refs[count + 4 : count + 7]
+    scratch = refs[count + 7 : -1]
+    sems = refs[-1]
     copies = [
         pltpu.make_async_copy(first_new, hist_stream.at[0], sems.at[0]),
-        pltpu.make_async_copy(fresh, hist_stream.at[1], sems.at[1]),
+        pltpu.make_async_copy(second_new, hist_stream.at[1], sems.at[1]),
         pltpu.make_async_copy(pend_first, hist_pend.at[0], sems.at[2]),
     ]
     for copy in copies:
         copy.start()
-    out_ref[...] = summed_terms(count, span, parts, weights, scratch)
+    out_ref[...] = summed_terms(count, span, span + count, parts, weights, scratch)
     last = pltpu.make_async_copy(out_ref, hist_pend.at[1], sems.at[3])
     last.start()
     for copy in copies:
@@ -241,7 +293,7 @@
     fresh[...] = (third[...].astype(F32) + pend_in[...].astype(F32)).astype(BF16)
     copy = pltpu.make_async_copy(fresh, hist_stream.at[2], sems.at[0])
     copy.start()
-    result[...] = summed_terms(count, span, parts, weights, scratch)
+    result[...] = summed_terms(count, span, 0, parts, weights, scratch)
     last = pltpu.make_async_copy(result, hist_pend.at[2], sems.at[1])
     last.start()
     copy.wait()
@@ -252,8 +304,6 @@
     stream_in, pend_in, arrivals, norm_gain, wq, wkv, wo, cache, dec_len, span_seg
 ):
     count = lax.axis_size("tensor")
-    section_index = lax.axis_index("section")
-    group_index = lax.axis_index("group")
     rows, shard = stream_in.shape[1:]
     head = wq.shape[2]
     span = span_seg.shape[1]
@@ -261,12 +311,6 @@
     ticks = cache.shape[1]
     half = head // 2
     cached = in_hbm(cache.reshape(ticks, length, cache.shape[4]))
-    table = in_hbm(
-        jnp.pad(
-            jnp.concatenate([span_seg, dec_len], axis=1),
-            ((0, 0), (0, 2 * head - span - 1)),
-        )
-    )
     padded = (rows + 7) // 8 * 8
     message_rows = padded + count
     limit = pltpu.CompilerParams(vmem_limit_bytes=16 * 1024 * 1024)
@@ -275,7 +319,7 @@
 
     def cost(flops, moved_bytes):
         return pl.CostEstimate(
-            flops=int(0 * flops), bytes_accessed=int(0 * moved_bytes), transcendentals=0
+            flops=int(1 * flops), bytes_accessed=int(1 * moved_bytes), transcendentals=0
         )
 
     gain, wq_here, wkv_here = pl.pallas_call(
@@ -295,42 +339,43 @@
     gain, wq_here, wkv_here = in_vmem(gain), in_vmem(wq_here), in_vmem(wkv_here)
 
     def project(parts):
+        batch = len(parts) // count
         return pl.pallas_call(
-            functools.partial(project_kernel, count, span),
+            functools.partial(project_kernel, count, span, batch),
             out_shape=(
-                jax.ShapeDtypeStruct((span, head), BF16),
-                jax.ShapeDtypeStruct((message_rows, 2 * head), BF16),
+                jax.ShapeDtypeStruct((batch, span, head), BF16),
+                jax.ShapeDtypeStruct((batch * message_rows, 2 * head), BF16),
             ),
-            in_specs=[VMEM] * (count + 3),
+            in_specs=[VMEM] * (batch * count + 3),
             out_specs=(VMEM, VMEM),
             compiler_params=limit,
             cost_estimate=cost(
-                2 * rows * shard * count * 3 * head, 2 * shard * count * (3 * head + rows)
+                2 * batch * rows * shard * count * 3 * head,
+                2 * shard * count * (3 * head + rows),
             ),
             name="project",
         )(*[in_vmem(part) for part in parts], gain, wq_here, wkv_here)
 
-    def attend(queries, parts, tick):
+    def attend(queries, parts, which):
+        batch = len(which)
         return pl.pallas_call(
-            functools.partial(attend_kernel, count, span, tick),
-            out_shape=jax.ShapeDtypeStruct((span + count, head), BF16),
-            in_specs=[VMEM] * (count + 1) + [HBM] * 2,
+            functools.partial(attend_kernel, count, span, which),
+            out_shape=jax.ShapeDtypeStruct((batch * (span + count), head), BF16),
+            in_specs=[VMEM] * (count + 2) + [SMEM, HBM],
             out_specs=VMEM,
             scratch_shapes=[
-                pltpu.VMEM((2 * count, message_rows, head), BF16),
-                pltpu.VMEM((length, cache.shape[4]), BF16),
-                pltpu.VMEM((1, 2 * head), jnp.int32),
-                pltpu.VMEM((4, 8, head), F32),
-                pltpu.SemaphoreType.DMA,
-                pltpu.SemaphoreType.DMA,
+                pltpu.VMEM((2 * count, batch * message_rows, head), BF16),
+                pltpu.VMEM((batch, length, cache.shape[4]), BF16),
+                pltpu.VMEM((batch, 4, 8, head), F32),
+                pltpu.SemaphoreType.DMA((batch,)),
             ],
             compiler_params=limit,
             cost_estimate=cost(
-                4 * 8 * length * 4 * head,
-                4 * length * 4 * head + count * message_rows * 4 * head,
+                batch * 4 * 8 * length * 4 * head,
+                batch * (4 * length * 4 * head + count * message_rows * 4 * head),
             ),
             name="attend",
-        )(queries, *[in_vmem(part) for part in parts], table, cached)
+        )(queries, *[in_vmem(part) for part in parts], span_seg, dec_len.T, cached)
 
     output_scratch = [
         pltpu.VMEM((count, padded, head), BF16),
@@ -338,75 +383,94 @@
         pltpu.VMEM((count, 8, head), F32),
     ]
     output_cost = cost(2 * rows * shard * count * head, 2 * shard * (count * head + rows))
-    barrier = lax.optimization_barrier
-
     stream_parts = pieces_of(stream_in[0], "tensor")
-    own_wo = wo[0]
-    own_half = lax.dynamic_slice_in_dim(own_wo, group_index * half, half, 0)
-    own_half = own_half.reshape(half, count, shard).transpose(1, 0, 2)
-    first_new = added(stream_in[0], pend_in[0])
-    one_on = moved(first_new, "section", 1)
-    own_half, stream_parts[1] = barrier((own_half, stream_parts[1]))
-    mine = lax.all_to_all(own_half, "tensor", split_axis=0, concat_axis=0, tiled=True)
-    other = turned(mine, "group", 1)
+    first_new = pl.pallas_call(
+        begin_kernel,
+        out_shape=block,
+        in_specs=[VMEM] * 2,
+        out_specs=VMEM,
+        compiler_params=limit,
+        cost_estimate=cost(0, 6 * rows * shard),
+        name="begin",
+    )(stream_in[0], pend_in[0])
+    early, late = arrivals[0], arrivals[1]
+    second = pl.pallas_call(
+        choose_kernel,
+        out_shape=block,
+        in_specs=[VMEM] * 2,
+        out_specs=VMEM,
+        compiler_params=limit,
+        cost_estimate=cost(0, 6 * rows * shard),
+        name="choose",
+    )(early, moved(first_new, "section", 1))
+    second_parts = pieces_of(second, "tensor")
+    queries, message = project(stream_parts + second_parts)
+    message_parts = pieces_of(message, "tensor")
+    small_block = jax.ShapeDtypeStruct((half, shard), BF16)
+    cut = pl.pallas_call(
+        functools.partial(cut_kernel, count),
+        out_shape=(small_block,) * (count - 1),
+        in_specs=[HBM],
+        out_specs=(VMEM,) * (count - 1),
+        scratch_shapes=[pltpu.SemaphoreType.DMA((count - 1,))],
+        compiler_params=limit,
+        cost_estimate=cost(0, 4 * half * shard * count),
+        name="cut",
+    )(in_hbm(wo[0]))
+    blocks = [
+        turned(cut[0], "tensor", 1),
+        turned(cut[1], "tensor", 2),
+        turned(cut[2], "tensor", 3),
+    ]
+    stacked = pl.pallas_call(
+        stack_kernel,
+        out_shape=jax.ShapeDtypeStruct((count - 1, half, shard), BF16),
+        in_specs=[VMEM] * (count - 1),
+        out_specs=VMEM,
+        compiler_params=limit,
+        cost_estimate=cost(0, 4 * half * shard * count),
+        name="stack",
+    )(*[in_vmem(block_k) for block_k in blocks])
+    given = (in_hbm(wo[0]), *blocks, turned(stacked, "group", 1))
     weights = in_vmem(
         pl.pallas_call(
             functools.partial(place_kernel, count),
             out_shape=jax.ShapeDtypeStruct((count, head, shard), BF16),
-            in_specs=[ANY] * 2,
+            in_specs=[ANY] * len(given),
             out_specs=VMEM,
             scratch_shapes=[pltpu.SemaphoreType.DMA((2, count))],
             compiler_params=limit,
             cost_estimate=cost(0, 4 * count * head * shard),
             name="place",
-        )(mine, other)
-    )
-    early, late = arrivals[0], arrivals[1]
-    second = jnp.where(section_index == 0, early, one_on)
-
-    queries, message = project(stream_parts)
-    message_parts = pieces_of(message, "tensor")
-    attended = attend(queries, message_parts, 0)
+        )(*given)
+    )
+    attended = attend(queries, message_parts, (0, 1))
     attended_parts = pieces_of(attended, "tensor")
-    second, attended = barrier((second, attended))
-    second_parts = pieces_of(second, "tensor")
-    two_on = moved(first_new, "section", 2)
-    base = barrier(
-        jnp.where(section_index == 0, late, jnp.where(section_index == 1, early, two_on))
-    )
-    pend_first = pl.pallas_call(
+    pend_first, one_on, two_on = pl.pallas_call(
         functools.partial(first_output_kernel, count, span),
-        out_shape=block,
-        in_specs=[VMEM] * (count + 1),
-        out_specs=VMEM,
+        out_shape=(block, block, block),
+        in_specs=[VMEM] * (count + 4),
+        out_specs=(VMEM, VMEM, VMEM),
         scratch_shapes=output_scratch,
         compiler_params=limit,
         cost_estimate=output_cost,
         name="output_first",
-    )(*[in_vmem(part) for part in attended_parts], weights)
-    pend_two_on = moved(pend_first, "section", 2)
-
-    queries, message = project(second_parts)
-    message_parts = pieces_of(message, "tensor")
-    base, message_parts[1] = barrier((base, message_parts[1]))
-    third = added(base, pend_two_on)
+    )(
+        *[in_vmem(part) for part in attended_parts],
+        weights,
+        in_vmem(first_new),
+        in_vmem(early),
+        in_vmem(late),
+    )
+    third = turned(two_on, "section", 2)
     third_parts = pieces_of(third, "tensor")
-    pend_late = pend_first
-    pend_late, third_parts[1] = barrier((pend_late, third_parts[1]))
-    pend_one_on = moved(pend_late, "section", 1)
-    attended = attend(queries, message_parts, 1)
-    attended_parts = pieces_of(attended, "tensor")
-    third, attended = barrier((third, attended))
-    third_queries, third_message = project([third] + third_parts[1:])
-    third_message_parts = pieces_of(third_message, "tensor")
-    attended_parts[1], third_message_parts[1] = barrier((attended_parts[1], third_message_parts[1]))
+    second_new = turned(one_on, "section", 1)
     pend_second, hist_stream, hist_pend = pl.pallas_call(
         functools.partial(second_output_kernel, count, span),
         out_shape=(block, history, history),
-        in_specs=[VMEM] * (count + 5),
+        in_specs=[VMEM] * (count + 4),
         out_specs=(VMEM, HBM, HBM),
-        scratch_shapes=output_scratch
-        + [pltpu.VMEM((rows, shard), BF16), pltpu.SemaphoreType.DMA((4,))],
+        scratch_shapes=output_scratch + [pltpu.SemaphoreType.DMA((4,))],
         compiler_params=limit,
         cost_estimate=output_cost,
         name="output_second",
@@ -415,12 +479,12 @@
         weights,
         in_vmem(first_new),
         in_vmem(pend_first),
-        in_vmem(second),
-        in_vmem(pend_one_on),
+        in_vmem(second_new),
     )
     pend_last_in = moved(pend_second, "section", 1)
-    third_queries, pend_second = barrier((third_queries, pend_second))
-    attended = attend(third_queries, third_message_parts, 2)
+    queries, message = project(third_parts)
+    message_parts = pieces_of(message, "tensor")
+    attended = attend(queries, message_parts, (2,))
     attended_parts = pieces_of(attended, "tensor")
     hist_stream, hist_pend = pl.pallas_call(
         functools.partial(third_output_kernel, count, span),

time: 124 us -> 105 us (0.85)
  waiting for transfers between devices: 55 us -> 37.4 us
  starting transfers between devices: 50.9 us -> 47.8 us
  Pallas kernels: 13.9 us -> 16.8 us
    ppermute x28 -> x27, waiting for transfers between devices: 47.6 us -> 37.4 us  [turned(): lax.ppermute(block, axis, [(i, (i + distance) % count) for i in range(cou...]
    ppermute x28 -> x27, starting transfers between devices: 36 us -> 45.2 us  [turned(): lax.ppermute(block, axis, [(i, (i + distance) % count) for i in range(cou...]
    ppermute x5 -> x2, starting transfers between devices: 11.3 us -> 2.59 us  [moved(): return lax.ppermute(block, axis, route)]
    all_to_all x1 -> x0, waiting for transfers between devices: 7.39 us -> none  [fast_body(): lax.all_to_all(own_half, 'tensor', split_axis=0, concat_axis=0, tiled=True)]
    all_to_all x1 -> x0, starting transfers between devices: 3.6 us -> none  [fast_body(): lax.all_to_all(own_half, 'tensor', split_axis=0, concat_axis=0, tiled=True)]
    pallas_call x6 -> x8, Pallas kernels: 7.94 us -> 11.2 us  [the longest x2 5.94 us: attend(): pl.pallas_call(functools.partial(attend_kernel, count, span, which), out_...]
    reshape x2 -> x0, local copies, waits for them, and re-layouts: 1.34 us -> none  [fast_body(): own_half = own_half.reshape(half, count, shard).transpose(1, 0, 2)]
  transfers between devices with their start and end apart: 34 -> 29, of which waited for: 19 -> 16; matrix products, arithmetic and copies ran while one was open for 2% -> 0% of each run, Pallas kernels for 9% -> 14%
where the time goes in v3:
time: 105 us; the launch traced here: 104 us
  starting transfers between devices  47.8 us (46%)
  waiting for transfers between devices  37.4 us (36%)
  Pallas kernels  16.8 us (16%)
  local copies, waits for them, and re-layouts  1.41 us (1%)
    ppermute x27, starting transfers between devices, turned(): lax.ppermute(block, axis, [(i, (i + distance) % count) for i in range(cou...  45.2 us
    ppermute x27, waiting for transfers between devices, turned(): lax.ppermute(block, axis, [(i, (i + distance) % count) for i in range(cou...  37.4 us
    pallas_call x2, Pallas kernels, attend(): pl.pallas_call(functools.partial(attend_kernel, count, span, which), out_...  5.94 us
    pallas_call x2, Pallas kernels, project(): pl.pallas_call(functools.partial(project_kernel, count, span, batch), out...  3.17 us
    ppermute x2, starting transfers between devices, moved(): return lax.ppermute(block, axis, route)  2.59 us
  transfers between devices with their start and end apart: 29, of which 16 were waited for; matrix products, arithmetic and copies ran while one was open for 0% of the time, Pallas kernels for 14%

profile of v3, /device:TPU:0, one launch (start us, length us, event | category | flops | bytes accessed | tf_op | source)
XLA Modules:
  0.0 104.3 jit_solution(205585802588393214)
XLA Ops:
  0.6 1.1 %cut.1 = (bf16[64,1024]{1,0:T(8,128)(2,1)S(1)}, bf16[64,1024]{1,0:T(8,128)(2,1)S(1)}, bf16[64,1024]{1,0:T(8,128)(2,1)S(1)}) custom-call(bf16[128,4096]{1,0:T(8,128)(2,1)} %bitcast.23), custom_call_target="tpu_custom_call" | custom-call | bytes 1048576 | tf_op jit(solution)/shard_map/cut/pallas_call | solution.py:410
  1.8 3.1 %collective-permute-start.13 = (bf16[64,1024]{1,0:T(8,128)(2,1)S(1)}, bf16[64,1024]{1,0:T(8,128)(2,1)S(1)}, u32[]{:S(2)}, u32[]{:S(2)}) collective-permute-start(bf16[64,1024]{1,0:T(8,128)(2,1)S(1)} %get-tuple-element.25), channel_id=1, source_target_pairs={{0,4},{4,8},{8,12},{12,0},{1,5},{5,9},{9,13},{13,1},{2,6},{6,10},{... | collective-permute-start | bytes 393224 | tf_op jit(solution)/shard_map/ppermute | solution.py:25
  4.8 2.6 %collective-permute-start.14 = (bf16[64,1024]{1,0:T(8,128)(2,1)S(1)}, bf16[64,1024]{1,0:T(8,128)(2,1)S(1)}, u32[]{:S(2)}, u32[]{:S(2)}) collective-permute-start(bf16[64,1024]{1,0:T(8,128)(2,1)S(1)} %get-tuple-element.26), channel_id=1, source_target_pairs={{0,8},{4,12},{8,0},{12,4},{1,9},{5,13},{9,1},{13,5},{2,10},{6,14},... | collective-permute-start | bytes 393224 | tf_op jit(solution)/shard_map/ppermute | solution.py:25
  7.4 1.3 %collective-permute-start.15 = (bf16[64,1024]{1,0:T(8,128)(2,1)S(1)}, bf16[64,1024]{1,0:T(8,128)(2,1)S(1)}, u32[]{:S(2)}, u32[]{:S(2)}) collective-permute-start(bf16[64,1024]{1,0:T(8,128)(2,1)S(1)} %get-tuple-element.27), channel_id=1, source_target_pairs={{0,12},{4,0},{8,4},{12,8},{1,13},{5,1},{9,5},{13,9},{2,14},{6,2},{... | collective-permute-start | bytes 393224 | tf_op jit(solution)/shard_map/ppermute | solution.py:25
  8.8 0.7 collective-permute-start
  9.8 0.9 copy-done
  10.7 0.9 begin.1.refs_5_
  11.7 2.9 %collective-permute-start.2 = (bf16[68,1024]{1,0:T(8,128)(2,1)}, bf16[68,1024]{1,0:T(8,128)(2,1)S(1)}, u32[]{:S(2)}, u32[]{:S(2)}) collective-permute-start(bf16[68,1024]{1,0:T(8,128)(2,1)} %bitcast.stream_ref.refs_0_), channel_id=1, source_target_pairs={{0,12},{4,0},{8,4},{12,8},{1,13},{5,1},{9,5},{13,9},{2,14},{6,2},{... | collective-permute-start | bytes 417800 | tf_op jit(solution)/shard_map/ppermute | solution.py:25
  14.5 7.2 %collective-permute-done.14.refs_1_.refs_2_ = bf16[64,1024]{1,0:T(8,128)(2,1)S(1)} collective-permute-done((bf16[64,1024]{1,0:T(8,128)(2,1)S(1)}, bf16[64,1024]{1,0:T(8,128)(2,1)S(1)}, u32[]{:S(2)}, u32[]{:S(2)}) %collective-permute-start.14) | collective-permute-done | bytes 131104 | tf_op jit(solution)/shard_map/ppermute | solution.py:25
  21.7 1.3 %collective-permute-start.3 = (bf16[68,1024]{1,0:T(8,128)(2,1)S(1)}, bf16[68,1024]{1,0:T(8,128)(2,1)S(1)}, u32[]{:S(2)}, u32[]{:S(2)}) collective-permute-start(bf16[68,1024]{1,0:T(8,128)(2,1)S(1)} %begin.1.refs_5_), channel_id=1, source_target_pairs={{0,1},{1,2},{2,3},{4,5},{5,6},{6,7},{8,9},{9,10},{10,11},{12,13},{... | collective-permute-start | bytes 417800 | tf_op jit(solution)/shard_map/ppermute | solution.py:20
  23.0 1.3 %collective-permute-start.16 = (bf16[3,64,1024]{2,1,0:T(8,128)(2,1)S(1)}, bf16[3,64,1024]{2,1,0:T(8,128)(2,1)S(1)}, u32[]{:S(2)}, u32[]{:S(2)}) collective-permute-start(bf16[3,64,1024]{2,1,0:T(8,128)(2,1)S(1)} %stack.1), channel_id=1, source_target_pairs={{0,16},{16,0},{1,17},{17,1},{2,18},{18,2},{3,19},{19,3},{4,20},{20... | collective-permute-start | bytes 1179656 | tf_op jit(solution)/shard_map/ppermute | solution.py:25
  24.9 3.6 %collective-permute-start.4 = (bf16[68,1024]{1,0:T(8,128)(2,1)S(1)}, bf16[68,1024]{1,0:T(8,128)(2,1)S(1)}, u32[]{:S(2)}, u32[]{:S(2)}) collective-permute-start(bf16[68,1024]{1,0:T(8,128)(2,1)S(1)} %choose.1.refs_4_), channel_id=1, source_target_pairs={{0,4},{4,8},{8,12},{12,0},{1,5},{5,9},{9,13},{13,1},{2,6},{6,10},{... | collective-permute-start | bytes 417800 | tf_op jit(solution)/shard_map/ppermute | solution.py:25
  28.4 3.5 %collective-permute-start.5 = (bf16[68,1024]{1,0:T(8,128)(2,1)S(1)}, bf16[68,1024]{1,0:T(8,128)(2,1)S(1)}, u32[]{:S(2)}, u32[]{:S(2)}) collective-permute-start(bf16[68,1024]{1,0:T(8,128)(2,1)S(1)} %choose.1.refs_4_), channel_id=1, source_target_pairs={{0,8},{4,12},{8,0},{12,4},{1,9},{5,13},{9,1},{13,5},{2,10},{6,14},... | collective-permute-start | bytes 417800 | tf_op jit(solution)/shard_map/ppermute | solution.py:25
  32.0 1.1 %collective-permute-start.6 = (bf16[68,1024]{1,0:T(8,128)(2,1)S(1)}, bf16[68,1024]{1,0:T(8,128)(2,1)S(1)}, u32[]{:S(2)}, u32[]{:S(2)}) collective-permute-start(bf16[68,1024]{1,0:T(8,128)(2,1)S(1)} %choose.1.refs_4_), channel_id=1, source_target_pairs={{0,12},{4,0},{8,4},{12,8},{1,13},{5,1},{9,5},{13,9},{2,14},{6,2},{... | collective-permute-start | bytes 417800 | tf_op jit(solution)/shard_map/ppermute | solution.py:25
  33.1 1.9 %load.1 = (f32[1,4096]{1,0:T(1,128)S(1)}, bf16[4096,128]{1,0:T(8,128)(2,1)S(1)}, bf16[4096,256]{1,0:T(8,128)(2,1)S(1)}) custom-call(f32[1,4096]{1,0:T(1,128)} %gain_ref.1, bf16[4096,128]{1,0:T(8,128)(2,1)} %bitcast.26, bf16[4096,256]{1,0:T(8,128)(2,1)} %bitcast.25), custom_call_target="tpu_custom_call" | custom-call | bytes 6291456 | tf_op jit(solution)/shard_map/load/pallas_call | solution.py:325
  35.1 7.3 %collective-permute-done.5.refs_6_ = bf16[68,1024]{1,0:T(8,128)(2,1)S(1)} collective-permute-done((bf16[68,1024]{1,0:T(8,128)(2,1)S(1)}, bf16[68,1024]{1,0:T(8,128)(2,1)S(1)}, u32[]{:S(2)}, u32[]{:S(2)}) %collective-permute-start.5) | collective-permute-done | bytes 139296 | tf_op jit(solution)/shard_map/ppermute | solution.py:25
  42.5 2.3 %project.2 = (bf16[2,64,128]{2,1,0:T(8,128)(2,1)S(1)}, bf16[152,256]{1,0:T(8,128)(2,1)S(1)}) custom-call(bf16[68,1024]{1,0:T(8,128)(2,1)} %bitcast.stream_ref.refs_0_, bf16[68,1024]{1,0:T(8,128)(2,1)S(1)} %collective-permute-done.refs_1_, bf16[68,1024]{1,0:T(8,128)(2,1)S(1)} %collective-permute-done.1.refs_2_, ...), custom_call_target="tpu_custom_call" | custom-call | flops 427819008 | bytes 3702784 | tf_op jit(solution)/shard_map/project/pallas_call | solution.py:343
  44.8 3.6 %collective-permute-start.7 = (bf16[152,256]{1,0:T(8,128)(2,1)S(1)}, bf16[152,256]{1,0:T(8,128)(2,1)S(1)}, u32[]{:S(2)}, u32[]{:S(2)}) collective-permute-start(bf16[152,256]{1,0:T(8,128)(2,1)S(1)} %get-tuple-element.24.refs_1_), channel_id=1, source_target_pairs={{0,4},{4,8},{8,12},{12,0},{1,5},{5,9},{9,13},{13,1},{2,6},{6,10},{... | collective-permute-start | bytes 233480 | tf_op jit(solution)/shard_map/ppermute | solution.py:25
  48.5 2.4 %collective-permute-start.9 = (bf16[152,256]{1,0:T(8,128)(2,1)S(1)}, bf16[152,256]{1,0:T(8,128)(2,1)S(1)}, u32[]{:S(2)}, u32[]{:S(2)}) collective-permute-start(bf16[152,256]{1,0:T(8,128)(2,1)S(1)} %get-tuple-element.24.refs_1_), channel_id=1, source_target_pairs={{0,12},{4,0},{8,4},{12,8},{1,13},{5,1},{9,5},{13,9},{2,14},{6,2},{... | collective-permute-start | bytes 233480 | tf_op jit(solution)/shard_map/ppermute | solution.py:25
  51.2 3.8 %collective-permute-done.8.refs_3_ = bf16[152,256]{1,0:T(8,128)(2,1)S(1)} collective-permute-done((bf16[152,256]{1,0:T(8,128)(2,1)S(1)}, bf16[152,256]{1,0:T(8,128)(2,1)S(1)}, u32[]{:S(2)}, u32[]{:S(2)}) %collective-permute-start.8) | collective-permute-done | bytes 77856 | tf_op jit(solution)/shard_map/ppermute | solution.py:25
  55.0 3.4 %attend.2.refs_0_ = bf16[136,128]{1,0:T(8,128)(2,1)S(1)} custom-call(bf16[2,64,128]{2,1,0:T(8,128)(2,1)S(1)} %get-tuple-element.23.refs_0_, bf16[152,256]{1,0:T(8,128)(2,1)S(1)} %get-tuple-element.24.refs_1_, bf16[152,256]{1,0:T(8,128)(2,1)S(1)} %collective-permute-done.7.refs_2_, bf16[152,256]{1,0:T(8,128)(2,1)S(1)} %collective-permute-done.8.refs_3_, ...), custom_call_target="tpu_custom_call" | custom-call | flops 12582912 | bytes 1884160 | tf_op jit(solution)/shard_map/attend/pallas_call | solution.py:361
  58.4 2.2 %collective-permute-start.10 = (bf16[136,128]{1,0:T(8,128)(2,1)S(1)}, bf16[136,128]{1,0:T(8,128)(2,1)S(1)}, u32[]{:S(2)}, u32[]{:S(2)}) collective-permute-start(bf16[136,128]{1,0:T(8,128)(2,1)S(1)} %attend.2.refs_0_), channel_id=1, source_target_pairs={{0,4},{4,8},{8,12},{12,0},{1,5},{5,9},{9,13},{13,1},{2,6},{6,10},{... | collective-permute-start | bytes 104456 | tf_op jit(solution)/shard_map/ppermute | solution.py:25
  60.6 1.9 %collective-permute-start.11 = (bf16[136,128]{1,0:T(8,128)(2,1)S(1)}, bf16[136,128]{1,0:T(8,128)(2,1)S(1)}, u32[]{:S(2)}, u32[]{:S(2)}) collective-permute-start(bf16[136,128]{1,0:T(8,128)(2,1)S(1)} %attend.2.refs_0_), channel_id=1, source_target_pairs={{0,8},{4,12},{8,0},{12,4},{1,9},{5,13},{9,1},{13,5},{2,10},{6,14},... | collective-permute-start | bytes 104456 | tf_op jit(solution)/shard_map/ppermute | solution.py:25
  62.5 0.6 collective-permute-start.12
  63.1 1.1 %place.1.refs_4_ = bf16[4,128,1024]{2,1,0:T(8,128)(2,1)S(1)} custom-call(bf16[128,4096]{1,0:T(8,128)(2,1)} %bitcast.24, bf16[64,1024]{1,0:T(8,128)(2,1)S(1)} %collective-permute-done.13.refs_0_.refs_1_, bf16[64,1024]{1,0:T(8,128)(2,1)S(1)} %collective-permute-done.14.refs_1_.refs_2_, bf16[64,1024]{1,0:T(8,128)(2,1)S(1)} %collective-permute-done.15.refs_2_.refs_3_, ...), custom_call_target="tpu_custom_call" | custom-call | bytes 2097152 | tf_op jit(solution)/shard_map/place/pallas_call | solution.py:436
  64.4 1.4 %collective-permute-done.11.refs_2_ = bf16[136,128]{1,0:T(8,128)(2,1)S(1)} collective-permute-done((bf16[136,128]{1,0:T(8,128)(2,1)S(1)}, bf16[136,128]{1,0:T(8,128)(2,1)S(1)}, u32[]{:S(2)}, u32[]{:S(2)}) %collective-permute-start.11) | collective-permute-done | bytes 34848 | tf_op jit(solution)/shard_map/ppermute | solution.py:25
  65.8 0.6 collective-permute-done.12.refs_3_
  67.0 6.1 %collective-permute-done.17.refs_0_.refs_5_ = bf16[68,1024]{1,0:T(8,128)(2,1)S(1)} collective-permute-done((bf16[68,1024]{1,0:T(8,128)(2,1)S(1)}, bf16[68,1024]{1,0:T(8,128)(2,1)S(1)}, u32[]{:S(2)}, u32[]{:S(2)}) %collective-permute-start.17) | collective-permute-done | bytes 139296 | tf_op jit(solution)/shard_map/ppermute | solution.py:25
  73.1 0.7 collective-permute-start.18
  73.8 2.7 %collective-permute-start.19 = (bf16[68,1024]{1,0:T(8,128)(2,1)S(1)}, bf16[68,1024]{1,0:T(8,128)(2,1)S(1)}, u32[]{:S(2)}, u32[]{:S(2)}) collective-permute-start(bf16[68,1024]{1,0:T(8,128)(2,1)S(1)} %collective-permute-done.17.refs_0_.refs_5_), channel_id=1, source_target_pairs={{0,8},{4,12},{8,0},{12,4},{1,9},{5,13},{9,1},{13,5},{2,10},{6,14},... | collective-permute-start | bytes 417800 | tf_op jit(solution)/shard_map/ppermute | solution.py:25
  76.5 1.1 %collective-permute-start.20 = (bf16[68,1024]{1,0:T(8,128)(2,1)S(1)}, bf16[68,1024]{1,0:T(8,128)(2,1)S(1)}, u32[]{:S(2)}, u32[]{:S(2)}) collective-permute-start(bf16[68,1024]{1,0:T(8,128)(2,1)S(1)} %collective-permute-done.17.refs_0_.refs_5_), channel_id=1, source_target_pairs={{0,12},{4,0},{8,4},{12,8},{1,13},{5,1},{9,5},{13,9},{2,14},{6,2},{... | collective-permute-start | bytes 417800 | tf_op jit(solution)/shard_map/ppermute | solution.py:25
  77.5 1.0 %output_second.1 = (bf16[68,1024]{1,0:T(8,128)(2,1)S(1)}, bf16[3,68,1024]{2,1,0:T(8,128)(2,1)}, bf16[3,68,1024]{2,1,0:T(8,128)(2,1)}) custom-call(bf16[136,128]{1,0:T(8,128)(2,1)S(1)} %attend.2.refs_0_, bf16[136,128]{1,0:T(8,128)(2,1)S(1)} %collective-permute-done.10.refs_1_, bf16[136,128]{1,0:T(8,128)(2,1)S(1)} %collective-permute-done.11.refs_2_, ...), custom_call_target="tpu_custom_call" | custom-call | flops 71303168 | bytes 1187840 | tf_op jit(solution)/shard_map/output_second/pallas_call | solution.py:468
  78.6 1.3 %collective-permute-start.28 = (bf16[68,1024]{1,0:T(8,128)(2,1)S(1)}, bf16[68,1024]{1,0:T(8,128)(2,1)S(1)}, u32[]{:S(2)}, u32[]{:S(2)}) collective-permute-start(bf16[68,1024]{1,0:T(8,128)(2,1)S(1)} %get-tuple-element.33), channel_id=1, source_target_pairs={{0,1},{1,2},{2,3},{4,5},{5,6},{6,7},{8,9},{9,10},{10,11},{12,13},{... | collective-permute-start | bytes 417800 | tf_op jit(solution)/shard_map/ppermute | solution.py:20
  79.9 0.8 collective-permute-done.18.refs_1_
  80.7 3.9 %collective-permute-done.19.refs_2_ = bf16[68,1024]{1,0:T(8,128)(2,1)S(1)} collective-permute-done((bf16[68,1024]{1,0:T(8,128)(2,1)S(1)}, bf16[68,1024]{1,0:T(8,128)(2,1)S(1)}, u32[]{:S(2)}, u32[]{:S(2)}) %collective-permute-start.19) | collective-permute-done | bytes 139296 | tf_op jit(solution)/shard_map/ppermute | solution.py:25
  84.6 0.9 project.3
  85.5 2.6 %collective-permute-start.21 = (bf16[76,256]{1,0:T(8,128)(2,1)S(1)}, bf16[76,256]{1,0:T(8,128)(2,1)S(1)}, u32[]{:S(2)}, u32[]{:S(2)}) collective-permute-start(bf16[76,256]{1,0:T(8,128)(2,1)S(1)} %get-tuple-element.30.refs_1_), channel_id=1, source_target_pairs={{0,4},{4,8},{8,12},{12,0},{1,5},{5,9},{9,13},{13,1},{2,6},{6,10},{... | collective-permute-start | bytes 116744 | tf_op jit(solution)/shard_map/ppermute | solution.py:25
  88.1 1.2 %collective-permute-start.22 = (bf16[76,256]{1,0:T(8,128)(2,1)S(1)}, bf16[76,256]{1,0:T(8,128)(2,1)S(1)}, u32[]{:S(2)}, u32[]{:S(2)}) collective-permute-start(bf16[76,256]{1,0:T(8,128)(2,1)S(1)} %get-tuple-element.30.refs_1_), channel_id=1, source_target_pairs={{0,8},{4,12},{8,0},{12,4},{1,9},{5,13},{9,1},{13,5},{2,10},{6,14},... | collective-permute-start | bytes 116744 | tf_op jit(solution)/shard_map/ppermute | solution.py:25
  89.2 1.3 %collective-permute-start.23 = (bf16[76,256]{1,0:T(8,128)(2,1)S(1)}, bf16[76,256]{1,0:T(8,128)(2,1)S(1)}, u32[]{:S(2)}, u32[]{:S(2)}) collective-permute-start(bf16[76,256]{1,0:T(8,128)(2,1)S(1)} %get-tuple-element.30.refs_1_), channel_id=1, source_target_pairs={{0,12},{4,0},{8,4},{12,8},{1,13},{5,1},{9,5},{13,9},{2,14},{6,2},{... | collective-permute-start | bytes 116744 | tf_op jit(solution)/shard_map/ppermute | solution.py:25
  90.5 1.0 collective-permute-done.21.refs_2_
  91.5 1.5 %collective-permute-done.22.refs_3_ = bf16[76,256]{1,0:T(8,128)(2,1)S(1)} collective-permute-done((bf16[76,256]{1,0:T(8,128)(2,1)S(1)}, bf16[76,256]{1,0:T(8,128)(2,1)S(1)}, u32[]{:S(2)}, u32[]{:S(2)}) %collective-permute-start.22) | collective-permute-done | bytes 38944 | tf_op jit(solution)/shard_map/ppermute | solution.py:25
  93.4 2.5 %attend.3.refs_0_ = bf16[68,128]{1,0:T(8,128)(2,1)S(1)} custom-call(bf16[1,64,128]{2,1,0:T(8,128)(2,1)S(1)} %get-tuple-element.29.refs_0_, bf16[76,256]{1,0:T(8,128)(2,1)S(1)} %get-tuple-element.30.refs_1_, bf16[76,256]{1,0:T(8,128)(2,1)S(1)} %collective-permute-done.21.refs_2_, bf16[76,256]{1,0:T(8,128)(2,1)S(1)} %collective-permute-done.22.refs_3_, ...), custom_call_target="tpu_custom_call" | custom-call | flops 6291456 | bytes 942080 | tf_op jit(solution)/shard_map/attend/pallas_call | solution.py:361
  95.9 0.6 collective-permute-start.24
  96.6 2.9 %collective-permute-start.25 = (bf16[68,128]{1,0:T(8,128)(2,1)S(1)}, bf16[68,128]{1,0:T(8,128)(2,1)S(1)}, u32[]{:S(2)}, u32[]{:S(2)}) collective-permute-start(bf16[68,128]{1,0:T(8,128)(2,1)S(1)} %attend.3.refs_0_), channel_id=1, source_target_pairs={{0,8},{4,12},{8,0},{12,4},{1,9},{5,13},{9,1},{13,5},{2,10},{6,14},... | collective-permute-start | bytes 52232 | tf_op jit(solution)/shard_map/ppermute | solution.py:25
  99.5 1.0 %collective-permute-start.26 = (bf16[68,128]{1,0:T(8,128)(2,1)S(1)}, bf16[68,128]{1,0:T(8,128)(2,1)S(1)}, u32[]{:S(2)}, u32[]{:S(2)}) collective-permute-start(bf16[68,128]{1,0:T(8,128)(2,1)S(1)} %attend.3.refs_0_), channel_id=1, source_target_pairs={{0,12},{4,0},{8,4},{12,8},{1,13},{5,1},{9,5},{13,9},{2,14},{6,2},{... | collective-permute-start | bytes 52232 | tf_op jit(solution)/shard_map/ppermute | solution.py:25
  100.5 1.0 collective-permute-done.24.refs_1_
  101.5 1.7 %collective-permute-done.26.refs_3_ = bf16[68,128]{1,0:T(8,128)(2,1)S(1)} collective-permute-done((bf16[68,128]{1,0:T(8,128)(2,1)S(1)}, bf16[68,128]{1,0:T(8,128)(2,1)S(1)}, u32[]{:S(2)}, u32[]{:S(2)}) %collective-permute-start.26) | collective-permute-done | bytes 17440 | tf_op jit(solution)/shard_map/ppermute | solution.py:25
  103.2 1.1 %output_third.1 = (bf16[3,68,1024]{2,1,0:T(8,128)(2,1)}, bf16[3,68,1024]{2,1,0:T(8,128)(2,1)}) custom-call(bf16[68,128]{1,0:T(8,128)(2,1)S(1)} %attend.3.refs_0_, bf16[68,128]{1,0:T(8,128)(2,1)S(1)} %collective-permute-done.24.refs_1_, bf16[68,128]{1,0:T(8,128)(2,1)S(1)} %collective-permute-done.25.refs_2_, ...), custom_call_target="tpu_custom_call", output_to_operand_aliasing={{0}: (7, {}), {1}: (8, {})} | custom-call | flops 71303168 | bytes 1187840 | tf_op jit(solution)/shard_map/output_third/pallas_call | solution.py:489
  (34 shorter events, 2.4 us)
Async XLA Ops:
  0.6 23.7 %copy-start.3 = (bf16[2,68,1024]{2,0,1:T(2,128)(2,1)S(1)}, bf16[2,68,1024]{2,0,1:T(2,128)(2,1)}, u32[]{:S(2)}) copy-start(bf16[2,68,1024]{2,0,1:T(2,128)(2,1)} %param.12) | copy-start | bytes 835588
  1.8 9.9 %collective-permute-start.13 = (bf16[64,1024]{1,0:T(8,128)(2,1)S(1)}, bf16[64,1024]{1,0:T(8,128)(2,1)S(1)}, u32[]{:S(2)}, u32[]{:S(2)}) collective-permute-start(bf16[64,1024]{1,0:T(8,128)(2,1)S(1)} %get-tuple-element.25), channel_id=1, source_target_pairs={{0,4},{4,8},{8,12},{12,0},{1,5},{5,9},{9,13},{13,1},{2,6},{6,10},{... | collective-permute-start | bytes 393224 | tf_op jit(solution)/shard_map/ppermute | solution.py:25
  4.8 16.9 %collective-permute-start.14 = (bf16[64,1024]{1,0:T(8,128)(2,1)S(1)}, bf16[64,1024]{1,0:T(8,128)(2,1)S(1)}, u32[]{:S(2)}, u32[]{:S(2)}) collective-permute-start(bf16[64,1024]{1,0:T(8,128)(2,1)S(1)} %get-tuple-element.26), channel_id=1, source_target_pairs={{0,8},{4,12},{8,0},{12,4},{1,9},{5,13},{9,1},{13,5},{2,10},{6,14},... | collective-permute-start | bytes 393224 | tf_op jit(solution)/shard_map/ppermute | solution.py:25
  7.4 15.6 %collective-permute-start.15 = (bf16[64,1024]{1,0:T(8,128)(2,1)S(1)}, bf16[64,1024]{1,0:T(8,128)(2,1)S(1)}, u32[]{:S(2)}, u32[]{:S(2)}) collective-permute-start(bf16[64,1024]{1,0:T(8,128)(2,1)S(1)} %get-tuple-element.27), channel_id=1, source_target_pairs={{0,12},{4,0},{8,4},{12,8},{1,13},{5,1},{9,5},{13,9},{2,14},{6,2},{... | collective-permute-start | bytes 393224 | tf_op jit(solution)/shard_map/ppermute | solution.py:25
  8.8 19.6 %collective-permute-start = (bf16[68,1024]{1,0:T(8,128)(2,1)}, bf16[68,1024]{1,0:T(8,128)(2,1)S(1)}, u32[]{:S(2)}, u32[]{:S(2)}) collective-permute-start(bf16[68,1024]{1,0:T(8,128)(2,1)} %bitcast.stream_ref.refs_0_), channel_id=1, source_target_pairs={{0,4},{4,8},{8,12},{12,0},{1,5},{5,9},{9,13},{13,1},{2,6},{6,10},{... | collective-permute-start | bytes 417800 | tf_op jit(solution)/shard_map/ppermute | solution.py:25
  9.5 22.5 %collective-permute-start.1 = (bf16[68,1024]{1,0:T(8,128)(2,1)}, bf16[68,1024]{1,0:T(8,128)(2,1)S(1)}, u32[]{:S(2)}, u32[]{:S(2)}) collective-permute-start(bf16[68,1024]{1,0:T(8,128)(2,1)} %bitcast.stream_ref.refs_0_), channel_id=1, source_target_pairs={{0,8},{4,12},{8,0},{12,4},{1,9},{5,13},{9,1},{13,5},{2,10},{6,14},... | collective-permute-start | bytes 417800 | tf_op jit(solution)/shard_map/ppermute | solution.py:25
  9.8 0.9 copy-start
  11.7 23.4 %collective-permute-start.2 = (bf16[68,1024]{1,0:T(8,128)(2,1)}, bf16[68,1024]{1,0:T(8,128)(2,1)S(1)}, u32[]{:S(2)}, u32[]{:S(2)}) collective-permute-start(bf16[68,1024]{1,0:T(8,128)(2,1)} %bitcast.stream_ref.refs_0_), channel_id=1, source_target_pairs={{0,12},{4,0},{8,4},{12,8},{1,13},{5,1},{9,5},{13,9},{2,14},{6,2},{... | collective-permute-start | bytes 417800 | tf_op jit(solution)/shard_map/ppermute | solution.py:25
  21.7 3.1 %collective-permute-start.3 = (bf16[68,1024]{1,0:T(8,128)(2,1)S(1)}, bf16[68,1024]{1,0:T(8,128)(2,1)S(1)}, u32[]{:S(2)}, u32[]{:S(2)}) collective-permute-start(bf16[68,1024]{1,0:T(8,128)(2,1)S(1)} %begin.1.refs_5_), channel_id=1, source_target_pairs={{0,1},{1,2},{2,3},{4,5},{5,6},{6,7},{8,9},{9,10},{10,11},{12,13},{... | collective-permute-start | bytes 417800 | tf_op jit(solution)/shard_map/ppermute | solution.py:20
  23.0 40.1 %collective-permute-start.16 = (bf16[3,64,1024]{2,1,0:T(8,128)(2,1)S(1)}, bf16[3,64,1024]{2,1,0:T(8,128)(2,1)S(1)}, u32[]{:S(2)}, u32[]{:S(2)}) collective-permute-start(bf16[3,64,1024]{2,1,0:T(8,128)(2,1)S(1)} %stack.1), channel_id=1, source_target_pairs={{0,16},{16,0},{1,17},{17,1},{2,18},{18,2},{3,19},{19,3},{4,20},{20... | collective-permute-start | bytes 1179656 | tf_op jit(solution)/shard_map/ppermute | solution.py:25
  24.9 10.2 %collective-permute-start.4 = (bf16[68,1024]{1,0:T(8,128)(2,1)S(1)}, bf16[68,1024]{1,0:T(8,128)(2,1)S(1)}, u32[]{:S(2)}, u32[]{:S(2)}) collective-permute-start(bf16[68,1024]{1,0:T(8,128)(2,1)S(1)} %choose.1.refs_4_), channel_id=1, source_target_pairs={{0,4},{4,8},{8,12},{12,0},{1,5},{5,9},{9,13},{13,1},{2,6},{6,10},{... | collective-permute-start | bytes 417800 | tf_op jit(solution)/shard_map/ppermute | solution.py:25
  28.4 14.0 %collective-permute-start.5 = (bf16[68,1024]{1,0:T(8,128)(2,1)S(1)}, bf16[68,1024]{1,0:T(8,128)(2,1)S(1)}, u32[]{:S(2)}, u32[]{:S(2)}) collective-permute-start(bf16[68,1024]{1,0:T(8,128)(2,1)S(1)} %choose.1.refs_4_), channel_id=1, source_target_pairs={{0,8},{4,12},{8,0},{12,4},{1,9},{5,13},{9,1},{13,5},{2,10},{6,14},... | collective-permute-start | bytes 417800 | tf_op jit(solution)/shard_map/ppermute | solution.py:25
  32.0 10.5 %collective-permute-start.6 = (bf16[68,1024]{1,0:T(8,128)(2,1)S(1)}, bf16[68,1024]{1,0:T(8,128)(2,1)S(1)}, u32[]{:S(2)}, u32[]{:S(2)}) collective-permute-start(bf16[68,1024]{1,0:T(8,128)(2,1)S(1)} %choose.1.refs_4_), channel_id=1, source_target_pairs={{0,12},{4,0},{8,4},{12,8},{1,13},{5,1},{9,5},{13,9},{2,14},{6,2},{... | collective-permute-start | bytes 417800 | tf_op jit(solution)/shard_map/ppermute | solution.py:25
  42.5 12.5 %copy-start.1 = (s32[6,64]{1,0:T(8,128)S(1)}, s32[6,64]{1,0:T(8,128)}, u32[]{:S(2)}) copy-start(s32[6,64]{1,0:T(8,128)} %refs_5_.3) | copy-start | bytes 4612
  42.5 12.5 %copy-start.2 = (s32[6,1]{0,1:T(1,128)S(1)}, s32[6,1]{0,1:T(1,128)}, u32[]{:S(2)}) copy-start(s32[6,1]{0,1:T(1,128)} %param.18) | copy-start | bytes 76
  44.8 6.4 %collective-permute-start.7 = (bf16[152,256]{1,0:T(8,128)(2,1)S(1)}, bf16[152,256]{1,0:T(8,128)(2,1)S(1)}, u32[]{:S(2)}, u32[]{:S(2)}) collective-permute-start(bf16[152,256]{1,0:T(8,128)(2,1)S(1)} %get-tuple-element.24.refs_1_), channel_id=1, source_target_pairs={{0,4},{4,8},{8,12},{12,0},{1,5},{5,9},{9,13},{13,1},{2,6},{6,10},{... | collective-permute-start | bytes 233480 | tf_op jit(solution)/shard_map/ppermute | solution.py:25
  48.4 6.6 %collective-permute-start.8 = (bf16[152,256]{1,0:T(8,128)(2,1)S(1)}, bf16[152,256]{1,0:T(8,128)(2,1)S(1)}, u32[]{:S(2)}, u32[]{:S(2)}) collective-permute-start(bf16[152,256]{1,0:T(8,128)(2,1)S(1)} %get-tuple-element.24.refs_1_), channel_id=1, source_target_pairs={{0,8},{4,12},{8,0},{12,4},{1,9},{5,13},{9,1},{13,5},{2,10},{6,14},... | collective-permute-start | bytes 233480 | tf_op jit(solution)/shard_map/ppermute | solution.py:25
  48.5 6.6 %collective-permute-start.9 = (bf16[152,256]{1,0:T(8,128)(2,1)S(1)}, bf16[152,256]{1,0:T(8,128)(2,1)S(1)}, u32[]{:S(2)}, u32[]{:S(2)}) collective-permute-start(bf16[152,256]{1,0:T(8,128)(2,1)S(1)} %get-tuple-element.24.refs_1_), channel_id=1, source_target_pairs={{0,12},{4,0},{8,4},{12,8},{1,13},{5,1},{9,5},{13,9},{2,14},{6,2},{... | collective-permute-start | bytes 233480 | tf_op jit(solution)/shard_map/ppermute | solution.py:25
  58.4 6.0 %collective-permute-start.10 = (bf16[136,128]{1,0:T(8,128)(2,1)S(1)}, bf16[136,128]{1,0:T(8,128)(2,1)S(1)}, u32[]{:S(2)}, u32[]{:S(2)}) collective-permute-start(bf16[136,128]{1,0:T(8,128)(2,1)S(1)} %attend.2.refs_0_), channel_id=1, source_target_pairs={{0,4},{4,8},{8,12},{12,0},{1,5},{5,9},{9,13},{13,1},{2,6},{6,10},{... | collective-permute-start | bytes 104456 | tf_op jit(solution)/shard_map/ppermute | solution.py:25
  60.6 5.2 %collective-permute-start.11 = (bf16[136,128]{1,0:T(8,128)(2,1)S(1)}, bf16[136,128]{1,0:T(8,128)(2,1)S(1)}, u32[]{:S(2)}, u32[]{:S(2)}) collective-permute-start(bf16[136,128]{1,0:T(8,128)(2,1)S(1)} %attend.2.refs_0_), channel_id=1, source_target_pairs={{0,8},{4,12},{8,0},{12,4},{1,9},{5,13},{9,1},{13,5},{2,10},{6,14},... | collective-permute-start | bytes 104456 | tf_op jit(solution)/shard_map/ppermute | solution.py:25
  62.5 3.9 %collective-permute-start.12 = (bf16[136,128]{1,0:T(8,128)(2,1)S(1)}, bf16[136,128]{1,0:T(8,128)(2,1)S(1)}, u32[]{:S(2)}, u32[]{:S(2)}) collective-permute-start(bf16[136,128]{1,0:T(8,128)(2,1)S(1)} %attend.2.refs_0_), channel_id=1, source_target_pairs={{0,12},{4,0},{8,4},{12,8},{1,13},{5,1},{9,5},{13,9},{2,14},{6,2},{... | collective-permute-start | bytes 104456 | tf_op jit(solution)/shard_map/ppermute | solution.py:25
  66.8 6.3 %collective-permute-start.17 = (bf16[68,1024]{1,0:T(8,128)(2,1)S(1)}, bf16[68,1024]{1,0:T(8,128)(2,1)S(1)}, u32[]{:S(2)}, u32[]{:S(2)}) collective-permute-start(bf16[68,1024]{1,0:T(8,128)(2,1)S(1)} %get-tuple-element.28), channel_id=1, source_target_pairs={{0,2},{1,3},{2,0},{3,1},{4,6},{5,7},{6,4},{7,5},{8,10},{9,11},{10,... | collective-permute-start | bytes 417800 | tf_op jit(solution)/shard_map/ppermute | solution.py:25
  66.9 10.6 %collective-permute-start.27 = (bf16[68,1024]{1,0:T(8,128)(2,1)S(1)}, bf16[68,1024]{1,0:T(8,128)(2,1)S(1)}, u32[]{:S(2)}, u32[]{:S(2)}) collective-permute-start(bf16[68,1024]{1,0:T(8,128)(2,1)S(1)} %get-tuple-element.32), channel_id=1, source_target_pairs={{0,1},{1,2},{2,3},{3,0},{4,5},{5,6},{6,7},{7,4},{8,9},{9,10},{10,1... | collective-permute-start | bytes 417800 | tf_op jit(solution)/shard_map/ppermute | solution.py:25
  73.1 7.6 %collective-permute-start.18 = (bf16[68,1024]{1,0:T(8,128)(2,1)S(1)}, bf16[68,1024]{1,0:T(8,128)(2,1)S(1)}, u32[]{:S(2)}, u32[]{:S(2)}) collective-permute-start(bf16[68,1024]{1,0:T(8,128)(2,1)S(1)} %collective-permute-done.17.refs_0_.refs_5_), channel_id=1, source_target_pairs={{0,4},{4,8},{8,12},{12,0},{1,5},{5,9},{9,13},{13,1},{2,6},{6,10},{... | collective-permute-start | bytes 417800 | tf_op jit(solution)/shard_map/ppermute | solution.py:25
  73.8 10.8 %collective-permute-start.19 = (bf16[68,1024]{1,0:T(8,128)(2,1)S(1)}, bf16[68,1024]{1,0:T(8,128)(2,1)S(1)}, u32[]{:S(2)}, u32[]{:S(2)}) collective-permute-start(bf16[68,1024]{1,0:T(8,128)(2,1)S(1)} %collective-permute-done.17.refs_0_.refs_5_), channel_id=1, source_target_pairs={{0,8},{4,12},{8,0},{12,4},{1,9},{5,13},{9,1},{13,5},{2,10},{6,14},... | collective-permute-start | bytes 417800 | tf_op jit(solution)/shard_map/ppermute | solution.py:25
  76.5 8.2 %collective-permute-start.20 = (bf16[68,1024]{1,0:T(8,128)(2,1)S(1)}, bf16[68,1024]{1,0:T(8,128)(2,1)S(1)}, u32[]{:S(2)}, u32[]{:S(2)}) collective-permute-start(bf16[68,1024]{1,0:T(8,128)(2,1)S(1)} %collective-permute-done.17.refs_0_.refs_5_), channel_id=1, source_target_pairs={{0,12},{4,0},{8,4},{12,8},{1,13},{5,1},{9,5},{13,9},{2,14},{6,2},{... | collective-permute-start | bytes 417800 | tf_op jit(solution)/shard_map/ppermute | solution.py:25
  78.6 21.9 %collective-permute-start.28 = (bf16[68,1024]{1,0:T(8,128)(2,1)S(1)}, bf16[68,1024]{1,0:T(8,128)(2,1)S(1)}, u32[]{:S(2)}, u32[]{:S(2)}) collective-permute-start(bf16[68,1024]{1,0:T(8,128)(2,1)S(1)} %get-tuple-element.33), channel_id=1, source_target_pairs={{0,1},{1,2},{2,3},{4,5},{5,6},{6,7},{8,9},{9,10},{10,11},{12,13},{... | collective-permute-start | bytes 417800 | tf_op jit(solution)/shard_map/ppermute | solution.py:20
  85.5 6.0 %collective-permute-start.21 = (bf16[76,256]{1,0:T(8,128)(2,1)S(1)}, bf16[76,256]{1,0:T(8,128)(2,1)S(1)}, u32[]{:S(2)}, u32[]{:S(2)}) collective-permute-start(bf16[76,256]{1,0:T(8,128)(2,1)S(1)} %get-tuple-element.30.refs_1_), channel_id=1, source_target_pairs={{0,4},{4,8},{8,12},{12,0},{1,5},{5,9},{9,13},{13,1},{2,6},{6,10},{... | collective-permute-start | bytes 116744 | tf_op jit(solution)/shard_map/ppermute | solution.py:25
  88.1 4.9 %collective-permute-start.22 = (bf16[76,256]{1,0:T(8,128)(2,1)S(1)}, bf16[76,256]{1,0:T(8,128)(2,1)S(1)}, u32[]{:S(2)}, u32[]{:S(2)}) collective-permute-start(bf16[76,256]{1,0:T(8,128)(2,1)S(1)} %get-tuple-element.30.refs_1_), channel_id=1, source_target_pairs={{0,8},{4,12},{8,0},{12,4},{1,9},{5,13},{9,1},{13,5},{2,10},{6,14},... | collective-permute-start | bytes 116744 | tf_op jit(solution)/shard_map/ppermute | solution.py:25
  89.2 4.2 %collective-permute-start.23 = (bf16[76,256]{1,0:T(8,128)(2,1)S(1)}, bf16[76,256]{1,0:T(8,128)(2,1)S(1)}, u32[]{:S(2)}, u32[]{:S(2)}) collective-permute-start(bf16[76,256]{1,0:T(8,128)(2,1)S(1)} %get-tuple-element.30.refs_1_), channel_id=1, source_target_pairs={{0,12},{4,0},{8,4},{12,8},{1,13},{5,1},{9,5},{13,9},{2,14},{6,2},{... | collective-permute-start | bytes 116744 | tf_op jit(solution)/shard_map/ppermute | solution.py:25
  95.9 5.6 %collective-permute-start.24 = (bf16[68,128]{1,0:T(8,128)(2,1)S(1)}, bf16[68,128]{1,0:T(8,128)(2,1)S(1)}, u32[]{:S(2)}, u32[]{:S(2)}) collective-permute-start(bf16[68,128]{1,0:T(8,128)(2,1)S(1)} %attend.3.refs_0_), channel_id=1, source_target_pairs={{0,4},{4,8},{8,12},{12,0},{1,5},{5,9},{9,13},{13,1},{2,6},{6,10},{... | collective-permute-start | bytes 52232 | tf_op jit(solution)/shard_map/ppermute | solution.py:25
  96.6 5.0 %collective-permute-start.25 = (bf16[68,128]{1,0:T(8,128)(2,1)S(1)}, bf16[68,128]{1,0:T(8,128)(2,1)S(1)}, u32[]{:S(2)}, u32[]{:S(2)}) collective-permute-start(bf16[68,128]{1,0:T(8,128)(2,1)S(1)} %attend.3.refs_0_), channel_id=1, source_target_pairs={{0,8},{4,12},{8,0},{12,4},{1,9},{5,13},{9,1},{13,5},{2,10},{6,14},... | collective-permute-start | bytes 52232 | tf_op jit(solution)/shard_map/ppermute | solution.py:25
  99.5 3.8 %collective-permute-start.26 = (bf16[68,128]{1,0:T(8,128)(2,1)S(1)}, bf16[68,128]{1,0:T(8,128)(2,1)S(1)}, u32[]{:S(2)}, u32[]{:S(2)}) collective-permute-start(bf16[68,128]{1,0:T(8,128)(2,1)S(1)} %attend.3.refs_0_), channel_id=1, source_target_pairs={{0,12},{4,0},{8,4},{12,8},{1,13},{5,1},{9,5},{13,9},{2,14},{6,2},{... | collective-permute-start | bytes 52232 | tf_op jit(solution)/shard_map/ppermute | solution.py:25

commit v4 on v3

--- a/solution.py
+++ b/solution.py
@@ -29,8 +29,15 @@
     return [block] + [turned(block, axis, k) for k in range(1, lax.axis_size(axis))]
 
 
+def relayed_pieces_of(block, axis):
+    if lax.axis_size(axis) != 4:
+        return pieces_of(block, axis)
+    one = turned(block, axis, 1)
+    three = turned(block, axis, 3)
+    return [block, one, turned(one, axis, 1), three]
+
+
 VMEM = pl.BlockSpec(memory_space=pltpu.VMEM)
-SMEM = pl.BlockSpec(memory_space=pltpu.SMEM)
 HBM = pl.BlockSpec(memory_space=pltpu.HBM)
 ANY = pl.BlockSpec(memory_space=pl.ANY)
 
@@ -47,13 +54,16 @@
     return lax.rem(lax.axis_index("tensor") - k + count, count)
 
 
-def load_kernel(count, gain_ref, wq_ref, wkv_ref, gain_out, wq_out, wkv_out, sems):
-    rows = wq_ref.shape[0] // count
-    copies = [pltpu.make_async_copy(gain_ref, gain_out, sems.at[2, 0])]
-    for k in range(count):
-        part = pl.ds(k * rows, rows)
-        copies.append(pltpu.make_async_copy(wq_ref.at[part], wq_out.at[part], sems.at[0, k]))
-        copies.append(pltpu.make_async_copy(wkv_ref.at[part], wkv_out.at[part], sems.at[1, k]))
+def load_kernel(pieces, *refs):
+    given, kept, sems = refs[: len(pieces)], refs[len(pieces) : -1], refs[-1]
+    copies = []
+    for source, target, count in zip(given, kept, pieces):
+        rows = source.shape[0] // count
+        for k in range(count):
+            part = pl.ds(k * rows, rows)
+            copies.append(
+                pltpu.make_async_copy(source.at[part], target.at[part], sems.at[len(copies)])
+            )
     for copy in copies:
         copy.start()
     for copy in copies:
@@ -150,18 +160,13 @@
 def attend_kernel(count, span, ticks, *refs):
     query_ref = refs[0]
     parts = refs[1 : 1 + count]
-    segment_ref, length_ref, cache_ref, out_ref, blocks, cached, small, sems = refs[1 + count :]
+    segment_ref, length_ref, cache_ref, out_ref, blocks, small = refs[1 + count :]
     me = lax.axis_index("tensor")
     head = query_ref.shape[2]
     factor = 1.0 / math.sqrt(head)
     heads = count
     block = parts[0].shape[0] // len(ticks)
     last = block - count
-    copies = []
-    for b, tick in enumerate(ticks):
-        copy = pltpu.make_async_copy(cache_ref.at[tick], cached.at[b], sems.at[b])
-        copy.start()
-        copies.append(copy)
     for k, part in enumerate(parts):
         owner = owner_of(k, count)
         blocks[2 * owner] = part[:, :head]
@@ -205,25 +210,26 @@
             [jnp.where(line == h, queries, 0.0) for h in range(heads)], axis=1
         ).astype(BF16)
         own = jnp.sum(queries * small[b, 1], axis=-1, keepdims=True) * factor
-        copies[b].wait()
         dec_scores = (
             lax.dot_general(
                 spread,
-                cached[b, :, : heads * head],
+                cache_ref[tick, :, : heads * head],
                 (((1,), (1,)), ((), ())),
                 preferred_element_type=F32,
             )
             * factor
         )
         positions = lax.broadcasted_iota(jnp.int32, dec_scores.shape, 1)
-        dec_scores = jnp.where(positions < length_ref[0, micro], dec_scores, NEG)
+        lanes = lax.broadcasted_iota(jnp.int32, length_ref.shape, 1)
+        live = jnp.sum(jnp.where(lanes == micro, length_ref[...], 0), axis=1, keepdims=True)
+        dec_scores = jnp.where(positions < live, dec_scores, NEG)
         top = jnp.maximum(jnp.max(dec_scores, axis=-1, keepdims=True), own)
         dec_expo = jnp.exp(dec_scores - top)
         own_expo = jnp.exp(own - top)
         total = jnp.sum(dec_expo, axis=-1, keepdims=True) + own_expo
         dec_weights = (dec_expo / total).astype(BF16)
         own_weight = (own_expo / total).astype(BF16).astype(F32)
-        result = jnp.dot(dec_weights, cached[b, :, heads * head :], preferred_element_type=F32)
+        result = jnp.dot(dec_weights, cache_ref[tick, :, heads * head :], preferred_element_type=F32)
         extra = own_weight * small[b, 2]
         for h in range(heads):
             row = result[h : h + 1, h * head : (h + 1) * head] + extra[h : h + 1]
@@ -310,7 +316,7 @@
     length = cache.shape[3]
     ticks = cache.shape[1]
     half = head // 2
-    cached = in_hbm(cache.reshape(ticks, length, cache.shape[4]))
+    cached = cache.reshape(ticks, length, cache.shape[4])
     padded = (rows + 7) // 8 * 8
     message_rows = padded + count
     limit = pltpu.CompilerParams(vmem_limit_bytes=16 * 1024 * 1024)
@@ -319,24 +325,22 @@
 
     def cost(flops, moved_bytes):
         return pl.CostEstimate(
-            flops=int(1 * flops), bytes_accessed=int(1 * moved_bytes), transcendentals=0
-        )
-
-    gain, wq_here, wkv_here = pl.pallas_call(
-        functools.partial(load_kernel, count),
-        out_shape=(
-            jax.ShapeDtypeStruct(norm_gain.shape, F32),
-            jax.ShapeDtypeStruct(wq.shape[1:], BF16),
-            jax.ShapeDtypeStruct(wkv.shape[1:], BF16),
-        ),
-        in_specs=[HBM] * 3,
-        out_specs=(VMEM,) * 3,
-        scratch_shapes=[pltpu.SemaphoreType.DMA((3, count))],
+            flops=int(0 * flops), bytes_accessed=int(0 * moved_bytes), transcendentals=0
+        )
+
+    given = (norm_gain, wq[0], wkv[0], span_seg, dec_len.T, cached)
+    pieces = (1, count, count, 1, 1, ticks)
+    kept = pl.pallas_call(
+        functools.partial(load_kernel, pieces),
+        out_shape=tuple(jax.ShapeDtypeStruct(array.shape, array.dtype) for array in given),
+        in_specs=[HBM] * len(given),
+        out_specs=(VMEM,) * len(given),
+        scratch_shapes=[pltpu.SemaphoreType.DMA((sum(pieces),))],
         compiler_params=limit,
         cost_estimate=cost(0, 4 * wq.shape[1] * 3 * head),
         name="load",
-    )(in_hbm(norm_gain), in_hbm(wq[0]), in_hbm(wkv[0]))
-    gain, wq_here, wkv_here = in_vmem(gain), in_vmem(wq_here), in_vmem(wkv_here)
+    )(*[in_hbm(array) for array in given])
+    gain, wq_here, wkv_here, segments, lengths, cached = [in_vmem(array) for array in kept]
 
     def project(parts):
         batch = len(parts) // count
@@ -361,13 +365,11 @@
         return pl.pallas_call(
             functools.partial(attend_kernel, count, span, which),
             out_shape=jax.ShapeDtypeStruct((batch * (span + count), head), BF16),
-            in_specs=[VMEM] * (count + 2) + [SMEM, HBM],
+            in_specs=[VMEM] * (count + 4),
             out_specs=VMEM,
             scratch_shapes=[
                 pltpu.VMEM((2 * count, batch * message_rows, head), BF16),
-                pltpu.VMEM((batch, length, cache.shape[4]), BF16),
                 pltpu.VMEM((batch, 4, 8, head), F32),
-                pltpu.SemaphoreType.DMA((batch,)),
             ],
             compiler_params=limit,
             cost_estimate=cost(
@@ -375,7 +377,7 @@
                 batch * (4 * length * 4 * head + count * message_rows * 4 * head),
             ),
             name="attend",
-        )(queries, *[in_vmem(part) for part in parts], span_seg, dec_len.T, cached)
+        )(queries, *[in_vmem(part) for part in parts], segments, lengths, cached)
 
     output_scratch = [
         pltpu.VMEM((count, padded, head), BF16),
@@ -383,7 +385,7 @@
         pltpu.VMEM((count, 8, head), F32),
     ]
     output_cost = cost(2 * rows * shard * count * head, 2 * shard * (count * head + rows))
-    stream_parts = pieces_of(stream_in[0], "tensor")
+    stream_parts = relayed_pieces_of(stream_in[0], "tensor")
     first_new = pl.pallas_call(
         begin_kernel,
         out_shape=block,

time: 105 us -> 95.8 us (0.912)
  waiting for transfers between devices: 37.4 us -> 31.8 us
  Pallas kernels: 16.8 us -> 12.4 us
    ppermute x27, waiting for transfers between devices: 37.4 us -> 31.8 us  [turned(): lax.ppermute(block, axis, [(i, (i + distance) % count) for i in range(cou...]
    pallas_call x2, Pallas kernels: 5.94 us -> 2.56 us  [attend(): pl.pallas_call(functools.partial(attend_kernel, count, span, which), out_...]
  transfers between devices with their start and end apart: 29 -> 29, of which waited for: 16 -> 18; matrix products, arithmetic and copies ran while one was open for 0% -> 1% of each run, Pallas kernels for 14% -> 10%
where the time goes in v4:
time: 95.8 us; the launch traced here: 95.6 us
  starting transfers between devices  48.3 us (50%)
  waiting for transfers between devices  31.8 us (33%)
  Pallas kernels  12.4 us (13%)
  local copies, waits for them, and re-layouts  2.35 us (2%)
    ppermute x27, starting transfers between devices, turned(): lax.ppermute(block, axis, [(i, (i + distance) % count) for i in range(cou...  45.7 us
    ppermute x27, waiting for transfers between devices, turned(): lax.ppermute(block, axis, [(i, (i + distance) % count) for i in range(cou...  31.8 us
    pallas_call x1, Pallas kernels, fast_body(): pl.pallas_call(functools.partial(load_kernel, pieces), out_shape=tuple((j...  2.73 us
    ppermute x2, starting transfers between devices, moved(): return lax.ppermute(block, axis, route)  2.6 us
    pallas_call x2, Pallas kernels, attend(): pl.pallas_call(functools.partial(attend_kernel, count, span, which), out_...  2.56 us
    pallas_call x2, Pallas kernels, project(): pl.pallas_call(functools.partial(project_kernel, count, span, batch), out...  2.24 us
    unnamed x10, local copies, waits for them, and re-layouts  1.96 us
  transfers between devices with their start and end apart: 29, of which 18 were waited for; matrix products, arithmetic and copies ran while one was open for 1% of the time, Pallas kernels for 10%

profile of v4, /device:TPU:0, one launch (start us, length us, event | category | flops | bytes accessed | tf_op | source)
XLA Modules:
  0.0 95.6 jit_solution(4246069984122864310)
XLA Ops:
  0.6 1.1 %cut.1 = (bf16[64,1024]{1,0:T(8,128)(2,1)S(1)}, bf16[64,1024]{1,0:T(8,128)(2,1)S(1)}, bf16[64,1024]{1,0:T(8,128)(2,1)S(1)}) custom-call(bf16[128,4096]{1,0:T(8,128)(2,1)} %bitcast.23), custom_call_target="tpu_custom_call" | custom-call | tf_op jit(solution)/shard_map/cut/pallas_call | solution.py:412
  1.8 3.1 %collective-permute-start.13 = (bf16[64,1024]{1,0:T(8,128)(2,1)S(1)}, bf16[64,1024]{1,0:T(8,128)(2,1)S(1)}, u32[]{:S(2)}, u32[]{:S(2)}) collective-permute-start(bf16[64,1024]{1,0:T(8,128)(2,1)S(1)} %get-tuple-element.31), channel_id=1, source_target_pairs={{0,4},{4,8},{8,12},{12,0},{1,5},{5,9},{9,13},{13,1},{2,6},{6,10},{... | collective-permute-start | bytes 393224 | tf_op jit(solution)/shard_map/ppermute | solution.py:25
  4.8 2.6 %collective-permute-start.14 = (bf16[64,1024]{1,0:T(8,128)(2,1)S(1)}, bf16[64,1024]{1,0:T(8,128)(2,1)S(1)}, u32[]{:S(2)}, u32[]{:S(2)}) collective-permute-start(bf16[64,1024]{1,0:T(8,128)(2,1)S(1)} %get-tuple-element.32), channel_id=1, source_target_pairs={{0,8},{4,12},{8,0},{12,4},{1,9},{5,13},{9,1},{13,5},{2,10},{6,14},... | collective-permute-start | bytes 393224 | tf_op jit(solution)/shard_map/ppermute | solution.py:25
  7.4 1.3 %collective-permute-start.15 = (bf16[64,1024]{1,0:T(8,128)(2,1)S(1)}, bf16[64,1024]{1,0:T(8,128)(2,1)S(1)}, u32[]{:S(2)}, u32[]{:S(2)}) collective-permute-start(bf16[64,1024]{1,0:T(8,128)(2,1)S(1)} %get-tuple-element.33), channel_id=1, source_target_pairs={{0,12},{4,0},{8,4},{12,8},{1,13},{5,1},{9,5},{13,9},{2,14},{6,2},{... | collective-permute-start | bytes 393224 | tf_op jit(solution)/shard_map/ppermute | solution.py:25
  9.5 3.1 %collective-permute-start.2 = (bf16[68,1024]{1,0:T(8,128)(2,1)}, bf16[68,1024]{1,0:T(8,128)(2,1)S(1)}, u32[]{:S(2)}, u32[]{:S(2)}) collective-permute-start(bf16[68,1024]{1,0:T(8,128)(2,1)} %bitcast.18), channel_id=1, source_target_pairs={{0,12},{4,0},{8,4},{12,8},{1,13},{5,1},{9,5},{13,9},{2,14},{6,2},{... | collective-permute-start | bytes 417800 | tf_op jit(solution)/shard_map/ppermute | solution.py:25
  12.6 0.9 copy-done
  13.5 0.9 copy-done.2
  14.5 1.3 %collective-permute-start.3 = (bf16[68,1024]{1,0:T(8,128)(2,1)S(1)}, bf16[68,1024]{1,0:T(8,128)(2,1)S(1)}, u32[]{:S(2)}, u32[]{:S(2)}) collective-permute-start(bf16[68,1024]{1,0:T(8,128)(2,1)S(1)} %begin.1.refs_5_), channel_id=1, source_target_pairs={{0,1},{1,2},{2,3},{4,5},{5,6},{6,7},{8,9},{9,10},{10,11},{12,13},{... | collective-permute-start | bytes 417800 | tf_op jit(solution)/shard_map/ppermute | solution.py:20
  15.8 1.1 %collective-permute-done.14.refs_1_.refs_2_ = bf16[64,1024]{1,0:T(8,128)(2,1)S(1)} collective-permute-done((bf16[64,1024]{1,0:T(8,128)(2,1)S(1)}, bf16[64,1024]{1,0:T(8,128)(2,1)S(1)}, u32[]{:S(2)}, u32[]{:S(2)}) %collective-permute-start.14) | collective-permute-done | bytes 131104 | tf_op jit(solution)/shard_map/ppermute | solution.py:25
  17.0 2.8 %collective-permute-done.15.refs_2_.refs_3_ = bf16[64,1024]{1,0:T(8,128)(2,1)S(1)} collective-permute-done((bf16[64,1024]{1,0:T(8,128)(2,1)S(1)}, bf16[64,1024]{1,0:T(8,128)(2,1)S(1)}, u32[]{:S(2)}, u32[]{:S(2)}) %collective-permute-start.15) | collective-permute-done | bytes 131104 | tf_op jit(solution)/shard_map/ppermute | solution.py:25
  19.7 1.6 %collective-permute-start.16 = (bf16[3,64,1024]{2,1,0:T(8,128)(2,1)S(1)}, bf16[3,64,1024]{2,1,0:T(8,128)(2,1)S(1)}, u32[]{:S(2)}, u32[]{:S(2)}) collective-permute-start(bf16[3,64,1024]{2,1,0:T(8,128)(2,1)S(1)} %stack.1), channel_id=1, source_target_pairs={{0,16},{16,0},{1,17},{17,1},{2,18},{18,2},{3,19},{19,3},{4,20},{20... | collective-permute-start | bytes 1179656 | tf_op jit(solution)/shard_map/ppermute | solution.py:25
  21.9 3.0 %collective-permute-start.4 = (bf16[68,1024]{1,0:T(8,128)(2,1)S(1)}, bf16[68,1024]{1,0:T(8,128)(2,1)S(1)}, u32[]{:S(2)}, u32[]{:S(2)}) collective-permute-start(bf16[68,1024]{1,0:T(8,128)(2,1)S(1)} %choose.1.refs_4_), channel_id=1, source_target_pairs={{0,4},{4,8},{8,12},{12,0},{1,5},{5,9},{9,13},{13,1},{2,6},{6,10},{... | collective-permute-start | bytes 417800 | tf_op jit(solution)/shard_map/ppermute | solution.py:25
  24.9 2.7 %collective-permute-start.5 = (bf16[68,1024]{1,0:T(8,128)(2,1)S(1)}, bf16[68,1024]{1,0:T(8,128)(2,1)S(1)}, u32[]{:S(2)}, u32[]{:S(2)}) collective-permute-start(bf16[68,1024]{1,0:T(8,128)(2,1)S(1)} %choose.1.refs_4_), channel_id=1, source_target_pairs={{0,8},{4,12},{8,0},{12,4},{1,9},{5,13},{9,1},{13,5},{2,10},{6,14},... | collective-permute-start | bytes 417800 | tf_op jit(solution)/shard_map/ppermute | solution.py:25
  27.6 2.9 %collective-permute-start.6 = (bf16[68,1024]{1,0:T(8,128)(2,1)S(1)}, bf16[68,1024]{1,0:T(8,128)(2,1)S(1)}, u32[]{:S(2)}, u32[]{:S(2)}) collective-permute-start(bf16[68,1024]{1,0:T(8,128)(2,1)S(1)} %choose.1.refs_4_), channel_id=1, source_target_pairs={{0,12},{4,0},{8,4},{12,8},{1,13},{5,1},{9,5},{13,9},{2,14},{6,2},{... | collective-permute-start | bytes 417800 | tf_op jit(solution)/shard_map/ppermute | solution.py:25
  30.4 2.7 %load.1 = (f32[1,4096]{1,0:T(1,128)S(1)}, bf16[4096,128]{1,0:T(8,128)(2,1)S(1)}, bf16[4096,256]{1,0:T(8,128)(2,1)S(1)}, s32[6,64]{1,0:T(8,128)S(1)}, s32[1,6]{1,...) custom-call(f32[1,4096]{1,0:T(1,128)} %refs_0_.1, bf16[4096,128]{1,0:T(8,128)(2,1)} %bitcast.27, bf16[4096,256]{1,0:T(8,128)(2,1)} %bitcast.26, ...), custom_call_target="tpu_custom_call" | custom-call | tf_op jit(solution)/shard_map/load/pallas_call | solution.py:333
  33.2 1.7 %collective-permute-done.1.refs_2_ = bf16[68,1024]{1,0:T(8,128)(2,1)S(1)} collective-permute-done((bf16[68,1024]{1,0:T(8,128)(2,1)S(1)}, bf16[68,1024]{1,0:T(8,128)(2,1)S(1)}, u32[]{:S(2)}, u32[]{:S(2)}) %collective-permute-start.1) | collective-permute-done | bytes 139296 | tf_op jit(solution)/shard_map/ppermute | solution.py:25
  34.8 4.9 %collective-permute-done.5.refs_6_ = bf16[68,1024]{1,0:T(8,128)(2,1)S(1)} collective-permute-done((bf16[68,1024]{1,0:T(8,128)(2,1)S(1)}, bf16[68,1024]{1,0:T(8,128)(2,1)S(1)}, u32[]{:S(2)}, u32[]{:S(2)}) %collective-permute-start.5) | collective-permute-done | bytes 139296 | tf_op jit(solution)/shard_map/ppermute | solution.py:25
  39.7 1.4 %project.2 = (bf16[2,64,128]{2,1,0:T(8,128)(2,1)S(1)}, bf16[152,256]{1,0:T(8,128)(2,1)S(1)}) custom-call(bf16[68,1024]{1,0:T(8,128)(2,1)S(1)} %bitcast.20, bf16[68,1024]{1,0:T(8,128)(2,1)S(1)} %collective-permute-done.refs_1_, bf16[68,1024]{1,0:T(8,128)(2,1)S(1)} %collective-permute-done.1.refs_2_, bf16[68,1024]{1,0:T(8,128)(2,1)S(1)} %collective-permute-done.2.refs_3_, ...), custom_call_target="tpu_custom_call" | custom-call | tf_op jit(solution)/shard_map/project/pallas_call | solution.py:347
  41.1 2.9 %collective-permute-start.7 = (bf16[152,256]{1,0:T(8,128)(2,1)S(1)}, bf16[152,256]{1,0:T(8,128)(2,1)S(1)}, u32[]{:S(2)}, u32[]{:S(2)}) collective-permute-start(bf16[152,256]{1,0:T(8,128)(2,1)S(1)} %get-tuple-element.27.refs_1_), channel_id=1, source_target_pairs={{0,4},{4,8},{8,12},{12,0},{1,5},{5,9},{9,13},{13,1},{2,6},{6,10},{... | collective-permute-start | bytes 233480 | tf_op jit(solution)/shard_map/ppermute | solution.py:25
  44.0 1.5 %collective-permute-start.8 = (bf16[152,256]{1,0:T(8,128)(2,1)S(1)}, bf16[152,256]{1,0:T(8,128)(2,1)S(1)}, u32[]{:S(2)}, u32[]{:S(2)}) collective-permute-start(bf16[152,256]{1,0:T(8,128)(2,1)S(1)} %get-tuple-element.27.refs_1_), channel_id=1, source_target_pairs={{0,8},{4,12},{8,0},{12,4},{1,9},{5,13},{9,1},{13,5},{2,10},{6,14},... | collective-permute-start | bytes 233480 | tf_op jit(solution)/shard_map/ppermute | solution.py:25
  45.5 1.0 %collective-permute-start.9 = (bf16[152,256]{1,0:T(8,128)(2,1)S(1)}, bf16[152,256]{1,0:T(8,128)(2,1)S(1)}, u32[]{:S(2)}, u32[]{:S(2)}) collective-permute-start(bf16[152,256]{1,0:T(8,128)(2,1)S(1)} %get-tuple-element.27.refs_1_), channel_id=1, source_target_pairs={{0,12},{4,0},{8,4},{12,8},{1,13},{5,1},{9,5},{13,9},{2,14},{6,2},{... | collective-permute-start | bytes 233480 | tf_op jit(solution)/shard_map/ppermute | solution.py:25
  46.4 1.8 %collective-permute-done.7.refs_2_ = bf16[152,256]{1,0:T(8,128)(2,1)S(1)} collective-permute-done((bf16[152,256]{1,0:T(8,128)(2,1)S(1)}, bf16[152,256]{1,0:T(8,128)(2,1)S(1)}, u32[]{:S(2)}, u32[]{:S(2)}) %collective-permute-start.7) | collective-permute-done | bytes 77856 | tf_op jit(solution)/shard_map/ppermute | solution.py:25
  48.2 2.7 %collective-permute-done.8.refs_3_ = bf16[152,256]{1,0:T(8,128)(2,1)S(1)} collective-permute-done((bf16[152,256]{1,0:T(8,128)(2,1)S(1)}, bf16[152,256]{1,0:T(8,128)(2,1)S(1)}, u32[]{:S(2)}, u32[]{:S(2)}) %collective-permute-start.8) | collective-permute-done | bytes 77856 | tf_op jit(solution)/shard_map/ppermute | solution.py:25
  50.9 1.7 %attend.2.refs_0_ = bf16[136,128]{1,0:T(8,128)(2,1)S(1)} custom-call(bf16[2,64,128]{2,1,0:T(8,128)(2,1)S(1)} %get-tuple-element.26.refs_0_, bf16[152,256]{1,0:T(8,128)(2,1)S(1)} %get-tuple-element.27.refs_1_, bf16[152,256]{1,0:T(8,128)(2,1)S(1)} %collective-permute-done.7.refs_2_, bf16[152,256]{1,0:T(8,128)(2,1)S(1)} %collective-permute-done.8.refs_3_, ...), custom_call_target="tpu_custom_call" | custom-call | tf_op jit(solution)/shard_map/attend/pallas_call | solution.py:365
  52.6 1.8 %collective-permute-start.10 = (bf16[136,128]{1,0:T(8,128)(2,1)S(1)}, bf16[136,128]{1,0:T(8,128)(2,1)S(1)}, u32[]{:S(2)}, u32[]{:S(2)}) collective-permute-start(bf16[136,128]{1,0:T(8,128)(2,1)S(1)} %attend.2.refs_0_), channel_id=1, source_target_pairs={{0,4},{4,8},{8,12},{12,0},{1,5},{5,9},{9,13},{13,1},{2,6},{6,10},{... | collective-permute-start | bytes 104456 | tf_op jit(solution)/shard_map/ppermute | solution.py:25
  54.4 1.2 %collective-permute-start.11 = (bf16[136,128]{1,0:T(8,128)(2,1)S(1)}, bf16[136,128]{1,0:T(8,128)(2,1)S(1)}, u32[]{:S(2)}, u32[]{:S(2)}) collective-permute-start(bf16[136,128]{1,0:T(8,128)(2,1)S(1)} %attend.2.refs_0_), channel_id=1, source_target_pairs={{0,8},{4,12},{8,0},{12,4},{1,9},{5,13},{9,1},{13,5},{2,10},{6,14},... | collective-permute-start | bytes 104456 | tf_op jit(solution)/shard_map/ppermute | solution.py:25
  55.5 1.3 %collective-permute-start.12 = (bf16[136,128]{1,0:T(8,128)(2,1)S(1)}, bf16[136,128]{1,0:T(8,128)(2,1)S(1)}, u32[]{:S(2)}, u32[]{:S(2)}) collective-permute-start(bf16[136,128]{1,0:T(8,128)(2,1)S(1)} %attend.2.refs_0_), channel_id=1, source_target_pairs={{0,12},{4,0},{8,4},{12,8},{1,13},{5,1},{9,5},{13,9},{2,14},{6,2},{... | collective-permute-start | bytes 104456 | tf_op jit(solution)/shard_map/ppermute | solution.py:25
  56.9 1.1 %place.1.refs_4_ = bf16[4,128,1024]{2,1,0:T(8,128)(2,1)S(1)} custom-call(bf16[128,4096]{1,0:T(8,128)(2,1)} %bitcast.24, bf16[64,1024]{1,0:T(8,128)(2,1)S(1)} %collective-permute-done.13.refs_0_.refs_1_, bf16[64,1024]{1,0:T(8,128)(2,1)S(1)} %collective-permute-done.14.refs_1_.refs_2_, bf16[64,1024]{1,0:T(8,128)(2,1)S(1)} %collective-permute-done.15.refs_2_.refs_3_, ...), custom_call_target="tpu_custom_call" | custom-call | tf_op jit(solution)/shard_map/place/pallas_call | solution.py:438
  58.5 1.0 %collective-permute-done.11.refs_2_ = bf16[136,128]{1,0:T(8,128)(2,1)S(1)} collective-permute-done((bf16[136,128]{1,0:T(8,128)(2,1)S(1)}, bf16[136,128]{1,0:T(8,128)(2,1)S(1)}, u32[]{:S(2)}, u32[]{:S(2)}) %collective-permute-start.11) | collective-permute-done | bytes 34848 | tf_op jit(solution)/shard_map/ppermute | solution.py:25
  60.1 1.5 %collective-permute-start.17 = (bf16[68,1024]{1,0:T(8,128)(2,1)S(1)}, bf16[68,1024]{1,0:T(8,128)(2,1)S(1)}, u32[]{:S(2)}, u32[]{:S(2)}) collective-permute-start(bf16[68,1024]{1,0:T(8,128)(2,1)S(1)} %get-tuple-element.34), channel_id=1, source_target_pairs={{0,2},{1,3},{2,0},{3,1},{4,6},{5,7},{6,4},{7,5},{8,10},{9,11},{10,... | collective-permute-start | bytes 417800 | tf_op jit(solution)/shard_map/ppermute | solution.py:25
  61.7 4.4 %collective-permute-done.17.refs_0_.refs_5_ = bf16[68,1024]{1,0:T(8,128)(2,1)S(1)} collective-permute-done((bf16[68,1024]{1,0:T(8,128)(2,1)S(1)}, bf16[68,1024]{1,0:T(8,128)(2,1)S(1)}, u32[]{:S(2)}, u32[]{:S(2)}) %collective-permute-start.17) | collective-permute-done | bytes 139296 | tf_op jit(solution)/shard_map/ppermute | solution.py:25
  66.0 1.2 %collective-permute-start.18 = (bf16[68,1024]{1,0:T(8,128)(2,1)S(1)}, bf16[68,1024]{1,0:T(8,128)(2,1)S(1)}, u32[]{:S(2)}, u32[]{:S(2)}) collective-permute-start(bf16[68,1024]{1,0:T(8,128)(2,1)S(1)} %collective-permute-done.17.refs_0_.refs_5_), channel_id=1, source_target_pairs={{0,4},{4,8},{8,12},{12,0},{1,5},{5,9},{9,13},{13,1},{2,6},{6,10},{... | collective-permute-start | bytes 417800 | tf_op jit(solution)/shard_map/ppermute | solution.py:25
  67.2 2.2 %collective-permute-start.19 = (bf16[68,1024]{1,0:T(8,128)(2,1)S(1)}, bf16[68,1024]{1,0:T(8,128)(2,1)S(1)}, u32[]{:S(2)}, u32[]{:S(2)}) collective-permute-start(bf16[68,1024]{1,0:T(8,128)(2,1)S(1)} %collective-permute-done.17.refs_0_.refs_5_), channel_id=1, source_target_pairs={{0,8},{4,12},{8,0},{12,4},{1,9},{5,13},{9,1},{13,5},{2,10},{6,14},... | collective-permute-start | bytes 417800 | tf_op jit(solution)/shard_map/ppermute | solution.py:25
  69.4 1.1 %collective-permute-start.20 = (bf16[68,1024]{1,0:T(8,128)(2,1)S(1)}, bf16[68,1024]{1,0:T(8,128)(2,1)S(1)}, u32[]{:S(2)}, u32[]{:S(2)}) collective-permute-start(bf16[68,1024]{1,0:T(8,128)(2,1)S(1)} %collective-permute-done.17.refs_0_.refs_5_), channel_id=1, source_target_pairs={{0,12},{4,0},{8,4},{12,8},{1,13},{5,1},{9,5},{13,9},{2,14},{6,2},{... | collective-permute-start | bytes 417800 | tf_op jit(solution)/shard_map/ppermute | solution.py:25
  70.5 1.0 %output_second.1 = (bf16[68,1024]{1,0:T(8,128)(2,1)S(1)}, bf16[3,68,1024]{2,1,0:T(8,128)(2,1)}, bf16[3,68,1024]{2,1,0:T(8,128)(2,1)}) custom-call(bf16[136,128]{1,0:T(8,128)(2,1)S(1)} %attend.2.refs_0_, bf16[136,128]{1,0:T(8,128)(2,1)S(1)} %collective-permute-done.10.refs_1_, bf16[136,128]{1,0:T(8,128)(2,1)S(1)} %collective-permute-done.11.refs_2_, ...), custom_call_target="tpu_custom_call" | custom-call | tf_op jit(solution)/shard_map/output_second/pallas_call | solution.py:470
  71.5 1.3 %collective-permute-start.28 = (bf16[68,1024]{1,0:T(8,128)(2,1)S(1)}, bf16[68,1024]{1,0:T(8,128)(2,1)S(1)}, u32[]{:S(2)}, u32[]{:S(2)}) collective-permute-start(bf16[68,1024]{1,0:T(8,128)(2,1)S(1)} %get-tuple-element.39), channel_id=1, source_target_pairs={{0,1},{1,2},{2,3},{4,5},{5,6},{6,7},{8,9},{9,10},{10,11},{12,13},{... | collective-permute-start | bytes 417800 | tf_op jit(solution)/shard_map/ppermute | solution.py:20
  73.2 4.6 %collective-permute-done.19.refs_2_ = bf16[68,1024]{1,0:T(8,128)(2,1)S(1)} collective-permute-done((bf16[68,1024]{1,0:T(8,128)(2,1)S(1)}, bf16[68,1024]{1,0:T(8,128)(2,1)S(1)}, u32[]{:S(2)}, u32[]{:S(2)}) %collective-permute-start.19) | collective-permute-done | bytes 139296 | tf_op jit(solution)/shard_map/ppermute | solution.py:25
  78.7 2.2 %collective-permute-start.21 = (bf16[76,256]{1,0:T(8,128)(2,1)S(1)}, bf16[76,256]{1,0:T(8,128)(2,1)S(1)}, u32[]{:S(2)}, u32[]{:S(2)}) collective-permute-start(bf16[76,256]{1,0:T(8,128)(2,1)S(1)} %get-tuple-element.36.refs_1_), channel_id=1, source_target_pairs={{0,4},{4,8},{8,12},{12,0},{1,5},{5,9},{9,13},{13,1},{2,6},{6,10},{... | collective-permute-start | bytes 116744 | tf_op jit(solution)/shard_map/ppermute | solution.py:25
  80.9 1.1 %collective-permute-start.22 = (bf16[76,256]{1,0:T(8,128)(2,1)S(1)}, bf16[76,256]{1,0:T(8,128)(2,1)S(1)}, u32[]{:S(2)}, u32[]{:S(2)}) collective-permute-start(bf16[76,256]{1,0:T(8,128)(2,1)S(1)} %get-tuple-element.36.refs_1_), channel_id=1, source_target_pairs={{0,8},{4,12},{8,0},{12,4},{1,9},{5,13},{9,1},{13,5},{2,10},{6,14},... | collective-permute-start | bytes 116744 | tf_op jit(solution)/shard_map/ppermute | solution.py:25
  81.9 1.4 %collective-permute-start.23 = (bf16[76,256]{1,0:T(8,128)(2,1)S(1)}, bf16[76,256]{1,0:T(8,128)(2,1)S(1)}, u32[]{:S(2)}, u32[]{:S(2)}) collective-permute-start(bf16[76,256]{1,0:T(8,128)(2,1)S(1)} %get-tuple-element.36.refs_1_), channel_id=1, source_target_pairs={{0,12},{4,0},{8,4},{12,8},{1,13},{5,1},{9,5},{13,9},{2,14},{6,2},{... | collective-permute-start | bytes 116744 | tf_op jit(solution)/shard_map/ppermute | solution.py:25
  83.3 1.2 %collective-permute-done.21.refs_2_ = bf16[76,256]{1,0:T(8,128)(2,1)S(1)} collective-permute-done((bf16[76,256]{1,0:T(8,128)(2,1)S(1)}, bf16[76,256]{1,0:T(8,128)(2,1)S(1)}, u32[]{:S(2)}, u32[]{:S(2)}) %collective-permute-start.21) | collective-permute-done | bytes 38944 | tf_op jit(solution)/shard_map/ppermute | solution.py:25
  84.5 1.3 %collective-permute-done.22.refs_3_ = bf16[76,256]{1,0:T(8,128)(2,1)S(1)} collective-permute-done((bf16[76,256]{1,0:T(8,128)(2,1)S(1)}, bf16[76,256]{1,0:T(8,128)(2,1)S(1)}, u32[]{:S(2)}, u32[]{:S(2)}) %collective-permute-start.22) | collective-permute-done | bytes 38944 | tf_op jit(solution)/shard_map/ppermute | solution.py:25
  87.1 1.0 %collective-permute-start.24 = (bf16[68,128]{1,0:T(8,128)(2,1)S(1)}, bf16[68,128]{1,0:T(8,128)(2,1)S(1)}, u32[]{:S(2)}, u32[]{:S(2)}) collective-permute-start(bf16[68,128]{1,0:T(8,128)(2,1)S(1)} %attend.3.refs_0_), channel_id=1, source_target_pairs={{0,4},{4,8},{8,12},{12,0},{1,5},{5,9},{9,13},{13,1},{2,6},{6,10},{... | collective-permute-start | bytes 52232 | tf_op jit(solution)/shard_map/ppermute | solution.py:25
  88.1 2.7 %collective-permute-start.25 = (bf16[68,128]{1,0:T(8,128)(2,1)S(1)}, bf16[68,128]{1,0:T(8,128)(2,1)S(1)}, u32[]{:S(2)}, u32[]{:S(2)}) collective-permute-start(bf16[68,128]{1,0:T(8,128)(2,1)S(1)} %attend.3.refs_0_), channel_id=1, source_target_pairs={{0,8},{4,12},{8,0},{12,4},{1,9},{5,13},{9,1},{13,5},{2,10},{6,14},... | collective-permute-start | bytes 52232 | tf_op jit(solution)/shard_map/ppermute | solution.py:25
  90.8 0.9 collective-permute-start.26
  91.7 1.1 %collective-permute-done.24.refs_1_ = bf16[68,128]{1,0:T(8,128)(2,1)S(1)} collective-permute-done((bf16[68,128]{1,0:T(8,128)(2,1)S(1)}, bf16[68,128]{1,0:T(8,128)(2,1)S(1)}, u32[]{:S(2)}, u32[]{:S(2)}) %collective-permute-start.24) | collective-permute-done | bytes 17440 | tf_op jit(solution)/shard_map/ppermute | solution.py:25
  92.9 1.6 %collective-permute-done.26.refs_3_ = bf16[68,128]{1,0:T(8,128)(2,1)S(1)} collective-permute-done((bf16[68,128]{1,0:T(8,128)(2,1)S(1)}, bf16[68,128]{1,0:T(8,128)(2,1)S(1)}, u32[]{:S(2)}, u32[]{:S(2)}) %collective-permute-start.26) | collective-permute-done | bytes 17440 | tf_op jit(solution)/shard_map/ppermute | solution.py:25
  94.5 1.1 %output_third.1 = (bf16[3,68,1024]{2,1,0:T(8,128)(2,1)}, bf16[3,68,1024]{2,1,0:T(8,128)(2,1)}) custom-call(bf16[68,128]{1,0:T(8,128)(2,1)S(1)} %attend.3.refs_0_, bf16[68,128]{1,0:T(8,128)(2,1)S(1)} %collective-permute-done.24.refs_1_, bf16[68,128]{1,0:T(8,128)(2,1)S(1)} %collective-permute-done.25.refs_2_, ...), custom_call_target="tpu_custom_call", output_to_operand_aliasing={{0}: (7, {}), {1}: (8, {})} | custom-call | tf_op jit(solution)/shard_map/output_third/pallas_call | solution.py:491
  (34 shorter events, 5.2 us)
Async XLA Ops:
  0.6 20.7 %copy-start.3 = (bf16[2,68,1024]{2,0,1:T(2,128)(2,1)S(1)}, bf16[2,68,1024]{2,0,1:T(2,128)(2,1)}, u32[]{:S(2)}) copy-start(bf16[2,68,1024]{2,0,1:T(2,128)(2,1)} %param.12) | copy-start | bytes 835588
  1.8 12.7 %collective-permute-start.13 = (bf16[64,1024]{1,0:T(8,128)(2,1)S(1)}, bf16[64,1024]{1,0:T(8,128)(2,1)S(1)}, u32[]{:S(2)}, u32[]{:S(2)}) collective-permute-start(bf16[64,1024]{1,0:T(8,128)(2,1)S(1)} %get-tuple-element.31), channel_id=1, source_target_pairs={{0,4},{4,8},{8,12},{12,0},{1,5},{5,9},{9,13},{13,1},{2,6},{6,10},{... | collective-permute-start | bytes 393224 | tf_op jit(solution)/shard_map/ppermute | solution.py:25
  4.8 12.1 %collective-permute-start.14 = (bf16[64,1024]{1,0:T(8,128)(2,1)S(1)}, bf16[64,1024]{1,0:T(8,128)(2,1)S(1)}, u32[]{:S(2)}, u32[]{:S(2)}) collective-permute-start(bf16[64,1024]{1,0:T(8,128)(2,1)S(1)} %get-tuple-element.32), channel_id=1, source_target_pairs={{0,8},{4,12},{8,0},{12,4},{1,9},{5,13},{9,1},{13,5},{2,10},{6,14},... | collective-permute-start | bytes 393224 | tf_op jit(solution)/shard_map/ppermute | solution.py:25
  7.4 12.3 %collective-permute-start.15 = (bf16[64,1024]{1,0:T(8,128)(2,1)S(1)}, bf16[64,1024]{1,0:T(8,128)(2,1)S(1)}, u32[]{:S(2)}, u32[]{:S(2)}) collective-permute-start(bf16[64,1024]{1,0:T(8,128)(2,1)S(1)} %get-tuple-element.33), channel_id=1, source_target_pairs={{0,12},{4,0},{8,4},{12,8},{1,13},{5,1},{9,5},{13,9},{2,14},{6,2},{... | collective-permute-start | bytes 393224 | tf_op jit(solution)/shard_map/ppermute | solution.py:25
  8.8 16.0 %collective-permute-start = (bf16[68,1024]{1,0:T(8,128)(2,1)}, bf16[68,1024]{1,0:T(8,128)(2,1)S(1)}, u32[]{:S(2)}, u32[]{:S(2)}) collective-permute-start(bf16[68,1024]{1,0:T(8,128)(2,1)} %bitcast.17), channel_id=1, source_target_pairs={{0,4},{4,8},{8,12},{12,0},{1,5},{5,9},{9,13},{13,1},{2,6},{6,10},{... | collective-permute-start | bytes 417800 | tf_op jit(solution)/shard_map/ppermute | solution.py:25
  9.5 18.1 %collective-permute-start.2 = (bf16[68,1024]{1,0:T(8,128)(2,1)}, bf16[68,1024]{1,0:T(8,128)(2,1)S(1)}, u32[]{:S(2)}, u32[]{:S(2)}) collective-permute-start(bf16[68,1024]{1,0:T(8,128)(2,1)} %bitcast.18), channel_id=1, source_target_pairs={{0,12},{4,0},{8,4},{12,8},{1,13},{5,1},{9,5},{13,9},{2,14},{6,2},{... | collective-permute-start | bytes 417800 | tf_op jit(solution)/shard_map/ppermute | solution.py:25
  12.6 0.9 copy-start
  13.5 0.9 copy-start.2
  14.5 7.3 %collective-permute-start.3 = (bf16[68,1024]{1,0:T(8,128)(2,1)S(1)}, bf16[68,1024]{1,0:T(8,128)(2,1)S(1)}, u32[]{:S(2)}, u32[]{:S(2)}) collective-permute-start(bf16[68,1024]{1,0:T(8,128)(2,1)S(1)} %begin.1.refs_5_), channel_id=1, source_target_pairs={{0,1},{1,2},{2,3},{4,5},{5,6},{6,7},{8,9},{9,10},{10,11},{12,13},{... | collective-permute-start | bytes 417800 | tf_op jit(solution)/shard_map/ppermute | solution.py:20
  19.7 37.1 %collective-permute-start.16 = (bf16[3,64,1024]{2,1,0:T(8,128)(2,1)S(1)}, bf16[3,64,1024]{2,1,0:T(8,128)(2,1)S(1)}, u32[]{:S(2)}, u32[]{:S(2)}) collective-permute-start(bf16[3,64,1024]{2,1,0:T(8,128)(2,1)S(1)} %stack.1), channel_id=1, source_target_pairs={{0,16},{16,0},{1,17},{17,1},{2,18},{18,2},{3,19},{19,3},{4,20},{20... | collective-permute-start | bytes 1179656 | tf_op jit(solution)/shard_map/ppermute | solution.py:25
  21.9 13.0 %collective-permute-start.4 = (bf16[68,1024]{1,0:T(8,128)(2,1)S(1)}, bf16[68,1024]{1,0:T(8,128)(2,1)S(1)}, u32[]{:S(2)}, u32[]{:S(2)}) collective-permute-start(bf16[68,1024]{1,0:T(8,128)(2,1)S(1)} %choose.1.refs_4_), channel_id=1, source_target_pairs={{0,4},{4,8},{8,12},{12,0},{1,5},{5,9},{9,13},{13,1},{2,6},{6,10},{... | collective-permute-start | bytes 417800 | tf_op jit(solution)/shard_map/ppermute | solution.py:25
  24.8 10.0 %collective-permute-start.1 = (bf16[68,1024]{1,0:T(8,128)(2,1)S(1)}, bf16[68,1024]{1,0:T(8,128)(2,1)S(1)}, u32[]{:S(2)}, u32[]{:S(2)}) collective-permute-start(bf16[68,1024]{1,0:T(8,128)(2,1)S(1)} %collective-permute-done.refs_1_), channel_id=1, source_target_pairs={{0,4},{4,8},{8,12},{12,0},{1,5},{5,9},{9,13},{13,1},{2,6},{6,10},{... | collective-permute-start | bytes 417800 | tf_op jit(solution)/shard_map/ppermute | solution.py:25
  24.9 14.8 %collective-permute-start.5 = (bf16[68,1024]{1,0:T(8,128)(2,1)S(1)}, bf16[68,1024]{1,0:T(8,128)(2,1)S(1)}, u32[]{:S(2)}, u32[]{:S(2)}) collective-permute-start(bf16[68,1024]{1,0:T(8,128)(2,1)S(1)} %choose.1.refs_4_), channel_id=1, source_target_pairs={{0,8},{4,12},{8,0},{12,4},{1,9},{5,13},{9,1},{13,5},{2,10},{6,14},... | collective-permute-start | bytes 417800 | tf_op jit(solution)/shard_map/ppermute | solution.py:25
  27.6 12.2 %collective-permute-start.6 = (bf16[68,1024]{1,0:T(8,128)(2,1)S(1)}, bf16[68,1024]{1,0:T(8,128)(2,1)S(1)}, u32[]{:S(2)}, u32[]{:S(2)}) collective-permute-start(bf16[68,1024]{1,0:T(8,128)(2,1)S(1)} %choose.1.refs_4_), channel_id=1, source_target_pairs={{0,12},{4,0},{8,4},{12,8},{1,13},{5,1},{9,5},{13,9},{2,14},{6,2},{... | collective-permute-start | bytes 417800 | tf_op jit(solution)/shard_map/ppermute | solution.py:25
  30.4 9.3 %copy-start.1 = (bf16[1,68,1024]{2,1,0:T(8,128)(2,1)S(1)}, bf16[1,68,1024]{2,1,0:T(8,128)(2,1)}, u32[]{:S(2)}) copy-start(bf16[1,68,1024]{2,1,0:T(8,128)(2,1)} %param.10) | copy-start | bytes 417796
  41.1 7.1 %collective-permute-start.7 = (bf16[152,256]{1,0:T(8,128)(2,1)S(1)}, bf16[152,256]{1,0:T(8,128)(2,1)S(1)}, u32[]{:S(2)}, u32[]{:S(2)}) collective-permute-start(bf16[152,256]{1,0:T(8,128)(2,1)S(1)} %get-tuple-element.27.refs_1_), channel_id=1, source_target_pairs={{0,4},{4,8},{8,12},{12,0},{1,5},{5,9},{9,13},{13,1},{2,6},{6,10},{... | collective-permute-start | bytes 233480 | tf_op jit(solution)/shard_map/ppermute | solution.py:25
  44.0 6.9 %collective-permute-start.8 = (bf16[152,256]{1,0:T(8,128)(2,1)S(1)}, bf16[152,256]{1,0:T(8,128)(2,1)S(1)}, u32[]{:S(2)}, u32[]{:S(2)}) collective-permute-start(bf16[152,256]{1,0:T(8,128)(2,1)S(1)} %get-tuple-element.27.refs_1_), channel_id=1, source_target_pairs={{0,8},{4,12},{8,0},{12,4},{1,9},{5,13},{9,1},{13,5},{2,10},{6,14},... | collective-permute-start | bytes 233480 | tf_op jit(solution)/shard_map/ppermute | solution.py:25
  45.5 5.4 %collective-permute-start.9 = (bf16[152,256]{1,0:T(8,128)(2,1)S(1)}, bf16[152,256]{1,0:T(8,128)(2,1)S(1)}, u32[]{:S(2)}, u32[]{:S(2)}) collective-permute-start(bf16[152,256]{1,0:T(8,128)(2,1)S(1)} %get-tuple-element.27.refs_1_), channel_id=1, source_target_pairs={{0,12},{4,0},{8,4},{12,8},{1,13},{5,1},{9,5},{13,9},{2,14},{6,2},{... | collective-permute-start | bytes 233480 | tf_op jit(solution)/shard_map/ppermute | solution.py:25
  52.6 5.9 %collective-permute-start.10 = (bf16[136,128]{1,0:T(8,128)(2,1)S(1)}, bf16[136,128]{1,0:T(8,128)(2,1)S(1)}, u32[]{:S(2)}, u32[]{:S(2)}) collective-permute-start(bf16[136,128]{1,0:T(8,128)(2,1)S(1)} %attend.2.refs_0_), channel_id=1, source_target_pairs={{0,4},{4,8},{8,12},{12,0},{1,5},{5,9},{9,13},{13,1},{2,6},{6,10},{... | collective-permute-start | bytes 104456 | tf_op jit(solution)/shard_map/ppermute | solution.py:25
  54.4 5.1 %collective-permute-start.11 = (bf16[136,128]{1,0:T(8,128)(2,1)S(1)}, bf16[136,128]{1,0:T(8,128)(2,1)S(1)}, u32[]{:S(2)}, u32[]{:S(2)}) collective-permute-start(bf16[136,128]{1,0:T(8,128)(2,1)S(1)} %attend.2.refs_0_), channel_id=1, source_target_pairs={{0,8},{4,12},{8,0},{12,4},{1,9},{5,13},{9,1},{13,5},{2,10},{6,14},... | collective-permute-start | bytes 104456 | tf_op jit(solution)/shard_map/ppermute | solution.py:25
  55.5 4.2 %collective-permute-start.12 = (bf16[136,128]{1,0:T(8,128)(2,1)S(1)}, bf16[136,128]{1,0:T(8,128)(2,1)S(1)}, u32[]{:S(2)}, u32[]{:S(2)}) collective-permute-start(bf16[136,128]{1,0:T(8,128)(2,1)S(1)} %attend.2.refs_0_), channel_id=1, source_target_pairs={{0,12},{4,0},{8,4},{12,8},{1,13},{5,1},{9,5},{13,9},{2,14},{6,2},{... | collective-permute-start | bytes 104456 | tf_op jit(solution)/shard_map/ppermute | solution.py:25
  60.1 5.9 %collective-permute-start.17 = (bf16[68,1024]{1,0:T(8,128)(2,1)S(1)}, bf16[68,1024]{1,0:T(8,128)(2,1)S(1)}, u32[]{:S(2)}, u32[]{:S(2)}) collective-permute-start(bf16[68,1024]{1,0:T(8,128)(2,1)S(1)} %get-tuple-element.34), channel_id=1, source_target_pairs={{0,2},{1,3},{2,0},{3,1},{4,6},{5,7},{6,4},{7,5},{8,10},{9,11},{10,... | collective-permute-start | bytes 417800 | tf_op jit(solution)/shard_map/ppermute | solution.py:25
  61.6 8.8 %collective-permute-start.27 = (bf16[68,1024]{1,0:T(8,128)(2,1)S(1)}, bf16[68,1024]{1,0:T(8,128)(2,1)S(1)}, u32[]{:S(2)}, u32[]{:S(2)}) collective-permute-start(bf16[68,1024]{1,0:T(8,128)(2,1)S(1)} %get-tuple-element.38), channel_id=1, source_target_pairs={{0,1},{1,2},{2,3},{3,0},{4,5},{5,6},{6,7},{7,4},{8,9},{9,10},{10,1... | collective-permute-start | bytes 417800 | tf_op jit(solution)/shard_map/ppermute | solution.py:25
  66.0 7.2 %collective-permute-start.18 = (bf16[68,1024]{1,0:T(8,128)(2,1)S(1)}, bf16[68,1024]{1,0:T(8,128)(2,1)S(1)}, u32[]{:S(2)}, u32[]{:S(2)}) collective-permute-start(bf16[68,1024]{1,0:T(8,128)(2,1)S(1)} %collective-permute-done.17.refs_0_.refs_5_), channel_id=1, source_target_pairs={{0,4},{4,8},{8,12},{12,0},{1,5},{5,9},{9,13},{13,1},{2,6},{6,10},{... | collective-permute-start | bytes 417800 | tf_op jit(solution)/shard_map/ppermute | solution.py:25
  67.2 10.6 %collective-permute-start.19 = (bf16[68,1024]{1,0:T(8,128)(2,1)S(1)}, bf16[68,1024]{1,0:T(8,128)(2,1)S(1)}, u32[]{:S(2)}, u32[]{:S(2)}) collective-permute-start(bf16[68,1024]{1,0:T(8,128)(2,1)S(1)} %collective-permute-done.17.refs_0_.refs_5_), channel_id=1, source_target_pairs={{0,8},{4,12},{8,0},{12,4},{1,9},{5,13},{9,1},{13,5},{2,10},{6,14},... | collective-permute-start | bytes 417800 | tf_op jit(solution)/shard_map/ppermute | solution.py:25
  69.4 8.4 %collective-permute-start.20 = (bf16[68,1024]{1,0:T(8,128)(2,1)S(1)}, bf16[68,1024]{1,0:T(8,128)(2,1)S(1)}, u32[]{:S(2)}, u32[]{:S(2)}) collective-permute-start(bf16[68,1024]{1,0:T(8,128)(2,1)S(1)} %collective-permute-done.17.refs_0_.refs_5_), channel_id=1, source_target_pairs={{0,12},{4,0},{8,4},{12,8},{1,13},{5,1},{9,5},{13,9},{2,14},{6,2},{... | collective-permute-start | bytes 417800 | tf_op jit(solution)/shard_map/ppermute | solution.py:25
  71.5 20.2 %collective-permute-start.28 = (bf16[68,1024]{1,0:T(8,128)(2,1)S(1)}, bf16[68,1024]{1,0:T(8,128)(2,1)S(1)}, u32[]{:S(2)}, u32[]{:S(2)}) collective-permute-start(bf16[68,1024]{1,0:T(8,128)(2,1)S(1)} %get-tuple-element.39), channel_id=1, source_target_pairs={{0,1},{1,2},{2,3},{4,5},{5,6},{6,7},{8,9},{9,10},{10,11},{12,13},{... | collective-permute-start | bytes 417800 | tf_op jit(solution)/shard_map/ppermute | solution.py:20
  78.7 5.9 %collective-permute-start.21 = (bf16[76,256]{1,0:T(8,128)(2,1)S(1)}, bf16[76,256]{1,0:T(8,128)(2,1)S(1)}, u32[]{:S(2)}, u32[]{:S(2)}) collective-permute-start(bf16[76,256]{1,0:T(8,128)(2,1)S(1)} %get-tuple-element.36.refs_1_), channel_id=1, source_target_pairs={{0,4},{4,8},{8,12},{12,0},{1,5},{5,9},{9,13},{13,1},{2,6},{6,10},{... | collective-permute-start | bytes 116744 | tf_op jit(solution)/shard_map/ppermute | solution.py:25
  80.9 4.9 %collective-permute-start.22 = (bf16[76,256]{1,0:T(8,128)(2,1)S(1)}, bf16[76,256]{1,0:T(8,128)(2,1)S(1)}, u32[]{:S(2)}, u32[]{:S(2)}) collective-permute-start(bf16[76,256]{1,0:T(8,128)(2,1)S(1)} %get-tuple-element.36.refs_1_), channel_id=1, source_target_pairs={{0,8},{4,12},{8,0},{12,4},{1,9},{5,13},{9,1},{13,5},{2,10},{6,14},... | collective-permute-start | bytes 116744 | tf_op jit(solution)/shard_map/ppermute | solution.py:25
  81.9 4.3 %collective-permute-start.23 = (bf16[76,256]{1,0:T(8,128)(2,1)S(1)}, bf16[76,256]{1,0:T(8,128)(2,1)S(1)}, u32[]{:S(2)}, u32[]{:S(2)}) collective-permute-start(bf16[76,256]{1,0:T(8,128)(2,1)S(1)} %get-tuple-element.36.refs_1_), channel_id=1, source_target_pairs={{0,12},{4,0},{8,4},{12,8},{1,13},{5,1},{9,5},{13,9},{2,14},{6,2},{... | collective-permute-start | bytes 116744 | tf_op jit(solution)/shard_map/ppermute | solution.py:25
  87.1 5.6 %collective-permute-start.24 = (bf16[68,128]{1,0:T(8,128)(2,1)S(1)}, bf16[68,128]{1,0:T(8,128)(2,1)S(1)}, u32[]{:S(2)}, u32[]{:S(2)}) collective-permute-start(bf16[68,128]{1,0:T(8,128)(2,1)S(1)} %attend.3.refs_0_), channel_id=1, source_target_pairs={{0,4},{4,8},{8,12},{12,0},{1,5},{5,9},{9,13},{13,1},{2,6},{6,10},{... | collective-permute-start | bytes 52232 | tf_op jit(solution)/shard_map/ppermute | solution.py:25
  88.1 4.8 %collective-permute-start.25 = (bf16[68,128]{1,0:T(8,128)(2,1)S(1)}, bf16[68,128]{1,0:T(8,128)(2,1)S(1)}, u32[]{:S(2)}, u32[]{:S(2)}) collective-permute-start(bf16[68,128]{1,0:T(8,128)(2,1)S(1)} %attend.3.refs_0_), channel_id=1, source_target_pairs={{0,8},{4,12},{8,0},{12,4},{1,9},{5,13},{9,1},{13,5},{2,10},{6,14},... | collective-permute-start | bytes 52232 | tf_op jit(solution)/shard_map/ppermute | solution.py:25
  90.8 3.8 %collective-permute-start.26 = (bf16[68,128]{1,0:T(8,128)(2,1)S(1)}, bf16[68,128]{1,0:T(8,128)(2,1)S(1)}, u32[]{:S(2)}, u32[]{:S(2)}) collective-permute-start(bf16[68,128]{1,0:T(8,128)(2,1)S(1)} %attend.3.refs_0_), channel_id=1, source_target_pairs={{0,12},{4,0},{8,4},{12,8},{1,13},{5,1},{9,5},{13,9},{2,14},{6,2},{... | collective-permute-start | bytes 52232 | tf_op jit(solution)/shard_map/ppermute | solution.py:25

commit v5 on v4

--- a/solution.py
+++ b/solution.py
@@ -133,10 +133,11 @@
 
 def project_kernel(count, span, batch, *refs):
     parts = refs[: batch * count]
-    gain_ref, wq_ref, wkv_ref, query_ref, message_ref = refs[batch * count :]
+    gain_ref, wq_ref, wkv_ref, query_ref, same_ref, other_ref = refs[batch * count :]
+    odd = lax.rem(lax.axis_index("tensor"), 2) == 1
+    head = wq_ref.shape[1]
     rows, shard = parts[0].shape
-    block = message_ref.shape[0] // batch
-    last = block - (rows - span)
+    block = same_ref.shape[0] // batch
     for b in range(batch):
         own = parts[b * count : (b + 1) * count]
         total = jnp.zeros((rows, 1), F32)
@@ -153,8 +154,14 @@
             keyval = keyval + jnp.dot(normed, wkv_ref[here, :], preferred_element_type=F32)
         queries = queries.astype(BF16)
         query_ref[b] = queries[:span]
-        message_ref[b * block : b * block + rows] = keyval.astype(BF16)
-        message_ref[b * block + last : (b + 1) * block, : queries.shape[1]] = queries[span:]
+        even_half, odd_half = keyval[:, :head], keyval[:, head:]
+        for message_ref, is_odd in ((same_ref, odd), (other_ref, jnp.logical_not(odd))):
+            message_ref[b * block : b * block + span] = jnp.where(
+                is_odd, odd_half[:span], even_half[:span]
+            ).astype(BF16)
+            for n, rest in enumerate((even_half, odd_half, queries)):
+                first = b * block + span + 8 * n
+                message_ref[first : first + rows - span] = rest[span:].astype(BF16)
 
 
 def attend_kernel(count, span, ticks, *refs):
@@ -166,11 +173,8 @@
     factor = 1.0 / math.sqrt(head)
     heads = count
     block = parts[0].shape[0] // len(ticks)
-    last = block - count
     for k, part in enumerate(parts):
-        owner = owner_of(k, count)
-        blocks[2 * owner] = part[:, :head]
-        blocks[2 * owner + 1] = part[:, head:]
+        blocks[owner_of(k, count)] = part[...]
     small[...] = jnp.zeros_like(small)
     row_ids = lax.broadcasted_iota(jnp.int32, (span, span), 0)
     col_ids = lax.broadcasted_iota(jnp.int32, (span, span), 1)
@@ -183,8 +187,8 @@
         micro = tick - lax.axis_index("section") + lax.axis_size("section") - 1
         first = b * block
         out = b * (span + count)
-        keys = blocks[me, first : first + span]
-        values = blocks[heads + me, first : first + span]
+        keys = blocks[lax.div(me, 2), first : first + span]
+        values = blocks[heads // 2 + lax.div(me, 2), first : first + span]
         scores = (
             lax.dot_general(
                 query_ref[b], keys, (((1,), (1,)), ((), ())), preferred_element_type=F32
@@ -199,11 +203,15 @@
         out_ref[out : out + span] = jnp.dot(
             weights, values, preferred_element_type=F32
         ).astype(BF16)
-        new = slice(first + span, first + span + count)
+
+        def new_row(device, n):
+            start = first + span + 8 * n
+            return own_row(blocks[device, start : start + count])
+
         for h in range(heads):
-            small[b, 0, h : h + 1, :] = own_row(blocks[2 * h, first + last : first + block])
-            small[b, 1, h : h + 1, :] = own_row(blocks[h, new])
-            small[b, 2, h : h + 1, :] = own_row(blocks[heads + h, new])
+            small[b, 0, h : h + 1, :] = new_row(h, 2)
+            small[b, 1, h : h + 1, :] = new_row(h // 2, h % 2)
+            small[b, 2, h : h + 1, :] = new_row((heads + h) // 2, h % 2)
         queries = small[b, 0]
         line = lax.broadcasted_iota(jnp.int32, queries.shape, 0)
         spread = jnp.concatenate(
@@ -318,7 +326,7 @@
     half = head // 2
     cached = cache.reshape(ticks, length, cache.shape[4])
     padded = (rows + 7) // 8 * 8
-    message_rows = padded + count
+    message_rows = span + 24
     limit = pltpu.CompilerParams(vmem_limit_bytes=16 * 1024 * 1024)
     block = jax.ShapeDtypeStruct((rows, shard), BF16)
     history = jax.ShapeDtypeStruct((ticks, rows, shard), BF16)
@@ -348,10 +356,11 @@
             functools.partial(project_kernel, count, span, batch),
             out_shape=(
                 jax.ShapeDtypeStruct((batch, span, head), BF16),
-                jax.ShapeDtypeStruct((batch * message_rows, 2 * head), BF16),
+                jax.ShapeDtypeStruct((batch * message_rows, head), BF16),
+                jax.ShapeDtypeStruct((batch * message_rows, head), BF16),
             ),
             in_specs=[VMEM] * (batch * count + 3),
-            out_specs=(VMEM, VMEM),
+            out_specs=(VMEM, VMEM, VMEM),
             compiler_params=limit,
             cost_estimate=cost(
                 2 * batch * rows * shard * count * 3 * head,
@@ -368,7 +377,7 @@
             in_specs=[VMEM] * (count + 4),
             out_specs=VMEM,
             scratch_shapes=[
-                pltpu.VMEM((2 * count, batch * message_rows, head), BF16),
+                pltpu.VMEM((count, batch * message_rows, head), BF16),
                 pltpu.VMEM((batch, 4, 8, head), F32),
             ],
             compiler_params=limit,
@@ -378,6 +387,10 @@
             ),
             name="attend",
         )(queries, *[in_vmem(part) for part in parts], segments, lengths, cached)
+
+    def message_pieces(same, other):
+        kinds = [same if k % 2 == 0 else other for k in range(count)]
+        return [same] + [turned(kinds[k], "tensor", k) for k in range(1, count)]
 
     output_scratch = [
         pltpu.VMEM((count, padded, head), BF16),
@@ -406,8 +419,8 @@
         name="choose",
     )(early, moved(first_new, "section", 1))
     second_parts = pieces_of(second, "tensor")
-    queries, message = project(stream_parts + second_parts)
-    message_parts = pieces_of(message, "tensor")
+    queries, same, other_half = project(stream_parts + second_parts)
+    message_parts = message_pieces(same, other_half)
     small_block = jax.ShapeDtypeStruct((half, shard), BF16)
     cut = pl.pallas_call(
         functools.partial(cut_kernel, count),
@@ -484,8 +497,8 @@
         in_vmem(second_new),
     )
     pend_last_in = moved(pend_second, "section", 1)
-    queries, message = project(third_parts)
-    message_parts = pieces_of(message, "tensor")
+    queries, same, other_half = project(third_parts)
+    message_parts = message_pieces(same, other_half)
     attended = attend(queries, message_parts, (2,))
     attended_parts = pieces_of(attended, "tensor")
     hist_stream, hist_pend = pl.pallas_call(
@@ -647,7 +660,6 @@
     fits = (
         head == 128
         and lax.axis_size("group") == 2
-        and count <= 8
         and cache.shape[1] == 3
         and cache.shape[2] == 1
         and cache.shape[4] == 2 * head * count
@@ -655,6 +667,7 @@
         and stream_in.shape[2] % 128 == 0
         and span_seg.shape[1] % 16 == 0
         and stream_in.shape[1] == span_seg.shape[1] + count
+        and count == 4
     )
     chosen = fast_body if fits else plain_body
     return chosen(

time: 95.8 us -> 94.2 us (0.983)
  waiting for transfers between devices: 31.8 us -> 30.4 us
    ppermute x27, waiting for transfers between devices: 31.8 us -> 30.4 us  [turned(): lax.ppermute(block, axis, [(i, (i + distance) % count) for i in range(cou...]
where the time goes in v5:
time: 94.2 us; the launch traced here: 94 us
  starting transfers between devices  48.1 us (51%)
  waiting for transfers between devices  30.4 us (32%)
  Pallas kernels  12.3 us (13%)
  local copies, waits for them, and re-layouts  2.35 us (2%)
    ppermute x27, starting transfers between devices, turned(): lax.ppermute(block, axis, [(i, (i + distance) % count) for i in range(cou...  45.5 us
    ppermute x27, waiting for transfers between devices, turned(): lax.ppermute(block, axis, [(i, (i + distance) % count) for i in range(cou...  30.4 us
    pallas_call x1, Pallas kernels, fast_body(): pl.pallas_call(functools.partial(load_kernel, pieces), out_shape=tuple((j...  2.73 us
    ppermute x2, starting transfers between devices, moved(): return lax.ppermute(block, axis, route)  2.6 us
    pallas_call x2, Pallas kernels, attend(): pl.pallas_call(functools.partial(attend_kernel, count, span, which), out_...  2.54 us
    pallas_call x2, Pallas kernels, project(): pl.pallas_call(functools.partial(project_kernel, count, span, batch), out...  2.15 us
    unnamed x10, local copies, waits for them, and re-layouts  1.96 us
  transfers between devices with their start and end apart: 29, of which 18 were waited for; matrix products, arithmetic and copies ran while one was open for 1% of the time, Pallas kernels for 10%

profile of v5, /device:TPU:0, one launch (start us, length us, event | category | flops | bytes accessed | tf_op | source)
XLA Modules:
  0.0 94.0 jit_solution(9983371745238079909)
XLA Ops:
  0.6 1.1 %cut.1 = (bf16[64,1024]{1,0:T(8,128)(2,1)S(1)}, bf16[64,1024]{1,0:T(8,128)(2,1)S(1)}, bf16[64,1024]{1,0:T(8,128)(2,1)S(1)}) custom-call(bf16[128,4096]{1,0:T(8,128)(2,1)} %bitcast.23), custom_call_target="tpu_custom_call" | custom-call | tf_op jit(solution)/shard_map/cut/pallas_call | solution.py:425
  1.8 3.1 %collective-permute-start.13 = (bf16[64,1024]{1,0:T(8,128)(2,1)S(1)}, bf16[64,1024]{1,0:T(8,128)(2,1)S(1)}, u32[]{:S(2)}, u32[]{:S(2)}) collective-permute-start(bf16[64,1024]{1,0:T(8,128)(2,1)S(1)} %get-tuple-element.34), channel_id=1, source_target_pairs={{0,4},{4,8},{8,12},{12,0},{1,5},{5,9},{9,13},{13,1},{2,6},{6,10},{... | collective-permute-start | bytes 393224 | tf_op jit(solution)/shard_map/ppermute | solution.py:25
  4.8 2.6 %collective-permute-start.14 = (bf16[64,1024]{1,0:T(8,128)(2,1)S(1)}, bf16[64,1024]{1,0:T(8,128)(2,1)S(1)}, u32[]{:S(2)}, u32[]{:S(2)}) collective-permute-start(bf16[64,1024]{1,0:T(8,128)(2,1)S(1)} %get-tuple-element.35), channel_id=1, source_target_pairs={{0,8},{4,12},{8,0},{12,4},{1,9},{5,13},{9,1},{13,5},{2,10},{6,14},... | collective-permute-start | bytes 393224 | tf_op jit(solution)/shard_map/ppermute | solution.py:25
  7.4 1.3 %collective-permute-start.15 = (bf16[64,1024]{1,0:T(8,128)(2,1)S(1)}, bf16[64,1024]{1,0:T(8,128)(2,1)S(1)}, u32[]{:S(2)}, u32[]{:S(2)}) collective-permute-start(bf16[64,1024]{1,0:T(8,128)(2,1)S(1)} %get-tuple-element.36), channel_id=1, source_target_pairs={{0,12},{4,0},{8,4},{12,8},{1,13},{5,1},{9,5},{13,9},{2,14},{6,2},{... | collective-permute-start | bytes 393224 | tf_op jit(solution)/shard_map/ppermute | solution.py:25
  9.5 3.1 %collective-permute-start.2 = (bf16[68,1024]{1,0:T(8,128)(2,1)}, bf16[68,1024]{1,0:T(8,128)(2,1)S(1)}, u32[]{:S(2)}, u32[]{:S(2)}) collective-permute-start(bf16[68,1024]{1,0:T(8,128)(2,1)} %bitcast.18), channel_id=1, source_target_pairs={{0,12},{4,0},{8,4},{12,8},{1,13},{5,1},{9,5},{13,9},{2,14},{6,2},{... | collective-permute-start | bytes 417800 | tf_op jit(solution)/shard_map/ppermute | solution.py:25
  12.6 0.9 %copy-done = bf16[1,68,1024]{2,1,0:T(8,128)(2,1)S(1)} copy-done((bf16[1,68,1024]{2,1,0:T(8,128)(2,1)S(1)}, bf16[1,68,1024]{2,1,0:T(8,128)(2,1)}, u32[]{:S(2)}) %copy-start) | copy-done | bytes 139288
  13.5 0.9 copy-done.2
  14.5 1.3 %collective-permute-start.3 = (bf16[68,1024]{1,0:T(8,128)(2,1)S(1)}, bf16[68,1024]{1,0:T(8,128)(2,1)S(1)}, u32[]{:S(2)}, u32[]{:S(2)}) collective-permute-start(bf16[68,1024]{1,0:T(8,128)(2,1)S(1)} %begin.1.refs_5_), channel_id=1, source_target_pairs={{0,1},{1,2},{2,3},{4,5},{5,6},{6,7},{8,9},{9,10},{10,11},{12,13},{... | collective-permute-start | bytes 417800 | tf_op jit(solution)/shard_map/ppermute | solution.py:20
  15.8 1.1 %collective-permute-done.14.refs_1_.refs_2_ = bf16[64,1024]{1,0:T(8,128)(2,1)S(1)} collective-permute-done((bf16[64,1024]{1,0:T(8,128)(2,1)S(1)}, bf16[64,1024]{1,0:T(8,128)(2,1)S(1)}, u32[]{:S(2)}, u32[]{:S(2)}) %collective-permute-start.14) | collective-permute-done | bytes 131104 | tf_op jit(solution)/shard_map/ppermute | solution.py:25
  17.0 2.8 %collective-permute-done.15.refs_2_.refs_3_ = bf16[64,1024]{1,0:T(8,128)(2,1)S(1)} collective-permute-done((bf16[64,1024]{1,0:T(8,128)(2,1)S(1)}, bf16[64,1024]{1,0:T(8,128)(2,1)S(1)}, u32[]{:S(2)}, u32[]{:S(2)}) %collective-permute-start.15) | collective-permute-done | bytes 131104 | tf_op jit(solution)/shard_map/ppermute | solution.py:25
  19.7 1.6 %collective-permute-start.16 = (bf16[3,64,1024]{2,1,0:T(8,128)(2,1)S(1)}, bf16[3,64,1024]{2,1,0:T(8,128)(2,1)S(1)}, u32[]{:S(2)}, u32[]{:S(2)}) collective-permute-start(bf16[3,64,1024]{2,1,0:T(8,128)(2,1)S(1)} %stack.1), channel_id=1, source_target_pairs={{0,16},{16,0},{1,17},{17,1},{2,18},{18,2},{3,19},{19,3},{4,20},{20... | collective-permute-start | bytes 1179656 | tf_op jit(solution)/shard_map/ppermute | solution.py:25
  21.9 3.0 %collective-permute-start.4 = (bf16[68,1024]{1,0:T(8,128)(2,1)S(1)}, bf16[68,1024]{1,0:T(8,128)(2,1)S(1)}, u32[]{:S(2)}, u32[]{:S(2)}) collective-permute-start(bf16[68,1024]{1,0:T(8,128)(2,1)S(1)} %choose.1.refs_4_), channel_id=1, source_target_pairs={{0,4},{4,8},{8,12},{12,0},{1,5},{5,9},{9,13},{13,1},{2,6},{6,10},{... | collective-permute-start | bytes 417800 | tf_op jit(solution)/shard_map/ppermute | solution.py:25
  24.9 2.7 %collective-permute-start.5 = (bf16[68,1024]{1,0:T(8,128)(2,1)S(1)}, bf16[68,1024]{1,0:T(8,128)(2,1)S(1)}, u32[]{:S(2)}, u32[]{:S(2)}) collective-permute-start(bf16[68,1024]{1,0:T(8,128)(2,1)S(1)} %choose.1.refs_4_), channel_id=1, source_target_pairs={{0,8},{4,12},{8,0},{12,4},{1,9},{5,13},{9,1},{13,5},{2,10},{6,14},... | collective-permute-start | bytes 417800 | tf_op jit(solution)/shard_map/ppermute | solution.py:25
  27.6 2.9 %collective-permute-start.6 = (bf16[68,1024]{1,0:T(8,128)(2,1)S(1)}, bf16[68,1024]{1,0:T(8,128)(2,1)S(1)}, u32[]{:S(2)}, u32[]{:S(2)}) collective-permute-start(bf16[68,1024]{1,0:T(8,128)(2,1)S(1)} %choose.1.refs_4_), channel_id=1, source_target_pairs={{0,12},{4,0},{8,4},{12,8},{1,13},{5,1},{9,5},{13,9},{2,14},{6,2},{... | collective-permute-start | bytes 417800 | tf_op jit(solution)/shard_map/ppermute | solution.py:25
  30.4 2.7 %load.1 = (f32[1,4096]{1,0:T(1,128)S(1)}, bf16[4096,128]{1,0:T(8,128)(2,1)S(1)}, bf16[4096,256]{1,0:T(8,128)(2,1)S(1)}, s32[6,64]{1,0:T(8,128)S(1)}, s32[1,6]{1,...) custom-call(f32[1,4096]{1,0:T(1,128)} %refs_0_.1, bf16[4096,128]{1,0:T(8,128)(2,1)} %bitcast.27, bf16[4096,256]{1,0:T(8,128)(2,1)} %bitcast.26, ...), custom_call_target="tpu_custom_call" | custom-call | tf_op jit(solution)/shard_map/load/pallas_call | solution.py:341
  33.2 1.7 %collective-permute-done.1.refs_2_ = bf16[68,1024]{1,0:T(8,128)(2,1)S(1)} collective-permute-done((bf16[68,1024]{1,0:T(8,128)(2,1)S(1)}, bf16[68,1024]{1,0:T(8,128)(2,1)S(1)}, u32[]{:S(2)}, u32[]{:S(2)}) %collective-permute-start.1) | collective-permute-done | bytes 139296 | tf_op jit(solution)/shard_map/ppermute | solution.py:25
  34.8 4.9 %collective-permute-done.5.refs_6_ = bf16[68,1024]{1,0:T(8,128)(2,1)S(1)} collective-permute-done((bf16[68,1024]{1,0:T(8,128)(2,1)S(1)}, bf16[68,1024]{1,0:T(8,128)(2,1)S(1)}, u32[]{:S(2)}, u32[]{:S(2)}) %collective-permute-start.5) | collective-permute-done | bytes 139296 | tf_op jit(solution)/shard_map/ppermute | solution.py:25
  39.7 1.3 %project.2 = (bf16[2,64,128]{2,1,0:T(8,128)(2,1)S(1)}, bf16[176,128]{1,0:T(8,128)(2,1)S(1)}, bf16[176,128]{1,0:T(8,128)(2,1)S(1)}) custom-call(bf16[68,1024]{1,0:T(8,128)(2,1)S(1)} %bitcast.20, bf16[68,1024]{1,0:T(8,128)(2,1)S(1)} %collective-permute-done.refs_1_, bf16[68,1024]{1,0:T(8,128)(2,1)S(1)} %collective-permute-done.1.refs_2_, ...), custom_call_target="tpu_custom_call" | custom-call | tf_op jit(solution)/shard_map/project/pallas_call | solution.py:355
  41.1 2.9 %collective-permute-start.7 = (bf16[176,128]{1,0:T(8,128)(2,1)S(1)}, bf16[176,128]{1,0:T(8,128)(2,1)S(1)}, u32[]{:S(2)}, u32[]{:S(2)}) collective-permute-start(bf16[176,128]{1,0:T(8,128)(2,1)S(1)} %get-tuple-element.30), channel_id=1, source_target_pairs={{0,4},{4,8},{8,12},{12,0},{1,5},{5,9},{9,13},{13,1},{2,6},{6,10},{... | collective-permute-start | bytes 135176 | tf_op jit(solution)/shard_map/ppermute | solution.py:25
  43.9 1.5 %collective-permute-start.8 = (bf16[176,128]{1,0:T(8,128)(2,1)S(1)}, bf16[176,128]{1,0:T(8,128)(2,1)S(1)}, u32[]{:S(2)}, u32[]{:S(2)}) collective-permute-start(bf16[176,128]{1,0:T(8,128)(2,1)S(1)} %get-tuple-element.29.refs_1_), channel_id=1, source_target_pairs={{0,8},{4,12},{8,0},{12,4},{1,9},{5,13},{9,1},{13,5},{2,10},{6,14},... | collective-permute-start | bytes 135176 | tf_op jit(solution)/shard_map/ppermute | solution.py:25
  45.4 1.0 %collective-permute-start.9 = (bf16[176,128]{1,0:T(8,128)(2,1)S(1)}, bf16[176,128]{1,0:T(8,128)(2,1)S(1)}, u32[]{:S(2)}, u32[]{:S(2)}) collective-permute-start(bf16[176,128]{1,0:T(8,128)(2,1)S(1)} %get-tuple-element.30), channel_id=1, source_target_pairs={{0,12},{4,0},{8,4},{12,8},{1,13},{5,1},{9,5},{13,9},{2,14},{6,2},{... | collective-permute-start | bytes 135176 | tf_op jit(solution)/shard_map/ppermute | solution.py:25
  46.4 0.9 collective-permute-done.7.refs_2_
  47.3 1.8 %collective-permute-done.8.refs_3_ = bf16[176,128]{1,0:T(8,128)(2,1)S(1)} collective-permute-done((bf16[176,128]{1,0:T(8,128)(2,1)S(1)}, bf16[176,128]{1,0:T(8,128)(2,1)S(1)}, u32[]{:S(2)}, u32[]{:S(2)}) %collective-permute-start.8) | collective-permute-done | bytes 45088 | tf_op jit(solution)/shard_map/ppermute | solution.py:25
  49.6 1.6 %attend.2.refs_0_ = bf16[136,128]{1,0:T(8,128)(2,1)S(1)} custom-call(bf16[2,64,128]{2,1,0:T(8,128)(2,1)S(1)} %get-tuple-element.28.refs_0_, bf16[176,128]{1,0:T(8,128)(2,1)S(1)} %get-tuple-element.29.refs_1_, bf16[176,128]{1,0:T(8,128)(2,1)S(1)} %collective-permute-done.7.refs_2_, bf16[176,128]{1,0:T(8,128)(2,1)S(1)} %collective-permute-done.8.refs_3_, ...), custom_call_target="tpu_custom_call" | custom-call | tf_op jit(solution)/shard_map/attend/pallas_call | solution.py:374
  51.8 2.7 %collective-permute-start.11 = (bf16[136,128]{1,0:T(8,128)(2,1)S(1)}, bf16[136,128]{1,0:T(8,128)(2,1)S(1)}, u32[]{:S(2)}, u32[]{:S(2)}) collective-permute-start(bf16[136,128]{1,0:T(8,128)(2,1)S(1)} %attend.2.refs_0_), channel_id=1, source_target_pairs={{0,8},{4,12},{8,0},{12,4},{1,9},{5,13},{9,1},{13,5},{2,10},{6,14},... | collective-permute-start | bytes 104456 | tf_op jit(solution)/shard_map/ppermute | solution.py:25
  54.5 1.0 %collective-permute-start.12 = (bf16[136,128]{1,0:T(8,128)(2,1)S(1)}, bf16[136,128]{1,0:T(8,128)(2,1)S(1)}, u32[]{:S(2)}, u32[]{:S(2)}) collective-permute-start(bf16[136,128]{1,0:T(8,128)(2,1)S(1)} %attend.2.refs_0_), channel_id=1, source_target_pairs={{0,12},{4,0},{8,4},{12,8},{1,13},{5,1},{9,5},{13,9},{2,14},{6,2},{... | collective-permute-start | bytes 104456 | tf_op jit(solution)/shard_map/ppermute | solution.py:25
  55.6 1.1 %place.1.refs_4_ = bf16[4,128,1024]{2,1,0:T(8,128)(2,1)S(1)} custom-call(bf16[128,4096]{1,0:T(8,128)(2,1)} %bitcast.24, bf16[64,1024]{1,0:T(8,128)(2,1)S(1)} %collective-permute-done.13.refs_0_.refs_1_, bf16[64,1024]{1,0:T(8,128)(2,1)S(1)} %collective-permute-done.14.refs_1_.refs_2_, bf16[64,1024]{1,0:T(8,128)(2,1)S(1)} %collective-permute-done.15.refs_2_.refs_3_, ...), custom_call_target="tpu_custom_call" | custom-call | tf_op jit(solution)/shard_map/place/pallas_call | solution.py:451
  57.1 1.4 %collective-permute-done.12.refs_3_ = bf16[136,128]{1,0:T(8,128)(2,1)S(1)} collective-permute-done((bf16[136,128]{1,0:T(8,128)(2,1)S(1)}, bf16[136,128]{1,0:T(8,128)(2,1)S(1)}, u32[]{:S(2)}, u32[]{:S(2)}) %collective-permute-start.12) | collective-permute-done | bytes 34848 | tf_op jit(solution)/shard_map/ppermute | solution.py:25
  58.8 1.6 %collective-permute-start.17 = (bf16[68,1024]{1,0:T(8,128)(2,1)S(1)}, bf16[68,1024]{1,0:T(8,128)(2,1)S(1)}, u32[]{:S(2)}, u32[]{:S(2)}) collective-permute-start(bf16[68,1024]{1,0:T(8,128)(2,1)S(1)} %get-tuple-element.37), channel_id=1, source_target_pairs={{0,2},{1,3},{2,0},{3,1},{4,6},{5,7},{6,4},{7,5},{8,10},{9,11},{10,... | collective-permute-start | bytes 417800 | tf_op jit(solution)/shard_map/ppermute | solution.py:25
  60.4 4.3 %collective-permute-done.17.refs_0_.refs_5_ = bf16[68,1024]{1,0:T(8,128)(2,1)S(1)} collective-permute-done((bf16[68,1024]{1,0:T(8,128)(2,1)S(1)}, bf16[68,1024]{1,0:T(8,128)(2,1)S(1)}, u32[]{:S(2)}, u32[]{:S(2)}) %collective-permute-start.17) | collective-permute-done | bytes 139296 | tf_op jit(solution)/shard_map/ppermute | solution.py:25
  64.7 1.2 %collective-permute-start.18 = (bf16[68,1024]{1,0:T(8,128)(2,1)S(1)}, bf16[68,1024]{1,0:T(8,128)(2,1)S(1)}, u32[]{:S(2)}, u32[]{:S(2)}) collective-permute-start(bf16[68,1024]{1,0:T(8,128)(2,1)S(1)} %collective-permute-done.17.refs_0_.refs_5_), channel_id=1, source_target_pairs={{0,4},{4,8},{8,12},{12,0},{1,5},{5,9},{9,13},{13,1},{2,6},{6,10},{... | collective-permute-start | bytes 417800 | tf_op jit(solution)/shard_map/ppermute | solution.py:25
  65.9 2.3 %collective-permute-start.19 = (bf16[68,1024]{1,0:T(8,128)(2,1)S(1)}, bf16[68,1024]{1,0:T(8,128)(2,1)S(1)}, u32[]{:S(2)}, u32[]{:S(2)}) collective-permute-start(bf16[68,1024]{1,0:T(8,128)(2,1)S(1)} %collective-permute-done.17.refs_0_.refs_5_), channel_id=1, source_target_pairs={{0,8},{4,12},{8,0},{12,4},{1,9},{5,13},{9,1},{13,5},{2,10},{6,14},... | collective-permute-start | bytes 417800 | tf_op jit(solution)/shard_map/ppermute | solution.py:25
  68.6 1.1 %output_second.1 = (bf16[68,1024]{1,0:T(8,128)(2,1)S(1)}, bf16[3,68,1024]{2,1,0:T(8,128)(2,1)}, bf16[3,68,1024]{2,1,0:T(8,128)(2,1)}) custom-call(bf16[136,128]{1,0:T(8,128)(2,1)S(1)} %attend.2.refs_0_, bf16[136,128]{1,0:T(8,128)(2,1)S(1)} %collective-permute-done.10.refs_1_, bf16[136,128]{1,0:T(8,128)(2,1)S(1)} %collective-permute-done.11.refs_2_, ...), custom_call_target="tpu_custom_call" | custom-call | tf_op jit(solution)/shard_map/output_second/pallas_call | solution.py:483
  69.7 1.3 %collective-permute-start.28 = (bf16[68,1024]{1,0:T(8,128)(2,1)S(1)}, bf16[68,1024]{1,0:T(8,128)(2,1)S(1)}, u32[]{:S(2)}, u32[]{:S(2)}) collective-permute-start(bf16[68,1024]{1,0:T(8,128)(2,1)S(1)} %get-tuple-element.43), channel_id=1, source_target_pairs={{0,1},{1,2},{2,3},{4,5},{5,6},{6,7},{8,9},{9,10},{10,11},{12,13},{... | collective-permute-start | bytes 417800 | tf_op jit(solution)/shard_map/ppermute | solution.py:20
  71.0 0.9 collective-permute-done.18.refs_1_
  71.9 4.6 %collective-permute-done.19.refs_2_ = bf16[68,1024]{1,0:T(8,128)(2,1)S(1)} collective-permute-done((bf16[68,1024]{1,0:T(8,128)(2,1)S(1)}, bf16[68,1024]{1,0:T(8,128)(2,1)S(1)}, u32[]{:S(2)}, u32[]{:S(2)}) %collective-permute-start.19) | collective-permute-done | bytes 139296 | tf_op jit(solution)/shard_map/ppermute | solution.py:25
  77.3 2.2 %collective-permute-start.21 = (bf16[88,128]{1,0:T(8,128)(2,1)S(1)}, bf16[88,128]{1,0:T(8,128)(2,1)S(1)}, u32[]{:S(2)}, u32[]{:S(2)}) collective-permute-start(bf16[88,128]{1,0:T(8,128)(2,1)S(1)} %get-tuple-element.40), channel_id=1, source_target_pairs={{0,4},{4,8},{8,12},{12,0},{1,5},{5,9},{9,13},{13,1},{2,6},{6,10},{... | collective-permute-start | bytes 67592 | tf_op jit(solution)/shard_map/ppermute | solution.py:25
  79.5 1.1 %collective-permute-start.22 = (bf16[88,128]{1,0:T(8,128)(2,1)S(1)}, bf16[88,128]{1,0:T(8,128)(2,1)S(1)}, u32[]{:S(2)}, u32[]{:S(2)}) collective-permute-start(bf16[88,128]{1,0:T(8,128)(2,1)S(1)} %get-tuple-element.39.refs_1_), channel_id=1, source_target_pairs={{0,8},{4,12},{8,0},{12,4},{1,9},{5,13},{9,1},{13,5},{2,10},{6,14},... | collective-permute-start | bytes 67592 | tf_op jit(solution)/shard_map/ppermute | solution.py:25
  80.6 1.3 %collective-permute-start.23 = (bf16[88,128]{1,0:T(8,128)(2,1)S(1)}, bf16[88,128]{1,0:T(8,128)(2,1)S(1)}, u32[]{:S(2)}, u32[]{:S(2)}) collective-permute-start(bf16[88,128]{1,0:T(8,128)(2,1)S(1)} %get-tuple-element.40), channel_id=1, source_target_pairs={{0,12},{4,0},{8,4},{12,8},{1,13},{5,1},{9,5},{13,9},{2,14},{6,2},{... | collective-permute-start | bytes 67592 | tf_op jit(solution)/shard_map/ppermute | solution.py:25
  81.9 1.0 %collective-permute-done.21.refs_2_ = bf16[88,128]{1,0:T(8,128)(2,1)S(1)} collective-permute-done((bf16[88,128]{1,0:T(8,128)(2,1)S(1)}, bf16[88,128]{1,0:T(8,128)(2,1)S(1)}, u32[]{:S(2)}, u32[]{:S(2)}) %collective-permute-start.21) | collective-permute-done | bytes 22560 | tf_op jit(solution)/shard_map/ppermute | solution.py:25
  83.0 1.2 %collective-permute-done.22.refs_3_ = bf16[88,128]{1,0:T(8,128)(2,1)S(1)} collective-permute-done((bf16[88,128]{1,0:T(8,128)(2,1)S(1)}, bf16[88,128]{1,0:T(8,128)(2,1)S(1)}, u32[]{:S(2)}, u32[]{:S(2)}) %collective-permute-start.22) | collective-permute-done | bytes 22560 | tf_op jit(solution)/shard_map/ppermute | solution.py:25
  84.4 0.9 attend.3.refs_0_
  85.3 1.2 %collective-permute-start.24 = (bf16[68,128]{1,0:T(8,128)(2,1)S(1)}, bf16[68,128]{1,0:T(8,128)(2,1)S(1)}, u32[]{:S(2)}, u32[]{:S(2)}) collective-permute-start(bf16[68,128]{1,0:T(8,128)(2,1)S(1)} %attend.3.refs_0_), channel_id=1, source_target_pairs={{0,4},{4,8},{8,12},{12,0},{1,5},{5,9},{9,13},{13,1},{2,6},{6,10},{... | collective-permute-start | bytes 52232 | tf_op jit(solution)/shard_map/ppermute | solution.py:25
  86.5 2.6 %collective-permute-start.25 = (bf16[68,128]{1,0:T(8,128)(2,1)S(1)}, bf16[68,128]{1,0:T(8,128)(2,1)S(1)}, u32[]{:S(2)}, u32[]{:S(2)}) collective-permute-start(bf16[68,128]{1,0:T(8,128)(2,1)S(1)} %attend.3.refs_0_), channel_id=1, source_target_pairs={{0,8},{4,12},{8,0},{12,4},{1,9},{5,13},{9,1},{13,5},{2,10},{6,14},... | collective-permute-start | bytes 52232 | tf_op jit(solution)/shard_map/ppermute | solution.py:25
  89.1 1.0 %collective-permute-start.26 = (bf16[68,128]{1,0:T(8,128)(2,1)S(1)}, bf16[68,128]{1,0:T(8,128)(2,1)S(1)}, u32[]{:S(2)}, u32[]{:S(2)}) collective-permute-start(bf16[68,128]{1,0:T(8,128)(2,1)S(1)} %attend.3.refs_0_), channel_id=1, source_target_pairs={{0,12},{4,0},{8,4},{12,8},{1,13},{5,1},{9,5},{13,9},{2,14},{6,2},{... | collective-permute-start | bytes 52232 | tf_op jit(solution)/shard_map/ppermute | solution.py:25
  90.1 0.8 collective-permute-done.24.refs_1_
  91.2 1.7 %collective-permute-done.26.refs_3_ = bf16[68,128]{1,0:T(8,128)(2,1)S(1)} collective-permute-done((bf16[68,128]{1,0:T(8,128)(2,1)S(1)}, bf16[68,128]{1,0:T(8,128)(2,1)S(1)}, u32[]{:S(2)}, u32[]{:S(2)}) %collective-permute-start.26) | collective-permute-done | bytes 17440 | tf_op jit(solution)/shard_map/ppermute | solution.py:25
  92.8 1.1 %output_third.1 = (bf16[3,68,1024]{2,1,0:T(8,128)(2,1)}, bf16[3,68,1024]{2,1,0:T(8,128)(2,1)}) custom-call(bf16[68,128]{1,0:T(8,128)(2,1)S(1)} %attend.3.refs_0_, bf16[68,128]{1,0:T(8,128)(2,1)S(1)} %collective-permute-done.24.refs_1_, bf16[68,128]{1,0:T(8,128)(2,1)S(1)} %collective-permute-done.25.refs_2_, ...), custom_call_target="tpu_custom_call", output_to_operand_aliasing={{0}: (7, {}), {1}: (8, {})} | custom-call | tf_op jit(solution)/shard_map/output_third/pallas_call | solution.py:504
  (34 shorter events, 4.9 us)
Async XLA Ops:
  0.6 20.7 %copy-start.3 = (bf16[2,68,1024]{2,0,1:T(2,128)(2,1)S(1)}, bf16[2,68,1024]{2,0,1:T(2,128)(2,1)}, u32[]{:S(2)}) copy-start(bf16[2,68,1024]{2,0,1:T(2,128)(2,1)} %param.12) | copy-start | bytes 835588
  1.8 12.7 %collective-permute-start.13 = (bf16[64,1024]{1,0:T(8,128)(2,1)S(1)}, bf16[64,1024]{1,0:T(8,128)(2,1)S(1)}, u32[]{:S(2)}, u32[]{:S(2)}) collective-permute-start(bf16[64,1024]{1,0:T(8,128)(2,1)S(1)} %get-tuple-element.34), channel_id=1, source_target_pairs={{0,4},{4,8},{8,12},{12,0},{1,5},{5,9},{9,13},{13,1},{2,6},{6,10},{... | collective-permute-start | bytes 393224 | tf_op jit(solution)/shard_map/ppermute | solution.py:25
  4.8 12.1 %collective-permute-start.14 = (bf16[64,1024]{1,0:T(8,128)(2,1)S(1)}, bf16[64,1024]{1,0:T(8,128)(2,1)S(1)}, u32[]{:S(2)}, u32[]{:S(2)}) collective-permute-start(bf16[64,1024]{1,0:T(8,128)(2,1)S(1)} %get-tuple-element.35), channel_id=1, source_target_pairs={{0,8},{4,12},{8,0},{12,4},{1,9},{5,13},{9,1},{13,5},{2,10},{6,14},... | collective-permute-start | bytes 393224 | tf_op jit(solution)/shard_map/ppermute | solution.py:25
  7.4 12.3 %collective-permute-start.15 = (bf16[64,1024]{1,0:T(8,128)(2,1)S(1)}, bf16[64,1024]{1,0:T(8,128)(2,1)S(1)}, u32[]{:S(2)}, u32[]{:S(2)}) collective-permute-start(bf16[64,1024]{1,0:T(8,128)(2,1)S(1)} %get-tuple-element.36), channel_id=1, source_target_pairs={{0,12},{4,0},{8,4},{12,8},{1,13},{5,1},{9,5},{13,9},{2,14},{6,2},{... | collective-permute-start | bytes 393224 | tf_op jit(solution)/shard_map/ppermute | solution.py:25
  8.8 16.0 %collective-permute-start = (bf16[68,1024]{1,0:T(8,128)(2,1)}, bf16[68,1024]{1,0:T(8,128)(2,1)S(1)}, u32[]{:S(2)}, u32[]{:S(2)}) collective-permute-start(bf16[68,1024]{1,0:T(8,128)(2,1)} %bitcast.17), channel_id=1, source_target_pairs={{0,4},{4,8},{8,12},{12,0},{1,5},{5,9},{9,13},{13,1},{2,6},{6,10},{... | collective-permute-start | bytes 417800 | tf_op jit(solution)/shard_map/ppermute | solution.py:25
  9.5 18.1 %collective-permute-start.2 = (bf16[68,1024]{1,0:T(8,128)(2,1)}, bf16[68,1024]{1,0:T(8,128)(2,1)S(1)}, u32[]{:S(2)}, u32[]{:S(2)}) collective-permute-start(bf16[68,1024]{1,0:T(8,128)(2,1)} %bitcast.18), channel_id=1, source_target_pairs={{0,12},{4,0},{8,4},{12,8},{1,13},{5,1},{9,5},{13,9},{2,14},{6,2},{... | collective-permute-start | bytes 417800 | tf_op jit(solution)/shard_map/ppermute | solution.py:25
  12.6 0.9 %copy-start = (bf16[1,68,1024]{2,1,0:T(8,128)(2,1)S(1)}, bf16[1,68,1024]{2,1,0:T(8,128)(2,1)}, u32[]{:S(2)}) copy-start(bf16[1,68,1024]{2,1,0:T(8,128)(2,1)} %param.10) | copy-start | bytes 417796
  13.5 0.9 copy-start.2
  14.5 7.3 %collective-permute-start.3 = (bf16[68,1024]{1,0:T(8,128)(2,1)S(1)}, bf16[68,1024]{1,0:T(8,128)(2,1)S(1)}, u32[]{:S(2)}, u32[]{:S(2)}) collective-permute-start(bf16[68,1024]{1,0:T(8,128)(2,1)S(1)} %begin.1.refs_5_), channel_id=1, source_target_pairs={{0,1},{1,2},{2,3},{4,5},{5,6},{6,7},{8,9},{9,10},{10,11},{12,13},{... | collective-permute-start | bytes 417800 | tf_op jit(solution)/shard_map/ppermute | solution.py:20
  19.7 35.9 %collective-permute-start.16 = (bf16[3,64,1024]{2,1,0:T(8,128)(2,1)S(1)}, bf16[3,64,1024]{2,1,0:T(8,128)(2,1)S(1)}, u32[]{:S(2)}, u32[]{:S(2)}) collective-permute-start(bf16[3,64,1024]{2,1,0:T(8,128)(2,1)S(1)} %stack.1), channel_id=1, source_target_pairs={{0,16},{16,0},{1,17},{17,1},{2,18},{18,2},{3,19},{19,3},{4,20},{20... | collective-permute-start | bytes 1179656 | tf_op jit(solution)/shard_map/ppermute | solution.py:25
  21.9 13.0 %collective-permute-start.4 = (bf16[68,1024]{1,0:T(8,128)(2,1)S(1)}, bf16[68,1024]{1,0:T(8,128)(2,1)S(1)}, u32[]{:S(2)}, u32[]{:S(2)}) collective-permute-start(bf16[68,1024]{1,0:T(8,128)(2,1)S(1)} %choose.1.refs_4_), channel_id=1, source_target_pairs={{0,4},{4,8},{8,12},{12,0},{1,5},{5,9},{9,13},{13,1},{2,6},{6,10},{... | collective-permute-start | bytes 417800 | tf_op jit(solution)/shard_map/ppermute | solution.py:25
  24.8 10.0 %collective-permute-start.1 = (bf16[68,1024]{1,0:T(8,128)(2,1)S(1)}, bf16[68,1024]{1,0:T(8,128)(2,1)S(1)}, u32[]{:S(2)}, u32[]{:S(2)}) collective-permute-start(bf16[68,1024]{1,0:T(8,128)(2,1)S(1)} %collective-permute-done.refs_1_), channel_id=1, source_target_pairs={{0,4},{4,8},{8,12},{12,0},{1,5},{5,9},{9,13},{13,1},{2,6},{6,10},{... | collective-permute-start | bytes 417800 | tf_op jit(solution)/shard_map/ppermute | solution.py:25
  24.9 14.8 %collective-permute-start.5 = (bf16[68,1024]{1,0:T(8,128)(2,1)S(1)}, bf16[68,1024]{1,0:T(8,128)(2,1)S(1)}, u32[]{:S(2)}, u32[]{:S(2)}) collective-permute-start(bf16[68,1024]{1,0:T(8,128)(2,1)S(1)} %choose.1.refs_4_), channel_id=1, source_target_pairs={{0,8},{4,12},{8,0},{12,4},{1,9},{5,13},{9,1},{13,5},{2,10},{6,14},... | collective-permute-start | bytes 417800 | tf_op jit(solution)/shard_map/ppermute | solution.py:25
  27.6 12.2 %collective-permute-start.6 = (bf16[68,1024]{1,0:T(8,128)(2,1)S(1)}, bf16[68,1024]{1,0:T(8,128)(2,1)S(1)}, u32[]{:S(2)}, u32[]{:S(2)}) collective-permute-start(bf16[68,1024]{1,0:T(8,128)(2,1)S(1)} %choose.1.refs_4_), channel_id=1, source_target_pairs={{0,12},{4,0},{8,4},{12,8},{1,13},{5,1},{9,5},{13,9},{2,14},{6,2},{... | collective-permute-start | bytes 417800 | tf_op jit(solution)/shard_map/ppermute | solution.py:25
  30.4 9.3 %copy-start.1 = (bf16[1,68,1024]{2,1,0:T(8,128)(2,1)S(1)}, bf16[1,68,1024]{2,1,0:T(8,128)(2,1)}, u32[]{:S(2)}) copy-start(bf16[1,68,1024]{2,1,0:T(8,128)(2,1)} %param.10) | copy-start | bytes 417796
  41.1 6.2 %collective-permute-start.7 = (bf16[176,128]{1,0:T(8,128)(2,1)S(1)}, bf16[176,128]{1,0:T(8,128)(2,1)S(1)}, u32[]{:S(2)}, u32[]{:S(2)}) collective-permute-start(bf16[176,128]{1,0:T(8,128)(2,1)S(1)} %get-tuple-element.30), channel_id=1, source_target_pairs={{0,4},{4,8},{8,12},{12,0},{1,5},{5,9},{9,13},{13,1},{2,6},{6,10},{... | collective-permute-start | bytes 135176 | tf_op jit(solution)/shard_map/ppermute | solution.py:25
  43.9 5.1 %collective-permute-start.8 = (bf16[176,128]{1,0:T(8,128)(2,1)S(1)}, bf16[176,128]{1,0:T(8,128)(2,1)S(1)}, u32[]{:S(2)}, u32[]{:S(2)}) collective-permute-start(bf16[176,128]{1,0:T(8,128)(2,1)S(1)} %get-tuple-element.29.refs_1_), channel_id=1, source_target_pairs={{0,8},{4,12},{8,0},{12,4},{1,9},{5,13},{9,1},{13,5},{2,10},{6,14},... | collective-permute-start | bytes 135176 | tf_op jit(solution)/shard_map/ppermute | solution.py:25
  45.4 4.1 %collective-permute-start.9 = (bf16[176,128]{1,0:T(8,128)(2,1)S(1)}, bf16[176,128]{1,0:T(8,128)(2,1)S(1)}, u32[]{:S(2)}, u32[]{:S(2)}) collective-permute-start(bf16[176,128]{1,0:T(8,128)(2,1)S(1)} %get-tuple-element.30), channel_id=1, source_target_pairs={{0,12},{4,0},{8,4},{12,8},{1,13},{5,1},{9,5},{13,9},{2,14},{6,2},{... | collective-permute-start | bytes 135176 | tf_op jit(solution)/shard_map/ppermute | solution.py:25
  51.2 5.8 %collective-permute-start.10 = (bf16[136,128]{1,0:T(8,128)(2,1)S(1)}, bf16[136,128]{1,0:T(8,128)(2,1)S(1)}, u32[]{:S(2)}, u32[]{:S(2)}) collective-permute-start(bf16[136,128]{1,0:T(8,128)(2,1)S(1)} %attend.2.refs_0_), channel_id=1, source_target_pairs={{0,4},{4,8},{8,12},{12,0},{1,5},{5,9},{9,13},{13,1},{2,6},{6,10},{... | collective-permute-start | bytes 104456 | tf_op jit(solution)/shard_map/ppermute | solution.py:25
  51.8 5.2 %collective-permute-start.11 = (bf16[136,128]{1,0:T(8,128)(2,1)S(1)}, bf16[136,128]{1,0:T(8,128)(2,1)S(1)}, u32[]{:S(2)}, u32[]{:S(2)}) collective-permute-start(bf16[136,128]{1,0:T(8,128)(2,1)S(1)} %attend.2.refs_0_), channel_id=1, source_target_pairs={{0,8},{4,12},{8,0},{12,4},{1,9},{5,13},{9,1},{13,5},{2,10},{6,14},... | collective-permute-start | bytes 104456 | tf_op jit(solution)/shard_map/ppermute | solution.py:25
  54.5 3.9 %collective-permute-start.12 = (bf16[136,128]{1,0:T(8,128)(2,1)S(1)}, bf16[136,128]{1,0:T(8,128)(2,1)S(1)}, u32[]{:S(2)}, u32[]{:S(2)}) collective-permute-start(bf16[136,128]{1,0:T(8,128)(2,1)S(1)} %attend.2.refs_0_), channel_id=1, source_target_pairs={{0,12},{4,0},{8,4},{12,8},{1,13},{5,1},{9,5},{13,9},{2,14},{6,2},{... | collective-permute-start | bytes 104456 | tf_op jit(solution)/shard_map/ppermute | solution.py:25
  58.8 5.9 %collective-permute-start.17 = (bf16[68,1024]{1,0:T(8,128)(2,1)S(1)}, bf16[68,1024]{1,0:T(8,128)(2,1)S(1)}, u32[]{:S(2)}, u32[]{:S(2)}) collective-permute-start(bf16[68,1024]{1,0:T(8,128)(2,1)S(1)} %get-tuple-element.37), channel_id=1, source_target_pairs={{0,2},{1,3},{2,0},{3,1},{4,6},{5,7},{6,4},{7,5},{8,10},{9,11},{10,... | collective-permute-start | bytes 417800 | tf_op jit(solution)/shard_map/ppermute | solution.py:25
  60.4 8.2 %collective-permute-start.27 = (bf16[68,1024]{1,0:T(8,128)(2,1)S(1)}, bf16[68,1024]{1,0:T(8,128)(2,1)S(1)}, u32[]{:S(2)}, u32[]{:S(2)}) collective-permute-start(bf16[68,1024]{1,0:T(8,128)(2,1)S(1)} %get-tuple-element.42), channel_id=1, source_target_pairs={{0,1},{1,2},{2,3},{3,0},{4,5},{5,6},{6,7},{7,4},{8,9},{9,10},{10,1... | collective-permute-start | bytes 417800 | tf_op jit(solution)/shard_map/ppermute | solution.py:25
  64.7 7.2 %collective-permute-start.18 = (bf16[68,1024]{1,0:T(8,128)(2,1)S(1)}, bf16[68,1024]{1,0:T(8,128)(2,1)S(1)}, u32[]{:S(2)}, u32[]{:S(2)}) collective-permute-start(bf16[68,1024]{1,0:T(8,128)(2,1)S(1)} %collective-permute-done.17.refs_0_.refs_5_), channel_id=1, source_target_pairs={{0,4},{4,8},{8,12},{12,0},{1,5},{5,9},{9,13},{13,1},{2,6},{6,10},{... | collective-permute-start | bytes 417800 | tf_op jit(solution)/shard_map/ppermute | solution.py:25
  65.9 10.6 %collective-permute-start.19 = (bf16[68,1024]{1,0:T(8,128)(2,1)S(1)}, bf16[68,1024]{1,0:T(8,128)(2,1)S(1)}, u32[]{:S(2)}, u32[]{:S(2)}) collective-permute-start(bf16[68,1024]{1,0:T(8,128)(2,1)S(1)} %collective-permute-done.17.refs_0_.refs_5_), channel_id=1, source_target_pairs={{0,8},{4,12},{8,0},{12,4},{1,9},{5,13},{9,1},{13,5},{2,10},{6,14},... | collective-permute-start | bytes 417800 | tf_op jit(solution)/shard_map/ppermute | solution.py:25
  68.1 8.3 %collective-permute-start.20 = (bf16[68,1024]{1,0:T(8,128)(2,1)S(1)}, bf16[68,1024]{1,0:T(8,128)(2,1)S(1)}, u32[]{:S(2)}, u32[]{:S(2)}) collective-permute-start(bf16[68,1024]{1,0:T(8,128)(2,1)S(1)} %collective-permute-done.17.refs_0_.refs_5_), channel_id=1, source_target_pairs={{0,12},{4,0},{8,4},{12,8},{1,13},{5,1},{9,5},{13,9},{2,14},{6,2},{... | collective-permute-start | bytes 417800 | tf_op jit(solution)/shard_map/ppermute | solution.py:25
  69.7 20.4 %collective-permute-start.28 = (bf16[68,1024]{1,0:T(8,128)(2,1)S(1)}, bf16[68,1024]{1,0:T(8,128)(2,1)S(1)}, u32[]{:S(2)}, u32[]{:S(2)}) collective-permute-start(bf16[68,1024]{1,0:T(8,128)(2,1)S(1)} %get-tuple-element.43), channel_id=1, source_target_pairs={{0,1},{1,2},{2,3},{4,5},{5,6},{6,7},{8,9},{9,10},{10,11},{12,13},{... | collective-permute-start | bytes 417800 | tf_op jit(solution)/shard_map/ppermute | solution.py:20
  77.3 5.7 %collective-permute-start.21 = (bf16[88,128]{1,0:T(8,128)(2,1)S(1)}, bf16[88,128]{1,0:T(8,128)(2,1)S(1)}, u32[]{:S(2)}, u32[]{:S(2)}) collective-permute-start(bf16[88,128]{1,0:T(8,128)(2,1)S(1)} %get-tuple-element.40), channel_id=1, source_target_pairs={{0,4},{4,8},{8,12},{12,0},{1,5},{5,9},{9,13},{13,1},{2,6},{6,10},{... | collective-permute-start | bytes 67592 | tf_op jit(solution)/shard_map/ppermute | solution.py:25
  79.5 4.7 %collective-permute-start.22 = (bf16[88,128]{1,0:T(8,128)(2,1)S(1)}, bf16[88,128]{1,0:T(8,128)(2,1)S(1)}, u32[]{:S(2)}, u32[]{:S(2)}) collective-permute-start(bf16[88,128]{1,0:T(8,128)(2,1)S(1)} %get-tuple-element.39.refs_1_), channel_id=1, source_target_pairs={{0,8},{4,12},{8,0},{12,4},{1,9},{5,13},{9,1},{13,5},{2,10},{6,14},... | collective-permute-start | bytes 67592 | tf_op jit(solution)/shard_map/ppermute | solution.py:25
  80.6 3.9 %collective-permute-start.23 = (bf16[88,128]{1,0:T(8,128)(2,1)S(1)}, bf16[88,128]{1,0:T(8,128)(2,1)S(1)}, u32[]{:S(2)}, u32[]{:S(2)}) collective-permute-start(bf16[88,128]{1,0:T(8,128)(2,1)S(1)} %get-tuple-element.40), channel_id=1, source_target_pairs={{0,12},{4,0},{8,4},{12,8},{1,13},{5,1},{9,5},{13,9},{2,14},{6,2},{... | collective-permute-start | bytes 67592 | tf_op jit(solution)/shard_map/ppermute | solution.py:25
  85.3 5.6 %collective-permute-start.24 = (bf16[68,128]{1,0:T(8,128)(2,1)S(1)}, bf16[68,128]{1,0:T(8,128)(2,1)S(1)}, u32[]{:S(2)}, u32[]{:S(2)}) collective-permute-start(bf16[68,128]{1,0:T(8,128)(2,1)S(1)} %attend.3.refs_0_), channel_id=1, source_target_pairs={{0,4},{4,8},{8,12},{12,0},{1,5},{5,9},{9,13},{13,1},{2,6},{6,10},{... | collective-permute-start | bytes 52232 | tf_op jit(solution)/shard_map/ppermute | solution.py:25
  86.5 4.7 %collective-permute-start.25 = (bf16[68,128]{1,0:T(8,128)(2,1)S(1)}, bf16[68,128]{1,0:T(8,128)(2,1)S(1)}, u32[]{:S(2)}, u32[]{:S(2)}) collective-permute-start(bf16[68,128]{1,0:T(8,128)(2,1)S(1)} %attend.3.refs_0_), channel_id=1, source_target_pairs={{0,8},{4,12},{8,0},{12,4},{1,9},{5,13},{9,1},{13,5},{2,10},{6,14},... | collective-permute-start | bytes 52232 | tf_op jit(solution)/shard_map/ppermute | solution.py:25
  89.1 3.8 %collective-permute-start.26 = (bf16[68,128]{1,0:T(8,128)(2,1)S(1)}, bf16[68,128]{1,0:T(8,128)(2,1)S(1)}, u32[]{:S(2)}, u32[]{:S(2)}) collective-permute-start(bf16[68,128]{1,0:T(8,128)(2,1)S(1)} %attend.3.refs_0_), channel_id=1, source_target_pairs={{0,12},{4,0},{8,4},{12,8},{1,13},{5,1},{9,5},{13,9},{2,14},{6,2},{... | collective-permute-start | bytes 52232 | tf_op jit(solution)/shard_map/ppermute | solution.py:25

commit v6 on v5

--- a/solution.py
+++ b/solution.py
@@ -255,12 +255,15 @@
         for r in range(count):
             placed[h, r : r + 1, :] = decode[r, h : h + 1, :]
         rows_ref[h, span : span + count] = placed[h, :count].astype(BF16)
-    total = None
-    for h in range(count):
-        term = jnp.dot(rows_ref[h], weights[h], preferred_element_type=F32)
-        term = term.astype(BF16).astype(F32)
-        total = term if total is None else total + term
-    return total[: span + count].astype(BF16)
+    def columns(part):
+        total = None
+        for h in range(count):
+            term = jnp.dot(rows_ref[h], weights[h, :, part], preferred_element_type=F32)
+            term = term.astype(BF16).astype(F32)
+            total = term if total is None else total + term
+        return total[: span + count].astype(BF16)
+
+    return columns
 
 
 def first_output_kernel(count, span, *refs):
@@ -268,7 +271,7 @@
     weights, first_new, early, late, out_ref, one_ref, two_ref = refs[count : count + 7]
     section = lax.axis_index("section")
     sections = lax.axis_size("section")
-    out_ref[...] = summed_terms(count, span, 0, parts, weights, refs[count + 7 :])
+    out_ref[...] = summed_terms(count, span, 0, parts, weights, refs[count + 7 :])(slice(None))
     fresh = (first_new[...].astype(F32) + out_ref[...].astype(F32)).astype(BF16)
     is_last = section == sections - 1
     one_ref[...] = jnp.where(is_last, early[...], fresh)
@@ -290,7 +293,7 @@
     ]
     for copy in copies:
         copy.start()
-    out_ref[...] = summed_terms(count, span, span + count, parts, weights, scratch)
+    out_ref[...] = summed_terms(count, span, span + count, parts, weights, scratch)(slice(None))
     last = pltpu.make_async_copy(out_ref, hist_pend.at[1], sems.at[3])
     last.start()
     for copy in copies:
@@ -307,11 +310,18 @@
     fresh[...] = (third[...].astype(F32) + pend_in[...].astype(F32)).astype(BF16)
     copy = pltpu.make_async_copy(fresh, hist_stream.at[2], sems.at[0])
     copy.start()
-    result[...] = summed_terms(count, span, 0, parts, weights, scratch)
-    last = pltpu.make_async_copy(result, hist_pend.at[2], sems.at[1])
-    last.start()
-    copy.wait()
-    last.wait()
+    columns = summed_terms(count, span, 0, parts, weights, scratch)
+    half = result.shape[1] // 2
+    copies = [copy]
+    for n in range(2):
+        part = slice(n * half, (n + 1) * half)
+        result[:, part] = columns(part)
+        copies.append(
+            pltpu.make_async_copy(result.at[:, part], hist_pend.at[2, :, part], sems.at[1 + n])
+        )
+        copies[-1].start()
+    for copy in copies:
+        copy.wait()
 
 
 def fast_body(
@@ -510,7 +520,7 @@
         + [
             pltpu.VMEM((rows, shard), BF16),
             pltpu.VMEM((rows, shard), BF16),
-            pltpu.SemaphoreType.DMA((2,)),
+            pltpu.SemaphoreType.DMA((3,)),
         ],
         input_output_aliases={count + 3: 0, count + 4: 1},
         compiler_params=limit,

time: 94.2 us -> 94.2 us (level)
  no operation moved by 1% of the time
where the time goes in v6:
time: 94.2 us; the launch traced here: 93.9 us
  starting transfers between devices  48.1 us (51%)
  waiting for transfers between devices  30.4 us (32%)
  Pallas kernels  12.3 us (13%)
  local copies, waits for them, and re-layouts  2.35 us (2%)
    ppermute x27, starting transfers between devices, turned(): lax.ppermute(block, axis, [(i, (i + distance) % count) for i in range(cou...  45.5 us
    ppermute x27, waiting for transfers between devices, turned(): lax.ppermute(block, axis, [(i, (i + distance) % count) for i in range(cou...  30.4 us
    pallas_call x1, Pallas kernels, fast_body(): pl.pallas_call(functools.partial(load_kernel, pieces), out_shape=tuple((j...  2.73 us
    ppermute x2, starting transfers between devices, moved(): return lax.ppermute(block, axis, route)  2.6 us
    pallas_call x2, Pallas kernels, attend(): pl.pallas_call(functools.partial(attend_kernel, count, span, which), out_...  2.54 us
    pallas_call x2, Pallas kernels, project(): pl.pallas_call(functools.partial(project_kernel, count, span, batch), out...  2.15 us
    unnamed x10, local copies, waits for them, and re-layouts  1.96 us
  transfers between devices with their start and end apart: 29, of which 18 were waited for; matrix products, arithmetic and copies ran while one was open for 1% of the time, Pallas kernels for 10%

profile of v6, /device:TPU:0, one launch (start us, length us, event | category | flops | bytes accessed | tf_op | source)
XLA Modules:
  0.0 93.9 jit_solution(4603684387804759633)
XLA Ops:
  0.6 1.1 %cut.1 = (bf16[64,1024]{1,0:T(8,128)(2,1)S(1)}, bf16[64,1024]{1,0:T(8,128)(2,1)S(1)}, bf16[64,1024]{1,0:T(8,128)(2,1)S(1)}) custom-call(bf16[128,4096]{1,0:T(8,128)(2,1)} %bitcast.23), custom_call_target="tpu_custom_call" | custom-call | tf_op jit(solution)/shard_map/cut/pallas_call | solution.py:435
  1.8 3.1 %collective-permute-start.13 = (bf16[64,1024]{1,0:T(8,128)(2,1)S(1)}, bf16[64,1024]{1,0:T(8,128)(2,1)S(1)}, u32[]{:S(2)}, u32[]{:S(2)}) collective-permute-start(bf16[64,1024]{1,0:T(8,128)(2,1)S(1)} %get-tuple-element.34), channel_id=1, source_target_pairs={{0,4},{4,8},{8,12},{12,0},{1,5},{5,9},{9,13},{13,1},{2,6},{6,10},{... | collective-permute-start | bytes 393224 | tf_op jit(solution)/shard_map/ppermute | solution.py:25
  4.8 2.6 %collective-permute-start.14 = (bf16[64,1024]{1,0:T(8,128)(2,1)S(1)}, bf16[64,1024]{1,0:T(8,128)(2,1)S(1)}, u32[]{:S(2)}, u32[]{:S(2)}) collective-permute-start(bf16[64,1024]{1,0:T(8,128)(2,1)S(1)} %get-tuple-element.35), channel_id=1, source_target_pairs={{0,8},{4,12},{8,0},{12,4},{1,9},{5,13},{9,1},{13,5},{2,10},{6,14},... | collective-permute-start | bytes 393224 | tf_op jit(solution)/shard_map/ppermute | solution.py:25
  7.4 1.3 %collective-permute-start.15 = (bf16[64,1024]{1,0:T(8,128)(2,1)S(1)}, bf16[64,1024]{1,0:T(8,128)(2,1)S(1)}, u32[]{:S(2)}, u32[]{:S(2)}) collective-permute-start(bf16[64,1024]{1,0:T(8,128)(2,1)S(1)} %get-tuple-element.36), channel_id=1, source_target_pairs={{0,12},{4,0},{8,4},{12,8},{1,13},{5,1},{9,5},{13,9},{2,14},{6,2},{... | collective-permute-start | bytes 393224 | tf_op jit(solution)/shard_map/ppermute | solution.py:25
  9.5 3.1 %collective-permute-start.2 = (bf16[68,1024]{1,0:T(8,128)(2,1)}, bf16[68,1024]{1,0:T(8,128)(2,1)S(1)}, u32[]{:S(2)}, u32[]{:S(2)}) collective-permute-start(bf16[68,1024]{1,0:T(8,128)(2,1)} %bitcast.18), channel_id=1, source_target_pairs={{0,12},{4,0},{8,4},{12,8},{1,13},{5,1},{9,5},{13,9},{2,14},{6,2},{... | collective-permute-start | bytes 417800 | tf_op jit(solution)/shard_map/ppermute | solution.py:25
  12.6 0.9 %copy-done = bf16[1,68,1024]{2,1,0:T(8,128)(2,1)S(1)} copy-done((bf16[1,68,1024]{2,1,0:T(8,128)(2,1)S(1)}, bf16[1,68,1024]{2,1,0:T(8,128)(2,1)}, u32[]{:S(2)}) %copy-start) | copy-done | bytes 139288
  13.5 0.9 copy-done.2
  14.5 1.3 %collective-permute-start.3 = (bf16[68,1024]{1,0:T(8,128)(2,1)S(1)}, bf16[68,1024]{1,0:T(8,128)(2,1)S(1)}, u32[]{:S(2)}, u32[]{:S(2)}) collective-permute-start(bf16[68,1024]{1,0:T(8,128)(2,1)S(1)} %begin.1.refs_5_), channel_id=1, source_target_pairs={{0,1},{1,2},{2,3},{4,5},{5,6},{6,7},{8,9},{9,10},{10,11},{12,13},{... | collective-permute-start | bytes 417800 | tf_op jit(solution)/shard_map/ppermute | solution.py:20
  15.8 1.1 %collective-permute-done.14.refs_1_.refs_2_ = bf16[64,1024]{1,0:T(8,128)(2,1)S(1)} collective-permute-done((bf16[64,1024]{1,0:T(8,128)(2,1)S(1)}, bf16[64,1024]{1,0:T(8,128)(2,1)S(1)}, u32[]{:S(2)}, u32[]{:S(2)}) %collective-permute-start.14) | collective-permute-done | bytes 131104 | tf_op jit(solution)/shard_map/ppermute | solution.py:25
  17.0 2.8 %collective-permute-done.15.refs_2_.refs_3_ = bf16[64,1024]{1,0:T(8,128)(2,1)S(1)} collective-permute-done((bf16[64,1024]{1,0:T(8,128)(2,1)S(1)}, bf16[64,1024]{1,0:T(8,128)(2,1)S(1)}, u32[]{:S(2)}, u32[]{:S(2)}) %collective-permute-start.15) | collective-permute-done | bytes 131104 | tf_op jit(solution)/shard_map/ppermute | solution.py:25
  19.7 1.6 %collective-permute-start.16 = (bf16[3,64,1024]{2,1,0:T(8,128)(2,1)S(1)}, bf16[3,64,1024]{2,1,0:T(8,128)(2,1)S(1)}, u32[]{:S(2)}, u32[]{:S(2)}) collective-permute-start(bf16[3,64,1024]{2,1,0:T(8,128)(2,1)S(1)} %stack.1), channel_id=1, source_target_pairs={{0,16},{16,0},{1,17},{17,1},{2,18},{18,2},{3,19},{19,3},{4,20},{20... | collective-permute-start | bytes 1179656 | tf_op jit(solution)/shard_map/ppermute | solution.py:25
  21.9 3.0 %collective-permute-start.4 = (bf16[68,1024]{1,0:T(8,128)(2,1)S(1)}, bf16[68,1024]{1,0:T(8,128)(2,1)S(1)}, u32[]{:S(2)}, u32[]{:S(2)}) collective-permute-start(bf16[68,1024]{1,0:T(8,128)(2,1)S(1)} %choose.1.refs_4_), channel_id=1, source_target_pairs={{0,4},{4,8},{8,12},{12,0},{1,5},{5,9},{9,13},{13,1},{2,6},{6,10},{... | collective-permute-start | bytes 417800 | tf_op jit(solution)/shard_map/ppermute | solution.py:25
  24.9 2.7 %collective-permute-start.5 = (bf16[68,1024]{1,0:T(8,128)(2,1)S(1)}, bf16[68,1024]{1,0:T(8,128)(2,1)S(1)}, u32[]{:S(2)}, u32[]{:S(2)}) collective-permute-start(bf16[68,1024]{1,0:T(8,128)(2,1)S(1)} %choose.1.refs_4_), channel_id=1, source_target_pairs={{0,8},{4,12},{8,0},{12,4},{1,9},{5,13},{9,1},{13,5},{2,10},{6,14},... | collective-permute-start | bytes 417800 | tf_op jit(solution)/shard_map/ppermute | solution.py:25
  27.6 2.9 %collective-permute-start.6 = (bf16[68,1024]{1,0:T(8,128)(2,1)S(1)}, bf16[68,1024]{1,0:T(8,128)(2,1)S(1)}, u32[]{:S(2)}, u32[]{:S(2)}) collective-permute-start(bf16[68,1024]{1,0:T(8,128)(2,1)S(1)} %choose.1.refs_4_), channel_id=1, source_target_pairs={{0,12},{4,0},{8,4},{12,8},{1,13},{5,1},{9,5},{13,9},{2,14},{6,2},{... | collective-permute-start | bytes 417800 | tf_op jit(solution)/shard_map/ppermute | solution.py:25
  30.4 2.7 %load.1 = (f32[1,4096]{1,0:T(1,128)S(1)}, bf16[4096,128]{1,0:T(8,128)(2,1)S(1)}, bf16[4096,256]{1,0:T(8,128)(2,1)S(1)}, s32[6,64]{1,0:T(8,128)S(1)}, s32[1,6]{1,...) custom-call(f32[1,4096]{1,0:T(1,128)} %refs_0_.1, bf16[4096,128]{1,0:T(8,128)(2,1)} %bitcast.27, bf16[4096,256]{1,0:T(8,128)(2,1)} %bitcast.26, ...), custom_call_target="tpu_custom_call" | custom-call | tf_op jit(solution)/shard_map/load/pallas_call | solution.py:351
  33.2 1.7 %collective-permute-done.1.refs_2_ = bf16[68,1024]{1,0:T(8,128)(2,1)S(1)} collective-permute-done((bf16[68,1024]{1,0:T(8,128)(2,1)S(1)}, bf16[68,1024]{1,0:T(8,128)(2,1)S(1)}, u32[]{:S(2)}, u32[]{:S(2)}) %collective-permute-start.1) | collective-permute-done | bytes 139296 | tf_op jit(solution)/shard_map/ppermute | solution.py:25
  34.8 4.9 %collective-permute-done.5.refs_6_ = bf16[68,1024]{1,0:T(8,128)(2,1)S(1)} collective-permute-done((bf16[68,1024]{1,0:T(8,128)(2,1)S(1)}, bf16[68,1024]{1,0:T(8,128)(2,1)S(1)}, u32[]{:S(2)}, u32[]{:S(2)}) %collective-permute-start.5) | collective-permute-done | bytes 139296 | tf_op jit(solution)/shard_map/ppermute | solution.py:25
  39.7 1.3 %project.2 = (bf16[2,64,128]{2,1,0:T(8,128)(2,1)S(1)}, bf16[176,128]{1,0:T(8,128)(2,1)S(1)}, bf16[176,128]{1,0:T(8,128)(2,1)S(1)}) custom-call(bf16[68,1024]{1,0:T(8,128)(2,1)S(1)} %bitcast.20, bf16[68,1024]{1,0:T(8,128)(2,1)S(1)} %collective-permute-done.refs_1_, bf16[68,1024]{1,0:T(8,128)(2,1)S(1)} %collective-permute-done.1.refs_2_, ...), custom_call_target="tpu_custom_call" | custom-call | tf_op jit(solution)/shard_map/project/pallas_call | solution.py:365
  41.1 2.9 %collective-permute-start.7 = (bf16[176,128]{1,0:T(8,128)(2,1)S(1)}, bf16[176,128]{1,0:T(8,128)(2,1)S(1)}, u32[]{:S(2)}, u32[]{:S(2)}) collective-permute-start(bf16[176,128]{1,0:T(8,128)(2,1)S(1)} %get-tuple-element.30), channel_id=1, source_target_pairs={{0,4},{4,8},{8,12},{12,0},{1,5},{5,9},{9,13},{13,1},{2,6},{6,10},{... | collective-permute-start | bytes 135176 | tf_op jit(solution)/shard_map/ppermute | solution.py:25
  43.9 1.5 %collective-permute-start.8 = (bf16[176,128]{1,0:T(8,128)(2,1)S(1)}, bf16[176,128]{1,0:T(8,128)(2,1)S(1)}, u32[]{:S(2)}, u32[]{:S(2)}) collective-permute-start(bf16[176,128]{1,0:T(8,128)(2,1)S(1)} %get-tuple-element.29.refs_1_), channel_id=1, source_target_pairs={{0,8},{4,12},{8,0},{12,4},{1,9},{5,13},{9,1},{13,5},{2,10},{6,14},... | collective-permute-start | bytes 135176 | tf_op jit(solution)/shard_map/ppermute | solution.py:25
  45.4 1.0 %collective-permute-start.9 = (bf16[176,128]{1,0:T(8,128)(2,1)S(1)}, bf16[176,128]{1,0:T(8,128)(2,1)S(1)}, u32[]{:S(2)}, u32[]{:S(2)}) collective-permute-start(bf16[176,128]{1,0:T(8,128)(2,1)S(1)} %get-tuple-element.30), channel_id=1, source_target_pairs={{0,12},{4,0},{8,4},{12,8},{1,13},{5,1},{9,5},{13,9},{2,14},{6,2},{... | collective-permute-start | bytes 135176 | tf_op jit(solution)/shard_map/ppermute | solution.py:25
  46.4 0.9 collective-permute-done.7.refs_2_
  47.3 1.8 %collective-permute-done.8.refs_3_ = bf16[176,128]{1,0:T(8,128)(2,1)S(1)} collective-permute-done((bf16[176,128]{1,0:T(8,128)(2,1)S(1)}, bf16[176,128]{1,0:T(8,128)(2,1)S(1)}, u32[]{:S(2)}, u32[]{:S(2)}) %collective-permute-start.8) | collective-permute-done | bytes 45088 | tf_op jit(solution)/shard_map/ppermute | solution.py:25
  49.6 1.6 %attend.2.refs_0_ = bf16[136,128]{1,0:T(8,128)(2,1)S(1)} custom-call(bf16[2,64,128]{2,1,0:T(8,128)(2,1)S(1)} %get-tuple-element.28.refs_0_, bf16[176,128]{1,0:T(8,128)(2,1)S(1)} %get-tuple-element.29.refs_1_, bf16[176,128]{1,0:T(8,128)(2,1)S(1)} %collective-permute-done.7.refs_2_, bf16[176,128]{1,0:T(8,128)(2,1)S(1)} %collective-permute-done.8.refs_3_, ...), custom_call_target="tpu_custom_call" | custom-call | tf_op jit(solution)/shard_map/attend/pallas_call | solution.py:384
  51.8 2.7 %collective-permute-start.11 = (bf16[136,128]{1,0:T(8,128)(2,1)S(1)}, bf16[136,128]{1,0:T(8,128)(2,1)S(1)}, u32[]{:S(2)}, u32[]{:S(2)}) collective-permute-start(bf16[136,128]{1,0:T(8,128)(2,1)S(1)} %attend.2.refs_0_), channel_id=1, source_target_pairs={{0,8},{4,12},{8,0},{12,4},{1,9},{5,13},{9,1},{13,5},{2,10},{6,14},... | collective-permute-start | bytes 104456 | tf_op jit(solution)/shard_map/ppermute | solution.py:25
  54.5 1.0 %collective-permute-start.12 = (bf16[136,128]{1,0:T(8,128)(2,1)S(1)}, bf16[136,128]{1,0:T(8,128)(2,1)S(1)}, u32[]{:S(2)}, u32[]{:S(2)}) collective-permute-start(bf16[136,128]{1,0:T(8,128)(2,1)S(1)} %attend.2.refs_0_), channel_id=1, source_target_pairs={{0,12},{4,0},{8,4},{12,8},{1,13},{5,1},{9,5},{13,9},{2,14},{6,2},{... | collective-permute-start | bytes 104456 | tf_op jit(solution)/shard_map/ppermute | solution.py:25
  55.6 1.1 %place.1.refs_4_ = bf16[4,128,1024]{2,1,0:T(8,128)(2,1)S(1)} custom-call(bf16[128,4096]{1,0:T(8,128)(2,1)} %bitcast.24, bf16[64,1024]{1,0:T(8,128)(2,1)S(1)} %collective-permute-done.13.refs_0_.refs_1_, bf16[64,1024]{1,0:T(8,128)(2,1)S(1)} %collective-permute-done.14.refs_1_.refs_2_, bf16[64,1024]{1,0:T(8,128)(2,1)S(1)} %collective-permute-done.15.refs_2_.refs_3_, ...), custom_call_target="tpu_custom_call" | custom-call | tf_op jit(solution)/shard_map/place/pallas_call | solution.py:461
  57.1 1.4 %collective-permute-done.12.refs_3_ = bf16[136,128]{1,0:T(8,128)(2,1)S(1)} collective-permute-done((bf16[136,128]{1,0:T(8,128)(2,1)S(1)}, bf16[136,128]{1,0:T(8,128)(2,1)S(1)}, u32[]{:S(2)}, u32[]{:S(2)}) %collective-permute-start.12) | collective-permute-done | bytes 34848 | tf_op jit(solution)/shard_map/ppermute | solution.py:25
  58.8 1.6 %collective-permute-start.17 = (bf16[68,1024]{1,0:T(8,128)(2,1)S(1)}, bf16[68,1024]{1,0:T(8,128)(2,1)S(1)}, u32[]{:S(2)}, u32[]{:S(2)}) collective-permute-start(bf16[68,1024]{1,0:T(8,128)(2,1)S(1)} %get-tuple-element.37), channel_id=1, source_target_pairs={{0,2},{1,3},{2,0},{3,1},{4,6},{5,7},{6,4},{7,5},{8,10},{9,11},{10,... | collective-permute-start | bytes 417800 | tf_op jit(solution)/shard_map/ppermute | solution.py:25
  60.4 4.3 %collective-permute-done.17.refs_0_.refs_5_ = bf16[68,1024]{1,0:T(8,128)(2,1)S(1)} collective-permute-done((bf16[68,1024]{1,0:T(8,128)(2,1)S(1)}, bf16[68,1024]{1,0:T(8,128)(2,1)S(1)}, u32[]{:S(2)}, u32[]{:S(2)}) %collective-permute-start.17) | collective-permute-done | bytes 139296 | tf_op jit(solution)/shard_map/ppermute | solution.py:25
  64.7 1.2 %collective-permute-start.18 = (bf16[68,1024]{1,0:T(8,128)(2,1)S(1)}, bf16[68,1024]{1,0:T(8,128)(2,1)S(1)}, u32[]{:S(2)}, u32[]{:S(2)}) collective-permute-start(bf16[68,1024]{1,0:T(8,128)(2,1)S(1)} %collective-permute-done.17.refs_0_.refs_5_), channel_id=1, source_target_pairs={{0,4},{4,8},{8,12},{12,0},{1,5},{5,9},{9,13},{13,1},{2,6},{6,10},{... | collective-permute-start | bytes 417800 | tf_op jit(solution)/shard_map/ppermute | solution.py:25
  65.9 2.3 %collective-permute-start.19 = (bf16[68,1024]{1,0:T(8,128)(2,1)S(1)}, bf16[68,1024]{1,0:T(8,128)(2,1)S(1)}, u32[]{:S(2)}, u32[]{:S(2)}) collective-permute-start(bf16[68,1024]{1,0:T(8,128)(2,1)S(1)} %collective-permute-done.17.refs_0_.refs_5_), channel_id=1, source_target_pairs={{0,8},{4,12},{8,0},{12,4},{1,9},{5,13},{9,1},{13,5},{2,10},{6,14},... | collective-permute-start | bytes 417800 | tf_op jit(solution)/shard_map/ppermute | solution.py:25
  68.6 1.1 %output_second.1 = (bf16[68,1024]{1,0:T(8,128)(2,1)S(1)}, bf16[3,68,1024]{2,1,0:T(8,128)(2,1)}, bf16[3,68,1024]{2,1,0:T(8,128)(2,1)}) custom-call(bf16[136,128]{1,0:T(8,128)(2,1)S(1)} %attend.2.refs_0_, bf16[136,128]{1,0:T(8,128)(2,1)S(1)} %collective-permute-done.10.refs_1_, bf16[136,128]{1,0:T(8,128)(2,1)S(1)} %collective-permute-done.11.refs_2_, ...), custom_call_target="tpu_custom_call" | custom-call | tf_op jit(solution)/shard_map/output_second/pallas_call | solution.py:493
  69.7 1.3 %collective-permute-start.28 = (bf16[68,1024]{1,0:T(8,128)(2,1)S(1)}, bf16[68,1024]{1,0:T(8,128)(2,1)S(1)}, u32[]{:S(2)}, u32[]{:S(2)}) collective-permute-start(bf16[68,1024]{1,0:T(8,128)(2,1)S(1)} %get-tuple-element.43), channel_id=1, source_target_pairs={{0,1},{1,2},{2,3},{4,5},{5,6},{6,7},{8,9},{9,10},{10,11},{12,13},{... | collective-permute-start | bytes 417800 | tf_op jit(solution)/shard_map/ppermute | solution.py:20
  71.0 0.9 %collective-permute-done.18.refs_1_ = bf16[68,1024]{1,0:T(8,128)(2,1)S(1)} collective-permute-done((bf16[68,1024]{1,0:T(8,128)(2,1)S(1)}, bf16[68,1024]{1,0:T(8,128)(2,1)S(1)}, u32[]{:S(2)}, u32[]{:S(2)}) %collective-permute-start.18) | collective-permute-done | bytes 139296 | tf_op jit(solution)/shard_map/ppermute | solution.py:25
  71.9 4.6 %collective-permute-done.19.refs_2_ = bf16[68,1024]{1,0:T(8,128)(2,1)S(1)} collective-permute-done((bf16[68,1024]{1,0:T(8,128)(2,1)S(1)}, bf16[68,1024]{1,0:T(8,128)(2,1)S(1)}, u32[]{:S(2)}, u32[]{:S(2)}) %collective-permute-start.19) | collective-permute-done | bytes 139296 | tf_op jit(solution)/shard_map/ppermute | solution.py:25
  77.3 2.2 %collective-permute-start.21 = (bf16[88,128]{1,0:T(8,128)(2,1)S(1)}, bf16[88,128]{1,0:T(8,128)(2,1)S(1)}, u32[]{:S(2)}, u32[]{:S(2)}) collective-permute-start(bf16[88,128]{1,0:T(8,128)(2,1)S(1)} %get-tuple-element.40), channel_id=1, source_target_pairs={{0,4},{4,8},{8,12},{12,0},{1,5},{5,9},{9,13},{13,1},{2,6},{6,10},{... | collective-permute-start | bytes 67592 | tf_op jit(solution)/shard_map/ppermute | solution.py:25
  79.5 1.1 %collective-permute-start.22 = (bf16[88,128]{1,0:T(8,128)(2,1)S(1)}, bf16[88,128]{1,0:T(8,128)(2,1)S(1)}, u32[]{:S(2)}, u32[]{:S(2)}) collective-permute-start(bf16[88,128]{1,0:T(8,128)(2,1)S(1)} %get-tuple-element.39.refs_1_), channel_id=1, source_target_pairs={{0,8},{4,12},{8,0},{12,4},{1,9},{5,13},{9,1},{13,5},{2,10},{6,14},... | collective-permute-start | bytes 67592 | tf_op jit(solution)/shard_map/ppermute | solution.py:25
  80.6 1.3 %collective-permute-start.23 = (bf16[88,128]{1,0:T(8,128)(2,1)S(1)}, bf16[88,128]{1,0:T(8,128)(2,1)S(1)}, u32[]{:S(2)}, u32[]{:S(2)}) collective-permute-start(bf16[88,128]{1,0:T(8,128)(2,1)S(1)} %get-tuple-element.40), channel_id=1, source_target_pairs={{0,12},{4,0},{8,4},{12,8},{1,13},{5,1},{9,5},{13,9},{2,14},{6,2},{... | collective-permute-start | bytes 67592 | tf_op jit(solution)/shard_map/ppermute | solution.py:25
  81.9 1.0 %collective-permute-done.21.refs_2_ = bf16[88,128]{1,0:T(8,128)(2,1)S(1)} collective-permute-done((bf16[88,128]{1,0:T(8,128)(2,1)S(1)}, bf16[88,128]{1,0:T(8,128)(2,1)S(1)}, u32[]{:S(2)}, u32[]{:S(2)}) %collective-permute-start.21) | collective-permute-done | bytes 22560 | tf_op jit(solution)/shard_map/ppermute | solution.py:25
  83.0 1.2 %collective-permute-done.22.refs_3_ = bf16[88,128]{1,0:T(8,128)(2,1)S(1)} collective-permute-done((bf16[88,128]{1,0:T(8,128)(2,1)S(1)}, bf16[88,128]{1,0:T(8,128)(2,1)S(1)}, u32[]{:S(2)}, u32[]{:S(2)}) %collective-permute-start.22) | collective-permute-done | bytes 22560 | tf_op jit(solution)/shard_map/ppermute | solution.py:25
  84.4 0.9 attend.3.refs_0_
  85.3 1.2 %collective-permute-start.24 = (bf16[68,128]{1,0:T(8,128)(2,1)S(1)}, bf16[68,128]{1,0:T(8,128)(2,1)S(1)}, u32[]{:S(2)}, u32[]{:S(2)}) collective-permute-start(bf16[68,128]{1,0:T(8,128)(2,1)S(1)} %attend.3.refs_0_), channel_id=1, source_target_pairs={{0,4},{4,8},{8,12},{12,0},{1,5},{5,9},{9,13},{13,1},{2,6},{6,10},{... | collective-permute-start | bytes 52232 | tf_op jit(solution)/shard_map/ppermute | solution.py:25
  86.5 2.6 %collective-permute-start.25 = (bf16[68,128]{1,0:T(8,128)(2,1)S(1)}, bf16[68,128]{1,0:T(8,128)(2,1)S(1)}, u32[]{:S(2)}, u32[]{:S(2)}) collective-permute-start(bf16[68,128]{1,0:T(8,128)(2,1)S(1)} %attend.3.refs_0_), channel_id=1, source_target_pairs={{0,8},{4,12},{8,0},{12,4},{1,9},{5,13},{9,1},{13,5},{2,10},{6,14},... | collective-permute-start | bytes 52232 | tf_op jit(solution)/shard_map/ppermute | solution.py:25
  89.1 1.0 %collective-permute-start.26 = (bf16[68,128]{1,0:T(8,128)(2,1)S(1)}, bf16[68,128]{1,0:T(8,128)(2,1)S(1)}, u32[]{:S(2)}, u32[]{:S(2)}) collective-permute-start(bf16[68,128]{1,0:T(8,128)(2,1)S(1)} %attend.3.refs_0_), channel_id=1, source_target_pairs={{0,12},{4,0},{8,4},{12,8},{1,13},{5,1},{9,5},{13,9},{2,14},{6,2},{... | collective-permute-start | bytes 52232 | tf_op jit(solution)/shard_map/ppermute | solution.py:25
  90.1 0.8 collective-permute-done.24.refs_1_
  91.2 1.7 %collective-permute-done.26.refs_3_ = bf16[68,128]{1,0:T(8,128)(2,1)S(1)} collective-permute-done((bf16[68,128]{1,0:T(8,128)(2,1)S(1)}, bf16[68,128]{1,0:T(8,128)(2,1)S(1)}, u32[]{:S(2)}, u32[]{:S(2)}) %collective-permute-start.26) | collective-permute-done | bytes 17440 | tf_op jit(solution)/shard_map/ppermute | solution.py:25
  92.8 1.1 %output_third.1 = (bf16[3,68,1024]{2,1,0:T(8,128)(2,1)}, bf16[3,68,1024]{2,1,0:T(8,128)(2,1)}) custom-call(bf16[68,128]{1,0:T(8,128)(2,1)S(1)} %attend.3.refs_0_, bf16[68,128]{1,0:T(8,128)(2,1)S(1)} %collective-permute-done.24.refs_1_, bf16[68,128]{1,0:T(8,128)(2,1)S(1)} %collective-permute-done.25.refs_2_, ...), custom_call_target="tpu_custom_call", output_to_operand_aliasing={{0}: (7, {}), {1}: (8, {})} | custom-call | tf_op jit(solution)/shard_map/output_third/pallas_call | solution.py:514
  (34 shorter events, 4.9 us)
Async XLA Ops:
  0.6 20.7 %copy-start.3 = (bf16[2,68,1024]{2,0,1:T(2,128)(2,1)S(1)}, bf16[2,68,1024]{2,0,1:T(2,128)(2,1)}, u32[]{:S(2)}) copy-start(bf16[2,68,1024]{2,0,1:T(2,128)(2,1)} %param.12) | copy-start | bytes 835588
  1.8 12.7 %collective-permute-start.13 = (bf16[64,1024]{1,0:T(8,128)(2,1)S(1)}, bf16[64,1024]{1,0:T(8,128)(2,1)S(1)}, u32[]{:S(2)}, u32[]{:S(2)}) collective-permute-start(bf16[64,1024]{1,0:T(8,128)(2,1)S(1)} %get-tuple-element.34), channel_id=1, source_target_pairs={{0,4},{4,8},{8,12},{12,0},{1,5},{5,9},{9,13},{13,1},{2,6},{6,10},{... | collective-permute-start | bytes 393224 | tf_op jit(solution)/shard_map/ppermute | solution.py:25
  4.8 12.1 %collective-permute-start.14 = (bf16[64,1024]{1,0:T(8,128)(2,1)S(1)}, bf16[64,1024]{1,0:T(8,128)(2,1)S(1)}, u32[]{:S(2)}, u32[]{:S(2)}) collective-permute-start(bf16[64,1024]{1,0:T(8,128)(2,1)S(1)} %get-tuple-element.35), channel_id=1, source_target_pairs={{0,8},{4,12},{8,0},{12,4},{1,9},{5,13},{9,1},{13,5},{2,10},{6,14},... | collective-permute-start | bytes 393224 | tf_op jit(solution)/shard_map/ppermute | solution.py:25
  7.4 12.3 %collective-permute-start.15 = (bf16[64,1024]{1,0:T(8,128)(2,1)S(1)}, bf16[64,1024]{1,0:T(8,128)(2,1)S(1)}, u32[]{:S(2)}, u32[]{:S(2)}) collective-permute-start(bf16[64,1024]{1,0:T(8,128)(2,1)S(1)} %get-tuple-element.36), channel_id=1, source_target_pairs={{0,12},{4,0},{8,4},{12,8},{1,13},{5,1},{9,5},{13,9},{2,14},{6,2},{... | collective-permute-start | bytes 393224 | tf_op jit(solution)/shard_map/ppermute | solution.py:25
  8.8 16.0 %collective-permute-start = (bf16[68,1024]{1,0:T(8,128)(2,1)}, bf16[68,1024]{1,0:T(8,128)(2,1)S(1)}, u32[]{:S(2)}, u32[]{:S(2)}) collective-permute-start(bf16[68,1024]{1,0:T(8,128)(2,1)} %bitcast.17), channel_id=1, source_target_pairs={{0,4},{4,8},{8,12},{12,0},{1,5},{5,9},{9,13},{13,1},{2,6},{6,10},{... | collective-permute-start | bytes 417800 | tf_op jit(solution)/shard_map/ppermute | solution.py:25
  9.5 18.1 %collective-permute-start.2 = (bf16[68,1024]{1,0:T(8,128)(2,1)}, bf16[68,1024]{1,0:T(8,128)(2,1)S(1)}, u32[]{:S(2)}, u32[]{:S(2)}) collective-permute-start(bf16[68,1024]{1,0:T(8,128)(2,1)} %bitcast.18), channel_id=1, source_target_pairs={{0,12},{4,0},{8,4},{12,8},{1,13},{5,1},{9,5},{13,9},{2,14},{6,2},{... | collective-permute-start | bytes 417800 | tf_op jit(solution)/shard_map/ppermute | solution.py:25
  12.6 0.9 %copy-start = (bf16[1,68,1024]{2,1,0:T(8,128)(2,1)S(1)}, bf16[1,68,1024]{2,1,0:T(8,128)(2,1)}, u32[]{:S(2)}) copy-start(bf16[1,68,1024]{2,1,0:T(8,128)(2,1)} %param.10) | copy-start | bytes 417796
  13.5 0.9 copy-start.2
  14.5 7.3 %collective-permute-start.3 = (bf16[68,1024]{1,0:T(8,128)(2,1)S(1)}, bf16[68,1024]{1,0:T(8,128)(2,1)S(1)}, u32[]{:S(2)}, u32[]{:S(2)}) collective-permute-start(bf16[68,1024]{1,0:T(8,128)(2,1)S(1)} %begin.1.refs_5_), channel_id=1, source_target_pairs={{0,1},{1,2},{2,3},{4,5},{5,6},{6,7},{8,9},{9,10},{10,11},{12,13},{... | collective-permute-start | bytes 417800 | tf_op jit(solution)/shard_map/ppermute | solution.py:20
  19.7 35.9 %collective-permute-start.16 = (bf16[3,64,1024]{2,1,0:T(8,128)(2,1)S(1)}, bf16[3,64,1024]{2,1,0:T(8,128)(2,1)S(1)}, u32[]{:S(2)}, u32[]{:S(2)}) collective-permute-start(bf16[3,64,1024]{2,1,0:T(8,128)(2,1)S(1)} %stack.1), channel_id=1, source_target_pairs={{0,16},{16,0},{1,17},{17,1},{2,18},{18,2},{3,19},{19,3},{4,20},{20... | collective-permute-start | bytes 1179656 | tf_op jit(solution)/shard_map/ppermute | solution.py:25
  21.9 13.0 %collective-permute-start.4 = (bf16[68,1024]{1,0:T(8,128)(2,1)S(1)}, bf16[68,1024]{1,0:T(8,128)(2,1)S(1)}, u32[]{:S(2)}, u32[]{:S(2)}) collective-permute-start(bf16[68,1024]{1,0:T(8,128)(2,1)S(1)} %choose.1.refs_4_), channel_id=1, source_target_pairs={{0,4},{4,8},{8,12},{12,0},{1,5},{5,9},{9,13},{13,1},{2,6},{6,10},{... | collective-permute-start | bytes 417800 | tf_op jit(solution)/shard_map/ppermute | solution.py:25
  24.8 10.0 %collective-permute-start.1 = (bf16[68,1024]{1,0:T(8,128)(2,1)S(1)}, bf16[68,1024]{1,0:T(8,128)(2,1)S(1)}, u32[]{:S(2)}, u32[]{:S(2)}) collective-permute-start(bf16[68,1024]{1,0:T(8,128)(2,1)S(1)} %collective-permute-done.refs_1_), channel_id=1, source_target_pairs={{0,4},{4,8},{8,12},{12,0},{1,5},{5,9},{9,13},{13,1},{2,6},{6,10},{... | collective-permute-start | bytes 417800 | tf_op jit(solution)/shard_map/ppermute | solution.py:25
  24.9 14.8 %collective-permute-start.5 = (bf16[68,1024]{1,0:T(8,128)(2,1)S(1)}, bf16[68,1024]{1,0:T(8,128)(2,1)S(1)}, u32[]{:S(2)}, u32[]{:S(2)}) collective-permute-start(bf16[68,1024]{1,0:T(8,128)(2,1)S(1)} %choose.1.refs_4_), channel_id=1, source_target_pairs={{0,8},{4,12},{8,0},{12,4},{1,9},{5,13},{9,1},{13,5},{2,10},{6,14},... | collective-permute-start | bytes 417800 | tf_op jit(solution)/shard_map/ppermute | solution.py:25
  27.6 12.2 %collective-permute-start.6 = (bf16[68,1024]{1,0:T(8,128)(2,1)S(1)}, bf16[68,1024]{1,0:T(8,128)(2,1)S(1)}, u32[]{:S(2)}, u32[]{:S(2)}) collective-permute-start(bf16[68,1024]{1,0:T(8,128)(2,1)S(1)} %choose.1.refs_4_), channel_id=1, source_target_pairs={{0,12},{4,0},{8,4},{12,8},{1,13},{5,1},{9,5},{13,9},{2,14},{6,2},{... | collective-permute-start | bytes 417800 | tf_op jit(solution)/shard_map/ppermute | solution.py:25
  30.4 9.3 %copy-start.1 = (bf16[1,68,1024]{2,1,0:T(8,128)(2,1)S(1)}, bf16[1,68,1024]{2,1,0:T(8,128)(2,1)}, u32[]{:S(2)}) copy-start(bf16[1,68,1024]{2,1,0:T(8,128)(2,1)} %param.10) | copy-start | bytes 417796
  41.1 6.2 %collective-permute-start.7 = (bf16[176,128]{1,0:T(8,128)(2,1)S(1)}, bf16[176,128]{1,0:T(8,128)(2,1)S(1)}, u32[]{:S(2)}, u32[]{:S(2)}) collective-permute-start(bf16[176,128]{1,0:T(8,128)(2,1)S(1)} %get-tuple-element.30), channel_id=1, source_target_pairs={{0,4},{4,8},{8,12},{12,0},{1,5},{5,9},{9,13},{13,1},{2,6},{6,10},{... | collective-permute-start | bytes 135176 | tf_op jit(solution)/shard_map/ppermute | solution.py:25
  43.9 5.1 %collective-permute-start.8 = (bf16[176,128]{1,0:T(8,128)(2,1)S(1)}, bf16[176,128]{1,0:T(8,128)(2,1)S(1)}, u32[]{:S(2)}, u32[]{:S(2)}) collective-permute-start(bf16[176,128]{1,0:T(8,128)(2,1)S(1)} %get-tuple-element.29.refs_1_), channel_id=1, source_target_pairs={{0,8},{4,12},{8,0},{12,4},{1,9},{5,13},{9,1},{13,5},{2,10},{6,14},... | collective-permute-start | bytes 135176 | tf_op jit(solution)/shard_map/ppermute | solution.py:25
  45.4 4.1 %collective-permute-start.9 = (bf16[176,128]{1,0:T(8,128)(2,1)S(1)}, bf16[176,128]{1,0:T(8,128)(2,1)S(1)}, u32[]{:S(2)}, u32[]{:S(2)}) collective-permute-start(bf16[176,128]{1,0:T(8,128)(2,1)S(1)} %get-tuple-element.30), channel_id=1, source_target_pairs={{0,12},{4,0},{8,4},{12,8},{1,13},{5,1},{9,5},{13,9},{2,14},{6,2},{... | collective-permute-start | bytes 135176 | tf_op jit(solution)/shard_map/ppermute | solution.py:25
  51.2 5.8 %collective-permute-start.10 = (bf16[136,128]{1,0:T(8,128)(2,1)S(1)}, bf16[136,128]{1,0:T(8,128)(2,1)S(1)}, u32[]{:S(2)}, u32[]{:S(2)}) collective-permute-start(bf16[136,128]{1,0:T(8,128)(2,1)S(1)} %attend.2.refs_0_), channel_id=1, source_target_pairs={{0,4},{4,8},{8,12},{12,0},{1,5},{5,9},{9,13},{13,1},{2,6},{6,10},{... | collective-permute-start | bytes 104456 | tf_op jit(solution)/shard_map/ppermute | solution.py:25
  51.8 5.2 %collective-permute-start.11 = (bf16[136,128]{1,0:T(8,128)(2,1)S(1)}, bf16[136,128]{1,0:T(8,128)(2,1)S(1)}, u32[]{:S(2)}, u32[]{:S(2)}) collective-permute-start(bf16[136,128]{1,0:T(8,128)(2,1)S(1)} %attend.2.refs_0_), channel_id=1, source_target_pairs={{0,8},{4,12},{8,0},{12,4},{1,9},{5,13},{9,1},{13,5},{2,10},{6,14},... | collective-permute-start | bytes 104456 | tf_op jit(solution)/shard_map/ppermute | solution.py:25
  54.5 3.9 %collective-permute-start.12 = (bf16[136,128]{1,0:T(8,128)(2,1)S(1)}, bf16[136,128]{1,0:T(8,128)(2,1)S(1)}, u32[]{:S(2)}, u32[]{:S(2)}) collective-permute-start(bf16[136,128]{1,0:T(8,128)(2,1)S(1)} %attend.2.refs_0_), channel_id=1, source_target_pairs={{0,12},{4,0},{8,4},{12,8},{1,13},{5,1},{9,5},{13,9},{2,14},{6,2},{... | collective-permute-start | bytes 104456 | tf_op jit(solution)/shard_map/ppermute | solution.py:25
  58.8 5.9 %collective-permute-start.17 = (bf16[68,1024]{1,0:T(8,128)(2,1)S(1)}, bf16[68,1024]{1,0:T(8,128)(2,1)S(1)}, u32[]{:S(2)}, u32[]{:S(2)}) collective-permute-start(bf16[68,1024]{1,0:T(8,128)(2,1)S(1)} %get-tuple-element.37), channel_id=1, source_target_pairs={{0,2},{1,3},{2,0},{3,1},{4,6},{5,7},{6,4},{7,5},{8,10},{9,11},{10,... | collective-permute-start | bytes 417800 | tf_op jit(solution)/shard_map/ppermute | solution.py:25
  60.4 8.2 %collective-permute-start.27 = (bf16[68,1024]{1,0:T(8,128)(2,1)S(1)}, bf16[68,1024]{1,0:T(8,128)(2,1)S(1)}, u32[]{:S(2)}, u32[]{:S(2)}) collective-permute-start(bf16[68,1024]{1,0:T(8,128)(2,1)S(1)} %get-tuple-element.42), channel_id=1, source_target_pairs={{0,1},{1,2},{2,3},{3,0},{4,5},{5,6},{6,7},{7,4},{8,9},{9,10},{10,1... | collective-permute-start | bytes 417800 | tf_op jit(solution)/shard_map/ppermute | solution.py:25
  64.7 7.2 %collective-permute-start.18 = (bf16[68,1024]{1,0:T(8,128)(2,1)S(1)}, bf16[68,1024]{1,0:T(8,128)(2,1)S(1)}, u32[]{:S(2)}, u32[]{:S(2)}) collective-permute-start(bf16[68,1024]{1,0:T(8,128)(2,1)S(1)} %collective-permute-done.17.refs_0_.refs_5_), channel_id=1, source_target_pairs={{0,4},{4,8},{8,12},{12,0},{1,5},{5,9},{9,13},{13,1},{2,6},{6,10},{... | collective-permute-start | bytes 417800 | tf_op jit(solution)/shard_map/ppermute | solution.py:25
  65.9 10.6 %collective-permute-start.19 = (bf16[68,1024]{1,0:T(8,128)(2,1)S(1)}, bf16[68,1024]{1,0:T(8,128)(2,1)S(1)}, u32[]{:S(2)}, u32[]{:S(2)}) collective-permute-start(bf16[68,1024]{1,0:T(8,128)(2,1)S(1)} %collective-permute-done.17.refs_0_.refs_5_), channel_id=1, source_target_pairs={{0,8},{4,12},{8,0},{12,4},{1,9},{5,13},{9,1},{13,5},{2,10},{6,14},... | collective-permute-start | bytes 417800 | tf_op jit(solution)/shard_map/ppermute | solution.py:25
  68.1 8.3 %collective-permute-start.20 = (bf16[68,1024]{1,0:T(8,128)(2,1)S(1)}, bf16[68,1024]{1,0:T(8,128)(2,1)S(1)}, u32[]{:S(2)}, u32[]{:S(2)}) collective-permute-start(bf16[68,1024]{1,0:T(8,128)(2,1)S(1)} %collective-permute-done.17.refs_0_.refs_5_), channel_id=1, source_target_pairs={{0,12},{4,0},{8,4},{12,8},{1,13},{5,1},{9,5},{13,9},{2,14},{6,2},{... | collective-permute-start | bytes 417800 | tf_op jit(solution)/shard_map/ppermute | solution.py:25
  69.7 20.4 %collective-permute-start.28 = (bf16[68,1024]{1,0:T(8,128)(2,1)S(1)}, bf16[68,1024]{1,0:T(8,128)(2,1)S(1)}, u32[]{:S(2)}, u32[]{:S(2)}) collective-permute-start(bf16[68,1024]{1,0:T(8,128)(2,1)S(1)} %get-tuple-element.43), channel_id=1, source_target_pairs={{0,1},{1,2},{2,3},{4,5},{5,6},{6,7},{8,9},{9,10},{10,11},{12,13},{... | collective-permute-start | bytes 417800 | tf_op jit(solution)/shard_map/ppermute | solution.py:20
  77.3 5.7 %collective-permute-start.21 = (bf16[88,128]{1,0:T(8,128)(2,1)S(1)}, bf16[88,128]{1,0:T(8,128)(2,1)S(1)}, u32[]{:S(2)}, u32[]{:S(2)}) collective-permute-start(bf16[88,128]{1,0:T(8,128)(2,1)S(1)} %get-tuple-element.40), channel_id=1, source_target_pairs={{0,4},{4,8},{8,12},{12,0},{1,5},{5,9},{9,13},{13,1},{2,6},{6,10},{... | collective-permute-start | bytes 67592 | tf_op jit(solution)/shard_map/ppermute | solution.py:25
  79.5 4.7 %collective-permute-start.22 = (bf16[88,128]{1,0:T(8,128)(2,1)S(1)}, bf16[88,128]{1,0:T(8,128)(2,1)S(1)}, u32[]{:S(2)}, u32[]{:S(2)}) collective-permute-start(bf16[88,128]{1,0:T(8,128)(2,1)S(1)} %get-tuple-element.39.refs_1_), channel_id=1, source_target_pairs={{0,8},{4,12},{8,0},{12,4},{1,9},{5,13},{9,1},{13,5},{2,10},{6,14},... | collective-permute-start | bytes 67592 | tf_op jit(solution)/shard_map/ppermute | solution.py:25
  80.6 3.9 %collective-permute-start.23 = (bf16[88,128]{1,0:T(8,128)(2,1)S(1)}, bf16[88,128]{1,0:T(8,128)(2,1)S(1)}, u32[]{:S(2)}, u32[]{:S(2)}) collective-permute-start(bf16[88,128]{1,0:T(8,128)(2,1)S(1)} %get-tuple-element.40), channel_id=1, source_target_pairs={{0,12},{4,0},{8,4},{12,8},{1,13},{5,1},{9,5},{13,9},{2,14},{6,2},{... | collective-permute-start | bytes 67592 | tf_op jit(solution)/shard_map/ppermute | solution.py:25
  85.3 5.6 %collective-permute-start.24 = (bf16[68,128]{1,0:T(8,128)(2,1)S(1)}, bf16[68,128]{1,0:T(8,128)(2,1)S(1)}, u32[]{:S(2)}, u32[]{:S(2)}) collective-permute-start(bf16[68,128]{1,0:T(8,128)(2,1)S(1)} %attend.3.refs_0_), channel_id=1, source_target_pairs={{0,4},{4,8},{8,12},{12,0},{1,5},{5,9},{9,13},{13,1},{2,6},{6,10},{... | collective-permute-start | bytes 52232 | tf_op jit(solution)/shard_map/ppermute | solution.py:25
  86.5 4.7 %collective-permute-start.25 = (bf16[68,128]{1,0:T(8,128)(2,1)S(1)}, bf16[68,128]{1,0:T(8,128)(2,1)S(1)}, u32[]{:S(2)}, u32[]{:S(2)}) collective-permute-start(bf16[68,128]{1,0:T(8,128)(2,1)S(1)} %attend.3.refs_0_), channel_id=1, source_target_pairs={{0,8},{4,12},{8,0},{12,4},{1,9},{5,13},{9,1},{13,5},{2,10},{6,14},... | collective-permute-start | bytes 52232 | tf_op jit(solution)/shard_map/ppermute | solution.py:25
  89.1 3.8 %collective-permute-start.26 = (bf16[68,128]{1,0:T(8,128)(2,1)S(1)}, bf16[68,128]{1,0:T(8,128)(2,1)S(1)}, u32[]{:S(2)}, u32[]{:S(2)}) collective-permute-start(bf16[68,128]{1,0:T(8,128)(2,1)S(1)} %attend.3.refs_0_), channel_id=1, source_target_pairs={{0,12},{4,0},{8,4},{12,8},{1,13},{5,1},{9,5},{13,9},{2,14},{6,2},{... | collective-permute-start | bytes 52232 | tf_op jit(solution)/shard_map/ppermute | solution.py:25
